TPU v7x, 512 devices: a whole 4x8x8 slice. The times are simulated.
512 devices in a mesh: vintage: 16 (over y, core), inline: 4 (over z_hi), xline: 8 (over z_lo, x).
Axes of the slice: x: 4, y: 8, z: 8 (z_hi: 4, z_lo: 2; z = z_hi * 2 + z_lo), core: 2. Of those that a mesh axis runs over, the one named last changes fastest.
Arguments:
- amplitude: float32 [16, 32, 128, 256], P('vintage', 'inline', 'xline'), may hold values from -6 to 6
- inline_slope: int32 [16, 32, 128], P('vintage', 'inline', 'xline'), may hold values from -2 to 2
- crossline_slope: int32 [16, 32, 128], P('vintage', 'inline', 'xline'), may hold values from -2 to 2
Outputs:
- semblance: float32 [16, 32, 128, 256], P('vintage', 'inline', 'xline')
- lag_correl: float32 [16, 32, 128, 264], P('vintage', 'inline', 'xline')
All inputs are finite; a program needn't handle non-finite values.
Results may differ from a plain program's by a relative error of at most 0.0003.
Values sent between devices are 32-bit elements; how exact they have to be, the bound alone decides.
No kernel may reach another device: no remote copies, remote signals or barrier semaphores. Data moves between devices by JAX's collectives and lax.ppermute only.
A program may use at most 64 MiB of HBM per device.

v0:
```python
import jax
import jax.numpy as jnp
from jax import lax
from jax.sharding import PartitionSpec as P

TIME_SAMPLES = 256
MAX_DIP_STEP = 2
RT = 4
LAGS = 33
NWIN = 8


EPS = 1e-06


def padded_2(block, sides, width):
    for axis, dim in sides:
        count = lax.axis_size(axis)
        forward = [(i, i + 1) for i in range(count - 1)]
        backward = [(target, source) for source, target in forward]
        low = lax.ppermute(
            lax.slice_in_dim(block, block.shape[dim] - width, None, axis=dim), axis, forward
        )
        high = lax.ppermute(lax.slice_in_dim(block, 0, width, axis=dim), axis, backward)
        block = jnp.concatenate([low, block, high], axis=dim)
    return block


def from_root(shard, axis, root):
    mine = lax.axis_index(axis) == root
    return lax.psum(jnp.where(mine, shard, jnp.zeros_like(shard)), axis)


def attribute_padded(padded, dip_il, dip_xl):
    inner_i = padded.shape[0] - 2
    inner_x = padded.shape[1] - 2
    padding = 2 * MAX_DIP_STEP + RT
    extent = TIME_SAMPLES + 2 * RT
    stack = jnp.zeros((inner_i, inner_x, extent), jnp.float32)
    power = jnp.zeros((inner_i, inner_x, extent), jnp.float32)
    for row_step in (-1, 0, 1):
        for col_step in (-1, 0, 1):
            neighbor = padded[
                1 + row_step : 1 + row_step + inner_i, 1 + col_step : 1 + col_step + inner_x, :
            ]
            shift_map = row_step * dip_il + col_step * dip_xl
            reach = (abs(row_step) + abs(col_step)) * MAX_DIP_STEP
            moved = jnp.zeros((inner_i, inner_x, extent), jnp.float32)
            for offset_value in range(-reach, reach + 1):
                start = padding - RT + offset_value
                shifted = neighbor[:, :, start : start + extent]
                moved = jnp.where((shift_map == offset_value)[:, :, None], shifted, moved)
            stack = stack + moved
            power = power + moved * moved
    numer = jnp.zeros((inner_i, inner_x, TIME_SAMPLES), jnp.float32)
    denom = jnp.zeros((inner_i, inner_x, TIME_SAMPLES), jnp.float32)
    for window_step in range(2 * RT + 1):
        piece = stack[:, :, window_step : window_step + TIME_SAMPLES]
        numer = numer + piece * piece
        denom = denom + power[:, :, window_step : window_step + TIME_SAMPLES]
    semb = numer / (9.0 * denom + EPS)
    attr = semb * stack[:, :, RT : RT + TIME_SAMPLES] / 9.0
    return (semb, attr)


def time_pad(volume):
    padding = 2 * MAX_DIP_STEP + RT
    return jnp.pad(volume, ((0, 0), (0, 0), (padding, padding)))


def correlate(monitor, baseline):
    half_lags = LAGS // 2
    inner_i, inner_x = (monitor.shape[0], monitor.shape[1])
    base_pad = jnp.pad(baseline, ((0, 0), (0, 0), (half_lags, half_lags)))
    mon_energy = jnp.sum(monitor * monitor, axis=-1)
    base_energy = jnp.sum(baseline * baseline, axis=-1)
    factor = NWIN / jnp.sqrt(mon_energy * base_energy + EPS)
    columns = []
    for lag_index in range(LAGS):
        product = monitor * base_pad[:, :, lag_index : lag_index + TIME_SAMPLES]
        columns.append(
            jnp.sum(product.reshape(inner_i, inner_x, NWIN, TIME_SAMPLES // NWIN), axis=-1)
        )
    result = jnp.stack(columns, axis=2) * factor[:, :, None, None]
    return result.reshape(inner_i, inner_x, LAGS * NWIN)


def per_device(amplitude, inline_slope, crossline_slope):
    volume = amplitude[0]
    dips_il = inline_slope[0]
    dips_xl = crossline_slope[0]
    rimmed = padded_2(volume, (("inline", 0), ("xline", 1)), 1)
    semb, attr = attribute_padded(time_pad(rimmed), dips_il, dips_xl)
    base_attr = from_root(attr, "vintage", 0)
    correl = correlate(attr, base_attr)
    return (semb[None], correl[None])


def solution(mesh):
    return jax.shard_map(
        per_device,
        mesh=mesh,
        in_specs=(
            P("vintage", "inline", "xline", None),
            P("vintage", "inline", "xline"),
            P("vintage", "inline", "xline"),
        ),
        out_specs=(P("vintage", "inline", "xline", None), P("vintage", "inline", "xline", None)),
        check_vma=False,
    )
```

profile of v0, /device:TPU:1, one launch (start us, length us, event | category | flops | bytes accessed | tf_op | source)
XLA Modules:
  0.0 229.0 jit_solution(9999033739140127602)
XLA Ops:
  8.0 6.6 %collective-permute-start = (f32[1,16,256]{2,1,0:T(8,128)S(1)}, f32[1,16,256]{2,1,0:T(8,128)S(1)}, u32[]{:S(2)}, u32[]{:S(2)}) collective-permute-start(f32[1,16,256]{2,1,0:T(8,128)S(1)} %get-tuple-element.64), channel_id=1, source_target_pairs={{0,8},{8,16},{16,24},{1,9},{9,17},{17,25},{2,10},{10,18},{18,26},{... | collective-permute-start | bytes 49160 | tf_op jit(solution)/shard_map/ppermute | solution.py:21
  14.6 1.3 collective-permute-start.1
  16.7 6.0 %collective-permute-done.1 = f32[1,16,256]{2,1,0:T(8,128)S(1)} collective-permute-done((f32[1,16,256]{2,1,0:T(8,128)S(1)}, f32[1,16,256]{2,1,0:T(8,128)S(1)}, u32[]{:S(2)}, u32[]{:S(2)}) %collective-permute-start.1) | collective-permute-done | bytes 16416 | tf_op jit(solution)/shard_map/ppermute | solution.py:24
  22.7 0.9 pad_maximum_fusion.2
  23.6 3.1 %collective-permute-start.2 = (f32[10,1,256]{2,1,0:T(1,128)S(1)}, f32[10,1,256]{2,1,0:T(1,128)S(1)}, u32[]{:S(2)}, u32[]{:S(2)}) collective-permute-start(f32[10,1,256]{2,1,0:T(1,128)S(1)} %get-tuple-element.61), channel_id=1, source_target_pairs={{0,1},{1,2},{2,3},{3,4},{4,5},{5,6},{6,7},{8,9},{9,10},{10,11},{11... | collective-permute-start | bytes 30728 | tf_op jit(solution)/shard_map/ppermute | solution.py:21
  26.7 1.3 collective-permute-start.3
  28.1 3.1 %collective-permute-done.3 = f32[10,1,256]{2,1,0:T(1,128)S(1)} collective-permute-done((f32[10,1,256]{2,1,0:T(1,128)S(1)}, f32[10,1,256]{2,1,0:T(1,128)S(1)}, u32[]{:S(2)}, u32[]{:S(2)}) %collective-permute-start.3) | collective-permute-done | bytes 10272 | tf_op jit(solution)/shard_map/ppermute | solution.py:24
  31.2 1.1 select_maximum_fusion
  32.3 4.3 %add_add_fusion = (f32[8,16,264]{2,1,0:T(8,128)S(1)}, f32[8,16,264]{2,1,0:T(8,128)S(1)}, f32[8,16,264]{2,1,0:T(8,128)S(1)}, f32[8,16,264]{2,1,0:T(8,128)S(1)}, f...) fusion(f32[10,18,272]{2,1,0:T(8,128)S(1)} %select_maximum_fusio, ...), kind=kLoop, calls=%fused_computation.97 | loop fusion | flops 2162688 | bytes 8928256 | tf_op jit(solution)/shard_map/add | solution.py:53
  36.7 1.3 multiply_reduce_fusion.1
  38.7 117.5 %all-reduce.4.cloned.1.call-done = f32[8,16,256]{2,1,0:T(8,128)} async-done(((f32[8,16,256]{2,1,0:T(8,128)}), f32[8,16,256]{2,1,0:T(8,128)}) %all-reduce.4.cloned.1.call-update) | async-done | bytes 131088 | tf_op jit(solution)/shard_map/psum | solution.py:31
  156.2 3.0 %fusion.63 = (f32[8,16,256]{2,1,0:T(8,128)S(1)}, f32[8,16,256]{2,1,0:T(8,128)S(1)}, f32[8,16,256]{2,1,0:T(8,128)S(1)}, f32[8,16,256]{2,1,0:T(8,128)S(1)}, f32[8,...) fusion(f32[8,16,256]{2,1,0:T(8,128)S(1)} %get-tuple-element.9, ...), kind=kLoop, calls=%fused_computation.112 | loop fusion | flops 556928 | bytes 2228736 | tf_op jit(solution)/shard_map/mul | solution.py:80
  159.8 0.8 reduce_sum.328
  160.8 0.8 reduce_sum.327
  161.8 0.8 reduce_sum.326
  162.8 0.8 reduce_sum.325
  164.8 0.8 reduce_sum.323
  165.8 0.8 reduce_sum.322
  166.8 0.8 reduce_sum.321
  167.8 0.8 reduce_sum.320
  168.8 0.8 reduce_sum.319
  171.8 0.8 reduce_sum.316
  173.0 1.8 fusion.80
  174.8 1.1 reshape.509
  175.8 0.8 reduce_sum.347
  176.7 1.1 reshape.508
  178.6 1.1 reshape.507
  180.5 1.1 reshape.506
  182.4 1.1 reshape.505
  183.4 0.8 reduce_sum.343
  184.3 1.1 reshape.504
  185.3 0.8 reduce_sum.342
  186.2 1.1 reshape.503
  188.1 1.1 reshape.502
  190.0 1.1 reshape.501
  191.9 1.1 reshape.500
  193.8 1.1 reshape.499
  194.9 0.8 reduce_sum.337
  195.7 1.1 reshape.498
  197.8 0.8 reduce_sum.335
  198.8 0.8 reduce_sum.334
  199.8 0.8 reduce_sum.333
  202.9 0.8 reduce_sum.330
  203.7 0.9 constant_dynamic-update-slice_fusion.31
  204.6 0.8 constant_dynamic-update-slice_fusion.30
  205.4 0.8 constant_dynamic-update-slice_fusion.29
  206.3 0.8 constant_dynamic-update-slice_fusion.28
  207.1 0.8 constant_dynamic-update-slice_fusion.27
  208.0 0.8 constant_dynamic-update-slice_fusion.26
  208.8 0.8 constant_dynamic-update-slice_fusion.25
  209.8 0.8 constant_dynamic-update-slice_fusion.17
  210.6 0.8 constant_dynamic-update-slice_fusion.16
  211.5 0.8 constant_dynamic-update-slice_fusion.15
  212.3 0.8 constant_dynamic-update-slice_fusion.14
  213.2 0.8 constant_dynamic-update-slice_fusion.13
  214.0 0.8 constant_dynamic-update-slice_fusion.12
  214.9 0.8 constant_dynamic-update-slice_fusion.11
  215.7 0.8 constant_dynamic-update-slice_fusion.10
  216.6 0.8 constant_dynamic-update-slice_fusion.9
  217.4 0.8 constant_dynamic-update-slice_fusion.8
  218.2 0.8 constant_dynamic-update-slice_fusion.7
  219.1 0.8 constant_dynamic-update-slice_fusion.6
  220.1 0.9 copy.41
  221.0 1.1 copy.42
  (88 shorter events, 17.3 us)
Async XLA Ops:
  7.2 149.1 %all-reduce.4.cloned.1.call-start = ((), (), s32[]{:S(2)}) async-start(), calls=%async_computation | async-start | bytes 262144 | tf_op jit(solution)/shard_map/psum | solution.py:31
  8.0 8.7 %collective-permute-start = (f32[1,16,256]{2,1,0:T(8,128)S(1)}, f32[1,16,256]{2,1,0:T(8,128)S(1)}, u32[]{:S(2)}, u32[]{:S(2)}) collective-permute-start(f32[1,16,256]{2,1,0:T(8,128)S(1)} %get-tuple-element.64), channel_id=1, source_target_pairs={{0,8},{8,16},{16,24},{1,9},{9,17},{17,25},{2,10},{10,18},{18,26},{... | collective-permute-start | bytes 49160 | tf_op jit(solution)/shard_map/ppermute | solution.py:21
  14.6 8.1 %collective-permute-start.1 = (f32[1,16,256]{2,1,0:T(8,128)S(1)}, f32[1,16,256]{2,1,0:T(8,128)S(1)}, u32[]{:S(2)}, u32[]{:S(2)}) collective-permute-start(f32[1,16,256]{2,1,0:T(8,128)S(1)} %get-tuple-element.65), channel_id=1, source_target_pairs={{8,0},{16,8},{24,16},{9,1},{17,9},{25,17},{10,2},{18,10},{26,18},{... | collective-permute-start | bytes 49160 | tf_op jit(solution)/shard_map/ppermute | solution.py:24
  23.6 4.5 %collective-permute-start.2 = (f32[10,1,256]{2,1,0:T(1,128)S(1)}, f32[10,1,256]{2,1,0:T(1,128)S(1)}, u32[]{:S(2)}, u32[]{:S(2)}) collective-permute-start(f32[10,1,256]{2,1,0:T(1,128)S(1)} %get-tuple-element.61), channel_id=1, source_target_pairs={{0,1},{1,2},{2,3},{3,4},{4,5},{5,6},{6,7},{8,9},{9,10},{10,11},{11... | collective-permute-start | bytes 30728 | tf_op jit(solution)/shard_map/ppermute | solution.py:21
  26.7 4.4 %collective-permute-start.3 = (f32[10,1,256]{2,1,0:T(1,128)S(1)}, f32[10,1,256]{2,1,0:T(1,128)S(1)}, u32[]{:S(2)}, u32[]{:S(2)}) collective-permute-start(f32[10,1,256]{2,1,0:T(1,128)S(1)} %get-tuple-element.62), channel_id=1, source_target_pairs={{1,0},{2,1},{3,2},{4,3},{5,4},{6,5},{7,6},{9,8},{10,9},{11,10},{12... | collective-permute-start | bytes 30728 | tf_op jit(solution)/shard_map/ppermute | solution.py:24
  169.8 3.2 %copy-start = (f32[8,16,256]{2,1,0:T(8,128)S(1)}, f32[8,16,256]{2,1,0:T(8,128)}, u32[]{:S(2)}) copy-start(f32[8,16,256]{2,1,0:T(8,128)} %all-reduce.4.cloned.1.call-done) | copy-start | bytes 393220
  200.8 8.9 %copy-start.8 = (f32[8,16,8]{2,1,0:T(8,128)S(1)}, f32[8,16,8]{2,1,0:T(8,128)}, u32[]{:S(2)}) copy-start(f32[8,16,8]{2,1,0:T(8,128)} %reduce_sum.323) | copy-start | bytes 12292
  200.8 8.9 %copy-start.6 = (f32[8,16,8]{2,1,0:T(8,128)S(1)}, f32[8,16,8]{2,1,0:T(8,128)}, u32[]{:S(2)}) copy-start(f32[8,16,8]{2,1,0:T(8,128)} %reduce_sum.324) | copy-start | bytes 12292
  200.8 8.9 %copy-start.4 = (f32[8,16,8]{2,1,0:T(8,128)S(1)}, f32[8,16,8]{2,1,0:T(8,128)}, u32[]{:S(2)}) copy-start(f32[8,16,8]{2,1,0:T(8,128)} %reduce_sum.325) | copy-start | bytes 12292
  200.8 8.9 %copy-start.3 = (f32[8,16,8]{2,1,0:T(8,128)S(1)}, f32[8,16,8]{2,1,0:T(8,128)}, u32[]{:S(2)}) copy-start(f32[8,16,8]{2,1,0:T(8,128)} %reduce_sum.326) | copy-start | bytes 12292
  200.8 8.9 %copy-start.2 = (f32[8,16,8]{2,1,0:T(8,128)S(1)}, f32[8,16,8]{2,1,0:T(8,128)}, u32[]{:S(2)}) copy-start(f32[8,16,8]{2,1,0:T(8,128)} %reduce_sum.327) | copy-start | bytes 12292
  201.6 8.1 %copy-start.1 = (f32[8,16,8]{2,1,0:T(8,128)S(1)}, f32[8,16,8]{2,1,0:T(8,128)}, u32[]{:S(2)}) copy-start(f32[8,16,8]{2,1,0:T(8,128)} %reduce_sum.328) | copy-start | bytes 12292
  202.8 17.1 %copy-start.12 = (f32[8,16,8]{2,1,0:T(8,128)S(1)}, f32[8,16,8]{2,1,0:T(8,128)}, u32[]{:S(2)}) copy-start(f32[8,16,8]{2,1,0:T(8,128)} %reduce_sum.342) | copy-start | bytes 12292
  202.8 17.1 %copy-start.11 = (f32[8,16,8]{2,1,0:T(8,128)S(1)}, f32[8,16,8]{2,1,0:T(8,128)}, u32[]{:S(2)}) copy-start(f32[8,16,8]{2,1,0:T(8,128)} %reduce_sum.343) | copy-start | bytes 12292
  202.8 17.1 %copy-start.10 = (f32[8,16,8]{2,1,0:T(8,128)S(1)}, f32[8,16,8]{2,1,0:T(8,128)}, u32[]{:S(2)}) copy-start(f32[8,16,8]{2,1,0:T(8,128)} %reduce_sum.344) | copy-start | bytes 12292
  202.8 17.2 %copy-start.9 = (f32[8,16,8]{2,1,0:T(8,128)S(1)}, f32[8,16,8]{2,1,0:T(8,128)}, u32[]{:S(2)}) copy-start(f32[8,16,8]{2,1,0:T(8,128)} %reduce_sum.345) | copy-start | bytes 12292
  202.8 17.2 %copy-start.7 = (f32[8,16,8]{2,1,0:T(8,128)S(1)}, f32[8,16,8]{2,1,0:T(8,128)}, u32[]{:S(2)}) copy-start(f32[8,16,8]{2,1,0:T(8,128)} %reduce_sum.346) | copy-start | bytes 12292
  203.7 16.3 %copy-start.5 = (f32[8,16,8]{2,1,0:T(8,128)S(1)}, f32[8,16,8]{2,1,0:T(8,128)}, u32[]{:S(2)}) copy-start(f32[8,16,8]{2,1,0:T(8,128)} %reduce_sum.347) | copy-start | bytes 12292
Sparse Core Ops, SparseCore 0:
  38.8 117.3 all-reduce.3
where the time goes:
time: 230 us; the launch traced here: 229 us
  waiting for transfers between devices  127 us (55%)
  other arithmetic  40.2 us (17%)
  local copies, waits for them, and re-layouts  35.2 us (15%)
  between operations  14.5 us (6%)
  starting transfers between devices  12.4 us (5%)
    psum x1, waiting for transfers between devices, from_root(): return lax.psum(jnp.where(mine, shard, jnp.zeros_like(shard)), axis)  118 us
    reduce_sum x33, other arithmetic, correlate(): jnp.sum(product.reshape(inner_i, inner_x, NWIN, TIME_SAMPLES // NWIN), ax...  26.2 us
    unnamed x59, local copies, waits for them, and re-layouts  17.3 us
    reshape x33, local copies, waits for them, and re-layouts, correlate(): product.reshape(inner_i, inner_x, NWIN, TIME_SAMPLES // NWIN)  16.2 us
    ppermute x2, starting transfers between devices, padded_2(): lax.ppermute(lax.slice_in_dim(block, block.shape[dim] - width, None, axis...  9.74 us
    ppermute x2, waiting for transfers between devices, padded_2(): lax.ppermute(lax.slice_in_dim(block, 0, width, axis=dim), axis, backward)  9.12 us
    mul x2, other arithmetic, correlate(): product = monitor * base_pad[:, :, lag_index:lag_index + TIME_SAMPLES]  4.74 us
  transfers between devices with their start and end apart: 5, of which 3 were waited for; matrix products, arithmetic and copies ran while one was open for 0% of the time, Pallas kernels for 0%

commit v1 on v0

v1 whole, which is shorter than its diff:
```python
import jax
import jax.numpy as jnp
from jax import lax
from jax.experimental import pallas as pl
from jax.experimental.pallas import tpu as pltpu
from jax.sharding import PartitionSpec as P

TIME_SAMPLES = 256
MAX_DIP_STEP = 2
RT = 4
LAGS = 33
NWIN = 8
EPS = 1e-06

ROWS = 8
COLS = 16
TRACES = ROWS * COLS
PAD = 16
STEPS = (-1, 0, 1)


def steered(ref, lead, row, count, sign, dip):
    out = ref[lead, pl.ds(row, count), :]
    for k in range(-MAX_DIP_STEP, MAX_DIP_STEP + 1):
        if k:
            out = jnp.where(dip == k, ref[lead, pl.ds(row + sign * k, count), :], out)
    return out


def attr_kernel(tile, up, down, left, right, dip_il, dip_xl, semb_out, attr_out,
                rim, moved, inner, sums, three):
    rim[1:ROWS + 1, 1:COLS + 1, :] = tile[...]
    rim[0, 1:COLS + 1, :] = up[0]
    rim[ROWS + 1, 1:COLS + 1, :] = down[0]
    rim[:, 0:1, :] = left[...]
    rim[:, COLS + 1:COLS + 2, :] = right[...]
    zeros = jnp.zeros((PAD, TRACES), jnp.float32)
    for a in STEPS:
        for b in STEPS:
            n = 3 * (a + 1) + b + 1
            block = rim[1 + a:1 + a + ROWS, 1 + b:1 + b + COLS, :].reshape(TRACES, TIME_SAMPLES)
            moved[n, 0:PAD, :] = zeros
            moved[n, PAD + TIME_SAMPLES:, :] = zeros
            moved[n, PAD:PAD + TIME_SAMPLES, :] = block.T
    q = jnp.broadcast_to(dip_xl[...], (8, TRACES))
    p = jnp.broadcast_to(dip_il[...], (8, TRACES))
    for r in range(0, TIME_SAMPLES + 16, 8):
        for a in STEPS:
            n = 3 * (a + 1) + 1
            mid = moved[n, pl.ds(r + 8, 8), :]
            lo = steered(moved, n - 1, r + 8, 8, -1, q)
            hi = steered(moved, n + 1, r + 8, 8, 1, q)
            inner[2 * (a + 1), pl.ds(r, 8), :] = lo + mid + hi
            inner[2 * (a + 1) + 1, pl.ds(r, 8), :] = lo * lo + mid * mid + hi * hi
    for r in range(0, TIME_SAMPLES + 8, 8):
        total = []
        for part in (0, 1):
            total.append(
                inner[2 + part, pl.ds(r + 4, 8), :]
                + steered(inner, part, r + 4, 8, -1, p)
                + steered(inner, 4 + part, r + 4, 8, 1, p)
            )
        sums[0, pl.ds(r, 8), :] = total[0]
        sums[1, pl.ds(r, 8), :] = total[0] * total[0]
        sums[2, pl.ds(r, 8), :] = total[1]
    for r in range(0, TIME_SAMPLES, 8):
        numer = sums[1, pl.ds(r, 8), :]
        denom = sums[2, pl.ds(r, 8), :]
        for s in range(1, 2 * RT + 1):
            numer = numer + sums[1, pl.ds(r + s, 8), :]
            denom = denom + sums[2, pl.ds(r + s, 8), :]
        semb = numer / (9.0 * denom + EPS)
        three[pl.ds(r, 8), :] = semb
        attr_out[pl.ds(r, 8), :] = semb * sums[0, pl.ds(r + RT, 8), :] * (1.0 / 9.0)
    semb_out[...] = three[...].T.reshape(ROWS, COLS, TIME_SAMPLES)


def pair_sum(x, y, half, low):
    return jnp.where(low, x, pltpu.roll(y, half, 0)) + jnp.where(low, pltpu.roll(x, 8 - half, 0), y)


def correl_kernel(mon, own, far1, far2, far3, out, base, result):
    half_lags = LAGS // 2
    leader = lax.rem(lax.axis_index("vintage"), 4) == 0
    zeros = jnp.zeros((half_lags, TRACES), jnp.float32)
    base[0:half_lags, :] = zeros
    base[half_lags + TIME_SAMPLES:, :] = zeros

    @pl.when(leader)
    def _():
        base[half_lags:half_lags + TIME_SAMPLES, :] = own[...]

    @pl.when(jnp.logical_not(leader))
    def _():
        base[half_lags:half_lags + TIME_SAMPLES, :] = far1[...] + far2[...] + far3[...]

    mon_energy = jnp.zeros((8, TRACES), jnp.float32)
    base_energy = jnp.zeros((8, TRACES), jnp.float32)
    for r in range(0, TIME_SAMPLES, 8):
        m = mon[pl.ds(r, 8), :]
        b = base[pl.ds(half_lags + r, 8), :]
        mon_energy = mon_energy + m * m
        base_energy = base_energy + b * b
    mon_energy = jnp.sum(mon_energy, axis=0, keepdims=True)
    base_energy = jnp.sum(base_energy, axis=0, keepdims=True)
    factor = NWIN / jnp.sqrt(mon_energy * base_energy + EPS)
    sub = lax.broadcasted_iota(jnp.int32, (8, TRACES), 0)
    width = TIME_SAMPLES // NWIN
    for lag in range(LAGS):
        level = []
        for w in range(NWIN):
            acc = None
            for r in range(w * width, (w + 1) * width, 8):
                term = mon[pl.ds(r, 8), :] * base[pl.ds(r + lag, 8), :]
                acc = term if acc is None else acc + term
            level.append(acc)
        level = [pair_sum(level[w], level[w + 4], 4, sub < 4) for w in range(4)]
        level = [pair_sum(level[w], level[w + 2], 2, (sub & 2) == 0) for w in range(2)]
        row = pair_sum(level[0], level[1], 1, (sub & 1) == 0)
        result[pl.ds(lag * 8, 8), :] = row * factor
    out[...] = result[...].T.reshape(ROWS, COLS, LAGS * NWIN)


def vmem(n):
    return [pl.BlockSpec(memory_space=pltpu.VMEM)] * n


def attributes(tile, up, down, left, right, dip_il, dip_xl):
    return pl.pallas_call(
        attr_kernel,
        out_shape=(
            jax.ShapeDtypeStruct((ROWS, COLS, TIME_SAMPLES), jnp.float32),
            jax.ShapeDtypeStruct((TIME_SAMPLES, TRACES), jnp.float32),
        ),
        in_specs=vmem(7),
        out_specs=tuple(vmem(2)),
        scratch_shapes=[
            pltpu.VMEM((ROWS + 2, COLS + 8, TIME_SAMPLES), jnp.float32),
            pltpu.VMEM((9, TIME_SAMPLES + 2 * PAD, TRACES), jnp.float32),
            pltpu.VMEM((6, TIME_SAMPLES + 16, TRACES), jnp.float32),
            pltpu.VMEM((3, TIME_SAMPLES + 8, TRACES), jnp.float32),
            pltpu.VMEM((TIME_SAMPLES, TRACES), jnp.float32),
        ],
        compiler_params=pltpu.CompilerParams(vmem_limit_bytes=16 << 20),
        name="attributes",
    )(tile, up, down, left, right, dip_il, dip_xl)


def correlate(mon, own, far):
    return pl.pallas_call(
        correl_kernel,
        out_shape=jax.ShapeDtypeStruct((ROWS, COLS, LAGS * NWIN), jnp.float32),
        in_specs=vmem(5),
        out_specs=pl.BlockSpec(memory_space=pltpu.VMEM),
        scratch_shapes=[
            pltpu.VMEM((TIME_SAMPLES + LAGS - 1, TRACES), jnp.float32),
            pltpu.VMEM((LAGS * NWIN, TRACES), jnp.float32),
        ],
        compiler_params=pltpu.CompilerParams(vmem_limit_bytes=16 << 20),
        name="correlate",
    )(mon, own, *far)


def neighbours(block, axis, dim):
    count = lax.axis_size(axis)
    forward = [(i, i + 1) for i in range(count - 1)]
    backward = [(target, source) for source, target in forward]
    low = lax.ppermute(lax.slice_in_dim(block, block.shape[dim] - 1, None, axis=dim), axis, forward)
    high = lax.ppermute(lax.slice_in_dim(block, 0, 1, axis=dim), axis, backward)
    return low, high


def per_device(amplitude, inline_slope, crossline_slope):
    tile = amplitude[0]
    dip_il = inline_slope.reshape(1, TRACES)
    dip_xl = crossline_slope.reshape(1, TRACES)
    up, down = neighbours(tile, "inline", 0)
    left, right = neighbours(jnp.concatenate([up, tile, down], axis=0), "xline", 1)
    semb, attr = attributes(tile, up, down, left, right, dip_il, dip_xl)
    got = [lax.ppermute(attr, "vintage", [(0, k)]) for k in (8, 4, 12)]
    first = lax.axis_index("vintage") == 0
    own = jnp.where(first, attr, got[0] + got[1] + got[2])
    far = [lax.ppermute(own, "vintage", [(s, s + k) for s in (0, 4, 8, 12)]) for k in (3, 2, 1)]
    correl = correlate(attr, own, far)
    return (semb[None], correl[None])


def solution(mesh):
    return jax.shard_map(
        per_device,
        mesh=mesh,
        in_specs=(
            P("vintage", "inline", "xline", None),
            P("vintage", "inline", "xline"),
            P("vintage", "inline", "xline"),
        ),
        out_specs=(P("vintage", "inline", "xline", None), P("vintage", "inline", "xline", None)),
        check_vma=False,
    )
```

time: 230 us -> 47.9 us (0.21)
  the two profiles are of different devices: /device:TPU:1 before, /device:TPU:233 now
where the time goes in v1:
time: 47.9 us; the launch traced here: 47.5 us
  waiting for transfers between devices  23.2 us (48%)
  starting transfers between devices  19 us (40%)
  Pallas kernels  2.68 us (6%)
  local copies, waits for them, and re-layouts  0.96 us (2%)
  other arithmetic  0.93 us (2%)
  between operations  0.81 us (2%)
    ppermute x3, waiting for transfers between devices, per_device(): lax.ppermute(own, 'vintage', [(s, s + k) for s in (0, 4, 8, 12)])  17.9 us
    ppermute x2, starting transfers between devices, neighbours(): lax.ppermute(lax.slice_in_dim(block, block.shape[dim] - 1, None, axis=dim...  8.04 us
    ppermute x2, starting transfers between devices, neighbours(): high = lax.ppermute(lax.slice_in_dim(block, 0, 1, axis=dim), axis, backward)  6.28 us
    ppermute x2, waiting for transfers between devices, neighbours(): lax.ppermute(lax.slice_in_dim(block, block.shape[dim] - 1, None, axis=dim...  5.26 us
    ppermute x3, starting transfers between devices, per_device(): lax.ppermute(own, 'vintage', [(s, s + k) for s in (0, 4, 8, 12)])  2.63 us
    ppermute x3, starting transfers between devices, per_device(): got = [lax.ppermute(attr, 'vintage', [(0, k)]) for k in (8, 4, 12)]  1.99 us
    pallas_call x1, Pallas kernels, attributes(): pl.pallas_call(attr_kernel, out_shape=(jax.ShapeDtypeStruct((ROWS, COLS,...  1.48 us
    pallas_call x1, Pallas kernels, correlate(): pl.pallas_call(correl_kernel, out_shape=jax.ShapeDtypeStruct((ROWS, COLS,...  1.2 us
  transfers between devices with their start and end apart: 10, of which 3 were waited for; matrix products, arithmetic and copies ran while one was open for 0% of the time, Pallas kernels for 0%

profile of v1, /device:TPU:233, one launch (start us, length us, event | category | flops | bytes accessed | tf_op | source)
XLA Modules:
  0.0 47.5 jit_solution(8839825666391451095)
XLA Ops:
  0.6 0.0 copy-start
  0.6 0.8 %slice_bitcast_fusion = (f32[1,16,256]{2,1,0:T(8,128)S(1)}, f32[1,16,256]{2,1,0:T(8,128)S(1)}) fusion(f32[1,8,16,256]{3,2,1,0:T(8,128)} %param.3), kind=kLoop, calls=%fused_computation.1 | loop fusion | bytes 65536 | tf_op jit(solution)/shard_map/slice | solution.py:169
  1.4 1.9 %collective-permute-start.1 = (f32[1,16,256]{2,1,0:T(8,128)S(1)}, f32[1,16,256]{2,1,0:T(8,128)S(1)}, u32[]{:S(2)}, u32[]{:S(2)}) collective-permute-start(f32[1,16,256]{2,1,0:T(8,128)S(1)} %get-tuple-element.8), channel_id=1, source_target_pairs={{8,0},{16,8},{24,16},{9,1},{17,9},{25,17},{10,2},{18,10},{26,18},{... | collective-permute-start | bytes 49160 | tf_op jit(solution)/shard_map/ppermute | solution.py:169
  3.3 6.1 %collective-permute-start = (f32[1,16,256]{2,1,0:T(8,128)S(1)}, f32[1,16,256]{2,1,0:T(8,128)S(1)}, u32[]{:S(2)}, u32[]{:S(2)}) collective-permute-start(f32[1,16,256]{2,1,0:T(8,128)S(1)} %get-tuple-element.9), channel_id=1, source_target_pairs={{0,8},{8,16},{16,24},{1,9},{9,17},{17,25},{2,10},{10,18},{18,26},{... | collective-permute-start | bytes 49160 | tf_op jit(solution)/shard_map/ppermute | solution.py:168
  9.5 0.0 collective-permute-done.1.down
  9.5 0.8 %collective-permute-done.up = f32[1,16,256]{2,1,0:T(8,128)S(1)} collective-permute-done((f32[1,16,256]{2,1,0:T(8,128)S(1)}, f32[1,16,256]{2,1,0:T(8,128)S(1)}, u32[]{:S(2)}, u32[]{:S(2)}) %collective-permute-start) | collective-permute-done | bytes 16416 | tf_op jit(solution)/shard_map/ppermute | solution.py:168
  10.3 0.0 copy-start.1
  10.3 0.9 %pad_maximum_fusion = (f32[10,1,256]{2,1,0:T(1,128)S(1)}, f32[10,1,256]{2,1,0:T(1,128)S(1)}) fusion(f32[1,16,256]{2,1,0:T(8,128)S(1)} %collective-permute-done.1.down, f32[8,16,256]{2,1,0:T(8,128)} %bitcast.7, f32[1,16,256]{2,1,0:T(8,128)S(1)} %collective-permute-done.up), kind=kLoop, calls=%fused_computation.3 | loop fusion | flops 10240 | bytes 184320 | tf_op jit(solution)/shard_map/concatenate | solution.py:178
  11.2 0.0 copy-start.2
  11.2 4.4 %collective-permute-start.3 = (f32[10,1,256]{2,1,0:T(1,128)S(1)}, f32[10,1,256]{2,1,0:T(1,128)S(1)}, u32[]{:S(2)}, u32[]{:S(2)}) collective-permute-start(f32[10,1,256]{2,1,0:T(1,128)S(1)} %get-tuple-element.6), channel_id=1, source_target_pairs={{1,0},{2,1},{3,2},{4,3},{5,4},{6,5},{7,6},{9,8},{10,9},{11,10},{12... | collective-permute-start | bytes 30728 | tf_op jit(solution)/shard_map/ppermute | solution.py:169
  15.6 1.9 %collective-permute-start.2 = (f32[10,1,256]{2,1,0:T(1,128)S(1)}, f32[10,1,256]{2,1,0:T(1,128)S(1)}, u32[]{:S(2)}, u32[]{:S(2)}) collective-permute-start(f32[10,1,256]{2,1,0:T(1,128)S(1)} %get-tuple-element.7), channel_id=1, source_target_pairs={{0,1},{1,2},{2,3},{3,4},{4,5},{5,6},{6,7},{8,9},{9,10},{10,11},{11... | collective-permute-start | bytes 30728 | tf_op jit(solution)/shard_map/ppermute | solution.py:168
  17.6 0.0 copy-done.1
  17.6 0.1 reshape.12.dip_il
  17.6 0.0 copy-done.2
  17.6 0.1 reshape.13.dip_xl
  17.7 0.0 collective-permute-done.3.right
  17.7 4.4 %collective-permute-done.2.left = f32[10,1,256]{2,1,0:T(1,128)S(1)} collective-permute-done((f32[10,1,256]{2,1,0:T(1,128)S(1)}, f32[10,1,256]{2,1,0:T(1,128)S(1)}, u32[]{:S(2)}, u32[]{:S(2)}) %collective-permute-start.2) | collective-permute-done | bytes 10272 | tf_op jit(solution)/shard_map/ppermute | solution.py:168
  22.1 0.0 copy-done
  22.2 1.5 %attributes.1 = (f32[8,16,256]{2,1,0:T(8,128)}, f32[256,128]{1,0:T(8,128)S(1)}) custom-call(f32[8,16,256]{2,1,0:T(8,128)S(1)} %bitcast.8, f32[1,16,256]{2,1,0:T(8,128)S(1)} %collective-permute-done.up, f32[1,16,256]{2,1,0:T(8,128)S(1)} %collective-permute-done.1.down, f32[10,1,256]{2,1,0:T(1,128)S(1)} %collective-permute-done.2.left, ...), custom_call_target="tpu_custom_call" | custom-call | tf_op jit(solution)/shard_map/attributes/pallas_call | solution.py:129
  23.6 0.7 %collective-permute-start.6 = (f32[256,128]{1,0:T(8,128)S(1)}, f32[256,128]{1,0:T(8,128)S(1)}, u32[]{:S(2)}, u32[]{:S(2)}) collective-permute-start(f32[256,128]{1,0:T(8,128)S(1)} %get-tuple-element.5.mon), channel_id=1, source_target_pairs={{0,384},{1,385},{2,386},{3,387},{4,388},{5,389},{6,390},{7,391},{8... | collective-permute-start | bytes 393224 | tf_op jit(solution)/shard_map/ppermute | solution.py:180
  24.3 0.7 %collective-permute-start.5 = (f32[256,128]{1,0:T(8,128)S(1)}, f32[256,128]{1,0:T(8,128)S(1)}, u32[]{:S(2)}, u32[]{:S(2)}) collective-permute-start(f32[256,128]{1,0:T(8,128)S(1)} %get-tuple-element.5.mon), channel_id=1, source_target_pairs={{0,128},{1,129},{2,130},{3,131},{4,132},{5,133},{6,134},{7,135},{8... | collective-permute-start | bytes 393224 | tf_op jit(solution)/shard_map/ppermute | solution.py:180
  25.0 0.7 %collective-permute-start.4 = (f32[256,128]{1,0:T(8,128)S(1)}, f32[256,128]{1,0:T(8,128)S(1)}, u32[]{:S(2)}, u32[]{:S(2)}) collective-permute-start(f32[256,128]{1,0:T(8,128)S(1)} %get-tuple-element.5.mon), channel_id=1, source_target_pairs={{0,256},{1,257},{2,258},{3,259},{4,260},{5,261},{6,262},{7,263},{8... | collective-permute-start | bytes 393224 | tf_op jit(solution)/shard_map/ppermute | solution.py:180
  25.7 0.0 collective-permute-done.6
  25.7 0.0 collective-permute-done.5
  25.7 0.0 collective-permute-done.4
  25.7 0.7 %collective-permute-start.9 = (f32[256,128]{1,0:T(8,128)S(1)}, f32[256,128]{1,0:T(8,128)S(1)}, u32[]{:S(2)}, u32[]{:S(2)}) collective-permute-start(f32[256,128]{1,0:T(8,128)S(1)} %add_select_fusion.own), channel_id=1, source_target_pairs={{0,32},{128,160},{256,288},{384,416},{1,33},{129,161},{257,289},{3... | collective-permute-start | bytes 393224 | tf_op jit(solution)/shard_map/ppermute | solution.py:183
  26.4 0.7 %collective-permute-start.8 = (f32[256,128]{1,0:T(8,128)S(1)}, f32[256,128]{1,0:T(8,128)S(1)}, u32[]{:S(2)}, u32[]{:S(2)}) collective-permute-start(f32[256,128]{1,0:T(8,128)S(1)} %add_select_fusion.own), channel_id=1, source_target_pairs={{0,64},{128,192},{256,320},{384,448},{1,65},{129,193},{257,321},{3... | collective-permute-start | bytes 393224 | tf_op jit(solution)/shard_map/ppermute | solution.py:183
  27.1 1.3 %collective-permute-start.7 = (f32[256,128]{1,0:T(8,128)S(1)}, f32[256,128]{1,0:T(8,128)S(1)}, u32[]{:S(2)}, u32[]{:S(2)}) collective-permute-start(f32[256,128]{1,0:T(8,128)S(1)} %add_select_fusion.own), channel_id=1, source_target_pairs={{0,96},{128,224},{256,352},{384,480},{1,97},{129,225},{257,353},{3... | collective-permute-start | bytes 393224 | tf_op jit(solution)/shard_map/ppermute | solution.py:183
  28.4 0.0 collective-permute-done.9.far3
  28.4 0.0 collective-permute-done.8.far2
  28.4 17.9 %collective-permute-done.7.far1 = f32[256,128]{1,0:T(8,128)S(1)} collective-permute-done((f32[256,128]{1,0:T(8,128)S(1)}, f32[256,128]{1,0:T(8,128)S(1)}, u32[]{:S(2)}, u32[]{:S(2)}) %collective-permute-start.7) | collective-permute-done | bytes 131104 | tf_op jit(solution)/shard_map/ppermute | solution.py:183
  46.3 1.2 %correlate.1 = f32[8,16,264]{2,1,0:T(8,128)} custom-call(f32[256,128]{1,0:T(8,128)S(1)} %get-tuple-element.5.mon, f32[256,128]{1,0:T(8,128)S(1)} %add_select_fusion.own, f32[256,128]{1,0:T(8,128)S(1)} %collective-permute-done.7.far1, f32[256,128]{1,0:T(8,128)S(1)} %collective-permute-done.8.far2, f32[256,128]{1,0:T(8,128)S(1)} %collective-permute-done.9.far3), custom_call_target="tpu_custom_call" | custom-call | tf_op jit(solution)/shard_map/correlate/pallas_call | solution.py:150
  (1 shorter events, 0.0 us)
Async XLA Ops:
  0.6 21.5 %copy-start = (f32[1,8,16,256]{3,2,1,0:T(8,128)S(1)}, f32[1,8,16,256]{3,2,1,0:T(8,128)}, u32[]{:S(2)}) copy-start(f32[1,8,16,256]{3,2,1,0:T(8,128)} %param.3) | copy-start | bytes 393220
  1.4 8.0 %collective-permute-start.1 = (f32[1,16,256]{2,1,0:T(8,128)S(1)}, f32[1,16,256]{2,1,0:T(8,128)S(1)}, u32[]{:S(2)}, u32[]{:S(2)}) collective-permute-start(f32[1,16,256]{2,1,0:T(8,128)S(1)} %get-tuple-element.8), channel_id=1, source_target_pairs={{8,0},{16,8},{24,16},{9,1},{17,9},{25,17},{10,2},{18,10},{26,18},{... | collective-permute-start | bytes 49160 | tf_op jit(solution)/shard_map/ppermute | solution.py:169
  3.3 7.0 %collective-permute-start = (f32[1,16,256]{2,1,0:T(8,128)S(1)}, f32[1,16,256]{2,1,0:T(8,128)S(1)}, u32[]{:S(2)}, u32[]{:S(2)}) collective-permute-start(f32[1,16,256]{2,1,0:T(8,128)S(1)} %get-tuple-element.9), channel_id=1, source_target_pairs={{0,8},{8,16},{16,24},{1,9},{9,17},{17,25},{2,10},{10,18},{18,26},{... | collective-permute-start | bytes 49160 | tf_op jit(solution)/shard_map/ppermute | solution.py:168
  10.3 7.2 %copy-start.1 = (s32[1,8,16]{2,1,0:T(8,128)S(1)}, s32[1,8,16]{2,1,0:T(8,128)}, u32[]{:S(2)}) copy-start(s32[1,8,16]{2,1,0:T(8,128)} %param.4) | copy-start | bytes 1540
  11.2 6.4 %copy-start.2 = (s32[1,8,16]{2,1,0:T(8,128)S(1)}, s32[1,8,16]{2,1,0:T(8,128)}, u32[]{:S(2)}) copy-start(s32[1,8,16]{2,1,0:T(8,128)} %param.5) | copy-start | bytes 1540
  11.2 6.5 %collective-permute-start.3 = (f32[10,1,256]{2,1,0:T(1,128)S(1)}, f32[10,1,256]{2,1,0:T(1,128)S(1)}, u32[]{:S(2)}, u32[]{:S(2)}) collective-permute-start(f32[10,1,256]{2,1,0:T(1,128)S(1)} %get-tuple-element.6), channel_id=1, source_target_pairs={{1,0},{2,1},{3,2},{4,3},{5,4},{6,5},{7,6},{9,8},{10,9},{11,10},{12... | collective-permute-start | bytes 30728 | tf_op jit(solution)/shard_map/ppermute | solution.py:169
  15.6 6.5 %collective-permute-start.2 = (f32[10,1,256]{2,1,0:T(1,128)S(1)}, f32[10,1,256]{2,1,0:T(1,128)S(1)}, u32[]{:S(2)}, u32[]{:S(2)}) collective-permute-start(f32[10,1,256]{2,1,0:T(1,128)S(1)} %get-tuple-element.7), channel_id=1, source_target_pairs={{0,1},{1,2},{2,3},{3,4},{4,5},{5,6},{6,7},{8,9},{9,10},{10,11},{11... | collective-permute-start | bytes 30728 | tf_op jit(solution)/shard_map/ppermute | solution.py:168
  23.6 2.0 %collective-permute-start.6 = (f32[256,128]{1,0:T(8,128)S(1)}, f32[256,128]{1,0:T(8,128)S(1)}, u32[]{:S(2)}, u32[]{:S(2)}) collective-permute-start(f32[256,128]{1,0:T(8,128)S(1)} %get-tuple-element.5.mon), channel_id=1, source_target_pairs={{0,384},{1,385},{2,386},{3,387},{4,388},{5,389},{6,390},{7,391},{8... | collective-permute-start | bytes 393224 | tf_op jit(solution)/shard_map/ppermute | solution.py:180
  24.3 1.4 %collective-permute-start.5 = (f32[256,128]{1,0:T(8,128)S(1)}, f32[256,128]{1,0:T(8,128)S(1)}, u32[]{:S(2)}, u32[]{:S(2)}) collective-permute-start(f32[256,128]{1,0:T(8,128)S(1)} %get-tuple-element.5.mon), channel_id=1, source_target_pairs={{0,128},{1,129},{2,130},{3,131},{4,132},{5,133},{6,134},{7,135},{8... | collective-permute-start | bytes 393224 | tf_op jit(solution)/shard_map/ppermute | solution.py:180
  25.0 0.7 %collective-permute-start.4 = (f32[256,128]{1,0:T(8,128)S(1)}, f32[256,128]{1,0:T(8,128)S(1)}, u32[]{:S(2)}, u32[]{:S(2)}) collective-permute-start(f32[256,128]{1,0:T(8,128)S(1)} %get-tuple-element.5.mon), channel_id=1, source_target_pairs={{0,256},{1,257},{2,258},{3,259},{4,260},{5,261},{6,262},{7,263},{8... | collective-permute-start | bytes 393224 | tf_op jit(solution)/shard_map/ppermute | solution.py:180
  25.7 2.7 %collective-permute-start.9 = (f32[256,128]{1,0:T(8,128)S(1)}, f32[256,128]{1,0:T(8,128)S(1)}, u32[]{:S(2)}, u32[]{:S(2)}) collective-permute-start(f32[256,128]{1,0:T(8,128)S(1)} %add_select_fusion.own), channel_id=1, source_target_pairs={{0,32},{128,160},{256,288},{384,416},{1,33},{129,161},{257,289},{3... | collective-permute-start | bytes 393224 | tf_op jit(solution)/shard_map/ppermute | solution.py:183
  26.4 2.0 %collective-permute-start.8 = (f32[256,128]{1,0:T(8,128)S(1)}, f32[256,128]{1,0:T(8,128)S(1)}, u32[]{:S(2)}, u32[]{:S(2)}) collective-permute-start(f32[256,128]{1,0:T(8,128)S(1)} %add_select_fusion.own), channel_id=1, source_target_pairs={{0,64},{128,192},{256,320},{384,448},{1,65},{129,193},{257,321},{3... | collective-permute-start | bytes 393224 | tf_op jit(solution)/shard_map/ppermute | solution.py:183
  27.1 19.2 %collective-permute-start.7 = (f32[256,128]{1,0:T(8,128)S(1)}, f32[256,128]{1,0:T(8,128)S(1)}, u32[]{:S(2)}, u32[]{:S(2)}) collective-permute-start(f32[256,128]{1,0:T(8,128)S(1)} %add_select_fusion.own), channel_id=1, source_target_pairs={{0,96},{128,224},{256,352},{384,480},{1,97},{129,225},{257,353},{3... | collective-permute-start | bytes 393224 | tf_op jit(solution)/shard_map/ppermute | solution.py:183

commit v2 on v1

--- a/solution.py
+++ b/solution.py
@@ -27,8 +27,28 @@
     return out
 
 
-def attr_kernel(tile, up, down, left, right, dip_il, dip_xl, semb_out, attr_out,
-                rim, moved, inner, sums, three):
+def first_kernel(*refs):
+    @pl.when(lax.axis_index("vintage") == 0)
+    def _():
+        attr_body(*refs)
+
+
+def later_kernel(*refs):
+    ins, semb_first, attr_first, semb_out, attr_out = refs[:7], refs[7], refs[8], refs[9], refs[10]
+    first = lax.axis_index("vintage") == 0
+
+    @pl.when(first)
+    def _():
+        semb_out[...] = semb_first[...]
+        attr_out[...] = attr_first[...]
+
+    @pl.when(jnp.logical_not(first))
+    def _():
+        attr_body(*ins, *refs[9:])
+
+
+def attr_body(tile, up, down, left, right, dip_il, dip_xl, semb_out, attr_out,
+              rim, moved, inner, sums, three):
     rim[1:ROWS + 1, 1:COLS + 1, :] = tile[...]
     rim[0, 1:COLS + 1, :] = up[0]
     rim[ROWS + 1, 1:COLS + 1, :] = down[0]
@@ -79,20 +99,20 @@
     return jnp.where(low, x, pltpu.roll(y, half, 0)) + jnp.where(low, pltpu.roll(x, 8 - half, 0), y)
 
 
-def correl_kernel(mon, own, far1, far2, far3, out, base, result):
+def correl_kernel(mon, held, near, out, base, result):
     half_lags = LAGS // 2
-    leader = lax.rem(lax.axis_index("vintage"), 4) == 0
+    odd = lax.rem(lax.axis_index("vintage"), 2) == 1
     zeros = jnp.zeros((half_lags, TRACES), jnp.float32)
     base[0:half_lags, :] = zeros
     base[half_lags + TIME_SAMPLES:, :] = zeros
 
-    @pl.when(leader)
-    def _():
-        base[half_lags:half_lags + TIME_SAMPLES, :] = own[...]
-
-    @pl.when(jnp.logical_not(leader))
-    def _():
-        base[half_lags:half_lags + TIME_SAMPLES, :] = far1[...] + far2[...] + far3[...]
+    @pl.when(odd)
+    def _():
+        base[half_lags:half_lags + TIME_SAMPLES, :] = near[...]
+
+    @pl.when(jnp.logical_not(odd))
+    def _():
+        base[half_lags:half_lags + TIME_SAMPLES, :] = held[...]
 
     mon_energy = jnp.zeros((8, TRACES), jnp.float32)
     base_energy = jnp.zeros((8, TRACES), jnp.float32)
@@ -125,14 +145,14 @@
     return [pl.BlockSpec(memory_space=pltpu.VMEM)] * n
 
 
-def attributes(tile, up, down, left, right, dip_il, dip_xl):
+def attributes(kernel, name, *args):
     return pl.pallas_call(
-        attr_kernel,
+        kernel,
         out_shape=(
             jax.ShapeDtypeStruct((ROWS, COLS, TIME_SAMPLES), jnp.float32),
             jax.ShapeDtypeStruct((TIME_SAMPLES, TRACES), jnp.float32),
         ),
-        in_specs=vmem(7),
+        in_specs=vmem(len(args)),
         out_specs=tuple(vmem(2)),
         scratch_shapes=[
             pltpu.VMEM((ROWS + 2, COLS + 8, TIME_SAMPLES), jnp.float32),
@@ -142,15 +162,15 @@
             pltpu.VMEM((TIME_SAMPLES, TRACES), jnp.float32),
         ],
         compiler_params=pltpu.CompilerParams(vmem_limit_bytes=16 << 20),
-        name="attributes",
-    )(tile, up, down, left, right, dip_il, dip_xl)
-
-
-def correlate(mon, own, far):
+        name=name,
+    )(*args)
+
+
+def correlate(mon, held, near):
     return pl.pallas_call(
         correl_kernel,
         out_shape=jax.ShapeDtypeStruct((ROWS, COLS, LAGS * NWIN), jnp.float32),
-        in_specs=vmem(5),
+        in_specs=vmem(3),
         out_specs=pl.BlockSpec(memory_space=pltpu.VMEM),
         scratch_shapes=[
             pltpu.VMEM((TIME_SAMPLES + LAGS - 1, TRACES), jnp.float32),
@@ -158,30 +178,41 @@
         ],
         compiler_params=pltpu.CompilerParams(vmem_limit_bytes=16 << 20),
         name="correlate",
-    )(mon, own, *far)
-
-
-def neighbours(block, axis, dim):
+    )(mon, held, near)
+
+
+def exchange(last, first, axis, planes):
     count = lax.axis_size(axis)
-    forward = [(i, i + 1) for i in range(count - 1)]
-    backward = [(target, source) for source, target in forward]
-    low = lax.ppermute(lax.slice_in_dim(block, block.shape[dim] - 1, None, axis=dim), axis, forward)
-    high = lax.ppermute(lax.slice_in_dim(block, 0, 1, axis=dim), axis, backward)
+    steps = [(v * count + i, v * count + i + 1) for v in planes for i in range(count - 1)]
+    low = lax.ppermute(last, ("vintage", axis), steps)
+    high = lax.ppermute(first, ("vintage", axis), [(target, source) for source, target in steps])
     return low, high
+
+
+def rim_of(tile, last, first, planes):
+    up, down = exchange(last, first, "inline", planes)
+    wide = jnp.concatenate([up, tile, down], axis=0)
+    left, right = exchange(wide[:, -1:], wide[:, :1], "xline", planes)
+    return up, down, left, right
 
 
 def per_device(amplitude, inline_slope, crossline_slope):
     tile = amplitude[0]
-    dip_il = inline_slope.reshape(1, TRACES)
-    dip_xl = crossline_slope.reshape(1, TRACES)
-    up, down = neighbours(tile, "inline", 0)
-    left, right = neighbours(jnp.concatenate([up, tile, down], axis=0), "xline", 1)
-    semb, attr = attributes(tile, up, down, left, right, dip_il, dip_xl)
-    got = [lax.ppermute(attr, "vintage", [(0, k)]) for k in (8, 4, 12)]
-    first = lax.axis_index("vintage") == 0
-    own = jnp.where(first, attr, got[0] + got[1] + got[2])
-    far = [lax.ppermute(own, "vintage", [(s, s + k) for s in (0, 4, 8, 12)]) for k in (3, 2, 1)]
-    correl = correlate(attr, own, far)
+    dips = (inline_slope.reshape(1, TRACES), crossline_slope.reshape(1, TRACES))
+    vintages = lax.axis_size("vintage")
+    place = lax.axis_index("vintage")
+    last, first = tile[-1:], tile[:1]
+    semb0, attr0 = attributes(first_kernel, "baseline", tile, *rim_of(tile, last, first, [0]), *dips)
+    got = [lax.ppermute(attr0, "vintage", [(0, k)]) for k in (8, 4, 12)]
+    last, first, attr0 = lax.optimization_barrier((last, first, attr0))
+    rim = rim_of(tile, last, first, range(1, vintages))
+    semb, attr = attributes(later_kernel, "monitor", tile, *rim, *dips, semb0, attr0)
+    got = lax.optimization_barrier((*got, attr))[:3]
+    held = jnp.where(place == 0, attr0, got[0] + got[1] + got[2])
+    half = lax.ppermute(held, "vintage", [(s, s + 2) for s in range(0, vintages, 4)])
+    held = jnp.where(lax.rem(place, 4) == 0, held, half)
+    near = lax.ppermute(held, "vintage", [(s, s + 1) for s in range(0, vintages, 2)])
+    correl = correlate(attr, held, near)
     return (semb[None], correl[None])
 
 

time: 47.9 us -> 47.4 us (0.990)
  the two profiles are of different devices: /device:TPU:233 before, /device:TPU:63 now
where the time goes in v2:
time: 47.4 us; the launch traced here: 47 us
  waiting for transfers between devices  22.4 us (47%)
  starting transfers between devices  19 us (40%)
  Pallas kernels  2.69 us (6%)
  other arithmetic  1.04 us (2%)
  local copies, waits for them, and re-layouts  0.95 us (2%)
  between operations  0.89 us (2%)
    ppermute x1, waiting for transfers between devices, per_device(): lax.ppermute(held, 'vintage', [(s, s + 1) for s in range(0, vintages, 2)])  13.4 us
    ppermute x4, starting transfers between devices, exchange(): low = lax.ppermute(last, ('vintage', axis), steps)  10.1 us
    ppermute x4, waiting for transfers between devices, exchange(): lax.ppermute(first, ('vintage', axis), [(target, source) for source, targ...  9.04 us
    ppermute x4, starting transfers between devices, exchange(): lax.ppermute(first, ('vintage', axis), [(target, source) for source, targ...  4.88 us
    ppermute x3, starting transfers between devices, per_device(): got = [lax.ppermute(attr0, 'vintage', [(0, k)]) for k in (8, 4, 12)]  2.01 us
    pallas_call x2, Pallas kernels, attributes(): pl.pallas_call(kernel, out_shape=(jax.ShapeDtypeStruct((ROWS, COLS, TIME_...  1.5 us
    ppermute x1, starting transfers between devices, per_device(): lax.ppermute(held, 'vintage', [(s, s + 1) for s in range(0, vintages, 2)])  1.29 us
    pallas_call x1, Pallas kernels, correlate(): pl.pallas_call(correl_kernel, out_shape=jax.ShapeDtypeStruct((ROWS, COLS,...  1.19 us
  transfers between devices with their start and end apart: 13, of which 3 were waited for; matrix products, arithmetic and copies ran while one was open for 0% of the time, Pallas kernels for 3%

profile of v2, /device:TPU:63, one launch (start us, length us, event | category | flops | bytes accessed | tf_op | source)
XLA Modules:
  0.0 47.0 jit_solution(9550547643891827609)
XLA Ops:
  0.6 0.7 %slice_bitcast_fusion = (f32[1,16,256]{2,1,0:T(8,128)S(1)}, f32[1,16,256]{2,1,0:T(8,128)S(1)}) fusion(f32[1,8,16,256]{3,2,1,0:T(8,128)} %param.3), kind=kLoop, calls=%fused_computation.6 | loop fusion | bytes 65536 | tf_op jit(solution)/shard_map/slice | solution.py:204
  1.4 0.7 %collective-permute-start = (f32[1,16,256]{2,1,0:T(8,128)S(1)}, f32[1,16,256]{2,1,0:T(8,128)S(1)}, u32[]{:S(2)}, u32[]{:S(2)}) collective-permute-start(f32[1,16,256]{2,1,0:T(8,128)S(1)} %get-tuple-element.13), channel_id=1, source_target_pairs={{0,8},{8,16},{16,24},{1,9},{9,17},{17,25},{2,10},{10,18},{18,26},{... | collective-permute-start | bytes 49160 | tf_op jit(solution)/shard_map/ppermute | solution.py:187
  2.0 0.7 %collective-permute-start.1 = (f32[1,16,256]{2,1,0:T(8,128)S(1)}, f32[1,16,256]{2,1,0:T(8,128)S(1)}, u32[]{:S(2)}, u32[]{:S(2)}) collective-permute-start(f32[1,16,256]{2,1,0:T(8,128)S(1)} %get-tuple-element.14), channel_id=1, source_target_pairs={{8,0},{16,8},{24,16},{9,1},{17,9},{25,17},{10,2},{18,10},{26,18},{... | collective-permute-start | bytes 49160 | tf_op jit(solution)/shard_map/ppermute | solution.py:188
  2.7 0.0 collective-permute-done.refs_1_
  2.7 0.0 collective-permute-done.1.refs_2_
  2.7 0.0 copy-start
  2.7 1.0 %fusion = f32[10,16,256]{2,1,0:T(8,128)S(1)} fusion(f32[8,16,256]{2,1,0:T(8,128)} %bitcast.7, f32[1,16,256]{2,1,0:T(8,128)S(1)} %collective-permute-done.1.refs_2_, f32[1,16,256]{2,1,0:T(8,128)S(1)} %collective-permute-done.refs_1_), kind=kLoop, calls=%fused_computation.2 | loop fusion | flops 81920 | bytes 327680 | tf_op jit(solution)/shard_map/concatenate | solution.py:194
  3.7 0.0 copy-start.1
  3.8 0.0 copy-start.2
  3.8 0.7 %collective-permute-start.2 = (f32[10,1,256]{2,1,0:T(1,128)S(1)}, f32[10,1,256]{2,1,0:T(1,128)S(1)}, u32[]{:S(2)}, u32[]{:S(2)}) collective-permute-start(f32[10,1,256]{2,1,0:T(1,128)S(1)} %get-tuple-element.25), channel_id=1, source_target_pairs={{0,1},{1,2},{2,3},{3,4},{4,5},{5,6},{6,7},{8,9},{9,10},{10,11},{11... | collective-permute-start | bytes 30728 | tf_op jit(solution)/shard_map/ppermute | solution.py:187
  4.4 0.7 %collective-permute-start.3 = (f32[10,1,256]{2,1,0:T(1,128)S(1)}, f32[10,1,256]{2,1,0:T(1,128)S(1)}, u32[]{:S(2)}, u32[]{:S(2)}) collective-permute-start(f32[10,1,256]{2,1,0:T(1,128)S(1)} %get-tuple-element.24), channel_id=1, source_target_pairs={{1,0},{2,1},{3,2},{4,3},{5,4},{6,5},{7,6},{9,8},{10,9},{11,10},{12... | collective-permute-start | bytes 30728 | tf_op jit(solution)/shard_map/ppermute | solution.py:188
  5.1 0.0 copy-done.1
  5.1 0.1 reshape.12.refs_5_
  5.2 0.0 copy-done.2
  5.2 0.1 reshape.13.refs_6_
  5.3 0.0 collective-permute-done.2.refs_3_
  5.3 0.0 collective-permute-done.3.refs_4_
  5.3 0.0 copy-done
  5.3 5.8 %collective-permute-start.4 = (f32[1,16,256]{2,1,0:T(8,128)S(1)}, f32[1,16,256]{2,1,0:T(8,128)S(1)}, u32[]{:S(2)}, u32[]{:S(2)}) collective-permute-start(f32[1,16,256]{2,1,0:T(8,128)S(1)} %get-tuple-element.13), channel_id=1, source_target_pairs={{32,40},{40,48},{48,56},{64,72},{72,80},{80,88},{96,104},{104,112}... | collective-permute-start | bytes 49160 | tf_op jit(solution)/shard_map/ppermute | solution.py:187
  11.1 1.3 %collective-permute-start.5 = (f32[1,16,256]{2,1,0:T(8,128)S(1)}, f32[1,16,256]{2,1,0:T(8,128)S(1)}, u32[]{:S(2)}, u32[]{:S(2)}) collective-permute-start(f32[1,16,256]{2,1,0:T(8,128)S(1)} %get-tuple-element.14), channel_id=1, source_target_pairs={{40,32},{48,40},{56,48},{72,64},{80,72},{88,80},{104,96},{112,104}... | collective-permute-start | bytes 49160 | tf_op jit(solution)/shard_map/ppermute | solution.py:188
  12.4 0.7 %collective-permute-start.8 = (f32[256,128]{1,0:T(8,128)S(1)}, f32[256,128]{1,0:T(8,128)S(1)}, u32[]{:S(2)}, u32[]{:S(2)}) collective-permute-start(f32[256,128]{1,0:T(8,128)S(1)} %get-tuple-element.16.refs_8_), channel_id=1, source_target_pairs={{0,256},{1,257},{2,258},{3,259},{4,260},{5,261},{6,262},{7,263},{8... | collective-permute-start | bytes 393224 | tf_op jit(solution)/shard_map/ppermute | solution.py:206
  13.1 0.7 %collective-permute-start.9 = (f32[256,128]{1,0:T(8,128)S(1)}, f32[256,128]{1,0:T(8,128)S(1)}, u32[]{:S(2)}, u32[]{:S(2)}) collective-permute-start(f32[256,128]{1,0:T(8,128)S(1)} %get-tuple-element.16.refs_8_), channel_id=1, source_target_pairs={{0,128},{1,129},{2,130},{3,131},{4,132},{5,133},{6,134},{7,135},{8... | collective-permute-start | bytes 393224 | tf_op jit(solution)/shard_map/ppermute | solution.py:206
  13.8 0.7 %collective-permute-start.10 = (f32[256,128]{1,0:T(8,128)S(1)}, f32[256,128]{1,0:T(8,128)S(1)}, u32[]{:S(2)}, u32[]{:S(2)}) collective-permute-start(f32[256,128]{1,0:T(8,128)S(1)} %get-tuple-element.16.refs_8_), channel_id=1, source_target_pairs={{0,384},{1,385},{2,386},{3,387},{4,388},{5,389},{6,390},{7,391},{8... | collective-permute-start | bytes 393224 | tf_op jit(solution)/shard_map/ppermute | solution.py:206
  14.5 0.0 collective-permute-done.4.refs_1_
  14.5 4.8 %collective-permute-done.5.refs_2_ = f32[1,16,256]{2,1,0:T(8,128)S(1)} collective-permute-done((f32[1,16,256]{2,1,0:T(8,128)S(1)}, f32[1,16,256]{2,1,0:T(8,128)S(1)}, u32[]{:S(2)}, u32[]{:S(2)}) %collective-permute-start.5) | collective-permute-done | bytes 16416 | tf_op jit(solution)/shard_map/ppermute | solution.py:188
  19.3 3.0 %collective-permute-start.6 = (f32[10,1,256]{2,1,0:T(1,128)S(1)}, f32[10,1,256]{2,1,0:T(1,128)S(1)}, u32[]{:S(2)}, u32[]{:S(2)}) collective-permute-start(f32[10,1,256]{2,1,0:T(1,128)S(1)} %get-tuple-element.23), channel_id=1, source_target_pairs={{32,33},{33,34},{34,35},{35,36},{36,37},{37,38},{38,39},{64,65},{6... | collective-permute-start | bytes 30728 | tf_op jit(solution)/shard_map/ppermute | solution.py:187
  22.3 2.3 %collective-permute-start.7 = (f32[10,1,256]{2,1,0:T(1,128)S(1)}, f32[10,1,256]{2,1,0:T(1,128)S(1)}, u32[]{:S(2)}, u32[]{:S(2)}) collective-permute-start(f32[10,1,256]{2,1,0:T(1,128)S(1)} %get-tuple-element.22), channel_id=1, source_target_pairs={{33,32},{34,33},{35,34},{36,35},{37,36},{38,37},{39,38},{65,64},{6... | collective-permute-start | bytes 30728 | tf_op jit(solution)/shard_map/ppermute | solution.py:188
  24.6 0.0 collective-permute-done.6.refs_3_
  24.6 4.2 %collective-permute-done.7.refs_4_ = f32[10,1,256]{2,1,0:T(1,128)S(1)} collective-permute-done((f32[10,1,256]{2,1,0:T(1,128)S(1)}, f32[10,1,256]{2,1,0:T(1,128)S(1)}, u32[]{:S(2)}, u32[]{:S(2)}) %collective-permute-start.7) | collective-permute-done | bytes 10272 | tf_op jit(solution)/shard_map/ppermute | solution.py:188
  28.9 1.5 %monitor.1 = (f32[8,16,256]{2,1,0:T(8,128)}, f32[256,128]{1,0:T(8,128)S(1)}) custom-call(f32[8,16,256]{2,1,0:T(8,128)S(1)} %bitcast.10, f32[1,16,256]{2,1,0:T(8,128)S(1)} %collective-permute-done.4.refs_1_, f32[1,16,256]{2,1,0:T(8,128)S(1)} %collective-permute-done.5.refs_2_, f32[10,1,256]{2,1,0:T(1,128)S(1)} %collective-permute-done.6.refs_3_, ...), custom_call_target="tpu_custom_call" | custom-call | tf_op jit(solution)/shard_map/monitor/pallas_call | solution.py:149
  30.4 0.0 collective-permute-done.8
  30.4 0.0 collective-permute-done.9
  30.4 0.0 collective-permute-done.10
  30.4 0.7 %collective-permute-start.11 = (f32[256,128]{1,0:T(8,128)S(1)}, f32[256,128]{1,0:T(8,128)S(1)}, u32[]{:S(2)}, u32[]{:S(2)}) collective-permute-start(f32[256,128]{1,0:T(8,128)S(1)} %add_select_fusion), channel_id=1, source_target_pairs={{0,64},{128,192},{256,320},{384,448},{1,65},{129,193},{257,321},{3... | collective-permute-start | bytes 393224 | tf_op jit(solution)/shard_map/ppermute | solution.py:212
  31.1 0.0 collective-permute-done.11
  31.1 1.3 %collective-permute-start.12 = (f32[256,128]{1,0:T(8,128)S(1)}, f32[256,128]{1,0:T(8,128)S(1)}, u32[]{:S(2)}, u32[]{:S(2)}) collective-permute-start(f32[256,128]{1,0:T(8,128)S(1)} %broadcast_select_fusion.held), channel_id=1, source_target_pairs={{0,32},{64,96},{128,160},{192,224},{256,288},{320,352},{384,416},{... | collective-permute-start | bytes 393224 | tf_op jit(solution)/shard_map/ppermute | solution.py:214
  32.4 13.4 %collective-permute-done.12.near = f32[256,128]{1,0:T(8,128)S(1)} collective-permute-done((f32[256,128]{1,0:T(8,128)S(1)}, f32[256,128]{1,0:T(8,128)S(1)}, u32[]{:S(2)}, u32[]{:S(2)}) %collective-permute-start.12) | collective-permute-done | bytes 131104 | tf_op jit(solution)/shard_map/ppermute | solution.py:214
  45.8 1.2 %correlate.1 = f32[8,16,264]{2,1,0:T(8,128)} custom-call(f32[256,128]{1,0:T(8,128)S(1)} %get-tuple-element.18.mon, f32[256,128]{1,0:T(8,128)S(1)} %broadcast_select_fusion.held, f32[256,128]{1,0:T(8,128)S(1)} %collective-permute-done.12.near), custom_call_target="tpu_custom_call" | custom-call | tf_op jit(solution)/shard_map/correlate/pallas_call | solution.py:170
  (6 shorter events, 0.1 us)
Async XLA Ops:
  1.4 1.3 %collective-permute-start = (f32[1,16,256]{2,1,0:T(8,128)S(1)}, f32[1,16,256]{2,1,0:T(8,128)S(1)}, u32[]{:S(2)}, u32[]{:S(2)}) collective-permute-start(f32[1,16,256]{2,1,0:T(8,128)S(1)} %get-tuple-element.13), channel_id=1, source_target_pairs={{0,8},{8,16},{16,24},{1,9},{9,17},{17,25},{2,10},{10,18},{18,26},{... | collective-permute-start | bytes 49160 | tf_op jit(solution)/shard_map/ppermute | solution.py:187
  2.0 0.7 %collective-permute-start.1 = (f32[1,16,256]{2,1,0:T(8,128)S(1)}, f32[1,16,256]{2,1,0:T(8,128)S(1)}, u32[]{:S(2)}, u32[]{:S(2)}) collective-permute-start(f32[1,16,256]{2,1,0:T(8,128)S(1)} %get-tuple-element.14), channel_id=1, source_target_pairs={{8,0},{16,8},{24,16},{9,1},{17,9},{25,17},{10,2},{18,10},{26,18},{... | collective-permute-start | bytes 49160 | tf_op jit(solution)/shard_map/ppermute | solution.py:188
  2.7 2.6 %copy-start = (f32[1,8,16,256]{3,2,1,0:T(8,128)S(1)}, f32[1,8,16,256]{3,2,1,0:T(8,128)}, u32[]{:S(2)}) copy-start(f32[1,8,16,256]{3,2,1,0:T(8,128)} %param.3) | copy-start | bytes 393220
  3.7 1.4 %copy-start.1 = (s32[1,8,16]{2,1,0:T(8,128)S(1)}, s32[1,8,16]{2,1,0:T(8,128)}, u32[]{:S(2)}) copy-start(s32[1,8,16]{2,1,0:T(8,128)} %param.4) | copy-start | bytes 1540
  3.8 1.4 %copy-start.2 = (s32[1,8,16]{2,1,0:T(8,128)S(1)}, s32[1,8,16]{2,1,0:T(8,128)}, u32[]{:S(2)}) copy-start(s32[1,8,16]{2,1,0:T(8,128)} %param.5) | copy-start | bytes 1540
  3.8 1.5 %collective-permute-start.2 = (f32[10,1,256]{2,1,0:T(1,128)S(1)}, f32[10,1,256]{2,1,0:T(1,128)S(1)}, u32[]{:S(2)}, u32[]{:S(2)}) collective-permute-start(f32[10,1,256]{2,1,0:T(1,128)S(1)} %get-tuple-element.25), channel_id=1, source_target_pairs={{0,1},{1,2},{2,3},{3,4},{4,5},{5,6},{6,7},{8,9},{9,10},{10,11},{11... | collective-permute-start | bytes 30728 | tf_op jit(solution)/shard_map/ppermute | solution.py:187
  4.4 0.9 %collective-permute-start.3 = (f32[10,1,256]{2,1,0:T(1,128)S(1)}, f32[10,1,256]{2,1,0:T(1,128)S(1)}, u32[]{:S(2)}, u32[]{:S(2)}) collective-permute-start(f32[10,1,256]{2,1,0:T(1,128)S(1)} %get-tuple-element.24), channel_id=1, source_target_pairs={{1,0},{2,1},{3,2},{4,3},{5,4},{6,5},{7,6},{9,8},{10,9},{11,10},{12... | collective-permute-start | bytes 30728 | tf_op jit(solution)/shard_map/ppermute | solution.py:188
  5.3 9.1 %collective-permute-start.4 = (f32[1,16,256]{2,1,0:T(8,128)S(1)}, f32[1,16,256]{2,1,0:T(8,128)S(1)}, u32[]{:S(2)}, u32[]{:S(2)}) collective-permute-start(f32[1,16,256]{2,1,0:T(8,128)S(1)} %get-tuple-element.13), channel_id=1, source_target_pairs={{32,40},{40,48},{48,56},{64,72},{72,80},{80,88},{96,104},{104,112}... | collective-permute-start | bytes 49160 | tf_op jit(solution)/shard_map/ppermute | solution.py:187
  11.1 8.1 %collective-permute-start.5 = (f32[1,16,256]{2,1,0:T(8,128)S(1)}, f32[1,16,256]{2,1,0:T(8,128)S(1)}, u32[]{:S(2)}, u32[]{:S(2)}) collective-permute-start(f32[1,16,256]{2,1,0:T(8,128)S(1)} %get-tuple-element.14), channel_id=1, source_target_pairs={{40,32},{48,40},{56,48},{72,64},{80,72},{88,80},{104,96},{112,104}... | collective-permute-start | bytes 49160 | tf_op jit(solution)/shard_map/ppermute | solution.py:188
  12.4 17.9 %collective-permute-start.8 = (f32[256,128]{1,0:T(8,128)S(1)}, f32[256,128]{1,0:T(8,128)S(1)}, u32[]{:S(2)}, u32[]{:S(2)}) collective-permute-start(f32[256,128]{1,0:T(8,128)S(1)} %get-tuple-element.16.refs_8_), channel_id=1, source_target_pairs={{0,256},{1,257},{2,258},{3,259},{4,260},{5,261},{6,262},{7,263},{8... | collective-permute-start | bytes 393224 | tf_op jit(solution)/shard_map/ppermute | solution.py:206
  13.1 17.2 %collective-permute-start.9 = (f32[256,128]{1,0:T(8,128)S(1)}, f32[256,128]{1,0:T(8,128)S(1)}, u32[]{:S(2)}, u32[]{:S(2)}) collective-permute-start(f32[256,128]{1,0:T(8,128)S(1)} %get-tuple-element.16.refs_8_), channel_id=1, source_target_pairs={{0,128},{1,129},{2,130},{3,131},{4,132},{5,133},{6,134},{7,135},{8... | collective-permute-start | bytes 393224 | tf_op jit(solution)/shard_map/ppermute | solution.py:206
  13.8 16.6 %collective-permute-start.10 = (f32[256,128]{1,0:T(8,128)S(1)}, f32[256,128]{1,0:T(8,128)S(1)}, u32[]{:S(2)}, u32[]{:S(2)}) collective-permute-start(f32[256,128]{1,0:T(8,128)S(1)} %get-tuple-element.16.refs_8_), channel_id=1, source_target_pairs={{0,384},{1,385},{2,386},{3,387},{4,388},{5,389},{6,390},{7,391},{8... | collective-permute-start | bytes 393224 | tf_op jit(solution)/shard_map/ppermute | solution.py:206
  19.3 5.3 %collective-permute-start.6 = (f32[10,1,256]{2,1,0:T(1,128)S(1)}, f32[10,1,256]{2,1,0:T(1,128)S(1)}, u32[]{:S(2)}, u32[]{:S(2)}) collective-permute-start(f32[10,1,256]{2,1,0:T(1,128)S(1)} %get-tuple-element.23), channel_id=1, source_target_pairs={{32,33},{33,34},{34,35},{35,36},{36,37},{37,38},{38,39},{64,65},{6... | collective-permute-start | bytes 30728 | tf_op jit(solution)/shard_map/ppermute | solution.py:187
  22.3 6.5 %collective-permute-start.7 = (f32[10,1,256]{2,1,0:T(1,128)S(1)}, f32[10,1,256]{2,1,0:T(1,128)S(1)}, u32[]{:S(2)}, u32[]{:S(2)}) collective-permute-start(f32[10,1,256]{2,1,0:T(1,128)S(1)} %get-tuple-element.22), channel_id=1, source_target_pairs={{33,32},{34,33},{35,34},{36,35},{37,36},{38,37},{39,38},{65,64},{6... | collective-permute-start | bytes 30728 | tf_op jit(solution)/shard_map/ppermute | solution.py:188
  30.4 0.7 %collective-permute-start.11 = (f32[256,128]{1,0:T(8,128)S(1)}, f32[256,128]{1,0:T(8,128)S(1)}, u32[]{:S(2)}, u32[]{:S(2)}) collective-permute-start(f32[256,128]{1,0:T(8,128)S(1)} %add_select_fusion), channel_id=1, source_target_pairs={{0,64},{128,192},{256,320},{384,448},{1,65},{129,193},{257,321},{3... | collective-permute-start | bytes 393224 | tf_op jit(solution)/shard_map/ppermute | solution.py:212
  31.1 14.7 %collective-permute-start.12 = (f32[256,128]{1,0:T(8,128)S(1)}, f32[256,128]{1,0:T(8,128)S(1)}, u32[]{:S(2)}, u32[]{:S(2)}) collective-permute-start(f32[256,128]{1,0:T(8,128)S(1)} %broadcast_select_fusion.held), channel_id=1, source_target_pairs={{0,32},{64,96},{128,160},{192,224},{256,288},{320,352},{384,416},{... | collective-permute-start | bytes 393224 | tf_op jit(solution)/shard_map/ppermute | solution.py:214

commit v3 on v2

--- a/solution.py
+++ b/solution.py
@@ -11,6 +11,13 @@
 LAGS = 33
 NWIN = 8
 EPS = 1e-06
+F = (0, 0, 0, 1)
+TT = (12, 4, 8)
+
+
+def FLIP(x, f):
+    return tuple(x)[::-1] if f else tuple(x)
+
 
 ROWS = 8
 COLS = 16
@@ -30,7 +37,8 @@
 def first_kernel(*refs):
     @pl.when(lax.axis_index("vintage") == 0)
     def _():
-        attr_body(*refs)
+        r = refs
+        attr_body(r[0], *FLIP(r[1:3], F[0]), *FLIP(r[3:5], F[1]), *r[5:])
 
 
 def later_kernel(*refs):
@@ -44,16 +52,19 @@
 
     @pl.when(jnp.logical_not(first))
     def _():
-        attr_body(*ins, *refs[9:])
-
-
-def attr_body(tile, up, down, left, right, dip_il, dip_xl, semb_out, attr_out,
+        r = ins
+        attr_body(r[0], *FLIP(r[1:3], F[2]), *FLIP(r[3:5], F[3]), *r[5:], *refs[9:])
+
+
+def attr_body(tile, row_a, row_b, col_a, col_b, dip_il, dip_xl, semb_out, attr_out,
               rim, moved, inner, sums, three):
+    odd_row = lax.rem(lax.axis_index("inline"), 2) == 1
+    odd_col = lax.rem(lax.axis_index("xline"), 2) == 1
     rim[1:ROWS + 1, 1:COLS + 1, :] = tile[...]
-    rim[0, 1:COLS + 1, :] = up[0]
-    rim[ROWS + 1, 1:COLS + 1, :] = down[0]
-    rim[:, 0:1, :] = left[...]
-    rim[:, COLS + 1:COLS + 2, :] = right[...]
+    rim[0, 1:COLS + 1, :] = jnp.where(odd_row, row_a[0], row_b[0])
+    rim[ROWS + 1, 1:COLS + 1, :] = jnp.where(odd_row, row_b[0], row_a[0])
+    rim[:, 0:1, :] = jnp.where(odd_col, col_a[...], col_b[...])
+    rim[:, COLS + 1:COLS + 2, :] = jnp.where(odd_col, col_b[...], col_a[...])
     zeros = jnp.zeros((PAD, TRACES), jnp.float32)
     for a in STEPS:
         for b in STEPS:
@@ -99,20 +110,20 @@
     return jnp.where(low, x, pltpu.roll(y, half, 0)) + jnp.where(low, pltpu.roll(x, 8 - half, 0), y)
 
 
-def correl_kernel(mon, held, near, out, base, result):
+def correl_kernel(mon, held, far3, far2, far1, out, base, result):
     half_lags = LAGS // 2
-    odd = lax.rem(lax.axis_index("vintage"), 2) == 1
+    holder = lax.rem(lax.axis_index("vintage"), 4) == 0
     zeros = jnp.zeros((half_lags, TRACES), jnp.float32)
     base[0:half_lags, :] = zeros
     base[half_lags + TIME_SAMPLES:, :] = zeros
 
-    @pl.when(odd)
-    def _():
-        base[half_lags:half_lags + TIME_SAMPLES, :] = near[...]
-
-    @pl.when(jnp.logical_not(odd))
+    @pl.when(holder)
     def _():
         base[half_lags:half_lags + TIME_SAMPLES, :] = held[...]
+
+    @pl.when(jnp.logical_not(holder))
+    def _():
+        base[half_lags:half_lags + TIME_SAMPLES, :] = far1[...] + far2[...] + far3[...]
 
     mon_energy = jnp.zeros((8, TRACES), jnp.float32)
     base_energy = jnp.zeros((8, TRACES), jnp.float32)
@@ -166,11 +177,11 @@
     )(*args)
 
 
-def correlate(mon, held, near):
+def correlate(mon, held, far):
     return pl.pallas_call(
         correl_kernel,
         out_shape=jax.ShapeDtypeStruct((ROWS, COLS, LAGS * NWIN), jnp.float32),
-        in_specs=vmem(3),
+        in_specs=vmem(5),
         out_specs=pl.BlockSpec(memory_space=pltpu.VMEM),
         scratch_shapes=[
             pltpu.VMEM((TIME_SAMPLES + LAGS - 1, TRACES), jnp.float32),
@@ -178,41 +189,53 @@
         ],
         compiler_params=pltpu.CompilerParams(vmem_limit_bytes=16 << 20),
         name="correlate",
-    )(mon, held, near)
-
-
-def exchange(last, first, axis, planes):
+    )(mon, held, *far)
+
+
+def pair_sends(first, last, axis):
+    odd = lax.rem(lax.axis_index(axis), 2) == 1
+    return jnp.where(odd, first, last), jnp.where(odd, last, first)
+
+
+def swap(sends, axis, planes):
     count = lax.axis_size(axis)
-    steps = [(v * count + i, v * count + i + 1) for v in planes for i in range(count - 1)]
-    low = lax.ppermute(last, ("vintage", axis), steps)
-    high = lax.ppermute(first, ("vintage", axis), [(target, source) for source, target in steps])
-    return low, high
-
-
-def rim_of(tile, last, first, planes):
-    up, down = exchange(last, first, "inline", planes)
-    wide = jnp.concatenate([up, tile, down], axis=0)
-    left, right = exchange(wide[:, -1:], wide[:, :1], "xline", planes)
-    return up, down, left, right
+    out = []
+    for start, send in enumerate(sends):
+        low = [(v * count + i, v * count + i + 1) for v in planes for i in range(start, count - 1, 2)]
+        out.append(lax.ppermute(send, ("vintage", axis), low + [(b, a) for a, b in low]))
+    return out
+
+
+def edge_columns(tile, rows):
+    odd = lax.rem(lax.axis_index("inline"), 2) == 1
+    above, below = jnp.where(odd, rows[0], rows[1]), jnp.where(odd, rows[1], rows[0])
+    first, last = (
+        jnp.concatenate([above[:, j:j + 1], tile[:, j:j + 1], below[:, j:j + 1]], axis=0)
+        for j in (0, COLS - 1)
+    )
+    return pair_sends(first, last, "xline")
 
 
 def per_device(amplitude, inline_slope, crossline_slope):
     tile = amplitude[0]
     dips = (inline_slope.reshape(1, TRACES), crossline_slope.reshape(1, TRACES))
     vintages = lax.axis_size("vintage")
-    place = lax.axis_index("vintage")
-    last, first = tile[-1:], tile[:1]
-    semb0, attr0 = attributes(first_kernel, "baseline", tile, *rim_of(tile, last, first, [0]), *dips)
-    got = [lax.ppermute(attr0, "vintage", [(0, k)]) for k in (8, 4, 12)]
-    last, first, attr0 = lax.optimization_barrier((last, first, attr0))
-    rim = rim_of(tile, last, first, range(1, vintages))
-    semb, attr = attributes(later_kernel, "monitor", tile, *rim, *dips, semb0, attr0)
+    others = range(1, vintages)
+    sends = pair_sends(tile[:1], tile[-1:], "inline")
+    rows = swap(sends, "inline", [0])
+    cols = edge_columns(tile, rows)
+    gated = lax.optimization_barrier((*cols, *sends))
+    cols, sends = gated[:2], gated[2:]
+    cols = swap(cols, "xline", [0])
+    semb0, attr0 = attributes(first_kernel, "baseline", tile, *FLIP(rows, F[0]), *FLIP(cols, F[1]), *dips)
+    got = [lax.ppermute(attr0, "vintage", [(0, k)]) for k in TT]
+    rows = swap(sends, "inline", others)
+    cols = swap(edge_columns(tile, rows), "xline", others)
+    semb, attr = attributes(later_kernel, "monitor", tile, *FLIP(rows, F[2]), *FLIP(cols, F[3]), *dips, semb0, attr0)
     got = lax.optimization_barrier((*got, attr))[:3]
-    held = jnp.where(place == 0, attr0, got[0] + got[1] + got[2])
-    half = lax.ppermute(held, "vintage", [(s, s + 2) for s in range(0, vintages, 4)])
-    held = jnp.where(lax.rem(place, 4) == 0, held, half)
-    near = lax.ppermute(held, "vintage", [(s, s + 1) for s in range(0, vintages, 2)])
-    correl = correlate(attr, held, near)
+    held = jnp.where(lax.axis_index("vintage") == 0, attr0, got[0] + got[1] + got[2])
+    far = [lax.ppermute(held, "vintage", [(s, s + k) for s in range(0, vintages, 4)]) for k in (1, 2, 3)]
+    correl = correlate(attr, held, far)
     return (semb[None], correl[None])
 
 

time: 47.4 us -> 42.7 us (0.901)
  the two profiles are of different devices: /device:TPU:63 before, /device:TPU:190 now
where the time goes in v3:
time: 42.7 us; the launch traced here: 42.3 us
  starting transfers between devices  25.6 us (60%)
  waiting for transfers between devices  11.2 us (26%)
  Pallas kernels  2.72 us (6%)
  local copies, waits for them, and re-layouts  1.08 us (3%)
  between operations  0.94 us (2%)
  other arithmetic  0.87 us (2%)
    ppermute x8, starting transfers between devices, swap(): lax.ppermute(send, ('vintage', axis), low + [(b, a) for a, b in low])  20.9 us
    ppermute x3, waiting for transfers between devices, per_device(): lax.ppermute(held, 'vintage', [(s, s + k) for s in range(0, vintages, 4)])  7.44 us
    ppermute x8, waiting for transfers between devices, swap(): lax.ppermute(send, ('vintage', axis), low + [(b, a) for a, b in low])  3.71 us
    ppermute x3, starting transfers between devices, per_device(): lax.ppermute(held, 'vintage', [(s, s + k) for s in range(0, vintages, 4)])  2.63 us
    ppermute x3, starting transfers between devices, per_device(): got = [lax.ppermute(attr0, 'vintage', [(0, k)]) for k in TT]  2.01 us
    pallas_call x2, Pallas kernels, attributes(): pl.pallas_call(kernel, out_shape=(jax.ShapeDtypeStruct((ROWS, COLS, TIME_...  1.52 us
    pallas_call x1, Pallas kernels, correlate(): pl.pallas_call(correl_kernel, out_shape=jax.ShapeDtypeStruct((ROWS, COLS,...  1.2 us
    slice x1, local copies, waits for them, and re-layouts, edge_columns(): tile[:, j:j + 1]  0.89 us
  transfers between devices with their start and end apart: 14, of which 2 were waited for; matrix products, arithmetic and copies ran while one was open for 3% of the time, Pallas kernels for 4%

profile of v3, /device:TPU:190, one launch (start us, length us, event | category | flops | bytes accessed | tf_op | source)
XLA Modules:
  0.0 42.3 jit_solution(10897508153018915609)
XLA Ops:
  0.6 0.0 copy-start
  0.6 0.8 %select_bitcast_fusion.1 = (f32[1,16,256]{2,1,0:T(8,128)S(1)}, f32[1,16,256]{2,1,0:T(8,128)S(1)}) fusion(f32[1,8,16,256]{3,2,1,0:T(8,128)} %param.3, pred[]{:T(512)S(6)} %eq.13), kind=kLoop, calls=%fused_computation.6 | loop fusion | flops 8192 | bytes 65537 | tf_op jit(solution)/shard_map/jit(_where)/select_n | solution.py:197
  1.4 0.7 %collective-permute-start = (f32[1,16,256]{2,1,0:T(8,128)S(1)}, f32[1,16,256]{2,1,0:T(8,128)S(1)}, u32[]{:S(2)}, u32[]{:S(2)}) collective-permute-start(f32[1,16,256]{2,1,0:T(8,128)S(1)} %get-tuple-element.13), channel_id=1, source_target_pairs={{0,8},{16,24},{8,0},{24,16},{1,9},{17,25},{9,1},{25,17},{2,10},{18... | collective-permute-start | bytes 49160 | tf_op jit(solution)/shard_map/ppermute | solution.py:205
  2.1 0.7 %collective-permute-start.1 = (f32[1,16,256]{2,1,0:T(8,128)S(1)}, f32[1,16,256]{2,1,0:T(8,128)S(1)}, u32[]{:S(2)}, u32[]{:S(2)}) collective-permute-start(f32[1,16,256]{2,1,0:T(8,128)S(1)} %get-tuple-element.14), channel_id=1, source_target_pairs={{8,16},{16,8},{9,17},{17,9},{10,18},{18,10},{11,19},{19,11},{12,20... | collective-permute-start | bytes 49160 | tf_op jit(solution)/shard_map/ppermute | solution.py:205
  2.8 0.9 %fusion = (f32[8,1,256]{2,1,0:T(1,128)S(1)}, f32[8,1,256]{2,1,0:T(1,128)S(1)}) fusion(f32[8,16,256]{2,1,0:T(8,128)} %bitcast.7), kind=kLoop, calls=%fused_computation.15 | loop fusion | bytes 32768 | tf_op jit(solution)/shard_map/slice | solution.py:213
  3.7 0.0 collective-permute-done.refs_1_
  3.7 0.0 collective-permute-done.1.refs_2_
  3.7 0.0 copy-start.1
  3.8 0.0 copy-start.2
  3.8 1.9 %collective-permute-start.2 = (f32[1,16,256]{2,1,0:T(8,128)S(1)}, f32[1,16,256]{2,1,0:T(8,128)S(1)}, u32[]{:S(2)}, u32[]{:S(2)}) collective-permute-start(f32[1,16,256]{2,1,0:T(8,128)S(1)} %get-tuple-element.13), channel_id=1, source_target_pairs={{32,40},{48,56},{64,72},{80,88},{96,104},{112,120},{128,136},{144,... | collective-permute-start | bytes 49160 | tf_op jit(solution)/shard_map/ppermute | solution.py:205
  5.7 9.7 %collective-permute-start.3 = (f32[1,16,256]{2,1,0:T(8,128)S(1)}, f32[1,16,256]{2,1,0:T(8,128)S(1)}, u32[]{:S(2)}, u32[]{:S(2)}) collective-permute-start(f32[1,16,256]{2,1,0:T(8,128)S(1)} %get-tuple-element.14), channel_id=1, source_target_pairs={{40,48},{72,80},{104,112},{136,144},{168,176},{200,208},{232,240},... | collective-permute-start | bytes 49160 | tf_op jit(solution)/shard_map/ppermute | solution.py:205
  15.4 0.7 %collective-permute-start.6 = (f32[10,1,256]{2,1,0:T(1,128)S(1)}, f32[10,1,256]{2,1,0:T(1,128)S(1)}, u32[]{:S(2)}, u32[]{:S(2)}) collective-permute-start(f32[10,1,256]{2,1,0:T(1,128)S(1)} %get-tuple-element.15), channel_id=1, source_target_pairs={{0,1},{2,3},{4,5},{6,7},{1,0},{3,2},{5,4},{7,6},{8,9},{10,11},{12,... | collective-permute-start | bytes 30728 | tf_op jit(solution)/shard_map/ppermute | solution.py:205
  16.0 0.7 %collective-permute-start.7 = (f32[10,1,256]{2,1,0:T(1,128)S(1)}, f32[10,1,256]{2,1,0:T(1,128)S(1)}, u32[]{:S(2)}, u32[]{:S(2)}) collective-permute-start(f32[10,1,256]{2,1,0:T(1,128)S(1)} %get-tuple-element.16), channel_id=1, source_target_pairs={{1,2},{3,4},{5,6},{2,1},{4,3},{6,5},{9,10},{11,12},{13,14},{10,9},... | collective-permute-start | bytes 30728 | tf_op jit(solution)/shard_map/ppermute | solution.py:205
  16.7 0.0 copy-done.1
  16.7 0.1 reshape.360.refs_5_
  16.8 0.0 copy-done.2
  16.8 0.1 reshape.361.refs_6_
  16.9 0.0 collective-permute-done.6.refs_3_
  16.9 0.0 collective-permute-done.7.refs_4_
  16.9 0.0 copy-done
  16.9 0.7 %collective-permute-start.10 = (f32[256,128]{1,0:T(8,128)S(1)}, f32[256,128]{1,0:T(8,128)S(1)}, u32[]{:S(2)}, u32[]{:S(2)}) collective-permute-start(f32[256,128]{1,0:T(8,128)S(1)} %get-tuple-element.18.refs_8_), channel_id=1, source_target_pairs={{0,256},{1,257},{2,258},{3,259},{4,260},{5,261},{6,262},{7,263},{8... | collective-permute-start | bytes 393224 | tf_op jit(solution)/shard_map/ppermute | solution.py:231
  17.6 0.7 %collective-permute-start.9 = (f32[256,128]{1,0:T(8,128)S(1)}, f32[256,128]{1,0:T(8,128)S(1)}, u32[]{:S(2)}, u32[]{:S(2)}) collective-permute-start(f32[256,128]{1,0:T(8,128)S(1)} %get-tuple-element.18.refs_8_), channel_id=1, source_target_pairs={{0,128},{1,129},{2,130},{3,131},{4,132},{5,133},{6,134},{7,135},{8... | collective-permute-start | bytes 393224 | tf_op jit(solution)/shard_map/ppermute | solution.py:231
  18.3 0.7 %collective-permute-start.8 = (f32[256,128]{1,0:T(8,128)S(1)}, f32[256,128]{1,0:T(8,128)S(1)}, u32[]{:S(2)}, u32[]{:S(2)}) collective-permute-start(f32[256,128]{1,0:T(8,128)S(1)} %get-tuple-element.18.refs_8_), channel_id=1, source_target_pairs={{0,384},{1,385},{2,386},{3,387},{4,388},{5,389},{6,390},{7,391},{8... | collective-permute-start | bytes 393224 | tf_op jit(solution)/shard_map/ppermute | solution.py:231
  19.0 0.0 collective-permute-done.2.refs_1_
  19.0 0.0 collective-permute-done.3.refs_2_
  19.1 2.7 %collective-permute-start.5 = (f32[10,1,256]{2,1,0:T(1,128)S(1)}, f32[10,1,256]{2,1,0:T(1,128)S(1)}, u32[]{:S(2)}, u32[]{:S(2)}) collective-permute-start(f32[10,1,256]{2,1,0:T(1,128)S(1)} %get-tuple-element.32), channel_id=1, source_target_pairs={{32,33},{34,35},{36,37},{38,39},{64,65},{66,67},{68,69},{70,71},{9... | collective-permute-start | bytes 30728 | tf_op jit(solution)/shard_map/ppermute | solution.py:205
  21.8 4.0 %collective-permute-start.4 = (f32[10,1,256]{2,1,0:T(1,128)S(1)}, f32[10,1,256]{2,1,0:T(1,128)S(1)}, u32[]{:S(2)}, u32[]{:S(2)}) collective-permute-start(f32[10,1,256]{2,1,0:T(1,128)S(1)} %get-tuple-element.33), channel_id=1, source_target_pairs={{33,34},{35,36},{37,38},{65,66},{67,68},{69,70},{97,98},{99,100},{... | collective-permute-start | bytes 30728 | tf_op jit(solution)/shard_map/ppermute | solution.py:205
  25.8 0.0 collective-permute-done.5.refs_4_
  25.8 3.7 %collective-permute-done.4.refs_3_ = f32[10,1,256]{2,1,0:T(1,128)S(1)} collective-permute-done((f32[10,1,256]{2,1,0:T(1,128)S(1)}, f32[10,1,256]{2,1,0:T(1,128)S(1)}, u32[]{:S(2)}, u32[]{:S(2)}) %collective-permute-start.4) | collective-permute-done | bytes 10272 | tf_op jit(solution)/shard_map/ppermute | solution.py:205
  29.5 1.5 %monitor.1 = (f32[8,16,256]{2,1,0:T(8,128)}, f32[256,128]{1,0:T(8,128)S(1)}) custom-call(f32[8,16,256]{2,1,0:T(8,128)S(1)} %bitcast.9, f32[1,16,256]{2,1,0:T(8,128)S(1)} %collective-permute-done.2.refs_1_, f32[1,16,256]{2,1,0:T(8,128)S(1)} %collective-permute-done.3.refs_2_, f32[10,1,256]{2,1,0:T(1,128)S(1)} %collective-permute-done.4.refs_3_, ...), custom_call_target="tpu_custom_call" | custom-call | tf_op jit(solution)/shard_map/monitor/pallas_call | solution.py:160
  31.0 0.0 collective-permute-done.10
  31.0 0.0 collective-permute-done.9
  31.0 0.0 collective-permute-done.8
  31.0 0.7 %collective-permute-start.13 = (f32[256,128]{1,0:T(8,128)S(1)}, f32[256,128]{1,0:T(8,128)S(1)}, u32[]{:S(2)}, u32[]{:S(2)}) collective-permute-start(f32[256,128]{1,0:T(8,128)S(1)} %add_select_fusion.held), channel_id=1, source_target_pairs={{0,96},{128,224},{256,352},{384,480},{1,97},{129,225},{257,353},{3... | collective-permute-start | bytes 393224 | tf_op jit(solution)/shard_map/ppermute | solution.py:237
  31.7 1.3 %collective-permute-start.12 = (f32[256,128]{1,0:T(8,128)S(1)}, f32[256,128]{1,0:T(8,128)S(1)}, u32[]{:S(2)}, u32[]{:S(2)}) collective-permute-start(f32[256,128]{1,0:T(8,128)S(1)} %add_select_fusion.held), channel_id=1, source_target_pairs={{0,64},{128,192},{256,320},{384,448},{1,65},{129,193},{257,321},{3... | collective-permute-start | bytes 393224 | tf_op jit(solution)/shard_map/ppermute | solution.py:237
  33.0 0.7 %collective-permute-start.11 = (f32[256,128]{1,0:T(8,128)S(1)}, f32[256,128]{1,0:T(8,128)S(1)}, u32[]{:S(2)}, u32[]{:S(2)}) collective-permute-start(f32[256,128]{1,0:T(8,128)S(1)} %add_select_fusion.held), channel_id=1, source_target_pairs={{0,32},{128,160},{256,288},{384,416},{1,33},{129,161},{257,289},{3... | collective-permute-start | bytes 393224 | tf_op jit(solution)/shard_map/ppermute | solution.py:237
  33.7 0.0 collective-permute-done.13.far1
  33.7 7.4 %collective-permute-done.12.far2 = f32[256,128]{1,0:T(8,128)S(1)} collective-permute-done((f32[256,128]{1,0:T(8,128)S(1)}, f32[256,128]{1,0:T(8,128)S(1)}, u32[]{:S(2)}, u32[]{:S(2)}) %collective-permute-start.12) | collective-permute-done | bytes 131104 | tf_op jit(solution)/shard_map/ppermute | solution.py:237
  41.1 0.0 collective-permute-done.11.far3
  41.1 1.2 %correlate.1 = f32[8,16,264]{2,1,0:T(8,128)} custom-call(f32[256,128]{1,0:T(8,128)S(1)} %get-tuple-element.20.mon, f32[256,128]{1,0:T(8,128)S(1)} %add_select_fusion.held, f32[256,128]{1,0:T(8,128)S(1)} %collective-permute-done.11.far3, f32[256,128]{1,0:T(8,128)S(1)} %collective-permute-done.12.far2, f32[256,128]{1,0:T(8,128)S(1)} %collective-permute-done.13.far1), custom_call_target="tpu_custom_call" | custom-call | tf_op jit(solution)/shard_map/correlate/pallas_call | solution.py:181
  (9 shorter events, 0.1 us)
Async XLA Ops:
  0.6 16.3 %copy-start = (f32[1,8,16,256]{3,2,1,0:T(8,128)S(1)}, f32[1,8,16,256]{3,2,1,0:T(8,128)}, u32[]{:S(2)}) copy-start(f32[1,8,16,256]{3,2,1,0:T(8,128)} %param.3) | copy-start | bytes 393220
  1.4 2.2 %collective-permute-start = (f32[1,16,256]{2,1,0:T(8,128)S(1)}, f32[1,16,256]{2,1,0:T(8,128)S(1)}, u32[]{:S(2)}, u32[]{:S(2)}) collective-permute-start(f32[1,16,256]{2,1,0:T(8,128)S(1)} %get-tuple-element.13), channel_id=1, source_target_pairs={{0,8},{16,24},{8,0},{24,16},{1,9},{17,25},{9,1},{25,17},{2,10},{18... | collective-permute-start | bytes 49160 | tf_op jit(solution)/shard_map/ppermute | solution.py:205
  2.1 1.6 %collective-permute-start.1 = (f32[1,16,256]{2,1,0:T(8,128)S(1)}, f32[1,16,256]{2,1,0:T(8,128)S(1)}, u32[]{:S(2)}, u32[]{:S(2)}) collective-permute-start(f32[1,16,256]{2,1,0:T(8,128)S(1)} %get-tuple-element.14), channel_id=1, source_target_pairs={{8,16},{16,8},{9,17},{17,9},{10,18},{18,10},{11,19},{19,11},{12,20... | collective-permute-start | bytes 49160 | tf_op jit(solution)/shard_map/ppermute | solution.py:205
  3.7 13.0 %copy-start.1 = (s32[1,8,16]{2,1,0:T(8,128)S(1)}, s32[1,8,16]{2,1,0:T(8,128)}, u32[]{:S(2)}) copy-start(s32[1,8,16]{2,1,0:T(8,128)} %param.4) | copy-start | bytes 1540
  3.8 13.1 %copy-start.2 = (s32[1,8,16]{2,1,0:T(8,128)S(1)}, s32[1,8,16]{2,1,0:T(8,128)}, u32[]{:S(2)}) copy-start(s32[1,8,16]{2,1,0:T(8,128)} %param.5) | copy-start | bytes 1540
  3.8 15.2 %collective-permute-start.2 = (f32[1,16,256]{2,1,0:T(8,128)S(1)}, f32[1,16,256]{2,1,0:T(8,128)S(1)}, u32[]{:S(2)}, u32[]{:S(2)}) collective-permute-start(f32[1,16,256]{2,1,0:T(8,128)S(1)} %get-tuple-element.13), channel_id=1, source_target_pairs={{32,40},{48,56},{64,72},{80,88},{96,104},{112,120},{128,136},{144,... | collective-permute-start | bytes 49160 | tf_op jit(solution)/shard_map/ppermute | solution.py:205
  5.7 13.3 %collective-permute-start.3 = (f32[1,16,256]{2,1,0:T(8,128)S(1)}, f32[1,16,256]{2,1,0:T(8,128)S(1)}, u32[]{:S(2)}, u32[]{:S(2)}) collective-permute-start(f32[1,16,256]{2,1,0:T(8,128)S(1)} %get-tuple-element.14), channel_id=1, source_target_pairs={{40,48},{72,80},{104,112},{136,144},{168,176},{200,208},{232,240},... | collective-permute-start | bytes 49160 | tf_op jit(solution)/shard_map/ppermute | solution.py:205
  15.4 1.5 %collective-permute-start.6 = (f32[10,1,256]{2,1,0:T(1,128)S(1)}, f32[10,1,256]{2,1,0:T(1,128)S(1)}, u32[]{:S(2)}, u32[]{:S(2)}) collective-permute-start(f32[10,1,256]{2,1,0:T(1,128)S(1)} %get-tuple-element.15), channel_id=1, source_target_pairs={{0,1},{2,3},{4,5},{6,7},{1,0},{3,2},{5,4},{7,6},{8,9},{10,11},{12,... | collective-permute-start | bytes 30728 | tf_op jit(solution)/shard_map/ppermute | solution.py:205
  16.0 0.9 %collective-permute-start.7 = (f32[10,1,256]{2,1,0:T(1,128)S(1)}, f32[10,1,256]{2,1,0:T(1,128)S(1)}, u32[]{:S(2)}, u32[]{:S(2)}) collective-permute-start(f32[10,1,256]{2,1,0:T(1,128)S(1)} %get-tuple-element.16), channel_id=1, source_target_pairs={{1,2},{3,4},{5,6},{2,1},{4,3},{6,5},{9,10},{11,12},{13,14},{10,9},... | collective-permute-start | bytes 30728 | tf_op jit(solution)/shard_map/ppermute | solution.py:205
  16.9 14.0 %collective-permute-start.10 = (f32[256,128]{1,0:T(8,128)S(1)}, f32[256,128]{1,0:T(8,128)S(1)}, u32[]{:S(2)}, u32[]{:S(2)}) collective-permute-start(f32[256,128]{1,0:T(8,128)S(1)} %get-tuple-element.18.refs_8_), channel_id=1, source_target_pairs={{0,256},{1,257},{2,258},{3,259},{4,260},{5,261},{6,262},{7,263},{8... | collective-permute-start | bytes 393224 | tf_op jit(solution)/shard_map/ppermute | solution.py:231
  17.6 13.4 %collective-permute-start.9 = (f32[256,128]{1,0:T(8,128)S(1)}, f32[256,128]{1,0:T(8,128)S(1)}, u32[]{:S(2)}, u32[]{:S(2)}) collective-permute-start(f32[256,128]{1,0:T(8,128)S(1)} %get-tuple-element.18.refs_8_), channel_id=1, source_target_pairs={{0,128},{1,129},{2,130},{3,131},{4,132},{5,133},{6,134},{7,135},{8... | collective-permute-start | bytes 393224 | tf_op jit(solution)/shard_map/ppermute | solution.py:231
  18.3 12.7 %collective-permute-start.8 = (f32[256,128]{1,0:T(8,128)S(1)}, f32[256,128]{1,0:T(8,128)S(1)}, u32[]{:S(2)}, u32[]{:S(2)}) collective-permute-start(f32[256,128]{1,0:T(8,128)S(1)} %get-tuple-element.18.refs_8_), channel_id=1, source_target_pairs={{0,384},{1,385},{2,386},{3,387},{4,388},{5,389},{6,390},{7,391},{8... | collective-permute-start | bytes 393224 | tf_op jit(solution)/shard_map/ppermute | solution.py:231
  19.1 6.7 %collective-permute-start.5 = (f32[10,1,256]{2,1,0:T(1,128)S(1)}, f32[10,1,256]{2,1,0:T(1,128)S(1)}, u32[]{:S(2)}, u32[]{:S(2)}) collective-permute-start(f32[10,1,256]{2,1,0:T(1,128)S(1)} %get-tuple-element.32), channel_id=1, source_target_pairs={{32,33},{34,35},{36,37},{38,39},{64,65},{66,67},{68,69},{70,71},{9... | collective-permute-start | bytes 30728 | tf_op jit(solution)/shard_map/ppermute | solution.py:205
  21.8 7.7 %collective-permute-start.4 = (f32[10,1,256]{2,1,0:T(1,128)S(1)}, f32[10,1,256]{2,1,0:T(1,128)S(1)}, u32[]{:S(2)}, u32[]{:S(2)}) collective-permute-start(f32[10,1,256]{2,1,0:T(1,128)S(1)} %get-tuple-element.33), channel_id=1, source_target_pairs={{33,34},{35,36},{37,38},{65,66},{67,68},{69,70},{97,98},{99,100},{... | collective-permute-start | bytes 30728 | tf_op jit(solution)/shard_map/ppermute | solution.py:205
  31.0 2.7 %collective-permute-start.13 = (f32[256,128]{1,0:T(8,128)S(1)}, f32[256,128]{1,0:T(8,128)S(1)}, u32[]{:S(2)}, u32[]{:S(2)}) collective-permute-start(f32[256,128]{1,0:T(8,128)S(1)} %add_select_fusion.held), channel_id=1, source_target_pairs={{0,96},{128,224},{256,352},{384,480},{1,97},{129,225},{257,353},{3... | collective-permute-start | bytes 393224 | tf_op jit(solution)/shard_map/ppermute | solution.py:237
  31.7 9.4 %collective-permute-start.12 = (f32[256,128]{1,0:T(8,128)S(1)}, f32[256,128]{1,0:T(8,128)S(1)}, u32[]{:S(2)}, u32[]{:S(2)}) collective-permute-start(f32[256,128]{1,0:T(8,128)S(1)} %add_select_fusion.held), channel_id=1, source_target_pairs={{0,64},{128,192},{256,320},{384,448},{1,65},{129,193},{257,321},{3... | collective-permute-start | bytes 393224 | tf_op jit(solution)/shard_map/ppermute | solution.py:237
  33.0 8.1 %collective-permute-start.11 = (f32[256,128]{1,0:T(8,128)S(1)}, f32[256,128]{1,0:T(8,128)S(1)}, u32[]{:S(2)}, u32[]{:S(2)}) collective-permute-start(f32[256,128]{1,0:T(8,128)S(1)} %add_select_fusion.held), channel_id=1, source_target_pairs={{0,32},{128,160},{256,288},{384,416},{1,33},{129,161},{257,289},{3... | collective-permute-start | bytes 393224 | tf_op jit(solution)/shard_map/ppermute | solution.py:237

commit v4 on v3

--- a/solution.py
+++ b/solution.py
@@ -1,3 +1,5 @@
+import functools
+
 import jax
 import jax.numpy as jnp
 from jax import lax
@@ -11,14 +13,9 @@
 LAGS = 33
 NWIN = 8
 EPS = 1e-06
-F = (0, 0, 0, 1)
-TT = (12, 4, 8)
-
-
-def FLIP(x, f):
-    return tuple(x)[::-1] if f else tuple(x)
-
-
+
+HEAD = 0, 1, 2, 14
+FANOUT = {0: (8, 4, 12), 1: (9, 5, 13), 2: (6, 7, 3), 14: (10, 11, 15)}
 ROWS = 8
 COLS = 16
 TRACES = ROWS * COLS
@@ -34,26 +31,28 @@
     return out
 
 
+def is_head(place):
+    return functools.reduce(jnp.logical_or, [place == v for v in HEAD])
+
+
 def first_kernel(*refs):
-    @pl.when(lax.axis_index("vintage") == 0)
-    def _():
-        r = refs
-        attr_body(r[0], *FLIP(r[1:3], F[0]), *FLIP(r[3:5], F[1]), *r[5:])
+    @pl.when(is_head(lax.axis_index("vintage")))
+    def _():
+        attr_body(refs[0], refs[1], refs[2], refs[4], refs[3], *refs[5:])
 
 
 def later_kernel(*refs):
     ins, semb_first, attr_first, semb_out, attr_out = refs[:7], refs[7], refs[8], refs[9], refs[10]
-    first = lax.axis_index("vintage") == 0
-
-    @pl.when(first)
+    head = is_head(lax.axis_index("vintage"))
+
+    @pl.when(head)
     def _():
         semb_out[...] = semb_first[...]
         attr_out[...] = attr_first[...]
 
-    @pl.when(jnp.logical_not(first))
-    def _():
-        r = ins
-        attr_body(r[0], *FLIP(r[1:3], F[2]), *FLIP(r[3:5], F[3]), *r[5:], *refs[9:])
+    @pl.when(jnp.logical_not(head))
+    def _():
+        attr_body(*ins, *refs[9:])
 
 
 def attr_body(tile, row_a, row_b, col_a, col_b, dip_il, dip_xl, semb_out, attr_out,
@@ -112,7 +111,7 @@
 
 def correl_kernel(mon, held, far3, far2, far1, out, base, result):
     half_lags = LAGS // 2
-    holder = lax.rem(lax.axis_index("vintage"), 4) == 0
+    holder = is_head(lax.axis_index("vintage"))
     zeros = jnp.zeros((half_lags, TRACES), jnp.float32)
     base[0:half_lags, :] = zeros
     base[half_lags + TIME_SAMPLES:, :] = zeros
@@ -206,12 +205,12 @@
     return out
 
 
-def edge_columns(tile, rows):
+def edge_columns(ends, rows):
     odd = lax.rem(lax.axis_index("inline"), 2) == 1
     above, below = jnp.where(odd, rows[0], rows[1]), jnp.where(odd, rows[1], rows[0])
     first, last = (
-        jnp.concatenate([above[:, j:j + 1], tile[:, j:j + 1], below[:, j:j + 1]], axis=0)
-        for j in (0, COLS - 1)
+        jnp.concatenate([above[:, j:j + 1], end, below[:, j:j + 1]], axis=0)
+        for j, end in zip((0, COLS - 1), ends)
     )
     return pair_sends(first, last, "xline")
 
@@ -219,22 +218,24 @@
 def per_device(amplitude, inline_slope, crossline_slope):
     tile = amplitude[0]
     dips = (inline_slope.reshape(1, TRACES), crossline_slope.reshape(1, TRACES))
-    vintages = lax.axis_size("vintage")
-    others = range(1, vintages)
+    others = [v for v in range(lax.axis_size("vintage")) if v not in HEAD]
     sends = pair_sends(tile[:1], tile[-1:], "inline")
-    rows = swap(sends, "inline", [0])
-    cols = edge_columns(tile, rows)
-    gated = lax.optimization_barrier((*cols, *sends))
-    cols, sends = gated[:2], gated[2:]
-    cols = swap(cols, "xline", [0])
-    semb0, attr0 = attributes(first_kernel, "baseline", tile, *FLIP(rows, F[0]), *FLIP(cols, F[1]), *dips)
-    got = [lax.ppermute(attr0, "vintage", [(0, k)]) for k in TT]
+    rows = swap(sends, "inline", HEAD)
+    gated = lax.optimization_barrier((*sends[::-1], tile[:, :1], tile[:, -1:]))
+    ends, sends = gated[2:], gated[1::-1]
+    cols = swap(edge_columns(ends, rows), "xline", HEAD)
+    semb0, attr0 = attributes(first_kernel, "head", tile, *rows, *cols[::-1], *dips)
+    got = [lax.ppermute(attr0, "vintage", [(0, k)]) for k in (1, 14, 2)]
+    held = jnp.where(lax.axis_index("vintage") == 0, attr0, got[0] + got[1] + got[2])
+    far = [
+        lax.ppermute(held, "vintage", [(s, FANOUT[s][n]) for s in HEAD])
+        for n in (2, 1, 0)
+    ]
     rows = swap(sends, "inline", others)
-    cols = swap(edge_columns(tile, rows), "xline", others)
-    semb, attr = attributes(later_kernel, "monitor", tile, *FLIP(rows, F[2]), *FLIP(cols, F[3]), *dips, semb0, attr0)
-    got = lax.optimization_barrier((*got, attr))[:3]
-    held = jnp.where(lax.axis_index("vintage") == 0, attr0, got[0] + got[1] + got[2])
-    far = [lax.ppermute(held, "vintage", [(s, s + k) for s in range(0, vintages, 4)]) for k in (1, 2, 3)]
+    cols = edge_columns(ends, rows)
+    cols = lax.optimization_barrier((*cols, held))[:2]
+    cols = swap(cols, "xline", others)
+    semb, attr = attributes(later_kernel, "tail", tile, *rows, *cols, *dips, semb0, attr0)
     correl = correlate(attr, held, far)
     return (semb[None], correl[None])
 

time: 42.7 us -> 46.7 us (1.094)
  the two profiles are of different devices: /device:TPU:190 before, /device:TPU:159 now
where the time goes in v4:
time: 46.7 us; the launch traced here: 46.3 us
  starting transfers between devices  24.4 us (52%)
  waiting for transfers between devices  15.7 us (34%)
  Pallas kernels  2.73 us (6%)
  local copies, waits for them, and re-layouts  1.66 us (4%)
  between operations  0.94 us (2%)
  other arithmetic  0.88 us (2%)
    ppermute x8, starting transfers between devices, swap(): lax.ppermute(send, ('vintage', axis), low + [(b, a) for a, b in low])  19.8 us
    ppermute x3, waiting for transfers between devices, per_device(): lax.ppermute(held, 'vintage', [(s, FANOUT[s][n]) for s in HEAD])  12.8 us
    ppermute x8, waiting for transfers between devices, swap(): lax.ppermute(send, ('vintage', axis), low + [(b, a) for a, b in low])  2.85 us
    ppermute x3, starting transfers between devices, per_device(): lax.ppermute(held, 'vintage', [(s, FANOUT[s][n]) for s in HEAD])  2.63 us
    ppermute x3, starting transfers between devices, per_device(): got = [lax.ppermute(attr0, 'vintage', [(0, k)]) for k in (1, 14, 2)]  2.01 us
    pallas_call x2, Pallas kernels, attributes(): pl.pallas_call(kernel, out_shape=(jax.ShapeDtypeStruct((ROWS, COLS, TIME_...  1.53 us
    pallas_call x1, Pallas kernels, correlate(): pl.pallas_call(correl_kernel, out_shape=jax.ShapeDtypeStruct((ROWS, COLS,...  1.2 us
  transfers between devices with their start and end apart: 14, of which 2 were waited for; matrix products, arithmetic and copies ran while one was open for 2% of the time, Pallas kernels for 3%

profile of v4, /device:TPU:159, one launch (start us, length us, event | category | flops | bytes accessed | tf_op | source)
XLA Modules:
  0.0 46.3 jit_solution(10137337247559168324)
XLA Ops:
  0.6 0.0 copy-start
  0.6 0.8 %select_bitcast_fusion = (f32[1,16,256]{2,1,0:T(8,128)S(1)}, f32[1,16,256]{2,1,0:T(8,128)S(1)}) fusion(f32[1,8,16,256]{3,2,1,0:T(8,128)} %param.3, pred[]{:T(512)S(6)} %eq.12), kind=kLoop, calls=%fused_computation.5 | loop fusion | flops 8192 | bytes 65537 | tf_op jit(solution)/shard_map/jit(_where)/select_n | solution.py:196
  1.4 0.7 %collective-permute-start.2 = (f32[1,16,256]{2,1,0:T(8,128)S(1)}, f32[1,16,256]{2,1,0:T(8,128)S(1)}, u32[]{:S(2)}, u32[]{:S(2)}) collective-permute-start(f32[1,16,256]{2,1,0:T(8,128)S(1)} %get-tuple-element.12), channel_id=1, source_target_pairs={{0,8},{16,24},{32,40},{48,56},{64,72},{80,88},{448,456},{464,472},... | collective-permute-start | bytes 49160 | tf_op jit(solution)/shard_map/ppermute | solution.py:204
  2.1 0.7 %collective-permute-start.3 = (f32[1,16,256]{2,1,0:T(8,128)S(1)}, f32[1,16,256]{2,1,0:T(8,128)S(1)}, u32[]{:S(2)}, u32[]{:S(2)}) collective-permute-start(f32[1,16,256]{2,1,0:T(8,128)S(1)} %get-tuple-element.13), channel_id=1, source_target_pairs={{8,16},{40,48},{72,80},{456,464},{16,8},{48,40},{80,72},{464,456},... | collective-permute-start | bytes 49160 | tf_op jit(solution)/shard_map/ppermute | solution.py:204
  2.8 0.9 %fusion = (f32[8,1,256]{2,1,0:T(1,128)S(1)}, f32[8,1,256]{2,1,0:T(1,128)S(1)}) fusion(f32[8,16,256]{2,1,0:T(8,128)} %bitcast.7), kind=kLoop, calls=%fused_computation.15 | loop fusion | bytes 32768 | tf_op jit(solution)/shard_map/slice | solution.py:224
  3.7 1.9 %collective-permute-start = (f32[1,16,256]{2,1,0:T(8,128)S(1)}, f32[1,16,256]{2,1,0:T(8,128)S(1)}, u32[]{:S(2)}, u32[]{:S(2)}) collective-permute-start(f32[1,16,256]{2,1,0:T(8,128)S(1)} %get-tuple-element.12), channel_id=1, source_target_pairs={{96,104},{112,120},{128,136},{144,152},{160,168},{176,184},{192,20... | collective-permute-start | bytes 49160 | tf_op jit(solution)/shard_map/ppermute | solution.py:204
  5.6 9.1 %collective-permute-start.1 = (f32[1,16,256]{2,1,0:T(8,128)S(1)}, f32[1,16,256]{2,1,0:T(8,128)S(1)}, u32[]{:S(2)}, u32[]{:S(2)}) collective-permute-start(f32[1,16,256]{2,1,0:T(8,128)S(1)} %get-tuple-element.13), channel_id=1, source_target_pairs={{104,112},{136,144},{168,176},{200,208},{232,240},{264,272},{296,3... | collective-permute-start | bytes 49160 | tf_op jit(solution)/shard_map/ppermute | solution.py:204
  14.7 0.0 collective-permute-done.2.refs_1_
  14.7 0.0 collective-permute-done.3.refs_2_
  14.8 0.7 %collective-permute-start.5 = (f32[10,1,256]{2,1,0:T(1,128)S(1)}, f32[10,1,256]{2,1,0:T(1,128)S(1)}, u32[]{:S(2)}, u32[]{:S(2)}) collective-permute-start(f32[10,1,256]{2,1,0:T(1,128)S(1)} %get-tuple-element.30), channel_id=1, source_target_pairs={{0,1},{2,3},{4,5},{6,7},{32,33},{34,35},{36,37},{38,39},{64,65},{6... | collective-permute-start | bytes 30728 | tf_op jit(solution)/shard_map/ppermute | solution.py:204
  15.5 0.0 copy-start.1
  15.5 0.7 %collective-permute-start.4 = (f32[10,1,256]{2,1,0:T(1,128)S(1)}, f32[10,1,256]{2,1,0:T(1,128)S(1)}, u32[]{:S(2)}, u32[]{:S(2)}) collective-permute-start(f32[10,1,256]{2,1,0:T(1,128)S(1)} %get-tuple-element.31), channel_id=1, source_target_pairs={{1,2},{3,4},{5,6},{33,34},{35,36},{37,38},{65,66},{67,68},{69,70},... | collective-permute-start | bytes 30728 | tf_op jit(solution)/shard_map/ppermute | solution.py:204
  16.1 0.0 copy-start.2
  16.2 0.0 copy-done.1
  16.2 0.1 reshape.360.refs_5_
  16.2 0.6 %copy-done.2 = s32[1,8,16]{2,1,0:T(8,128)S(1)} copy-done((s32[1,8,16]{2,1,0:T(8,128)S(1)}, s32[1,8,16]{2,1,0:T(8,128)}, u32[]{:S(2)}) %copy-start.2) | copy-done | bytes 536
  16.8 0.1 reshape.361.refs_6_
  16.9 0.0 collective-permute-done.5.refs_4_
  16.9 0.0 collective-permute-done.4.refs_3_
  16.9 0.0 copy-done
  17.0 0.7 %collective-permute-start.8 = (f32[256,128]{1,0:T(8,128)S(1)}, f32[256,128]{1,0:T(8,128)S(1)}, u32[]{:S(2)}, u32[]{:S(2)}) collective-permute-start(f32[256,128]{1,0:T(8,128)S(1)} %get-tuple-element.16.refs_8_), channel_id=1, source_target_pairs={{0,64},{1,65},{2,66},{3,67},{4,68},{5,69},{6,70},{7,71},{8,72},{9,... | collective-permute-start | bytes 393224 | tf_op jit(solution)/shard_map/ppermute | solution.py:228
  17.6 0.7 %collective-permute-start.7 = (f32[256,128]{1,0:T(8,128)S(1)}, f32[256,128]{1,0:T(8,128)S(1)}, u32[]{:S(2)}, u32[]{:S(2)}) collective-permute-start(f32[256,128]{1,0:T(8,128)S(1)} %get-tuple-element.16.refs_8_), channel_id=1, source_target_pairs={{0,448},{1,449},{2,450},{3,451},{4,452},{5,453},{6,454},{7,455},{8... | collective-permute-start | bytes 393224 | tf_op jit(solution)/shard_map/ppermute | solution.py:228
  18.3 0.7 %collective-permute-start.6 = (f32[256,128]{1,0:T(8,128)S(1)}, f32[256,128]{1,0:T(8,128)S(1)}, u32[]{:S(2)}, u32[]{:S(2)}) collective-permute-start(f32[256,128]{1,0:T(8,128)S(1)} %get-tuple-element.16.refs_8_), channel_id=1, source_target_pairs={{0,32},{1,33},{2,34},{3,35},{4,36},{5,37},{6,38},{7,39},{8,40},{9,... | collective-permute-start | bytes 393224 | tf_op jit(solution)/shard_map/ppermute | solution.py:228
  19.0 0.0 collective-permute-done.refs_1_
  19.0 0.0 collective-permute-done.1.refs_2_
  19.0 0.0 collective-permute-done.8
  19.0 0.0 collective-permute-done.7
  19.1 0.0 collective-permute-done.6
  19.1 0.7 %collective-permute-start.13 = (f32[256,128]{1,0:T(8,128)S(1)}, f32[256,128]{1,0:T(8,128)S(1)}, u32[]{:S(2)}, u32[]{:S(2)}) collective-permute-start(f32[256,128]{1,0:T(8,128)S(1)} %add_select_fusion.held), channel_id=1, source_target_pairs={{0,256},{32,288},{64,192},{448,320},{1,257},{33,289},{65,193},{449... | collective-permute-start | bytes 393224 | tf_op jit(solution)/shard_map/ppermute | solution.py:231
  19.8 1.3 %collective-permute-start.12 = (f32[256,128]{1,0:T(8,128)S(1)}, f32[256,128]{1,0:T(8,128)S(1)}, u32[]{:S(2)}, u32[]{:S(2)}) collective-permute-start(f32[256,128]{1,0:T(8,128)S(1)} %add_select_fusion.held), channel_id=1, source_target_pairs={{0,128},{32,160},{64,224},{448,352},{1,129},{33,161},{65,225},{449... | collective-permute-start | bytes 393224 | tf_op jit(solution)/shard_map/ppermute | solution.py:231
  21.1 0.7 %collective-permute-start.11 = (f32[256,128]{1,0:T(8,128)S(1)}, f32[256,128]{1,0:T(8,128)S(1)}, u32[]{:S(2)}, u32[]{:S(2)}) collective-permute-start(f32[256,128]{1,0:T(8,128)S(1)} %add_select_fusion.held), channel_id=1, source_target_pairs={{0,384},{32,416},{64,96},{448,480},{1,385},{33,417},{65,97},{449,4... | collective-permute-start | bytes 393224 | tf_op jit(solution)/shard_map/ppermute | solution.py:231
  21.8 2.5 %collective-permute-start.9 = (f32[10,1,256]{2,1,0:T(1,128)S(1)}, f32[10,1,256]{2,1,0:T(1,128)S(1)}, u32[]{:S(2)}, u32[]{:S(2)}) collective-permute-start(f32[10,1,256]{2,1,0:T(1,128)S(1)} %get-tuple-element.17), channel_id=1, source_target_pairs={{96,97},{98,99},{100,101},{102,103},{128,129},{130,131},{132,133},... | collective-permute-start | bytes 30728 | tf_op jit(solution)/shard_map/ppermute | solution.py:204
  24.3 3.7 %collective-permute-start.10 = (f32[10,1,256]{2,1,0:T(1,128)S(1)}, f32[10,1,256]{2,1,0:T(1,128)S(1)}, u32[]{:S(2)}, u32[]{:S(2)}) collective-permute-start(f32[10,1,256]{2,1,0:T(1,128)S(1)} %get-tuple-element.18), channel_id=1, source_target_pairs={{97,98},{99,100},{101,102},{129,130},{131,132},{133,134},{161,162}... | collective-permute-start | bytes 30728 | tf_op jit(solution)/shard_map/ppermute | solution.py:204
  27.9 0.0 collective-permute-done.9.refs_3_
  28.0 2.8 %collective-permute-done.10.refs_4_ = f32[10,1,256]{2,1,0:T(1,128)S(1)} collective-permute-done((f32[10,1,256]{2,1,0:T(1,128)S(1)}, f32[10,1,256]{2,1,0:T(1,128)S(1)}, u32[]{:S(2)}, u32[]{:S(2)}) %collective-permute-start.10) | collective-permute-done | bytes 10272 | tf_op jit(solution)/shard_map/ppermute | solution.py:204
  30.8 1.5 %tail.1 = (f32[8,16,256]{2,1,0:T(8,128)}, f32[256,128]{1,0:T(8,128)S(1)}) custom-call(f32[8,16,256]{2,1,0:T(8,128)S(1)} %bitcast.9, f32[1,16,256]{2,1,0:T(8,128)S(1)} %collective-permute-done.refs_1_, f32[1,16,256]{2,1,0:T(8,128)S(1)} %collective-permute-done.1.refs_2_, f32[10,1,256]{2,1,0:T(1,128)S(1)} %collective-permute-done.9.refs_3_, ...), custom_call_target="tpu_custom_call" | custom-call | tf_op jit(solution)/shard_map/tail/pallas_call | solution.py:159
  32.3 0.0 collective-permute-done.13.far1
  32.3 12.8 %collective-permute-done.12.far2 = f32[256,128]{1,0:T(8,128)S(1)} collective-permute-done((f32[256,128]{1,0:T(8,128)S(1)}, f32[256,128]{1,0:T(8,128)S(1)}, u32[]{:S(2)}, u32[]{:S(2)}) %collective-permute-start.12) | collective-permute-done | bytes 131104 | tf_op jit(solution)/shard_map/ppermute | solution.py:231
  45.1 0.0 collective-permute-done.11.far3
  45.1 1.2 %correlate.1 = f32[8,16,264]{2,1,0:T(8,128)} custom-call(f32[256,128]{1,0:T(8,128)S(1)} %get-tuple-element.21.mon, f32[256,128]{1,0:T(8,128)S(1)} %add_select_fusion.held, f32[256,128]{1,0:T(8,128)S(1)} %collective-permute-done.11.far3, f32[256,128]{1,0:T(8,128)S(1)} %collective-permute-done.12.far2, f32[256,128]{1,0:T(8,128)S(1)} %collective-permute-done.13.far1), custom_call_target="tpu_custom_call" | custom-call | tf_op jit(solution)/shard_map/correlate/pallas_call | solution.py:180
  (8 shorter events, 0.1 us)
Async XLA Ops:
  0.6 16.3 %copy-start = (f32[1,8,16,256]{3,2,1,0:T(8,128)S(1)}, f32[1,8,16,256]{3,2,1,0:T(8,128)}, u32[]{:S(2)}) copy-start(f32[1,8,16,256]{3,2,1,0:T(8,128)} %param.3) | copy-start | bytes 393220
  1.4 13.3 %collective-permute-start.2 = (f32[1,16,256]{2,1,0:T(8,128)S(1)}, f32[1,16,256]{2,1,0:T(8,128)S(1)}, u32[]{:S(2)}, u32[]{:S(2)}) collective-permute-start(f32[1,16,256]{2,1,0:T(8,128)S(1)} %get-tuple-element.12), channel_id=1, source_target_pairs={{0,8},{16,24},{32,40},{48,56},{64,72},{80,88},{448,456},{464,472},... | collective-permute-start | bytes 49160 | tf_op jit(solution)/shard_map/ppermute | solution.py:204
  2.1 12.6 %collective-permute-start.3 = (f32[1,16,256]{2,1,0:T(8,128)S(1)}, f32[1,16,256]{2,1,0:T(8,128)S(1)}, u32[]{:S(2)}, u32[]{:S(2)}) collective-permute-start(f32[1,16,256]{2,1,0:T(8,128)S(1)} %get-tuple-element.13), channel_id=1, source_target_pairs={{8,16},{40,48},{72,80},{456,464},{16,8},{48,40},{80,72},{464,456},... | collective-permute-start | bytes 49160 | tf_op jit(solution)/shard_map/ppermute | solution.py:204
  3.7 15.3 %collective-permute-start = (f32[1,16,256]{2,1,0:T(8,128)S(1)}, f32[1,16,256]{2,1,0:T(8,128)S(1)}, u32[]{:S(2)}, u32[]{:S(2)}) collective-permute-start(f32[1,16,256]{2,1,0:T(8,128)S(1)} %get-tuple-element.12), channel_id=1, source_target_pairs={{96,104},{112,120},{128,136},{144,152},{160,168},{176,184},{192,20... | collective-permute-start | bytes 49160 | tf_op jit(solution)/shard_map/ppermute | solution.py:204
  5.6 13.4 %collective-permute-start.1 = (f32[1,16,256]{2,1,0:T(8,128)S(1)}, f32[1,16,256]{2,1,0:T(8,128)S(1)}, u32[]{:S(2)}, u32[]{:S(2)}) collective-permute-start(f32[1,16,256]{2,1,0:T(8,128)S(1)} %get-tuple-element.13), channel_id=1, source_target_pairs={{104,112},{136,144},{168,176},{200,208},{232,240},{264,272},{296,3... | collective-permute-start | bytes 49160 | tf_op jit(solution)/shard_map/ppermute | solution.py:204
  14.8 2.1 %collective-permute-start.5 = (f32[10,1,256]{2,1,0:T(1,128)S(1)}, f32[10,1,256]{2,1,0:T(1,128)S(1)}, u32[]{:S(2)}, u32[]{:S(2)}) collective-permute-start(f32[10,1,256]{2,1,0:T(1,128)S(1)} %get-tuple-element.30), channel_id=1, source_target_pairs={{0,1},{2,3},{4,5},{6,7},{32,33},{34,35},{36,37},{38,39},{64,65},{6... | collective-permute-start | bytes 30728 | tf_op jit(solution)/shard_map/ppermute | solution.py:204
  15.5 0.7 %copy-start.1 = (s32[1,8,16]{2,1,0:T(8,128)S(1)}, s32[1,8,16]{2,1,0:T(8,128)}, u32[]{:S(2)}) copy-start(s32[1,8,16]{2,1,0:T(8,128)} %param.4) | copy-start | bytes 1540
  15.5 1.4 %collective-permute-start.4 = (f32[10,1,256]{2,1,0:T(1,128)S(1)}, f32[10,1,256]{2,1,0:T(1,128)S(1)}, u32[]{:S(2)}, u32[]{:S(2)}) collective-permute-start(f32[10,1,256]{2,1,0:T(1,128)S(1)} %get-tuple-element.31), channel_id=1, source_target_pairs={{1,2},{3,4},{5,6},{33,34},{35,36},{37,38},{65,66},{67,68},{69,70},... | collective-permute-start | bytes 30728 | tf_op jit(solution)/shard_map/ppermute | solution.py:204
  16.1 0.7 %copy-start.2 = (s32[1,8,16]{2,1,0:T(8,128)S(1)}, s32[1,8,16]{2,1,0:T(8,128)}, u32[]{:S(2)}) copy-start(s32[1,8,16]{2,1,0:T(8,128)} %param.5) | copy-start | bytes 1540
  17.0 2.1 %collective-permute-start.8 = (f32[256,128]{1,0:T(8,128)S(1)}, f32[256,128]{1,0:T(8,128)S(1)}, u32[]{:S(2)}, u32[]{:S(2)}) collective-permute-start(f32[256,128]{1,0:T(8,128)S(1)} %get-tuple-element.16.refs_8_), channel_id=1, source_target_pairs={{0,64},{1,65},{2,66},{3,67},{4,68},{5,69},{6,70},{7,71},{8,72},{9,... | collective-permute-start | bytes 393224 | tf_op jit(solution)/shard_map/ppermute | solution.py:228
  17.6 1.4 %collective-permute-start.7 = (f32[256,128]{1,0:T(8,128)S(1)}, f32[256,128]{1,0:T(8,128)S(1)}, u32[]{:S(2)}, u32[]{:S(2)}) collective-permute-start(f32[256,128]{1,0:T(8,128)S(1)} %get-tuple-element.16.refs_8_), channel_id=1, source_target_pairs={{0,448},{1,449},{2,450},{3,451},{4,452},{5,453},{6,454},{7,455},{8... | collective-permute-start | bytes 393224 | tf_op jit(solution)/shard_map/ppermute | solution.py:228
  18.3 0.7 %collective-permute-start.6 = (f32[256,128]{1,0:T(8,128)S(1)}, f32[256,128]{1,0:T(8,128)S(1)}, u32[]{:S(2)}, u32[]{:S(2)}) collective-permute-start(f32[256,128]{1,0:T(8,128)S(1)} %get-tuple-element.16.refs_8_), channel_id=1, source_target_pairs={{0,32},{1,33},{2,34},{3,35},{4,36},{5,37},{6,38},{7,39},{8,40},{9,... | collective-permute-start | bytes 393224 | tf_op jit(solution)/shard_map/ppermute | solution.py:228
  19.1 13.2 %collective-permute-start.13 = (f32[256,128]{1,0:T(8,128)S(1)}, f32[256,128]{1,0:T(8,128)S(1)}, u32[]{:S(2)}, u32[]{:S(2)}) collective-permute-start(f32[256,128]{1,0:T(8,128)S(1)} %add_select_fusion.held), channel_id=1, source_target_pairs={{0,256},{32,288},{64,192},{448,320},{1,257},{33,289},{65,193},{449... | collective-permute-start | bytes 393224 | tf_op jit(solution)/shard_map/ppermute | solution.py:231
  19.8 25.3 %collective-permute-start.12 = (f32[256,128]{1,0:T(8,128)S(1)}, f32[256,128]{1,0:T(8,128)S(1)}, u32[]{:S(2)}, u32[]{:S(2)}) collective-permute-start(f32[256,128]{1,0:T(8,128)S(1)} %add_select_fusion.held), channel_id=1, source_target_pairs={{0,128},{32,160},{64,224},{448,352},{1,129},{33,161},{65,225},{449... | collective-permute-start | bytes 393224 | tf_op jit(solution)/shard_map/ppermute | solution.py:231
  21.1 24.0 %collective-permute-start.11 = (f32[256,128]{1,0:T(8,128)S(1)}, f32[256,128]{1,0:T(8,128)S(1)}, u32[]{:S(2)}, u32[]{:S(2)}) collective-permute-start(f32[256,128]{1,0:T(8,128)S(1)} %add_select_fusion.held), channel_id=1, source_target_pairs={{0,384},{32,416},{64,96},{448,480},{1,385},{33,417},{65,97},{449,4... | collective-permute-start | bytes 393224 | tf_op jit(solution)/shard_map/ppermute | solution.py:231
  21.8 6.2 %collective-permute-start.9 = (f32[10,1,256]{2,1,0:T(1,128)S(1)}, f32[10,1,256]{2,1,0:T(1,128)S(1)}, u32[]{:S(2)}, u32[]{:S(2)}) collective-permute-start(f32[10,1,256]{2,1,0:T(1,128)S(1)} %get-tuple-element.17), channel_id=1, source_target_pairs={{96,97},{98,99},{100,101},{102,103},{128,129},{130,131},{132,133},... | collective-permute-start | bytes 30728 | tf_op jit(solution)/shard_map/ppermute | solution.py:204
  24.3 6.5 %collective-permute-start.10 = (f32[10,1,256]{2,1,0:T(1,128)S(1)}, f32[10,1,256]{2,1,0:T(1,128)S(1)}, u32[]{:S(2)}, u32[]{:S(2)}) collective-permute-start(f32[10,1,256]{2,1,0:T(1,128)S(1)} %get-tuple-element.18), channel_id=1, source_target_pairs={{97,98},{99,100},{101,102},{129,130},{131,132},{133,134},{161,162}... | collective-permute-start | bytes 30728 | tf_op jit(solution)/shard_map/ppermute | solution.py:204

commit v5 on v4

--- a/solution.py
+++ b/solution.py
@@ -1,5 +1,3 @@
-import functools
-
 import jax
 import jax.numpy as jnp
 from jax import lax
@@ -14,8 +12,7 @@
 NWIN = 8
 EPS = 1e-06
 
-HEAD = 0, 1, 2, 14
-FANOUT = {0: (8, 4, 12), 1: (9, 5, 13), 2: (6, 7, 3), 14: (10, 11, 15)}
+HOLDERS = 0, 4, 8, 12
 ROWS = 8
 COLS = 16
 TRACES = ROWS * COLS
@@ -31,19 +28,15 @@
     return out
 
 
-def is_head(place):
-    return functools.reduce(jnp.logical_or, [place == v for v in HEAD])
-
-
 def first_kernel(*refs):
-    @pl.when(is_head(lax.axis_index("vintage")))
-    def _():
-        attr_body(refs[0], refs[1], refs[2], refs[4], refs[3], *refs[5:])
+    @pl.when(lax.axis_index("vintage") == 0)
+    def _():
+        attr_body(*refs[:4], refs[5], refs[4], *refs[6:])
 
 
 def later_kernel(*refs):
-    ins, semb_first, attr_first, semb_out, attr_out = refs[:7], refs[7], refs[8], refs[9], refs[10]
-    head = is_head(lax.axis_index("vintage"))
+    ins, semb_first, attr_first, semb_out, attr_out = refs[:8], refs[8], refs[9], refs[10], refs[11]
+    head = lax.axis_index("vintage") == 0
 
     @pl.when(head)
     def _():
@@ -52,16 +45,17 @@
 
     @pl.when(jnp.logical_not(head))
     def _():
-        attr_body(*ins, *refs[9:])
-
-
-def attr_body(tile, row_a, row_b, col_a, col_b, dip_il, dip_xl, semb_out, attr_out,
+        attr_body(*ins, *refs[10:])
+
+
+def attr_body(tile, row_01, row_12, row_23, col_a, col_b, dip_il, dip_xl, semb_out, attr_out,
               rim, moved, inner, sums, three):
     odd_row = lax.rem(lax.axis_index("inline"), 2) == 1
     odd_col = lax.rem(lax.axis_index("xline"), 2) == 1
     rim[1:ROWS + 1, 1:COLS + 1, :] = tile[...]
-    rim[0, 1:COLS + 1, :] = jnp.where(odd_row, row_a[0], row_b[0])
-    rim[ROWS + 1, 1:COLS + 1, :] = jnp.where(odd_row, row_b[0], row_a[0])
+    row_a, row_b = row_01[0] + row_23[0], row_12[0]
+    rim[0, 1:COLS + 1, :] = jnp.where(odd_row, row_a, row_b)
+    rim[ROWS + 1, 1:COLS + 1, :] = jnp.where(odd_row, row_b, row_a)
     rim[:, 0:1, :] = jnp.where(odd_col, col_a[...], col_b[...])
     rim[:, COLS + 1:COLS + 2, :] = jnp.where(odd_col, col_b[...], col_a[...])
     zeros = jnp.zeros((PAD, TRACES), jnp.float32)
@@ -111,7 +105,7 @@
 
 def correl_kernel(mon, held, far3, far2, far1, out, base, result):
     half_lags = LAGS // 2
-    holder = is_head(lax.axis_index("vintage"))
+    holder = lax.rem(lax.axis_index("vintage"), 4) == 0
     zeros = jnp.zeros((half_lags, TRACES), jnp.float32)
     base[0:half_lags, :] = zeros
     base[half_lags + TIME_SAMPLES:, :] = zeros
@@ -196,18 +190,19 @@
     return jnp.where(odd, first, last), jnp.where(odd, last, first)
 
 
-def swap(sends, axis, planes):
+def swap(sends, axis, planes, rounds):
     count = lax.axis_size(axis)
     out = []
-    for start, send in enumerate(sends):
-        low = [(v * count + i, v * count + i + 1) for v in planes for i in range(start, count - 1, 2)]
-        out.append(lax.ppermute(send, ("vintage", axis), low + [(b, a) for a, b in low]))
+    for n, starts in enumerate(rounds):
+        low = [(v * count + i, v * count + i + 1) for v in planes for i in starts]
+        out.append(lax.ppermute(sends[n], ("vintage", axis), low + [(b, a) for a, b in low]))
     return out
 
 
 def edge_columns(ends, rows):
     odd = lax.rem(lax.axis_index("inline"), 2) == 1
-    above, below = jnp.where(odd, rows[0], rows[1]), jnp.where(odd, rows[1], rows[0])
+    row_a, row_b = rows[0] + rows[2], rows[1]
+    above, below = jnp.where(odd, row_a, row_b), jnp.where(odd, row_b, row_a)
     first, last = (
         jnp.concatenate([above[:, j:j + 1], end, below[:, j:j + 1]], axis=0)
         for j, end in zip((0, COLS - 1), ends)
@@ -218,24 +213,24 @@
 def per_device(amplitude, inline_slope, crossline_slope):
     tile = amplitude[0]
     dips = (inline_slope.reshape(1, TRACES), crossline_slope.reshape(1, TRACES))
-    others = [v for v in range(lax.axis_size("vintage")) if v not in HEAD]
+    others = range(1, lax.axis_size("vintage"))
+    along, across = ((0,), (1,), (2,)), ((0, 2, 4, 6), (1, 3, 5))
     sends = pair_sends(tile[:1], tile[-1:], "inline")
-    rows = swap(sends, "inline", HEAD)
-    gated = lax.optimization_barrier((*sends[::-1], tile[:, :1], tile[:, -1:]))
-    ends, sends = gated[2:], gated[1::-1]
-    cols = swap(edge_columns(ends, rows), "xline", HEAD)
-    semb0, attr0 = attributes(first_kernel, "head", tile, *rows, *cols[::-1], *dips)
-    got = [lax.ppermute(attr0, "vintage", [(0, k)]) for k in (1, 14, 2)]
+    outer = jnp.where(lax.axis_index("inline") == lax.axis_size("inline") - 1, tile[:1], tile[-1:])
+    sends = (*sends, outer)
+    rows = swap(sends, "inline", [0], along)
+    gated = lax.optimization_barrier((sends[1], sends[2], sends[0], tile[:, :1], tile[:, -1:]))
+    ends, sends = gated[3:], (gated[2], gated[0], gated[1])
+    cols = swap(edge_columns(ends, rows), "xline", [0], across)
+    semb0, attr0 = attributes(first_kernel, "head", tile, *[rows[n] for n in (0, 1, 2)], *cols[::-1], *dips)
+    got = [lax.ppermute(attr0, "vintage", [(0, k)]) for k in (12, 4, 8)]
+    rows = swap(sends, "inline", others, along)
+    cols = edge_columns(ends, rows)
+    cols = swap(lax.optimization_barrier((*cols, attr0))[:2], "xline", others, across)
+    semb, attr = attributes(later_kernel, "tail", tile, *[rows[n] for n in (0, 1, 2)], *cols, *dips, semb0, attr0)
+    got = lax.optimization_barrier((*got, attr))[:3]
     held = jnp.where(lax.axis_index("vintage") == 0, attr0, got[0] + got[1] + got[2])
-    far = [
-        lax.ppermute(held, "vintage", [(s, FANOUT[s][n]) for s in HEAD])
-        for n in (2, 1, 0)
-    ]
-    rows = swap(sends, "inline", others)
-    cols = edge_columns(ends, rows)
-    cols = lax.optimization_barrier((*cols, held))[:2]
-    cols = swap(cols, "xline", others)
-    semb, attr = attributes(later_kernel, "tail", tile, *rows, *cols, *dips, semb0, attr0)
+    far = [lax.ppermute(held, "vintage", [(s, s + k) for s in HOLDERS]) for k in (1, 2, 3)]
     correl = correlate(attr, held, far)
     return (semb[None], correl[None])
 

time: 46.7 us -> 40.1 us (0.86)
  the two profiles are of different devices: /device:TPU:159 before, /device:TPU:190 now
where the time goes in v5:
time: 40.1 us; the launch traced here: 39.5 us
  starting transfers between devices  23.7 us (59%)
  waiting for transfers between devices  10.3 us (26%)
  Pallas kernels  2.71 us (7%)
  local copies, waits for them, and re-layouts  1.08 us (3%)
  between operations  0.96 us (2%)
  other arithmetic  0.84 us (2%)
    ppermute x10, starting transfers between devices, swap(): lax.ppermute(sends[n], ('vintage', axis), low + [(b, a) for a, b in low])  19 us
    ppermute x3, waiting for transfers between devices, per_device(): lax.ppermute(held, 'vintage', [(s, s + k) for s in HOLDERS])  6.84 us
    ppermute x10, waiting for transfers between devices, swap(): lax.ppermute(sends[n], ('vintage', axis), low + [(b, a) for a, b in low])  3.43 us
    ppermute x3, starting transfers between devices, per_device(): lax.ppermute(held, 'vintage', [(s, s + k) for s in HOLDERS])  2.63 us
    ppermute x3, starting transfers between devices, per_device(): got = [lax.ppermute(attr0, 'vintage', [(0, k)]) for k in (12, 4, 8)]  2.01 us
    pallas_call x2, Pallas kernels, attributes(): pl.pallas_call(kernel, out_shape=(jax.ShapeDtypeStruct((ROWS, COLS, TIME_...  1.51 us
    pallas_call x1, Pallas kernels, correlate(): pl.pallas_call(correl_kernel, out_shape=jax.ShapeDtypeStruct((ROWS, COLS,...  1.2 us
    slice x1, local copies, waits for them, and re-layouts, per_device(): tile[:, -1:]  0.89 us
  transfers between devices with their start and end apart: 16, of which 2 were waited for; matrix products, arithmetic and copies ran while one was open for 3% of the time, Pallas kernels for 4%

profile of v5, /device:TPU:190, one launch (start us, length us, event | category | flops | bytes accessed | tf_op | source)
XLA Modules:
  0.0 39.5 jit_solution(5611319576306742485)
XLA Ops:
  0.6 0.7 %select_bitcast_fusion = (f32[1,16,256]{2,1,0:T(8,128)S(1)}, f32[1,16,256]{2,1,0:T(8,128)S(1)}, f32[1,16,256]{2,1,0:T(8,128)S(1)}) fusion(f32[1,8,16,256]{3,2,1,0:T(8,128)} %param.3, pred[]{:T(512)S(6)} %eq.15, pred[]{:T(512)S(6)} %eq.16), kind=kLoop, calls=%fused_computation.5 | loop fusion | flops 12288 | bytes 81922 | tf_op jit(solution)/shard_map/jit(_where)/select_n | solution.py:190
  1.4 0.7 %collective-permute-start.3 = (f32[1,16,256]{2,1,0:T(8,128)S(1)}, f32[1,16,256]{2,1,0:T(8,128)S(1)}, u32[]{:S(2)}, u32[]{:S(2)}) collective-permute-start(f32[1,16,256]{2,1,0:T(8,128)S(1)} %get-tuple-element.16), channel_id=1, source_target_pairs={{0,8},{8,0},{1,9},{9,1},{2,10},{10,2},{3,11},{11,3},{4,12},{12,4},... | collective-permute-start | bytes 49160 | tf_op jit(solution)/shard_map/ppermute | solution.py:198
  2.0 0.7 %collective-permute-start.4 = (f32[1,16,256]{2,1,0:T(8,128)S(1)}, f32[1,16,256]{2,1,0:T(8,128)S(1)}, u32[]{:S(2)}, u32[]{:S(2)}) collective-permute-start(f32[1,16,256]{2,1,0:T(8,128)S(1)} %get-tuple-element.17), channel_id=1, source_target_pairs={{8,16},{16,8},{9,17},{17,9},{10,18},{18,10},{11,19},{19,11},{12,20... | collective-permute-start | bytes 49160 | tf_op jit(solution)/shard_map/ppermute | solution.py:198
  2.7 0.7 %collective-permute-start.5 = (f32[1,16,256]{2,1,0:T(8,128)S(1)}, f32[1,16,256]{2,1,0:T(8,128)S(1)}, u32[]{:S(2)}, u32[]{:S(2)}) collective-permute-start(f32[1,16,256]{2,1,0:T(8,128)S(1)} %get-tuple-element.18), channel_id=1, source_target_pairs={{16,24},{24,16},{17,25},{25,17},{18,26},{26,18},{19,27},{27,19},{2... | collective-permute-start | bytes 49160 | tf_op jit(solution)/shard_map/ppermute | solution.py:198
  3.4 0.0 copy-start.1
  3.4 0.0 copy-start.2
  3.4 0.9 %fusion = (f32[8,1,256]{2,1,0:T(1,128)S(1)}, f32[8,1,256]{2,1,0:T(1,128)S(1)}) fusion(f32[8,16,256]{2,1,0:T(8,128)} %bitcast.9), kind=kLoop, calls=%fused_computation.16 | loop fusion | bytes 32768 | tf_op jit(solution)/shard_map/slice | solution.py:222
  4.3 0.0 copy-start
  4.3 2.1 %collective-permute-start = (f32[1,16,256]{2,1,0:T(8,128)S(1)}, f32[1,16,256]{2,1,0:T(8,128)S(1)}, u32[]{:S(2)}, u32[]{:S(2)}) collective-permute-start(f32[1,16,256]{2,1,0:T(8,128)S(1)} %get-tuple-element.16), channel_id=1, source_target_pairs={{32,40},{64,72},{96,104},{128,136},{160,168},{192,200},{224,232},{... | collective-permute-start | bytes 49160 | tf_op jit(solution)/shard_map/ppermute | solution.py:198
  6.4 6.0 %collective-permute-start.1 = (f32[1,16,256]{2,1,0:T(8,128)S(1)}, f32[1,16,256]{2,1,0:T(8,128)S(1)}, u32[]{:S(2)}, u32[]{:S(2)}) collective-permute-start(f32[1,16,256]{2,1,0:T(8,128)S(1)} %get-tuple-element.17), channel_id=1, source_target_pairs={{40,48},{72,80},{104,112},{136,144},{168,176},{200,208},{232,240},... | collective-permute-start | bytes 49160 | tf_op jit(solution)/shard_map/ppermute | solution.py:198
  12.4 0.0 copy-done.1
  12.4 0.1 reshape.382.refs_6_
  12.5 0.0 copy-done.2
  12.5 0.1 reshape.383.refs_7_
  12.6 0.0 collective-permute-done.3.refs_1_
  12.6 0.7 %collective-permute-start.2 = (f32[1,16,256]{2,1,0:T(8,128)S(1)}, f32[1,16,256]{2,1,0:T(8,128)S(1)}, u32[]{:S(2)}, u32[]{:S(2)}) collective-permute-start(f32[1,16,256]{2,1,0:T(8,128)S(1)} %get-tuple-element.18), channel_id=1, source_target_pairs={{48,56},{80,88},{112,120},{144,152},{176,184},{208,216},{240,248},... | collective-permute-start | bytes 49160 | tf_op jit(solution)/shard_map/ppermute | solution.py:198
  13.3 0.0 collective-permute-done.4.refs_2_
  13.3 0.0 collective-permute-done.5.refs_3_
  13.4 0.7 %collective-permute-start.7 = (f32[10,1,256]{2,1,0:T(1,128)S(1)}, f32[10,1,256]{2,1,0:T(1,128)S(1)}, u32[]{:S(2)}, u32[]{:S(2)}) collective-permute-start(f32[10,1,256]{2,1,0:T(1,128)S(1)} %get-tuple-element.39), channel_id=1, source_target_pairs={{0,1},{2,3},{4,5},{6,7},{1,0},{3,2},{5,4},{7,6},{8,9},{10,11},{12,... | collective-permute-start | bytes 30728 | tf_op jit(solution)/shard_map/ppermute | solution.py:198
  14.0 0.7 %collective-permute-start.6 = (f32[10,1,256]{2,1,0:T(1,128)S(1)}, f32[10,1,256]{2,1,0:T(1,128)S(1)}, u32[]{:S(2)}, u32[]{:S(2)}) collective-permute-start(f32[10,1,256]{2,1,0:T(1,128)S(1)} %get-tuple-element.40), channel_id=1, source_target_pairs={{1,2},{3,4},{5,6},{2,1},{4,3},{6,5},{9,10},{11,12},{13,14},{10,9},... | collective-permute-start | bytes 30728 | tf_op jit(solution)/shard_map/ppermute | solution.py:198
  14.7 0.0 collective-permute-done.refs_1_
  14.7 0.0 collective-permute-done.1.refs_2_
  14.7 0.0 collective-permute-done.2.refs_3_
  14.7 0.0 collective-permute-done.7.refs_5_
  14.8 0.0 collective-permute-done.6.refs_4_
  14.8 0.0 copy-done
  14.8 0.7 %collective-permute-start.12 = (f32[256,128]{1,0:T(8,128)S(1)}, f32[256,128]{1,0:T(8,128)S(1)}, u32[]{:S(2)}, u32[]{:S(2)}) collective-permute-start(f32[256,128]{1,0:T(8,128)S(1)} %get-tuple-element.21.refs_9_), channel_id=1, source_target_pairs={{0,256},{1,257},{2,258},{3,259},{4,260},{5,261},{6,262},{7,263},{8... | collective-permute-start | bytes 393224 | tf_op jit(solution)/shard_map/ppermute | solution.py:226
  15.5 0.7 %collective-permute-start.11 = (f32[256,128]{1,0:T(8,128)S(1)}, f32[256,128]{1,0:T(8,128)S(1)}, u32[]{:S(2)}, u32[]{:S(2)}) collective-permute-start(f32[256,128]{1,0:T(8,128)S(1)} %get-tuple-element.21.refs_9_), channel_id=1, source_target_pairs={{0,128},{1,129},{2,130},{3,131},{4,132},{5,133},{6,134},{7,135},{8... | collective-permute-start | bytes 393224 | tf_op jit(solution)/shard_map/ppermute | solution.py:226
  16.1 0.7 %collective-permute-start.10 = (f32[256,128]{1,0:T(8,128)S(1)}, f32[256,128]{1,0:T(8,128)S(1)}, u32[]{:S(2)}, u32[]{:S(2)}) collective-permute-start(f32[256,128]{1,0:T(8,128)S(1)} %get-tuple-element.21.refs_9_), channel_id=1, source_target_pairs={{0,384},{1,385},{2,386},{3,387},{4,388},{5,389},{6,390},{7,391},{8... | collective-permute-start | bytes 393224 | tf_op jit(solution)/shard_map/ppermute | solution.py:226
  16.9 2.7 %collective-permute-start.8 = (f32[10,1,256]{2,1,0:T(1,128)S(1)}, f32[10,1,256]{2,1,0:T(1,128)S(1)}, u32[]{:S(2)}, u32[]{:S(2)}) collective-permute-start(f32[10,1,256]{2,1,0:T(1,128)S(1)} %get-tuple-element.22), channel_id=1, source_target_pairs={{32,33},{34,35},{36,37},{38,39},{64,65},{66,67},{68,69},{70,71},{9... | collective-permute-start | bytes 30728 | tf_op jit(solution)/shard_map/ppermute | solution.py:198
  19.6 4.2 %collective-permute-start.9 = (f32[10,1,256]{2,1,0:T(1,128)S(1)}, f32[10,1,256]{2,1,0:T(1,128)S(1)}, u32[]{:S(2)}, u32[]{:S(2)}) collective-permute-start(f32[10,1,256]{2,1,0:T(1,128)S(1)} %get-tuple-element.23), channel_id=1, source_target_pairs={{33,34},{35,36},{37,38},{65,66},{67,68},{69,70},{97,98},{99,100},{... | collective-permute-start | bytes 30728 | tf_op jit(solution)/shard_map/ppermute | solution.py:198
  23.9 0.0 collective-permute-done.8.refs_4_
  23.9 3.4 %collective-permute-done.9.refs_5_ = f32[10,1,256]{2,1,0:T(1,128)S(1)} collective-permute-done((f32[10,1,256]{2,1,0:T(1,128)S(1)}, f32[10,1,256]{2,1,0:T(1,128)S(1)}, u32[]{:S(2)}, u32[]{:S(2)}) %collective-permute-start.9) | collective-permute-done | bytes 10272 | tf_op jit(solution)/shard_map/ppermute | solution.py:198
  27.3 1.5 %tail.1 = (f32[8,16,256]{2,1,0:T(8,128)}, f32[256,128]{1,0:T(8,128)S(1)}) custom-call(f32[8,16,256]{2,1,0:T(8,128)S(1)} %bitcast.11, f32[1,16,256]{2,1,0:T(8,128)S(1)} %collective-permute-done.refs_1_, f32[1,16,256]{2,1,0:T(8,128)S(1)} %collective-permute-done.1.refs_2_, f32[1,16,256]{2,1,0:T(8,128)S(1)} %collective-permute-done.2.refs_3_, ...), custom_call_target="tpu_custom_call" | custom-call | tf_op jit(solution)/shard_map/tail/pallas_call | solution.py:153
  28.8 0.0 collective-permute-done.12
  28.8 0.0 collective-permute-done.11
  28.8 0.0 collective-permute-done.10
  28.8 0.7 %collective-permute-start.15 = (f32[256,128]{1,0:T(8,128)S(1)}, f32[256,128]{1,0:T(8,128)S(1)}, u32[]{:S(2)}, u32[]{:S(2)}) collective-permute-start(f32[256,128]{1,0:T(8,128)S(1)} %add_select_fusion.held), channel_id=1, source_target_pairs={{0,96},{128,224},{256,352},{384,480},{1,97},{129,225},{257,353},{3... | collective-permute-start | bytes 393224 | tf_op jit(solution)/shard_map/ppermute | solution.py:233
  29.5 1.3 %collective-permute-start.14 = (f32[256,128]{1,0:T(8,128)S(1)}, f32[256,128]{1,0:T(8,128)S(1)}, u32[]{:S(2)}, u32[]{:S(2)}) collective-permute-start(f32[256,128]{1,0:T(8,128)S(1)} %add_select_fusion.held), channel_id=1, source_target_pairs={{0,64},{128,192},{256,320},{384,448},{1,65},{129,193},{257,321},{3... | collective-permute-start | bytes 393224 | tf_op jit(solution)/shard_map/ppermute | solution.py:233
  30.8 0.7 %collective-permute-start.13 = (f32[256,128]{1,0:T(8,128)S(1)}, f32[256,128]{1,0:T(8,128)S(1)}, u32[]{:S(2)}, u32[]{:S(2)}) collective-permute-start(f32[256,128]{1,0:T(8,128)S(1)} %add_select_fusion.held), channel_id=1, source_target_pairs={{0,32},{128,160},{256,288},{384,416},{1,33},{129,161},{257,289},{3... | collective-permute-start | bytes 393224 | tf_op jit(solution)/shard_map/ppermute | solution.py:233
  31.5 0.0 collective-permute-done.15.far1
  31.5 6.8 %collective-permute-done.14.far2 = f32[256,128]{1,0:T(8,128)S(1)} collective-permute-done((f32[256,128]{1,0:T(8,128)S(1)}, f32[256,128]{1,0:T(8,128)S(1)}, u32[]{:S(2)}, u32[]{:S(2)}) %collective-permute-start.14) | collective-permute-done | bytes 131104 | tf_op jit(solution)/shard_map/ppermute | solution.py:233
  38.3 0.0 collective-permute-done.13.far3
  38.3 1.2 %correlate.1 = f32[8,16,264]{2,1,0:T(8,128)} custom-call(f32[256,128]{1,0:T(8,128)S(1)} %get-tuple-element.26.mon, f32[256,128]{1,0:T(8,128)S(1)} %add_select_fusion.held, f32[256,128]{1,0:T(8,128)S(1)} %collective-permute-done.13.far3, f32[256,128]{1,0:T(8,128)S(1)} %collective-permute-done.14.far2, f32[256,128]{1,0:T(8,128)S(1)} %collective-permute-done.15.far1), custom_call_target="tpu_custom_call" | custom-call | tf_op jit(solution)/shard_map/correlate/pallas_call | solution.py:174
  (8 shorter events, 0.1 us)
Async XLA Ops:
  1.4 11.2 %collective-permute-start.3 = (f32[1,16,256]{2,1,0:T(8,128)S(1)}, f32[1,16,256]{2,1,0:T(8,128)S(1)}, u32[]{:S(2)}, u32[]{:S(2)}) collective-permute-start(f32[1,16,256]{2,1,0:T(8,128)S(1)} %get-tuple-element.16), channel_id=1, source_target_pairs={{0,8},{8,0},{1,9},{9,1},{2,10},{10,2},{3,11},{11,3},{4,12},{12,4},... | collective-permute-start | bytes 49160 | tf_op jit(solution)/shard_map/ppermute | solution.py:198
  2.0 11.2 %collective-permute-start.4 = (f32[1,16,256]{2,1,0:T(8,128)S(1)}, f32[1,16,256]{2,1,0:T(8,128)S(1)}, u32[]{:S(2)}, u32[]{:S(2)}) collective-permute-start(f32[1,16,256]{2,1,0:T(8,128)S(1)} %get-tuple-element.17), channel_id=1, source_target_pairs={{8,16},{16,8},{9,17},{17,9},{10,18},{18,10},{11,19},{19,11},{12,20... | collective-permute-start | bytes 49160 | tf_op jit(solution)/shard_map/ppermute | solution.py:198
  2.7 10.6 %collective-permute-start.5 = (f32[1,16,256]{2,1,0:T(8,128)S(1)}, f32[1,16,256]{2,1,0:T(8,128)S(1)}, u32[]{:S(2)}, u32[]{:S(2)}) collective-permute-start(f32[1,16,256]{2,1,0:T(8,128)S(1)} %get-tuple-element.18), channel_id=1, source_target_pairs={{16,24},{24,16},{17,25},{25,17},{18,26},{26,18},{19,27},{27,19},{2... | collective-permute-start | bytes 49160 | tf_op jit(solution)/shard_map/ppermute | solution.py:198
  3.4 9.0 %copy-start.1 = (s32[1,8,16]{2,1,0:T(8,128)S(1)}, s32[1,8,16]{2,1,0:T(8,128)}, u32[]{:S(2)}) copy-start(s32[1,8,16]{2,1,0:T(8,128)} %param.4) | copy-start | bytes 1540
  3.4 9.1 %copy-start.2 = (s32[1,8,16]{2,1,0:T(8,128)S(1)}, s32[1,8,16]{2,1,0:T(8,128)}, u32[]{:S(2)}) copy-start(s32[1,8,16]{2,1,0:T(8,128)} %param.5) | copy-start | bytes 1540
  4.3 10.5 %copy-start = (f32[1,8,16,256]{3,2,1,0:T(8,128)S(1)}, f32[1,8,16,256]{3,2,1,0:T(8,128)}, u32[]{:S(2)}) copy-start(f32[1,8,16,256]{3,2,1,0:T(8,128)} %param.3) | copy-start | bytes 393220
  4.3 10.4 %collective-permute-start = (f32[1,16,256]{2,1,0:T(8,128)S(1)}, f32[1,16,256]{2,1,0:T(8,128)S(1)}, u32[]{:S(2)}, u32[]{:S(2)}) collective-permute-start(f32[1,16,256]{2,1,0:T(8,128)S(1)} %get-tuple-element.16), channel_id=1, source_target_pairs={{32,40},{64,72},{96,104},{128,136},{160,168},{192,200},{224,232},{... | collective-permute-start | bytes 49160 | tf_op jit(solution)/shard_map/ppermute | solution.py:198
  6.4 8.3 %collective-permute-start.1 = (f32[1,16,256]{2,1,0:T(8,128)S(1)}, f32[1,16,256]{2,1,0:T(8,128)S(1)}, u32[]{:S(2)}, u32[]{:S(2)}) collective-permute-start(f32[1,16,256]{2,1,0:T(8,128)S(1)} %get-tuple-element.17), channel_id=1, source_target_pairs={{40,48},{72,80},{104,112},{136,144},{168,176},{200,208},{232,240},... | collective-permute-start | bytes 49160 | tf_op jit(solution)/shard_map/ppermute | solution.py:198
  12.6 2.1 %collective-permute-start.2 = (f32[1,16,256]{2,1,0:T(8,128)S(1)}, f32[1,16,256]{2,1,0:T(8,128)S(1)}, u32[]{:S(2)}, u32[]{:S(2)}) collective-permute-start(f32[1,16,256]{2,1,0:T(8,128)S(1)} %get-tuple-element.18), channel_id=1, source_target_pairs={{48,56},{80,88},{112,120},{144,152},{176,184},{208,216},{240,248},... | collective-permute-start | bytes 49160 | tf_op jit(solution)/shard_map/ppermute | solution.py:198
  13.4 1.4 %collective-permute-start.7 = (f32[10,1,256]{2,1,0:T(1,128)S(1)}, f32[10,1,256]{2,1,0:T(1,128)S(1)}, u32[]{:S(2)}, u32[]{:S(2)}) collective-permute-start(f32[10,1,256]{2,1,0:T(1,128)S(1)} %get-tuple-element.39), channel_id=1, source_target_pairs={{0,1},{2,3},{4,5},{6,7},{1,0},{3,2},{5,4},{7,6},{8,9},{10,11},{12,... | collective-permute-start | bytes 30728 | tf_op jit(solution)/shard_map/ppermute | solution.py:198
  14.0 0.7 %collective-permute-start.6 = (f32[10,1,256]{2,1,0:T(1,128)S(1)}, f32[10,1,256]{2,1,0:T(1,128)S(1)}, u32[]{:S(2)}, u32[]{:S(2)}) collective-permute-start(f32[10,1,256]{2,1,0:T(1,128)S(1)} %get-tuple-element.40), channel_id=1, source_target_pairs={{1,2},{3,4},{5,6},{2,1},{4,3},{6,5},{9,10},{11,12},{13,14},{10,9},... | collective-permute-start | bytes 30728 | tf_op jit(solution)/shard_map/ppermute | solution.py:198
  14.8 14.0 %collective-permute-start.12 = (f32[256,128]{1,0:T(8,128)S(1)}, f32[256,128]{1,0:T(8,128)S(1)}, u32[]{:S(2)}, u32[]{:S(2)}) collective-permute-start(f32[256,128]{1,0:T(8,128)S(1)} %get-tuple-element.21.refs_9_), channel_id=1, source_target_pairs={{0,256},{1,257},{2,258},{3,259},{4,260},{5,261},{6,262},{7,263},{8... | collective-permute-start | bytes 393224 | tf_op jit(solution)/shard_map/ppermute | solution.py:226
  15.5 13.3 %collective-permute-start.11 = (f32[256,128]{1,0:T(8,128)S(1)}, f32[256,128]{1,0:T(8,128)S(1)}, u32[]{:S(2)}, u32[]{:S(2)}) collective-permute-start(f32[256,128]{1,0:T(8,128)S(1)} %get-tuple-element.21.refs_9_), channel_id=1, source_target_pairs={{0,128},{1,129},{2,130},{3,131},{4,132},{5,133},{6,134},{7,135},{8... | collective-permute-start | bytes 393224 | tf_op jit(solution)/shard_map/ppermute | solution.py:226
  16.1 12.6 %collective-permute-start.10 = (f32[256,128]{1,0:T(8,128)S(1)}, f32[256,128]{1,0:T(8,128)S(1)}, u32[]{:S(2)}, u32[]{:S(2)}) collective-permute-start(f32[256,128]{1,0:T(8,128)S(1)} %get-tuple-element.21.refs_9_), channel_id=1, source_target_pairs={{0,384},{1,385},{2,386},{3,387},{4,388},{5,389},{6,390},{7,391},{8... | collective-permute-start | bytes 393224 | tf_op jit(solution)/shard_map/ppermute | solution.py:226
  16.9 7.0 %collective-permute-start.8 = (f32[10,1,256]{2,1,0:T(1,128)S(1)}, f32[10,1,256]{2,1,0:T(1,128)S(1)}, u32[]{:S(2)}, u32[]{:S(2)}) collective-permute-start(f32[10,1,256]{2,1,0:T(1,128)S(1)} %get-tuple-element.22), channel_id=1, source_target_pairs={{32,33},{34,35},{36,37},{38,39},{64,65},{66,67},{68,69},{70,71},{9... | collective-permute-start | bytes 30728 | tf_op jit(solution)/shard_map/ppermute | solution.py:198
  19.6 7.7 %collective-permute-start.9 = (f32[10,1,256]{2,1,0:T(1,128)S(1)}, f32[10,1,256]{2,1,0:T(1,128)S(1)}, u32[]{:S(2)}, u32[]{:S(2)}) collective-permute-start(f32[10,1,256]{2,1,0:T(1,128)S(1)} %get-tuple-element.23), channel_id=1, source_target_pairs={{33,34},{35,36},{37,38},{65,66},{67,68},{69,70},{97,98},{99,100},{... | collective-permute-start | bytes 30728 | tf_op jit(solution)/shard_map/ppermute | solution.py:198
  28.8 2.7 %collective-permute-start.15 = (f32[256,128]{1,0:T(8,128)S(1)}, f32[256,128]{1,0:T(8,128)S(1)}, u32[]{:S(2)}, u32[]{:S(2)}) collective-permute-start(f32[256,128]{1,0:T(8,128)S(1)} %add_select_fusion.held), channel_id=1, source_target_pairs={{0,96},{128,224},{256,352},{384,480},{1,97},{129,225},{257,353},{3... | collective-permute-start | bytes 393224 | tf_op jit(solution)/shard_map/ppermute | solution.py:233
  29.5 8.8 %collective-permute-start.14 = (f32[256,128]{1,0:T(8,128)S(1)}, f32[256,128]{1,0:T(8,128)S(1)}, u32[]{:S(2)}, u32[]{:S(2)}) collective-permute-start(f32[256,128]{1,0:T(8,128)S(1)} %add_select_fusion.held), channel_id=1, source_target_pairs={{0,64},{128,192},{256,320},{384,448},{1,65},{129,193},{257,321},{3... | collective-permute-start | bytes 393224 | tf_op jit(solution)/shard_map/ppermute | solution.py:233
  30.8 7.5 %collective-permute-start.13 = (f32[256,128]{1,0:T(8,128)S(1)}, f32[256,128]{1,0:T(8,128)S(1)}, u32[]{:S(2)}, u32[]{:S(2)}) collective-permute-start(f32[256,128]{1,0:T(8,128)S(1)} %add_select_fusion.held), channel_id=1, source_target_pairs={{0,32},{128,160},{256,288},{384,416},{1,33},{129,161},{257,289},{3... | collective-permute-start | bytes 393224 | tf_op jit(solution)/shard_map/ppermute | solution.py:233

commit v6 on v5

--- a/solution.py
+++ b/solution.py
@@ -1,3 +1,5 @@
+import functools
+
 import jax
 import jax.numpy as jnp
 from jax import lax
@@ -12,7 +14,7 @@
 NWIN = 8
 EPS = 1e-06
 
-HOLDERS = 0, 4, 8, 12
+FANOUT = {0: (8, 2, 14), 1: (9, 3, 15), 4: (6, 7, 5), 12: (10, 11, 13)}
 ROWS = 8
 COLS = 16
 TRACES = ROWS * COLS
@@ -105,7 +107,8 @@
 
 def correl_kernel(mon, held, far3, far2, far1, out, base, result):
     half_lags = LAGS // 2
-    holder = lax.rem(lax.axis_index("vintage"), 4) == 0
+    place = lax.axis_index("vintage")
+    holder = functools.reduce(jnp.logical_or, [place == v for v in FANOUT])
     zeros = jnp.zeros((half_lags, TRACES), jnp.float32)
     base[0:half_lags, :] = zeros
     base[half_lags + TIME_SAMPLES:, :] = zeros
@@ -223,14 +226,15 @@
     ends, sends = gated[3:], (gated[2], gated[0], gated[1])
     cols = swap(edge_columns(ends, rows), "xline", [0], across)
     semb0, attr0 = attributes(first_kernel, "head", tile, *[rows[n] for n in (0, 1, 2)], *cols[::-1], *dips)
-    got = [lax.ppermute(attr0, "vintage", [(0, k)]) for k in (12, 4, 8)]
+    got = [lax.ppermute(attr0, "vintage", [(0, k)]) for k in (1, 12, 4)]
     rows = swap(sends, "inline", others, along)
     cols = edge_columns(ends, rows)
     cols = swap(lax.optimization_barrier((*cols, attr0))[:2], "xline", others, across)
+    joined = lax.optimization_barrier((*got, *cols))
+    got, cols = joined[:3], joined[3:]
     semb, attr = attributes(later_kernel, "tail", tile, *[rows[n] for n in (0, 1, 2)], *cols, *dips, semb0, attr0)
-    got = lax.optimization_barrier((*got, attr))[:3]
     held = jnp.where(lax.axis_index("vintage") == 0, attr0, got[0] + got[1] + got[2])
-    far = [lax.ppermute(held, "vintage", [(s, s + k) for s in HOLDERS]) for k in (1, 2, 3)]
+    far = [lax.ppermute(held, "vintage", [(s, to[n]) for s, to in FANOUT.items()]) for n in (2, 1, 0)]
     correl = correlate(attr, held, far)
     return (semb[None], correl[None])
 

time: 40.1 us -> 42.7 us (1.065)
  the two profiles are of different devices: /device:TPU:190 before, /device:TPU:376 now
where the time goes in v6:
time: 42.7 us; the launch traced here: 42.2 us
  starting transfers between devices  20.2 us (47%)
  waiting for transfers between devices  16.4 us (38%)
  Pallas kernels  2.73 us (6%)
  local copies, waits for them, and re-layouts  1.08 us (3%)
  between operations  0.92 us (2%)
  other arithmetic  0.84 us (2%)
    ppermute x10, starting transfers between devices, swap(): lax.ppermute(sends[n], ('vintage', axis), low + [(b, a) for a, b in low])  15.5 us
    ppermute x3, waiting for transfers between devices, per_device(): lax.ppermute(held, 'vintage', [(s, to[n]) for s, to in FANOUT.items()])  8.87 us
    ppermute x10, waiting for transfers between devices, swap(): lax.ppermute(sends[n], ('vintage', axis), low + [(b, a) for a, b in low])  7.52 us
    ppermute x3, starting transfers between devices, per_device(): lax.ppermute(held, 'vintage', [(s, to[n]) for s, to in FANOUT.items()])  2.63 us
    ppermute x3, starting transfers between devices, per_device(): got = [lax.ppermute(attr0, 'vintage', [(0, k)]) for k in (1, 12, 4)]  2.01 us
    pallas_call x2, Pallas kernels, attributes(): pl.pallas_call(kernel, out_shape=(jax.ShapeDtypeStruct((ROWS, COLS, TIME_...  1.53 us
    pallas_call x1, Pallas kernels, correlate(): pl.pallas_call(correl_kernel, out_shape=jax.ShapeDtypeStruct((ROWS, COLS,...  1.2 us
    slice x1, local copies, waits for them, and re-layouts, per_device(): tile[:, -1:]  0.89 us
  transfers between devices with their start and end apart: 16, of which 4 were waited for; matrix products, arithmetic and copies ran while one was open for 3% of the time, Pallas kernels for 4%

profile of v6, /device:TPU:376, one launch (start us, length us, event | category | flops | bytes accessed | tf_op | source)
XLA Modules:
  0.0 42.2 jit_solution(13355556955811128300)
XLA Ops:
  0.6 0.7 %select_bitcast_fusion = (f32[1,16,256]{2,1,0:T(8,128)S(1)}, f32[1,16,256]{2,1,0:T(8,128)S(1)}, f32[1,16,256]{2,1,0:T(8,128)S(1)}) fusion(f32[1,8,16,256]{3,2,1,0:T(8,128)} %param.3, pred[]{:T(512)S(6)} %eq.15, pred[]{:T(512)S(6)} %eq.16), kind=kLoop, calls=%fused_computation.5 | loop fusion | flops 12288 | bytes 81922 | tf_op jit(solution)/shard_map/jit(_where)/select_n | solution.py:193
  1.4 0.7 %collective-permute-start.3 = (f32[1,16,256]{2,1,0:T(8,128)S(1)}, f32[1,16,256]{2,1,0:T(8,128)S(1)}, u32[]{:S(2)}, u32[]{:S(2)}) collective-permute-start(f32[1,16,256]{2,1,0:T(8,128)S(1)} %get-tuple-element.18), channel_id=1, source_target_pairs={{0,8},{8,0},{1,9},{9,1},{2,10},{10,2},{3,11},{11,3},{4,12},{12,4},... | collective-permute-start | bytes 49160 | tf_op jit(solution)/shard_map/ppermute | solution.py:201
  2.0 0.7 %collective-permute-start.4 = (f32[1,16,256]{2,1,0:T(8,128)S(1)}, f32[1,16,256]{2,1,0:T(8,128)S(1)}, u32[]{:S(2)}, u32[]{:S(2)}) collective-permute-start(f32[1,16,256]{2,1,0:T(8,128)S(1)} %get-tuple-element.19), channel_id=1, source_target_pairs={{8,16},{16,8},{9,17},{17,9},{10,18},{18,10},{11,19},{19,11},{12,20... | collective-permute-start | bytes 49160 | tf_op jit(solution)/shard_map/ppermute | solution.py:201
  2.7 0.7 %collective-permute-start.5 = (f32[1,16,256]{2,1,0:T(8,128)S(1)}, f32[1,16,256]{2,1,0:T(8,128)S(1)}, u32[]{:S(2)}, u32[]{:S(2)}) collective-permute-start(f32[1,16,256]{2,1,0:T(8,128)S(1)} %get-tuple-element.20), channel_id=1, source_target_pairs={{16,24},{24,16},{17,25},{25,17},{18,26},{26,18},{19,27},{27,19},{2... | collective-permute-start | bytes 49160 | tf_op jit(solution)/shard_map/ppermute | solution.py:201
  3.4 0.0 copy-start.1
  3.4 0.0 copy-start.2
  3.4 0.9 %fusion = (f32[8,1,256]{2,1,0:T(1,128)S(1)}, f32[8,1,256]{2,1,0:T(1,128)S(1)}) fusion(f32[8,16,256]{2,1,0:T(8,128)} %bitcast.9), kind=kLoop, calls=%fused_computation.16 | loop fusion | bytes 32768 | tf_op jit(solution)/shard_map/slice | solution.py:225
  4.3 0.0 copy-start
  4.3 0.8 %collective-permute-start = (f32[1,16,256]{2,1,0:T(8,128)S(1)}, f32[1,16,256]{2,1,0:T(8,128)S(1)}, u32[]{:S(2)}, u32[]{:S(2)}) collective-permute-start(f32[1,16,256]{2,1,0:T(8,128)S(1)} %get-tuple-element.18), channel_id=1, source_target_pairs={{32,40},{64,72},{96,104},{128,136},{160,168},{192,200},{224,232},{... | collective-permute-start | bytes 49160 | tf_op jit(solution)/shard_map/ppermute | solution.py:201
  5.1 2.8 %collective-permute-start.1 = (f32[1,16,256]{2,1,0:T(8,128)S(1)}, f32[1,16,256]{2,1,0:T(8,128)S(1)}, u32[]{:S(2)}, u32[]{:S(2)}) collective-permute-start(f32[1,16,256]{2,1,0:T(8,128)S(1)} %get-tuple-element.19), channel_id=1, source_target_pairs={{40,48},{72,80},{104,112},{136,144},{168,176},{200,208},{232,240},... | collective-permute-start | bytes 49160 | tf_op jit(solution)/shard_map/ppermute | solution.py:201
  7.9 0.0 copy-done.1
  7.9 0.1 reshape.382.refs_6_
  8.0 0.0 copy-done.2
  8.0 0.1 reshape.383.refs_7_
  8.1 0.0 collective-permute-done.3.refs_1_
  8.1 2.1 %collective-permute-start.2 = (f32[1,16,256]{2,1,0:T(8,128)S(1)}, f32[1,16,256]{2,1,0:T(8,128)S(1)}, u32[]{:S(2)}, u32[]{:S(2)}) collective-permute-start(f32[1,16,256]{2,1,0:T(8,128)S(1)} %get-tuple-element.20), channel_id=1, source_target_pairs={{48,56},{80,88},{112,120},{144,152},{176,184},{208,216},{240,248},... | collective-permute-start | bytes 49160 | tf_op jit(solution)/shard_map/ppermute | solution.py:201
  10.3 0.0 collective-permute-done.4.refs_2_
  10.3 0.0 collective-permute-done.5.refs_3_
  10.3 0.7 %collective-permute-start.7 = (f32[10,1,256]{2,1,0:T(1,128)S(1)}, f32[10,1,256]{2,1,0:T(1,128)S(1)}, u32[]{:S(2)}, u32[]{:S(2)}) collective-permute-start(f32[10,1,256]{2,1,0:T(1,128)S(1)} %get-tuple-element.45), channel_id=1, source_target_pairs={{0,1},{2,3},{4,5},{6,7},{1,0},{3,2},{5,4},{7,6},{8,9},{10,11},{12,... | collective-permute-start | bytes 30728 | tf_op jit(solution)/shard_map/ppermute | solution.py:201
  11.0 0.7 %collective-permute-start.6 = (f32[10,1,256]{2,1,0:T(1,128)S(1)}, f32[10,1,256]{2,1,0:T(1,128)S(1)}, u32[]{:S(2)}, u32[]{:S(2)}) collective-permute-start(f32[10,1,256]{2,1,0:T(1,128)S(1)} %get-tuple-element.46), channel_id=1, source_target_pairs={{1,2},{3,4},{5,6},{2,1},{4,3},{6,5},{9,10},{11,12},{13,14},{10,9},... | collective-permute-start | bytes 30728 | tf_op jit(solution)/shard_map/ppermute | solution.py:201
  11.7 0.0 collective-permute-done.refs_1_
  11.7 1.3 %collective-permute-done.1.refs_2_ = f32[1,16,256]{2,1,0:T(8,128)S(1)} collective-permute-done((f32[1,16,256]{2,1,0:T(8,128)S(1)}, f32[1,16,256]{2,1,0:T(8,128)S(1)}, u32[]{:S(2)}, u32[]{:S(2)}) %collective-permute-start.1) | collective-permute-done | bytes 16416 | tf_op jit(solution)/shard_map/ppermute | solution.py:201
  13.0 1.6 %collective-permute-done.2.refs_3_ = f32[1,16,256]{2,1,0:T(8,128)S(1)} collective-permute-done((f32[1,16,256]{2,1,0:T(8,128)S(1)}, f32[1,16,256]{2,1,0:T(8,128)S(1)}, u32[]{:S(2)}, u32[]{:S(2)}) %collective-permute-start.2) | collective-permute-done | bytes 16416 | tf_op jit(solution)/shard_map/ppermute | solution.py:201
  14.7 0.0 collective-permute-done.7.refs_5_
  14.7 0.0 collective-permute-done.6.refs_4_
  14.7 0.0 copy-done
  14.7 0.7 %collective-permute-start.10 = (f32[256,128]{1,0:T(8,128)S(1)}, f32[256,128]{1,0:T(8,128)S(1)}, u32[]{:S(2)}, u32[]{:S(2)}) collective-permute-start(f32[256,128]{1,0:T(8,128)S(1)} %get-tuple-element.23.refs_9_), channel_id=1, source_target_pairs={{0,128},{1,129},{2,130},{3,131},{4,132},{5,133},{6,134},{7,135},{8... | collective-permute-start | bytes 393224 | tf_op jit(solution)/shard_map/ppermute | solution.py:229
  15.4 0.7 %collective-permute-start.9 = (f32[256,128]{1,0:T(8,128)S(1)}, f32[256,128]{1,0:T(8,128)S(1)}, u32[]{:S(2)}, u32[]{:S(2)}) collective-permute-start(f32[256,128]{1,0:T(8,128)S(1)} %get-tuple-element.23.refs_9_), channel_id=1, source_target_pairs={{0,384},{1,385},{2,386},{3,387},{4,388},{5,389},{6,390},{7,391},{8... | collective-permute-start | bytes 393224 | tf_op jit(solution)/shard_map/ppermute | solution.py:229
  16.1 0.7 %collective-permute-start.8 = (f32[256,128]{1,0:T(8,128)S(1)}, f32[256,128]{1,0:T(8,128)S(1)}, u32[]{:S(2)}, u32[]{:S(2)}) collective-permute-start(f32[256,128]{1,0:T(8,128)S(1)} %get-tuple-element.23.refs_9_), channel_id=1, source_target_pairs={{0,32},{1,33},{2,34},{3,35},{4,36},{5,37},{6,38},{7,39},{8,40},{9,... | collective-permute-start | bytes 393224 | tf_op jit(solution)/shard_map/ppermute | solution.py:229
  16.8 3.4 %collective-permute-start.11 = (f32[10,1,256]{2,1,0:T(1,128)S(1)}, f32[10,1,256]{2,1,0:T(1,128)S(1)}, u32[]{:S(2)}, u32[]{:S(2)}) collective-permute-start(f32[10,1,256]{2,1,0:T(1,128)S(1)} %get-tuple-element.24), channel_id=1, source_target_pairs={{32,33},{34,35},{36,37},{38,39},{64,65},{66,67},{68,69},{70,71},{9... | collective-permute-start | bytes 30728 | tf_op jit(solution)/shard_map/ppermute | solution.py:201
  20.2 3.1 %collective-permute-start.12 = (f32[10,1,256]{2,1,0:T(1,128)S(1)}, f32[10,1,256]{2,1,0:T(1,128)S(1)}, u32[]{:S(2)}, u32[]{:S(2)}) collective-permute-start(f32[10,1,256]{2,1,0:T(1,128)S(1)} %get-tuple-element.25), channel_id=1, source_target_pairs={{33,34},{35,36},{37,38},{65,66},{67,68},{69,70},{97,98},{99,100},{... | collective-permute-start | bytes 30728 | tf_op jit(solution)/shard_map/ppermute | solution.py:201
  23.3 0.0 collective-permute-done.11.refs_4_
  23.3 4.5 %collective-permute-done.12.refs_5_ = f32[10,1,256]{2,1,0:T(1,128)S(1)} collective-permute-done((f32[10,1,256]{2,1,0:T(1,128)S(1)}, f32[10,1,256]{2,1,0:T(1,128)S(1)}, u32[]{:S(2)}, u32[]{:S(2)}) %collective-permute-start.12) | collective-permute-done | bytes 10272 | tf_op jit(solution)/shard_map/ppermute | solution.py:201
  27.9 0.0 collective-permute-done.10
  27.9 0.0 collective-permute-done.9
  27.9 0.0 collective-permute-done.8
  27.9 0.7 %collective-permute-start.15 = (f32[256,128]{1,0:T(8,128)S(1)}, f32[256,128]{1,0:T(8,128)S(1)}, u32[]{:S(2)}, u32[]{:S(2)}) collective-permute-start(f32[256,128]{1,0:T(8,128)S(1)} %add_select_fusion.held), channel_id=1, source_target_pairs={{0,256},{32,288},{128,192},{384,320},{1,257},{33,289},{129,193},{3... | collective-permute-start | bytes 393224 | tf_op jit(solution)/shard_map/ppermute | solution.py:237
  28.6 0.7 %collective-permute-start.14 = (f32[256,128]{1,0:T(8,128)S(1)}, f32[256,128]{1,0:T(8,128)S(1)}, u32[]{:S(2)}, u32[]{:S(2)}) collective-permute-start(f32[256,128]{1,0:T(8,128)S(1)} %add_select_fusion.held), channel_id=1, source_target_pairs={{0,64},{32,96},{128,224},{384,352},{1,65},{33,97},{129,225},{385,3... | collective-permute-start | bytes 393224 | tf_op jit(solution)/shard_map/ppermute | solution.py:237
  29.3 1.3 %collective-permute-start.13 = (f32[256,128]{1,0:T(8,128)S(1)}, f32[256,128]{1,0:T(8,128)S(1)}, u32[]{:S(2)}, u32[]{:S(2)}) collective-permute-start(f32[256,128]{1,0:T(8,128)S(1)} %add_select_fusion.held), channel_id=1, source_target_pairs={{0,448},{32,480},{128,160},{384,416},{1,449},{33,481},{129,161},{3... | collective-permute-start | bytes 393224 | tf_op jit(solution)/shard_map/ppermute | solution.py:237
  30.6 1.5 %tail.1 = (f32[8,16,256]{2,1,0:T(8,128)}, f32[256,128]{1,0:T(8,128)S(1)}) custom-call(f32[8,16,256]{2,1,0:T(8,128)S(1)} %bitcast.11, f32[1,16,256]{2,1,0:T(8,128)S(1)} %collective-permute-done.refs_1_, f32[1,16,256]{2,1,0:T(8,128)S(1)} %collective-permute-done.1.refs_2_, f32[1,16,256]{2,1,0:T(8,128)S(1)} %collective-permute-done.2.refs_3_, ...), custom_call_target="tpu_custom_call" | custom-call | tf_op jit(solution)/shard_map/tail/pallas_call | solution.py:156
  32.1 0.0 collective-permute-done.15.far1
  32.1 0.0 collective-permute-done.14.far2
  32.1 8.9 %collective-permute-done.13.far3 = f32[256,128]{1,0:T(8,128)S(1)} collective-permute-done((f32[256,128]{1,0:T(8,128)S(1)}, f32[256,128]{1,0:T(8,128)S(1)}, u32[]{:S(2)}, u32[]{:S(2)}) %collective-permute-start.13) | collective-permute-done | bytes 131104 | tf_op jit(solution)/shard_map/ppermute | solution.py:237
  41.0 1.2 %correlate.1 = f32[8,16,264]{2,1,0:T(8,128)} custom-call(f32[256,128]{1,0:T(8,128)S(1)} %get-tuple-element.30.mon, f32[256,128]{1,0:T(8,128)S(1)} %add_select_fusion.held, f32[256,128]{1,0:T(8,128)S(1)} %collective-permute-done.13.far3, f32[256,128]{1,0:T(8,128)S(1)} %collective-permute-done.14.far2, f32[256,128]{1,0:T(8,128)S(1)} %collective-permute-done.15.far1), custom_call_target="tpu_custom_call" | custom-call | tf_op jit(solution)/shard_map/correlate/pallas_call | solution.py:177
  (8 shorter events, 0.1 us)
Async XLA Ops:
  1.4 6.7 %collective-permute-start.3 = (f32[1,16,256]{2,1,0:T(8,128)S(1)}, f32[1,16,256]{2,1,0:T(8,128)S(1)}, u32[]{:S(2)}, u32[]{:S(2)}) collective-permute-start(f32[1,16,256]{2,1,0:T(8,128)S(1)} %get-tuple-element.18), channel_id=1, source_target_pairs={{0,8},{8,0},{1,9},{9,1},{2,10},{10,2},{3,11},{11,3},{4,12},{12,4},... | collective-permute-start | bytes 49160 | tf_op jit(solution)/shard_map/ppermute | solution.py:201
  2.0 8.2 %collective-permute-start.4 = (f32[1,16,256]{2,1,0:T(8,128)S(1)}, f32[1,16,256]{2,1,0:T(8,128)S(1)}, u32[]{:S(2)}, u32[]{:S(2)}) collective-permute-start(f32[1,16,256]{2,1,0:T(8,128)S(1)} %get-tuple-element.19), channel_id=1, source_target_pairs={{8,16},{16,8},{9,17},{17,9},{10,18},{18,10},{11,19},{19,11},{12,20... | collective-permute-start | bytes 49160 | tf_op jit(solution)/shard_map/ppermute | solution.py:201
  2.7 7.6 %collective-permute-start.5 = (f32[1,16,256]{2,1,0:T(8,128)S(1)}, f32[1,16,256]{2,1,0:T(8,128)S(1)}, u32[]{:S(2)}, u32[]{:S(2)}) collective-permute-start(f32[1,16,256]{2,1,0:T(8,128)S(1)} %get-tuple-element.20), channel_id=1, source_target_pairs={{16,24},{24,16},{17,25},{25,17},{18,26},{26,18},{19,27},{27,19},{2... | collective-permute-start | bytes 49160 | tf_op jit(solution)/shard_map/ppermute | solution.py:201
  3.4 4.6 %copy-start.1 = (s32[1,8,16]{2,1,0:T(8,128)S(1)}, s32[1,8,16]{2,1,0:T(8,128)}, u32[]{:S(2)}) copy-start(s32[1,8,16]{2,1,0:T(8,128)} %param.4) | copy-start | bytes 1540
  3.4 4.6 %copy-start.2 = (s32[1,8,16]{2,1,0:T(8,128)S(1)}, s32[1,8,16]{2,1,0:T(8,128)}, u32[]{:S(2)}) copy-start(s32[1,8,16]{2,1,0:T(8,128)} %param.5) | copy-start | bytes 1540
  4.3 10.4 %copy-start = (f32[1,8,16,256]{3,2,1,0:T(8,128)S(1)}, f32[1,8,16,256]{3,2,1,0:T(8,128)}, u32[]{:S(2)}) copy-start(f32[1,8,16,256]{3,2,1,0:T(8,128)} %param.3) | copy-start | bytes 393220
  4.3 7.4 %collective-permute-start = (f32[1,16,256]{2,1,0:T(8,128)S(1)}, f32[1,16,256]{2,1,0:T(8,128)S(1)}, u32[]{:S(2)}, u32[]{:S(2)}) collective-permute-start(f32[1,16,256]{2,1,0:T(8,128)S(1)} %get-tuple-element.18), channel_id=1, source_target_pairs={{32,40},{64,72},{96,104},{128,136},{160,168},{192,200},{224,232},{... | collective-permute-start | bytes 49160 | tf_op jit(solution)/shard_map/ppermute | solution.py:201
  5.1 7.9 %collective-permute-start.1 = (f32[1,16,256]{2,1,0:T(8,128)S(1)}, f32[1,16,256]{2,1,0:T(8,128)S(1)}, u32[]{:S(2)}, u32[]{:S(2)}) collective-permute-start(f32[1,16,256]{2,1,0:T(8,128)S(1)} %get-tuple-element.19), channel_id=1, source_target_pairs={{40,48},{72,80},{104,112},{136,144},{168,176},{200,208},{232,240},... | collective-permute-start | bytes 49160 | tf_op jit(solution)/shard_map/ppermute | solution.py:201
  8.1 6.5 %collective-permute-start.2 = (f32[1,16,256]{2,1,0:T(8,128)S(1)}, f32[1,16,256]{2,1,0:T(8,128)S(1)}, u32[]{:S(2)}, u32[]{:S(2)}) collective-permute-start(f32[1,16,256]{2,1,0:T(8,128)S(1)} %get-tuple-element.20), channel_id=1, source_target_pairs={{48,56},{80,88},{112,120},{144,152},{176,184},{208,216},{240,248},... | collective-permute-start | bytes 49160 | tf_op jit(solution)/shard_map/ppermute | solution.py:201
  10.3 4.3 %collective-permute-start.7 = (f32[10,1,256]{2,1,0:T(1,128)S(1)}, f32[10,1,256]{2,1,0:T(1,128)S(1)}, u32[]{:S(2)}, u32[]{:S(2)}) collective-permute-start(f32[10,1,256]{2,1,0:T(1,128)S(1)} %get-tuple-element.45), channel_id=1, source_target_pairs={{0,1},{2,3},{4,5},{6,7},{1,0},{3,2},{5,4},{7,6},{8,9},{10,11},{12,... | collective-permute-start | bytes 30728 | tf_op jit(solution)/shard_map/ppermute | solution.py:201
  11.0 3.6 %collective-permute-start.6 = (f32[10,1,256]{2,1,0:T(1,128)S(1)}, f32[10,1,256]{2,1,0:T(1,128)S(1)}, u32[]{:S(2)}, u32[]{:S(2)}) collective-permute-start(f32[10,1,256]{2,1,0:T(1,128)S(1)} %get-tuple-element.46), channel_id=1, source_target_pairs={{1,2},{3,4},{5,6},{2,1},{4,3},{6,5},{9,10},{11,12},{13,14},{10,9},... | collective-permute-start | bytes 30728 | tf_op jit(solution)/shard_map/ppermute | solution.py:201
  14.7 13.2 %collective-permute-start.10 = (f32[256,128]{1,0:T(8,128)S(1)}, f32[256,128]{1,0:T(8,128)S(1)}, u32[]{:S(2)}, u32[]{:S(2)}) collective-permute-start(f32[256,128]{1,0:T(8,128)S(1)} %get-tuple-element.23.refs_9_), channel_id=1, source_target_pairs={{0,128},{1,129},{2,130},{3,131},{4,132},{5,133},{6,134},{7,135},{8... | collective-permute-start | bytes 393224 | tf_op jit(solution)/shard_map/ppermute | solution.py:229
  15.4 12.5 %collective-permute-start.9 = (f32[256,128]{1,0:T(8,128)S(1)}, f32[256,128]{1,0:T(8,128)S(1)}, u32[]{:S(2)}, u32[]{:S(2)}) collective-permute-start(f32[256,128]{1,0:T(8,128)S(1)} %get-tuple-element.23.refs_9_), channel_id=1, source_target_pairs={{0,384},{1,385},{2,386},{3,387},{4,388},{5,389},{6,390},{7,391},{8... | collective-permute-start | bytes 393224 | tf_op jit(solution)/shard_map/ppermute | solution.py:229
  16.1 11.8 %collective-permute-start.8 = (f32[256,128]{1,0:T(8,128)S(1)}, f32[256,128]{1,0:T(8,128)S(1)}, u32[]{:S(2)}, u32[]{:S(2)}) collective-permute-start(f32[256,128]{1,0:T(8,128)S(1)} %get-tuple-element.23.refs_9_), channel_id=1, source_target_pairs={{0,32},{1,33},{2,34},{3,35},{4,36},{5,37},{6,38},{7,39},{8,40},{9,... | collective-permute-start | bytes 393224 | tf_op jit(solution)/shard_map/ppermute | solution.py:229
  16.8 6.5 %collective-permute-start.11 = (f32[10,1,256]{2,1,0:T(1,128)S(1)}, f32[10,1,256]{2,1,0:T(1,128)S(1)}, u32[]{:S(2)}, u32[]{:S(2)}) collective-permute-start(f32[10,1,256]{2,1,0:T(1,128)S(1)} %get-tuple-element.24), channel_id=1, source_target_pairs={{32,33},{34,35},{36,37},{38,39},{64,65},{66,67},{68,69},{70,71},{9... | collective-permute-start | bytes 30728 | tf_op jit(solution)/shard_map/ppermute | solution.py:201
  20.2 7.7 %collective-permute-start.12 = (f32[10,1,256]{2,1,0:T(1,128)S(1)}, f32[10,1,256]{2,1,0:T(1,128)S(1)}, u32[]{:S(2)}, u32[]{:S(2)}) collective-permute-start(f32[10,1,256]{2,1,0:T(1,128)S(1)} %get-tuple-element.25), channel_id=1, source_target_pairs={{33,34},{35,36},{37,38},{65,66},{67,68},{69,70},{97,98},{99,100},{... | collective-permute-start | bytes 30728 | tf_op jit(solution)/shard_map/ppermute | solution.py:201
  27.9 4.2 %collective-permute-start.15 = (f32[256,128]{1,0:T(8,128)S(1)}, f32[256,128]{1,0:T(8,128)S(1)}, u32[]{:S(2)}, u32[]{:S(2)}) collective-permute-start(f32[256,128]{1,0:T(8,128)S(1)} %add_select_fusion.held), channel_id=1, source_target_pairs={{0,256},{32,288},{128,192},{384,320},{1,257},{33,289},{129,193},{3... | collective-permute-start | bytes 393224 | tf_op jit(solution)/shard_map/ppermute | solution.py:237
  28.6 3.5 %collective-permute-start.14 = (f32[256,128]{1,0:T(8,128)S(1)}, f32[256,128]{1,0:T(8,128)S(1)}, u32[]{:S(2)}, u32[]{:S(2)}) collective-permute-start(f32[256,128]{1,0:T(8,128)S(1)} %add_select_fusion.held), channel_id=1, source_target_pairs={{0,64},{32,96},{128,224},{384,352},{1,65},{33,97},{129,225},{385,3... | collective-permute-start | bytes 393224 | tf_op jit(solution)/shard_map/ppermute | solution.py:237
  29.3 11.7 %collective-permute-start.13 = (f32[256,128]{1,0:T(8,128)S(1)}, f32[256,128]{1,0:T(8,128)S(1)}, u32[]{:S(2)}, u32[]{:S(2)}) collective-permute-start(f32[256,128]{1,0:T(8,128)S(1)} %add_select_fusion.held), channel_id=1, source_target_pairs={{0,448},{32,480},{128,160},{384,416},{1,449},{33,481},{129,161},{3... | collective-permute-start | bytes 393224 | tf_op jit(solution)/shard_map/ppermute | solution.py:237

commit v7 on v6

--- a/solution.py
+++ b/solution.py
@@ -14,7 +14,7 @@
 NWIN = 8
 EPS = 1e-06
 
-FANOUT = {0: (8, 2, 14), 1: (9, 3, 15), 4: (6, 7, 5), 12: (10, 11, 13)}
+FANOUT = {0: (8, 4, 12), 1: (9, 5, 13), 2: (6, 7, 3), 14: (10, 11, 15)}
 ROWS = 8
 COLS = 16
 TRACES = ROWS * COLS
@@ -30,27 +30,31 @@
     return out
 
 
-def first_kernel(*refs):
-    @pl.when(lax.axis_index("vintage") == 0)
+def is_head(place):
+    return functools.reduce(jnp.logical_or, [place == v for v in FANOUT])
+
+
+def head_kernel(*refs):
+    @pl.when(is_head(lax.axis_index("vintage")))
     def _():
         attr_body(*refs[:4], refs[5], refs[4], *refs[6:])
 
 
-def later_kernel(*refs):
-    ins, semb_first, attr_first, semb_out, attr_out = refs[:8], refs[8], refs[9], refs[10], refs[11]
-    head = lax.axis_index("vintage") == 0
+def tail_kernel(*refs):
+    ins, semb_head, attr_head, semb_out, attr_out = refs[:8], refs[8], refs[9], refs[10], refs[11]
+    head = is_head(lax.axis_index("vintage"))
 
     @pl.when(head)
     def _():
-        semb_out[...] = semb_first[...]
-        attr_out[...] = attr_first[...]
+        semb_out[...] = semb_head[...]
+        attr_out[...] = attr_head[...]
 
     @pl.when(jnp.logical_not(head))
     def _():
         attr_body(*ins, *refs[10:])
 
 
-def attr_body(tile, row_01, row_12, row_23, col_a, col_b, dip_il, dip_xl, semb_out, attr_out,
+def attr_body(tile, row_12, row_23, row_01, col_a, col_b, dip_il, dip_xl, semb_out, attr_out,
               rim, moved, inner, sums, three):
     odd_row = lax.rem(lax.axis_index("inline"), 2) == 1
     odd_col = lax.rem(lax.axis_index("xline"), 2) == 1
@@ -107,8 +111,7 @@
 
 def correl_kernel(mon, held, far3, far2, far1, out, base, result):
     half_lags = LAGS // 2
-    place = lax.axis_index("vintage")
-    holder = functools.reduce(jnp.logical_or, [place == v for v in FANOUT])
+    holder = is_head(lax.axis_index("vintage"))
     zeros = jnp.zeros((half_lags, TRACES), jnp.float32)
     base[0:half_lags, :] = zeros
     base[half_lags + TIME_SAMPLES:, :] = zeros
@@ -216,25 +219,20 @@
 def per_device(amplitude, inline_slope, crossline_slope):
     tile = amplitude[0]
     dips = (inline_slope.reshape(1, TRACES), crossline_slope.reshape(1, TRACES))
-    others = range(1, lax.axis_size("vintage"))
+    vintages = lax.axis_size("vintage")
+    others = [v for v in range(vintages) if v not in FANOUT]
     along, across = ((0,), (1,), (2,)), ((0, 2, 4, 6), (1, 3, 5))
     sends = pair_sends(tile[:1], tile[-1:], "inline")
     outer = jnp.where(lax.axis_index("inline") == lax.axis_size("inline") - 1, tile[:1], tile[-1:])
-    sends = (*sends, outer)
-    rows = swap(sends, "inline", [0], along)
-    gated = lax.optimization_barrier((sends[1], sends[2], sends[0], tile[:, :1], tile[:, -1:]))
-    ends, sends = gated[3:], (gated[2], gated[0], gated[1])
-    cols = swap(edge_columns(ends, rows), "xline", [0], across)
-    semb0, attr0 = attributes(first_kernel, "head", tile, *[rows[n] for n in (0, 1, 2)], *cols[::-1], *dips)
-    got = [lax.ppermute(attr0, "vintage", [(0, k)]) for k in (1, 12, 4)]
-    rows = swap(sends, "inline", others, along)
-    cols = edge_columns(ends, rows)
-    cols = swap(lax.optimization_barrier((*cols, attr0))[:2], "xline", others, across)
-    joined = lax.optimization_barrier((*got, *cols))
-    got, cols = joined[:3], joined[3:]
-    semb, attr = attributes(later_kernel, "tail", tile, *[rows[n] for n in (0, 1, 2)], *cols, *dips, semb0, attr0)
+    rows = swap((*sends, outer), "inline", range(vintages), along)
+    sends = edge_columns((tile[:, :1], tile[:, -1:]), rows)
+    cols = swap(sends, "xline", FANOUT, across)
+    semb0, attr0 = attributes(head_kernel, "head", tile, *[rows[n] for n in (1, 2, 0)], *cols[::-1], *dips)
+    got = [lax.ppermute(attr0, "vintage", [(0, k)]) for k in (14, 2, 1)]
     held = jnp.where(lax.axis_index("vintage") == 0, attr0, got[0] + got[1] + got[2])
     far = [lax.ppermute(held, "vintage", [(s, to[n]) for s, to in FANOUT.items()]) for n in (2, 1, 0)]
+    cols = swap(lax.optimization_barrier((*sends, held))[:2], "xline", others, across)
+    semb, attr = attributes(tail_kernel, "tail", tile, *[rows[n] for n in (1, 2, 0)], *cols, *dips, semb0, attr0)
     correl = correlate(attr, held, far)
     return (semb[None], correl[None])
 

time: 42.7 us -> 41.2 us (0.965)
  the two profiles are of different devices: /device:TPU:376 before, /device:TPU:175 now
where the time goes in v7:
time: 41.2 us; the launch traced here: 40.8 us
  starting transfers between devices  20.5 us (50%)
  waiting for transfers between devices  14.7 us (36%)
  Pallas kernels  2.72 us (7%)
  local copies, waits for them, and re-layouts  1.07 us (3%)
  between operations  0.9 us (2%)
  other arithmetic  0.85 us (2%)
    ppermute x7, starting transfers between devices, swap(): lax.ppermute(sends[n], ('vintage', axis), low + [(b, a) for a, b in low])  15.9 us
    ppermute x3, waiting for transfers between devices, per_device(): lax.ppermute(held, 'vintage', [(s, to[n]) for s, to in FANOUT.items()])  12 us
    ppermute x7, waiting for transfers between devices, swap(): lax.ppermute(sends[n], ('vintage', axis), low + [(b, a) for a, b in low])  2.72 us
    ppermute x3, starting transfers between devices, per_device(): lax.ppermute(held, 'vintage', [(s, to[n]) for s, to in FANOUT.items()])  2.63 us
    ppermute x3, starting transfers between devices, per_device(): got = [lax.ppermute(attr0, 'vintage', [(0, k)]) for k in (14, 2, 1)]  2.01 us
    pallas_call x2, Pallas kernels, attributes(): pl.pallas_call(kernel, out_shape=(jax.ShapeDtypeStruct((ROWS, COLS, TIME_...  1.51 us
    pallas_call x1, Pallas kernels, correlate(): pl.pallas_call(correl_kernel, out_shape=jax.ShapeDtypeStruct((ROWS, COLS,...  1.2 us
    slice x1, local copies, waits for them, and re-layouts, per_device(): sends = edge_columns((tile[:, :1], tile[:, -1:]), rows)  0.89 us
  transfers between devices with their start and end apart: 13, of which 2 were waited for; matrix products, arithmetic and copies ran while one was open for 3% of the time, Pallas kernels for 4%

profile of v7, /device:TPU:175, one launch (start us, length us, event | category | flops | bytes accessed | tf_op | source)
XLA Modules:
  0.0 40.8 jit_solution(13288720950340924961)
XLA Ops:
  0.6 0.0 copy-start
  0.6 0.8 %select_bitcast_fusion = (f32[1,16,256]{2,1,0:T(8,128)S(1)}, f32[1,16,256]{2,1,0:T(8,128)S(1)}, f32[1,16,256]{2,1,0:T(8,128)S(1)}) fusion(f32[1,8,16,256]{3,2,1,0:T(8,128)} %param.3, pred[]{:T(512)S(6)} %eq.13, pred[]{:T(512)S(6)} %eq.14), kind=kLoop, calls=%fused_computation.3 | loop fusion | flops 12288 | bytes 81922 | tf_op jit(solution)/shard_map/jit(_where)/select_n | solution.py:196
  1.4 1.9 %collective-permute-start.2 = (f32[1,16,256]{2,1,0:T(8,128)S(1)}, f32[1,16,256]{2,1,0:T(8,128)S(1)}, u32[]{:S(2)}, u32[]{:S(2)}) collective-permute-start(f32[1,16,256]{2,1,0:T(8,128)S(1)} %get-tuple-element.16), channel_id=1, source_target_pairs={{0,8},{32,40},{64,72},{96,104},{128,136},{160,168},{192,200},{224,... | collective-permute-start | bytes 49160 | tf_op jit(solution)/shard_map/ppermute | solution.py:204
  3.4 5.8 %collective-permute-start = (f32[1,16,256]{2,1,0:T(8,128)S(1)}, f32[1,16,256]{2,1,0:T(8,128)S(1)}, u32[]{:S(2)}, u32[]{:S(2)}) collective-permute-start(f32[1,16,256]{2,1,0:T(8,128)S(1)} %get-tuple-element.17), channel_id=1, source_target_pairs={{8,16},{40,48},{72,80},{104,112},{136,144},{168,176},{200,208},{23... | collective-permute-start | bytes 49160 | tf_op jit(solution)/shard_map/ppermute | solution.py:204
  9.1 0.7 %collective-permute-start.1 = (f32[1,16,256]{2,1,0:T(8,128)S(1)}, f32[1,16,256]{2,1,0:T(8,128)S(1)}, u32[]{:S(2)}, u32[]{:S(2)}) collective-permute-start(f32[1,16,256]{2,1,0:T(8,128)S(1)} %get-tuple-element.18), channel_id=1, source_target_pairs={{16,24},{48,56},{80,88},{112,120},{144,152},{176,184},{208,216},{2... | collective-permute-start | bytes 49160 | tf_op jit(solution)/shard_map/ppermute | solution.py:204
  9.8 0.9 %fusion = (f32[8,1,256]{2,1,0:T(1,128)S(1)}, f32[8,1,256]{2,1,0:T(1,128)S(1)}) fusion(f32[8,16,256]{2,1,0:T(8,128)} %bitcast.9), kind=kLoop, calls=%fused_computation.10 | loop fusion | bytes 32768 | tf_op jit(solution)/shard_map/slice | solution.py:228
  10.7 0.0 collective-permute-done.2.refs_3_
  10.7 0.0 collective-permute-done.refs_1_
  10.7 0.0 collective-permute-done.1.refs_2_
  10.8 0.0 copy-start.1
  10.8 0.0 copy-start.2
  10.8 0.7 %collective-permute-start.3 = (f32[10,1,256]{2,1,0:T(1,128)S(1)}, f32[10,1,256]{2,1,0:T(1,128)S(1)}, u32[]{:S(2)}, u32[]{:S(2)}) collective-permute-start(f32[10,1,256]{2,1,0:T(1,128)S(1)} %get-tuple-element.10), channel_id=1, source_target_pairs={{1,2},{3,4},{5,6},{33,34},{35,36},{37,38},{65,66},{67,68},{69,70},... | collective-permute-start | bytes 30728 | tf_op jit(solution)/shard_map/ppermute | solution.py:204
  11.5 0.7 %collective-permute-start.4 = (f32[10,1,256]{2,1,0:T(1,128)S(1)}, f32[10,1,256]{2,1,0:T(1,128)S(1)}, u32[]{:S(2)}, u32[]{:S(2)}) collective-permute-start(f32[10,1,256]{2,1,0:T(1,128)S(1)} %get-tuple-element.9), channel_id=1, source_target_pairs={{0,1},{2,3},{4,5},{6,7},{32,33},{34,35},{36,37},{38,39},{64,65},{6... | collective-permute-start | bytes 30728 | tf_op jit(solution)/shard_map/ppermute | solution.py:204
  12.1 0.0 copy-done.1
  12.2 0.1 reshape.230.refs_6_
  12.2 0.0 copy-done.2
  12.2 0.1 reshape.231.refs_7_
  12.3 0.0 collective-permute-done.3.refs_4_
  12.3 0.0 collective-permute-done.4.refs_5_
  12.3 0.0 copy-done
  12.4 0.7 %collective-permute-start.7 = (f32[256,128]{1,0:T(8,128)S(1)}, f32[256,128]{1,0:T(8,128)S(1)}, u32[]{:S(2)}, u32[]{:S(2)}) collective-permute-start(f32[256,128]{1,0:T(8,128)S(1)} %get-tuple-element.8.refs_9_), channel_id=1, source_target_pairs={{0,32},{1,33},{2,34},{3,35},{4,36},{5,37},{6,38},{7,39},{8,40},{9,... | collective-permute-start | bytes 393224 | tf_op jit(solution)/shard_map/ppermute | solution.py:231
  13.0 0.7 %collective-permute-start.6 = (f32[256,128]{1,0:T(8,128)S(1)}, f32[256,128]{1,0:T(8,128)S(1)}, u32[]{:S(2)}, u32[]{:S(2)}) collective-permute-start(f32[256,128]{1,0:T(8,128)S(1)} %get-tuple-element.8.refs_9_), channel_id=1, source_target_pairs={{0,64},{1,65},{2,66},{3,67},{4,68},{5,69},{6,70},{7,71},{8,72},{9,... | collective-permute-start | bytes 393224 | tf_op jit(solution)/shard_map/ppermute | solution.py:231
  13.7 0.7 %collective-permute-start.5 = (f32[256,128]{1,0:T(8,128)S(1)}, f32[256,128]{1,0:T(8,128)S(1)}, u32[]{:S(2)}, u32[]{:S(2)}) collective-permute-start(f32[256,128]{1,0:T(8,128)S(1)} %get-tuple-element.8.refs_9_), channel_id=1, source_target_pairs={{0,448},{1,449},{2,450},{3,451},{4,452},{5,453},{6,454},{7,455},{8... | collective-permute-start | bytes 393224 | tf_op jit(solution)/shard_map/ppermute | solution.py:231
  14.4 0.0 collective-permute-done.7
  14.4 0.0 collective-permute-done.6
  14.4 0.0 collective-permute-done.5
  14.5 0.7 %collective-permute-start.12 = (f32[256,128]{1,0:T(8,128)S(1)}, f32[256,128]{1,0:T(8,128)S(1)}, u32[]{:S(2)}, u32[]{:S(2)}) collective-permute-start(f32[256,128]{1,0:T(8,128)S(1)} %add_select_fusion.held), channel_id=1, source_target_pairs={{0,256},{32,288},{64,192},{448,320},{1,257},{33,289},{65,193},{449... | collective-permute-start | bytes 393224 | tf_op jit(solution)/shard_map/ppermute | solution.py:233
  15.2 1.3 %collective-permute-start.11 = (f32[256,128]{1,0:T(8,128)S(1)}, f32[256,128]{1,0:T(8,128)S(1)}, u32[]{:S(2)}, u32[]{:S(2)}) collective-permute-start(f32[256,128]{1,0:T(8,128)S(1)} %add_select_fusion.held), channel_id=1, source_target_pairs={{0,128},{32,160},{64,224},{448,352},{1,129},{33,161},{65,225},{449... | collective-permute-start | bytes 393224 | tf_op jit(solution)/shard_map/ppermute | solution.py:233
  16.5 0.7 %collective-permute-start.10 = (f32[256,128]{1,0:T(8,128)S(1)}, f32[256,128]{1,0:T(8,128)S(1)}, u32[]{:S(2)}, u32[]{:S(2)}) collective-permute-start(f32[256,128]{1,0:T(8,128)S(1)} %add_select_fusion.held), channel_id=1, source_target_pairs={{0,384},{32,416},{64,96},{448,480},{1,385},{33,417},{65,97},{449,4... | collective-permute-start | bytes 393224 | tf_op jit(solution)/shard_map/ppermute | solution.py:233
  17.1 2.5 %collective-permute-start.8 = (f32[10,1,256]{2,1,0:T(1,128)S(1)}, f32[10,1,256]{2,1,0:T(1,128)S(1)}, u32[]{:S(2)}, u32[]{:S(2)}) collective-permute-start(f32[10,1,256]{2,1,0:T(1,128)S(1)} %get-tuple-element.9), channel_id=1, source_target_pairs={{96,97},{98,99},{100,101},{102,103},{128,129},{130,131},{132,133},... | collective-permute-start | bytes 30728 | tf_op jit(solution)/shard_map/ppermute | solution.py:204
  19.6 3.8 %collective-permute-start.9 = (f32[10,1,256]{2,1,0:T(1,128)S(1)}, f32[10,1,256]{2,1,0:T(1,128)S(1)}, u32[]{:S(2)}, u32[]{:S(2)}) collective-permute-start(f32[10,1,256]{2,1,0:T(1,128)S(1)} %get-tuple-element.10), channel_id=1, source_target_pairs={{97,98},{99,100},{101,102},{129,130},{131,132},{133,134},{161,162}... | collective-permute-start | bytes 30728 | tf_op jit(solution)/shard_map/ppermute | solution.py:204
  23.4 0.0 collective-permute-done.8.refs_4_
  23.4 2.7 %collective-permute-done.9.refs_5_ = f32[10,1,256]{2,1,0:T(1,128)S(1)} collective-permute-done((f32[10,1,256]{2,1,0:T(1,128)S(1)}, f32[10,1,256]{2,1,0:T(1,128)S(1)}, u32[]{:S(2)}, u32[]{:S(2)}) %collective-permute-start.9) | collective-permute-done | bytes 10272 | tf_op jit(solution)/shard_map/ppermute | solution.py:204
  26.1 1.5 %tail.1 = (f32[8,16,256]{2,1,0:T(8,128)}, f32[256,128]{1,0:T(8,128)S(1)}) custom-call(f32[8,16,256]{2,1,0:T(8,128)S(1)} %bitcast.11, f32[1,16,256]{2,1,0:T(8,128)S(1)} %collective-permute-done.refs_1_, f32[1,16,256]{2,1,0:T(8,128)S(1)} %collective-permute-done.1.refs_2_, f32[1,16,256]{2,1,0:T(8,128)S(1)} %collective-permute-done.2.refs_3_, ...), custom_call_target="tpu_custom_call" | custom-call | tf_op jit(solution)/shard_map/tail/pallas_call | solution.py:159
  27.6 0.0 collective-permute-done.12.far1
  27.6 12.0 %collective-permute-done.11.far2 = f32[256,128]{1,0:T(8,128)S(1)} collective-permute-done((f32[256,128]{1,0:T(8,128)S(1)}, f32[256,128]{1,0:T(8,128)S(1)}, u32[]{:S(2)}, u32[]{:S(2)}) %collective-permute-start.11) | collective-permute-done | bytes 131104 | tf_op jit(solution)/shard_map/ppermute | solution.py:233
  39.6 0.0 collective-permute-done.10.far3
  39.6 1.2 %correlate.1 = f32[8,16,264]{2,1,0:T(8,128)} custom-call(f32[256,128]{1,0:T(8,128)S(1)} %get-tuple-element.13.mon, f32[256,128]{1,0:T(8,128)S(1)} %add_select_fusion.held, f32[256,128]{1,0:T(8,128)S(1)} %collective-permute-done.10.far3, f32[256,128]{1,0:T(8,128)S(1)} %collective-permute-done.11.far2, f32[256,128]{1,0:T(8,128)S(1)} %collective-permute-done.12.far1), custom_call_target="tpu_custom_call" | custom-call | tf_op jit(solution)/shard_map/correlate/pallas_call | solution.py:180
  (5 shorter events, 0.1 us)
Async XLA Ops:
  0.6 11.7 %copy-start = (f32[1,8,16,256]{3,2,1,0:T(8,128)S(1)}, f32[1,8,16,256]{3,2,1,0:T(8,128)}, u32[]{:S(2)}) copy-start(f32[1,8,16,256]{3,2,1,0:T(8,128)} %param.3) | copy-start | bytes 393220
  1.4 9.3 %collective-permute-start.2 = (f32[1,16,256]{2,1,0:T(8,128)S(1)}, f32[1,16,256]{2,1,0:T(8,128)S(1)}, u32[]{:S(2)}, u32[]{:S(2)}) collective-permute-start(f32[1,16,256]{2,1,0:T(8,128)S(1)} %get-tuple-element.16), channel_id=1, source_target_pairs={{0,8},{32,40},{64,72},{96,104},{128,136},{160,168},{192,200},{224,... | collective-permute-start | bytes 49160 | tf_op jit(solution)/shard_map/ppermute | solution.py:204
  3.4 7.3 %collective-permute-start = (f32[1,16,256]{2,1,0:T(8,128)S(1)}, f32[1,16,256]{2,1,0:T(8,128)S(1)}, u32[]{:S(2)}, u32[]{:S(2)}) collective-permute-start(f32[1,16,256]{2,1,0:T(8,128)S(1)} %get-tuple-element.17), channel_id=1, source_target_pairs={{8,16},{40,48},{72,80},{104,112},{136,144},{168,176},{200,208},{23... | collective-permute-start | bytes 49160 | tf_op jit(solution)/shard_map/ppermute | solution.py:204
  9.1 1.6 %collective-permute-start.1 = (f32[1,16,256]{2,1,0:T(8,128)S(1)}, f32[1,16,256]{2,1,0:T(8,128)S(1)}, u32[]{:S(2)}, u32[]{:S(2)}) collective-permute-start(f32[1,16,256]{2,1,0:T(8,128)S(1)} %get-tuple-element.18), channel_id=1, source_target_pairs={{16,24},{48,56},{80,88},{112,120},{144,152},{176,184},{208,216},{2... | collective-permute-start | bytes 49160 | tf_op jit(solution)/shard_map/ppermute | solution.py:204
  10.8 1.4 %copy-start.1 = (s32[1,8,16]{2,1,0:T(8,128)S(1)}, s32[1,8,16]{2,1,0:T(8,128)}, u32[]{:S(2)}) copy-start(s32[1,8,16]{2,1,0:T(8,128)} %param.4) | copy-start | bytes 1540
  10.8 1.4 %copy-start.2 = (s32[1,8,16]{2,1,0:T(8,128)S(1)}, s32[1,8,16]{2,1,0:T(8,128)}, u32[]{:S(2)}) copy-start(s32[1,8,16]{2,1,0:T(8,128)} %param.5) | copy-start | bytes 1540
  10.8 1.5 %collective-permute-start.3 = (f32[10,1,256]{2,1,0:T(1,128)S(1)}, f32[10,1,256]{2,1,0:T(1,128)S(1)}, u32[]{:S(2)}, u32[]{:S(2)}) collective-permute-start(f32[10,1,256]{2,1,0:T(1,128)S(1)} %get-tuple-element.10), channel_id=1, source_target_pairs={{1,2},{3,4},{5,6},{33,34},{35,36},{37,38},{65,66},{67,68},{69,70},... | collective-permute-start | bytes 30728 | tf_op jit(solution)/shard_map/ppermute | solution.py:204
  11.5 0.9 %collective-permute-start.4 = (f32[10,1,256]{2,1,0:T(1,128)S(1)}, f32[10,1,256]{2,1,0:T(1,128)S(1)}, u32[]{:S(2)}, u32[]{:S(2)}) collective-permute-start(f32[10,1,256]{2,1,0:T(1,128)S(1)} %get-tuple-element.9), channel_id=1, source_target_pairs={{0,1},{2,3},{4,5},{6,7},{32,33},{34,35},{36,37},{38,39},{64,65},{6... | collective-permute-start | bytes 30728 | tf_op jit(solution)/shard_map/ppermute | solution.py:204
  12.4 2.0 %collective-permute-start.7 = (f32[256,128]{1,0:T(8,128)S(1)}, f32[256,128]{1,0:T(8,128)S(1)}, u32[]{:S(2)}, u32[]{:S(2)}) collective-permute-start(f32[256,128]{1,0:T(8,128)S(1)} %get-tuple-element.8.refs_9_), channel_id=1, source_target_pairs={{0,32},{1,33},{2,34},{3,35},{4,36},{5,37},{6,38},{7,39},{8,40},{9,... | collective-permute-start | bytes 393224 | tf_op jit(solution)/shard_map/ppermute | solution.py:231
  13.0 1.4 %collective-permute-start.6 = (f32[256,128]{1,0:T(8,128)S(1)}, f32[256,128]{1,0:T(8,128)S(1)}, u32[]{:S(2)}, u32[]{:S(2)}) collective-permute-start(f32[256,128]{1,0:T(8,128)S(1)} %get-tuple-element.8.refs_9_), channel_id=1, source_target_pairs={{0,64},{1,65},{2,66},{3,67},{4,68},{5,69},{6,70},{7,71},{8,72},{9,... | collective-permute-start | bytes 393224 | tf_op jit(solution)/shard_map/ppermute | solution.py:231
  13.7 0.7 %collective-permute-start.5 = (f32[256,128]{1,0:T(8,128)S(1)}, f32[256,128]{1,0:T(8,128)S(1)}, u32[]{:S(2)}, u32[]{:S(2)}) collective-permute-start(f32[256,128]{1,0:T(8,128)S(1)} %get-tuple-element.8.refs_9_), channel_id=1, source_target_pairs={{0,448},{1,449},{2,450},{3,451},{4,452},{5,453},{6,454},{7,455},{8... | collective-permute-start | bytes 393224 | tf_op jit(solution)/shard_map/ppermute | solution.py:231
  14.5 13.1 %collective-permute-start.12 = (f32[256,128]{1,0:T(8,128)S(1)}, f32[256,128]{1,0:T(8,128)S(1)}, u32[]{:S(2)}, u32[]{:S(2)}) collective-permute-start(f32[256,128]{1,0:T(8,128)S(1)} %add_select_fusion.held), channel_id=1, source_target_pairs={{0,256},{32,288},{64,192},{448,320},{1,257},{33,289},{65,193},{449... | collective-permute-start | bytes 393224 | tf_op jit(solution)/shard_map/ppermute | solution.py:233
  15.2 24.5 %collective-permute-start.11 = (f32[256,128]{1,0:T(8,128)S(1)}, f32[256,128]{1,0:T(8,128)S(1)}, u32[]{:S(2)}, u32[]{:S(2)}) collective-permute-start(f32[256,128]{1,0:T(8,128)S(1)} %add_select_fusion.held), channel_id=1, source_target_pairs={{0,128},{32,160},{64,224},{448,352},{1,129},{33,161},{65,225},{449... | collective-permute-start | bytes 393224 | tf_op jit(solution)/shard_map/ppermute | solution.py:233
  16.5 23.2 %collective-permute-start.10 = (f32[256,128]{1,0:T(8,128)S(1)}, f32[256,128]{1,0:T(8,128)S(1)}, u32[]{:S(2)}, u32[]{:S(2)}) collective-permute-start(f32[256,128]{1,0:T(8,128)S(1)} %add_select_fusion.held), channel_id=1, source_target_pairs={{0,384},{32,416},{64,96},{448,480},{1,385},{33,417},{65,97},{449,4... | collective-permute-start | bytes 393224 | tf_op jit(solution)/shard_map/ppermute | solution.py:233
  17.1 6.3 %collective-permute-start.8 = (f32[10,1,256]{2,1,0:T(1,128)S(1)}, f32[10,1,256]{2,1,0:T(1,128)S(1)}, u32[]{:S(2)}, u32[]{:S(2)}) collective-permute-start(f32[10,1,256]{2,1,0:T(1,128)S(1)} %get-tuple-element.9), channel_id=1, source_target_pairs={{96,97},{98,99},{100,101},{102,103},{128,129},{130,131},{132,133},... | collective-permute-start | bytes 30728 | tf_op jit(solution)/shard_map/ppermute | solution.py:204
  19.6 6.5 %collective-permute-start.9 = (f32[10,1,256]{2,1,0:T(1,128)S(1)}, f32[10,1,256]{2,1,0:T(1,128)S(1)}, u32[]{:S(2)}, u32[]{:S(2)}) collective-permute-start(f32[10,1,256]{2,1,0:T(1,128)S(1)} %get-tuple-element.10), channel_id=1, source_target_pairs={{97,98},{99,100},{101,102},{129,130},{131,132},{133,134},{161,162}... | collective-permute-start | bytes 30728 | tf_op jit(solution)/shard_map/ppermute | solution.py:204

commit v8 on v7

--- a/solution.py
+++ b/solution.py
@@ -1,5 +1,3 @@
-import functools
-
 import jax
 import jax.numpy as jnp
 from jax import lax
@@ -14,7 +12,7 @@
 NWIN = 8
 EPS = 1e-06
 
-FANOUT = {0: (8, 4, 12), 1: (9, 5, 13), 2: (6, 7, 3), 14: (10, 11, 15)}
+FANOUT = {0: (3, 2, 1), 4: (7, 6, 5), 8: (11, 10, 9), 12: (15, 14, 13)}
 ROWS = 8
 COLS = 16
 TRACES = ROWS * COLS
@@ -30,19 +28,15 @@
     return out
 
 
-def is_head(place):
-    return functools.reduce(jnp.logical_or, [place == v for v in FANOUT])
-
-
 def head_kernel(*refs):
-    @pl.when(is_head(lax.axis_index("vintage")))
+    @pl.when(lax.axis_index("vintage") == 0)
     def _():
         attr_body(*refs[:4], refs[5], refs[4], *refs[6:])
 
 
 def tail_kernel(*refs):
     ins, semb_head, attr_head, semb_out, attr_out = refs[:8], refs[8], refs[9], refs[10], refs[11]
-    head = is_head(lax.axis_index("vintage"))
+    head = lax.axis_index("vintage") == 0
 
     @pl.when(head)
     def _():
@@ -111,7 +105,7 @@
 
 def correl_kernel(mon, held, far3, far2, far1, out, base, result):
     half_lags = LAGS // 2
-    holder = is_head(lax.axis_index("vintage"))
+    holder = lax.rem(lax.axis_index("vintage"), 4) == 0
     zeros = jnp.zeros((half_lags, TRACES), jnp.float32)
     base[0:half_lags, :] = zeros
     base[half_lags + TIME_SAMPLES:, :] = zeros
@@ -220,19 +214,21 @@
     tile = amplitude[0]
     dips = (inline_slope.reshape(1, TRACES), crossline_slope.reshape(1, TRACES))
     vintages = lax.axis_size("vintage")
-    others = [v for v in range(vintages) if v not in FANOUT]
     along, across = ((0,), (1,), (2,)), ((0, 2, 4, 6), (1, 3, 5))
     sends = pair_sends(tile[:1], tile[-1:], "inline")
     outer = jnp.where(lax.axis_index("inline") == lax.axis_size("inline") - 1, tile[:1], tile[-1:])
     rows = swap((*sends, outer), "inline", range(vintages), along)
     sends = edge_columns((tile[:, :1], tile[:, -1:]), rows)
-    cols = swap(sends, "xline", FANOUT, across)
-    semb0, attr0 = attributes(head_kernel, "head", tile, *[rows[n] for n in (1, 2, 0)], *cols[::-1], *dips)
-    got = [lax.ppermute(attr0, "vintage", [(0, k)]) for k in (14, 2, 1)]
+    rows = [rows[n] for n in (1, 2, 0)]
+    cols = swap(sends, "xline", [0], across)
+    semb0, attr0 = attributes(head_kernel, "head", tile, *rows, *cols[::-1], *dips)
+    got = [lax.ppermute(attr0, "vintage", [(0, k)]) for k in (12, 4, 8)]
+    cols = swap(lax.optimization_barrier((*sends, attr0))[:2], "xline", range(1, vintages), across)
+    joined = lax.optimization_barrier((*got, *cols))
+    got, cols = joined[:3], joined[3:]
     held = jnp.where(lax.axis_index("vintage") == 0, attr0, got[0] + got[1] + got[2])
     far = [lax.ppermute(held, "vintage", [(s, to[n]) for s, to in FANOUT.items()]) for n in (2, 1, 0)]
-    cols = swap(lax.optimization_barrier((*sends, held))[:2], "xline", others, across)
-    semb, attr = attributes(tail_kernel, "tail", tile, *[rows[n] for n in (1, 2, 0)], *cols, *dips, semb0, attr0)
+    semb, attr = attributes(tail_kernel, "tail", tile, *rows, *cols, *dips, semb0, attr0)
     correl = correlate(attr, held, far)
     return (semb[None], correl[None])
 

time: 41.2 us -> 39.5 us (0.959)
  the two profiles are of different devices: /device:TPU:175 before, /device:TPU:186 now
where the time goes in v8:
time: 39.5 us; the launch traced here: 39.1 us
  starting transfers between devices  21.1 us (53%)
  waiting for transfers between devices  12.5 us (32%)
  Pallas kernels  2.73 us (7%)
  local copies, waits for them, and re-layouts  1.07 us (3%)
  between operations  0.87 us (2%)
  other arithmetic  0.84 us (2%)
    ppermute x7, starting transfers between devices, swap(): lax.ppermute(sends[n], ('vintage', axis), low + [(b, a) for a, b in low])  16.4 us
    ppermute x3, waiting for transfers between devices, per_device(): lax.ppermute(held, 'vintage', [(s, to[n]) for s, to in FANOUT.items()])  10.7 us
    ppermute x3, starting transfers between devices, per_device(): lax.ppermute(held, 'vintage', [(s, to[n]) for s, to in FANOUT.items()])  2.63 us
    ppermute x3, starting transfers between devices, per_device(): got = [lax.ppermute(attr0, 'vintage', [(0, k)]) for k in (12, 4, 8)]  2.01 us
    ppermute x7, waiting for transfers between devices, swap(): lax.ppermute(sends[n], ('vintage', axis), low + [(b, a) for a, b in low])  1.76 us
    pallas_call x2, Pallas kernels, attributes(): pl.pallas_call(kernel, out_shape=(jax.ShapeDtypeStruct((ROWS, COLS, TIME_...  1.53 us
    pallas_call x1, Pallas kernels, correlate(): pl.pallas_call(correl_kernel, out_shape=jax.ShapeDtypeStruct((ROWS, COLS,...  1.2 us
    slice x1, local copies, waits for them, and re-layouts, per_device(): sends = edge_columns((tile[:, :1], tile[:, -1:]), rows)  0.89 us
  transfers between devices with their start and end apart: 13, of which 3 were waited for; matrix products, arithmetic and copies ran while one was open for 3% of the time, Pallas kernels for 4%

profile of v8, /device:TPU:186, one launch (start us, length us, event | category | flops | bytes accessed | tf_op | source)
XLA Modules:
  0.0 39.1 jit_solution(10074817543188121741)
XLA Ops:
  0.6 0.0 copy-start
  0.6 0.8 %select_bitcast_fusion = (f32[1,16,256]{2,1,0:T(8,128)S(1)}, f32[1,16,256]{2,1,0:T(8,128)S(1)}, f32[1,16,256]{2,1,0:T(8,128)S(1)}) fusion(f32[1,8,16,256]{3,2,1,0:T(8,128)} %param.3, pred[]{:T(512)S(6)} %eq.13, pred[]{:T(512)S(6)} %eq.14), kind=kLoop, calls=%fused_computation.3 | loop fusion | flops 12288 | bytes 81922 | tf_op jit(solution)/shard_map/jit(_where)/select_n | solution.py:190
  1.4 1.9 %collective-permute-start.2 = (f32[1,16,256]{2,1,0:T(8,128)S(1)}, f32[1,16,256]{2,1,0:T(8,128)S(1)}, u32[]{:S(2)}, u32[]{:S(2)}) collective-permute-start(f32[1,16,256]{2,1,0:T(8,128)S(1)} %get-tuple-element.26), channel_id=1, source_target_pairs={{0,8},{32,40},{64,72},{96,104},{128,136},{160,168},{192,200},{224,... | collective-permute-start | bytes 49160 | tf_op jit(solution)/shard_map/ppermute | solution.py:198
  3.4 6.0 %collective-permute-start = (f32[1,16,256]{2,1,0:T(8,128)S(1)}, f32[1,16,256]{2,1,0:T(8,128)S(1)}, u32[]{:S(2)}, u32[]{:S(2)}) collective-permute-start(f32[1,16,256]{2,1,0:T(8,128)S(1)} %get-tuple-element.27), channel_id=1, source_target_pairs={{8,16},{40,48},{72,80},{104,112},{136,144},{168,176},{200,208},{23... | collective-permute-start | bytes 49160 | tf_op jit(solution)/shard_map/ppermute | solution.py:198
  9.4 0.7 %collective-permute-start.1 = (f32[1,16,256]{2,1,0:T(8,128)S(1)}, f32[1,16,256]{2,1,0:T(8,128)S(1)}, u32[]{:S(2)}, u32[]{:S(2)}) collective-permute-start(f32[1,16,256]{2,1,0:T(8,128)S(1)} %get-tuple-element.28), channel_id=1, source_target_pairs={{16,24},{48,56},{80,88},{112,120},{144,152},{176,184},{208,216},{2... | collective-permute-start | bytes 49160 | tf_op jit(solution)/shard_map/ppermute | solution.py:198
  10.1 0.9 %fusion = (f32[8,1,256]{2,1,0:T(1,128)S(1)}, f32[8,1,256]{2,1,0:T(1,128)S(1)}) fusion(f32[8,16,256]{2,1,0:T(8,128)} %bitcast.9), kind=kLoop, calls=%fused_computation.10 | loop fusion | bytes 32768 | tf_op jit(solution)/shard_map/slice | solution.py:221
  11.0 0.0 collective-permute-done.2.refs_3_
  11.0 0.1 collective-permute-done.refs_1_
  11.1 0.0 collective-permute-done.1.refs_2_
  11.1 0.0 copy-start.1
  11.2 0.0 copy-start.2
  11.2 0.7 %collective-permute-start.4 = (f32[10,1,256]{2,1,0:T(1,128)S(1)}, f32[10,1,256]{2,1,0:T(1,128)S(1)}, u32[]{:S(2)}, u32[]{:S(2)}) collective-permute-start(f32[10,1,256]{2,1,0:T(1,128)S(1)} %get-tuple-element.14), channel_id=1, source_target_pairs={{0,1},{2,3},{4,5},{6,7},{1,0},{3,2},{5,4},{7,6},{8,9},{10,11},{12,... | collective-permute-start | bytes 30728 | tf_op jit(solution)/shard_map/ppermute | solution.py:198
  11.9 0.7 %collective-permute-start.3 = (f32[10,1,256]{2,1,0:T(1,128)S(1)}, f32[10,1,256]{2,1,0:T(1,128)S(1)}, u32[]{:S(2)}, u32[]{:S(2)}) collective-permute-start(f32[10,1,256]{2,1,0:T(1,128)S(1)} %get-tuple-element.15), channel_id=1, source_target_pairs={{1,2},{3,4},{5,6},{2,1},{4,3},{6,5},{9,10},{11,12},{13,14},{10,9},... | collective-permute-start | bytes 30728 | tf_op jit(solution)/shard_map/ppermute | solution.py:198
  12.5 0.0 copy-done.1
  12.5 0.1 reshape.230.refs_6_
  12.6 0.0 copy-done.2
  12.6 0.1 reshape.231.refs_7_
  12.7 0.0 collective-permute-done.4.refs_5_
  12.7 0.0 collective-permute-done.3.refs_4_
  12.7 0.0 copy-done
  12.8 0.7 %collective-permute-start.7 = (f32[256,128]{1,0:T(8,128)S(1)}, f32[256,128]{1,0:T(8,128)S(1)}, u32[]{:S(2)}, u32[]{:S(2)}) collective-permute-start(f32[256,128]{1,0:T(8,128)S(1)} %get-tuple-element.13.refs_9_), channel_id=1, source_target_pairs={{0,256},{1,257},{2,258},{3,259},{4,260},{5,261},{6,262},{7,263},{8... | collective-permute-start | bytes 393224 | tf_op jit(solution)/shard_map/ppermute | solution.py:225
  13.4 0.7 %collective-permute-start.6 = (f32[256,128]{1,0:T(8,128)S(1)}, f32[256,128]{1,0:T(8,128)S(1)}, u32[]{:S(2)}, u32[]{:S(2)}) collective-permute-start(f32[256,128]{1,0:T(8,128)S(1)} %get-tuple-element.13.refs_9_), channel_id=1, source_target_pairs={{0,128},{1,129},{2,130},{3,131},{4,132},{5,133},{6,134},{7,135},{8... | collective-permute-start | bytes 393224 | tf_op jit(solution)/shard_map/ppermute | solution.py:225
  14.1 0.7 %collective-permute-start.5 = (f32[256,128]{1,0:T(8,128)S(1)}, f32[256,128]{1,0:T(8,128)S(1)}, u32[]{:S(2)}, u32[]{:S(2)}) collective-permute-start(f32[256,128]{1,0:T(8,128)S(1)} %get-tuple-element.13.refs_9_), channel_id=1, source_target_pairs={{0,384},{1,385},{2,386},{3,387},{4,388},{5,389},{6,390},{7,391},{8... | collective-permute-start | bytes 393224 | tf_op jit(solution)/shard_map/ppermute | solution.py:225
  14.8 2.4 %collective-permute-start.8 = (f32[10,1,256]{2,1,0:T(1,128)S(1)}, f32[10,1,256]{2,1,0:T(1,128)S(1)}, u32[]{:S(2)}, u32[]{:S(2)}) collective-permute-start(f32[10,1,256]{2,1,0:T(1,128)S(1)} %get-tuple-element.14), channel_id=1, source_target_pairs={{32,33},{34,35},{36,37},{38,39},{64,65},{66,67},{68,69},{70,71},{9... | collective-permute-start | bytes 30728 | tf_op jit(solution)/shard_map/ppermute | solution.py:198
  17.2 4.1 %collective-permute-start.9 = (f32[10,1,256]{2,1,0:T(1,128)S(1)}, f32[10,1,256]{2,1,0:T(1,128)S(1)}, u32[]{:S(2)}, u32[]{:S(2)}) collective-permute-start(f32[10,1,256]{2,1,0:T(1,128)S(1)} %get-tuple-element.15), channel_id=1, source_target_pairs={{33,34},{35,36},{37,38},{65,66},{67,68},{69,70},{97,98},{99,100},{... | collective-permute-start | bytes 30728 | tf_op jit(solution)/shard_map/ppermute | solution.py:198
  21.3 0.0 collective-permute-done.8.refs_4_
  21.3 1.6 %collective-permute-done.9.refs_5_ = f32[10,1,256]{2,1,0:T(1,128)S(1)} collective-permute-done((f32[10,1,256]{2,1,0:T(1,128)S(1)}, f32[10,1,256]{2,1,0:T(1,128)S(1)}, u32[]{:S(2)}, u32[]{:S(2)}) %collective-permute-start.9) | collective-permute-done | bytes 10272 | tf_op jit(solution)/shard_map/ppermute | solution.py:198
  22.9 0.0 collective-permute-done.7
  22.9 0.0 collective-permute-done.6
  22.9 0.0 collective-permute-done.5
  23.0 0.7 %collective-permute-start.12 = (f32[256,128]{1,0:T(8,128)S(1)}, f32[256,128]{1,0:T(8,128)S(1)}, u32[]{:S(2)}, u32[]{:S(2)}) collective-permute-start(f32[256,128]{1,0:T(8,128)S(1)} %add_select_fusion.held), channel_id=1, source_target_pairs={{0,96},{128,224},{256,352},{384,480},{1,97},{129,225},{257,353},{3... | collective-permute-start | bytes 393224 | tf_op jit(solution)/shard_map/ppermute | solution.py:230
  23.7 1.3 %collective-permute-start.11 = (f32[256,128]{1,0:T(8,128)S(1)}, f32[256,128]{1,0:T(8,128)S(1)}, u32[]{:S(2)}, u32[]{:S(2)}) collective-permute-start(f32[256,128]{1,0:T(8,128)S(1)} %add_select_fusion.held), channel_id=1, source_target_pairs={{0,64},{128,192},{256,320},{384,448},{1,65},{129,193},{257,321},{3... | collective-permute-start | bytes 393224 | tf_op jit(solution)/shard_map/ppermute | solution.py:230
  25.0 0.7 %collective-permute-start.10 = (f32[256,128]{1,0:T(8,128)S(1)}, f32[256,128]{1,0:T(8,128)S(1)}, u32[]{:S(2)}, u32[]{:S(2)}) collective-permute-start(f32[256,128]{1,0:T(8,128)S(1)} %add_select_fusion.held), channel_id=1, source_target_pairs={{0,32},{128,160},{256,288},{384,416},{1,33},{129,161},{257,289},{3... | collective-permute-start | bytes 393224 | tf_op jit(solution)/shard_map/ppermute | solution.py:230
  25.6 1.5 %tail.1 = (f32[8,16,256]{2,1,0:T(8,128)}, f32[256,128]{1,0:T(8,128)S(1)}) custom-call(f32[8,16,256]{2,1,0:T(8,128)S(1)} %bitcast.11, f32[1,16,256]{2,1,0:T(8,128)S(1)} %collective-permute-done.refs_1_, f32[1,16,256]{2,1,0:T(8,128)S(1)} %collective-permute-done.1.refs_2_, f32[1,16,256]{2,1,0:T(8,128)S(1)} %collective-permute-done.2.refs_3_, ...), custom_call_target="tpu_custom_call" | custom-call | tf_op jit(solution)/shard_map/tail/pallas_call | solution.py:153
  27.2 0.0 collective-permute-done.12.far1
  27.2 10.7 %collective-permute-done.11.far2 = f32[256,128]{1,0:T(8,128)S(1)} collective-permute-done((f32[256,128]{1,0:T(8,128)S(1)}, f32[256,128]{1,0:T(8,128)S(1)}, u32[]{:S(2)}, u32[]{:S(2)}) %collective-permute-start.11) | collective-permute-done | bytes 131104 | tf_op jit(solution)/shard_map/ppermute | solution.py:230
  37.9 0.0 collective-permute-done.10.far3
  37.9 1.2 %correlate.1 = f32[8,16,264]{2,1,0:T(8,128)} custom-call(f32[256,128]{1,0:T(8,128)S(1)} %get-tuple-element.20.mon, f32[256,128]{1,0:T(8,128)S(1)} %add_select_fusion.held, f32[256,128]{1,0:T(8,128)S(1)} %collective-permute-done.10.far3, f32[256,128]{1,0:T(8,128)S(1)} %collective-permute-done.11.far2, f32[256,128]{1,0:T(8,128)S(1)} %collective-permute-done.12.far1), custom_call_target="tpu_custom_call" | custom-call | tf_op jit(solution)/shard_map/correlate/pallas_call | solution.py:174
  (5 shorter events, 0.1 us)
Async XLA Ops:
  0.6 12.1 %copy-start = (f32[1,8,16,256]{3,2,1,0:T(8,128)S(1)}, f32[1,8,16,256]{3,2,1,0:T(8,128)}, u32[]{:S(2)}) copy-start(f32[1,8,16,256]{3,2,1,0:T(8,128)} %param.3) | copy-start | bytes 393220
  1.4 9.5 %collective-permute-start.2 = (f32[1,16,256]{2,1,0:T(8,128)S(1)}, f32[1,16,256]{2,1,0:T(8,128)S(1)}, u32[]{:S(2)}, u32[]{:S(2)}) collective-permute-start(f32[1,16,256]{2,1,0:T(8,128)S(1)} %get-tuple-element.26), channel_id=1, source_target_pairs={{0,8},{32,40},{64,72},{96,104},{128,136},{160,168},{192,200},{224,... | collective-permute-start | bytes 49160 | tf_op jit(solution)/shard_map/ppermute | solution.py:198
  3.4 7.8 %collective-permute-start = (f32[1,16,256]{2,1,0:T(8,128)S(1)}, f32[1,16,256]{2,1,0:T(8,128)S(1)}, u32[]{:S(2)}, u32[]{:S(2)}) collective-permute-start(f32[1,16,256]{2,1,0:T(8,128)S(1)} %get-tuple-element.27), channel_id=1, source_target_pairs={{8,16},{40,48},{72,80},{104,112},{136,144},{168,176},{200,208},{23... | collective-permute-start | bytes 49160 | tf_op jit(solution)/shard_map/ppermute | solution.py:198
  9.4 1.7 %collective-permute-start.1 = (f32[1,16,256]{2,1,0:T(8,128)S(1)}, f32[1,16,256]{2,1,0:T(8,128)S(1)}, u32[]{:S(2)}, u32[]{:S(2)}) collective-permute-start(f32[1,16,256]{2,1,0:T(8,128)S(1)} %get-tuple-element.28), channel_id=1, source_target_pairs={{16,24},{48,56},{80,88},{112,120},{144,152},{176,184},{208,216},{2... | collective-permute-start | bytes 49160 | tf_op jit(solution)/shard_map/ppermute | solution.py:198
  11.1 1.4 %copy-start.1 = (s32[1,8,16]{2,1,0:T(8,128)S(1)}, s32[1,8,16]{2,1,0:T(8,128)}, u32[]{:S(2)}) copy-start(s32[1,8,16]{2,1,0:T(8,128)} %param.4) | copy-start | bytes 1540
  11.2 1.4 %copy-start.2 = (s32[1,8,16]{2,1,0:T(8,128)S(1)}, s32[1,8,16]{2,1,0:T(8,128)}, u32[]{:S(2)}) copy-start(s32[1,8,16]{2,1,0:T(8,128)} %param.5) | copy-start | bytes 1540
  11.2 1.5 %collective-permute-start.4 = (f32[10,1,256]{2,1,0:T(1,128)S(1)}, f32[10,1,256]{2,1,0:T(1,128)S(1)}, u32[]{:S(2)}, u32[]{:S(2)}) collective-permute-start(f32[10,1,256]{2,1,0:T(1,128)S(1)} %get-tuple-element.14), channel_id=1, source_target_pairs={{0,1},{2,3},{4,5},{6,7},{1,0},{3,2},{5,4},{7,6},{8,9},{10,11},{12,... | collective-permute-start | bytes 30728 | tf_op jit(solution)/shard_map/ppermute | solution.py:198
  11.9 0.9 %collective-permute-start.3 = (f32[10,1,256]{2,1,0:T(1,128)S(1)}, f32[10,1,256]{2,1,0:T(1,128)S(1)}, u32[]{:S(2)}, u32[]{:S(2)}) collective-permute-start(f32[10,1,256]{2,1,0:T(1,128)S(1)} %get-tuple-element.15), channel_id=1, source_target_pairs={{1,2},{3,4},{5,6},{2,1},{4,3},{6,5},{9,10},{11,12},{13,14},{10,9},... | collective-permute-start | bytes 30728 | tf_op jit(solution)/shard_map/ppermute | solution.py:198
  12.8 10.2 %collective-permute-start.7 = (f32[256,128]{1,0:T(8,128)S(1)}, f32[256,128]{1,0:T(8,128)S(1)}, u32[]{:S(2)}, u32[]{:S(2)}) collective-permute-start(f32[256,128]{1,0:T(8,128)S(1)} %get-tuple-element.13.refs_9_), channel_id=1, source_target_pairs={{0,256},{1,257},{2,258},{3,259},{4,260},{5,261},{6,262},{7,263},{8... | collective-permute-start | bytes 393224 | tf_op jit(solution)/shard_map/ppermute | solution.py:225
  13.4 9.5 %collective-permute-start.6 = (f32[256,128]{1,0:T(8,128)S(1)}, f32[256,128]{1,0:T(8,128)S(1)}, u32[]{:S(2)}, u32[]{:S(2)}) collective-permute-start(f32[256,128]{1,0:T(8,128)S(1)} %get-tuple-element.13.refs_9_), channel_id=1, source_target_pairs={{0,128},{1,129},{2,130},{3,131},{4,132},{5,133},{6,134},{7,135},{8... | collective-permute-start | bytes 393224 | tf_op jit(solution)/shard_map/ppermute | solution.py:225
  14.1 8.8 %collective-permute-start.5 = (f32[256,128]{1,0:T(8,128)S(1)}, f32[256,128]{1,0:T(8,128)S(1)}, u32[]{:S(2)}, u32[]{:S(2)}) collective-permute-start(f32[256,128]{1,0:T(8,128)S(1)} %get-tuple-element.13.refs_9_), channel_id=1, source_target_pairs={{0,384},{1,385},{2,386},{3,387},{4,388},{5,389},{6,390},{7,391},{8... | collective-permute-start | bytes 393224 | tf_op jit(solution)/shard_map/ppermute | solution.py:225
  14.8 6.5 %collective-permute-start.8 = (f32[10,1,256]{2,1,0:T(1,128)S(1)}, f32[10,1,256]{2,1,0:T(1,128)S(1)}, u32[]{:S(2)}, u32[]{:S(2)}) collective-permute-start(f32[10,1,256]{2,1,0:T(1,128)S(1)} %get-tuple-element.14), channel_id=1, source_target_pairs={{32,33},{34,35},{36,37},{38,39},{64,65},{66,67},{68,69},{70,71},{9... | collective-permute-start | bytes 30728 | tf_op jit(solution)/shard_map/ppermute | solution.py:198
  17.2 5.7 %collective-permute-start.9 = (f32[10,1,256]{2,1,0:T(1,128)S(1)}, f32[10,1,256]{2,1,0:T(1,128)S(1)}, u32[]{:S(2)}, u32[]{:S(2)}) collective-permute-start(f32[10,1,256]{2,1,0:T(1,128)S(1)} %get-tuple-element.15), channel_id=1, source_target_pairs={{33,34},{35,36},{37,38},{65,66},{67,68},{69,70},{97,98},{99,100},{... | collective-permute-start | bytes 30728 | tf_op jit(solution)/shard_map/ppermute | solution.py:198
  23.0 4.2 %collective-permute-start.12 = (f32[256,128]{1,0:T(8,128)S(1)}, f32[256,128]{1,0:T(8,128)S(1)}, u32[]{:S(2)}, u32[]{:S(2)}) collective-permute-start(f32[256,128]{1,0:T(8,128)S(1)} %add_select_fusion.held), channel_id=1, source_target_pairs={{0,96},{128,224},{256,352},{384,480},{1,97},{129,225},{257,353},{3... | collective-permute-start | bytes 393224 | tf_op jit(solution)/shard_map/ppermute | solution.py:230
  23.7 14.2 %collective-permute-start.11 = (f32[256,128]{1,0:T(8,128)S(1)}, f32[256,128]{1,0:T(8,128)S(1)}, u32[]{:S(2)}, u32[]{:S(2)}) collective-permute-start(f32[256,128]{1,0:T(8,128)S(1)} %add_select_fusion.held), channel_id=1, source_target_pairs={{0,64},{128,192},{256,320},{384,448},{1,65},{129,193},{257,321},{3... | collective-permute-start | bytes 393224 | tf_op jit(solution)/shard_map/ppermute | solution.py:230
  25.0 12.9 %collective-permute-start.10 = (f32[256,128]{1,0:T(8,128)S(1)}, f32[256,128]{1,0:T(8,128)S(1)}, u32[]{:S(2)}, u32[]{:S(2)}) collective-permute-start(f32[256,128]{1,0:T(8,128)S(1)} %add_select_fusion.held), channel_id=1, source_target_pairs={{0,32},{128,160},{256,288},{384,416},{1,33},{129,161},{257,289},{3... | collective-permute-start | bytes 393224 | tf_op jit(solution)/shard_map/ppermute | solution.py:230

commit v9 on v8

--- a/solution.py
+++ b/solution.py
@@ -28,14 +28,15 @@
     return out
 
 
-def head_kernel(*refs):
+def head_kernel(tile, row_12, row_23, row_01, cols, dip_il, dip_xl, *rest):
     @pl.when(lax.axis_index("vintage") == 0)
     def _():
-        attr_body(*refs[:4], refs[5], refs[4], *refs[6:])
-
-
-def tail_kernel(*refs):
-    ins, semb_head, attr_head, semb_out, attr_out = refs[:8], refs[8], refs[9], refs[10], refs[11]
+        edges = cols[0:ROWS + 2], cols[ROWS + 2:]
+        attr_body(tile, row_12, row_23, row_01, edges, dip_il, dip_xl, *rest)
+
+
+def tail_kernel(tile, row_12, row_23, row_01, col_a, col_b, dip_il, dip_xl, semb_head, attr_head,
+                semb_out, attr_out, *scratch):
     head = lax.axis_index("vintage") == 0
 
     @pl.when(head)
@@ -45,19 +46,20 @@
 
     @pl.when(jnp.logical_not(head))
     def _():
-        attr_body(*ins, *refs[10:])
-
-
-def attr_body(tile, row_12, row_23, row_01, col_a, col_b, dip_il, dip_xl, semb_out, attr_out,
+        odd = lax.rem(lax.axis_index("xline"), 2) == 1
+        edges = jnp.where(odd, col_a[...], col_b[...]), jnp.where(odd, col_b[...], col_a[...])
+        attr_body(tile, row_12, row_23, row_01, edges, dip_il, dip_xl, semb_out, attr_out, *scratch)
+
+
+def attr_body(tile, row_12, row_23, row_01, edges, dip_il, dip_xl, semb_out, attr_out,
               rim, moved, inner, sums, three):
     odd_row = lax.rem(lax.axis_index("inline"), 2) == 1
-    odd_col = lax.rem(lax.axis_index("xline"), 2) == 1
     rim[1:ROWS + 1, 1:COLS + 1, :] = tile[...]
     row_a, row_b = row_01[0] + row_23[0], row_12[0]
     rim[0, 1:COLS + 1, :] = jnp.where(odd_row, row_a, row_b)
     rim[ROWS + 1, 1:COLS + 1, :] = jnp.where(odd_row, row_b, row_a)
-    rim[:, 0:1, :] = jnp.where(odd_col, col_a[...], col_b[...])
-    rim[:, COLS + 1:COLS + 2, :] = jnp.where(odd_col, col_b[...], col_a[...])
+    rim[:, 0:1, :] = edges[0]
+    rim[:, COLS + 1:COLS + 2, :] = edges[1]
     zeros = jnp.zeros((PAD, TRACES), jnp.float32)
     for a in STEPS:
         for b in STEPS:
@@ -203,27 +205,30 @@
     odd = lax.rem(lax.axis_index("inline"), 2) == 1
     row_a, row_b = rows[0] + rows[2], rows[1]
     above, below = jnp.where(odd, row_a, row_b), jnp.where(odd, row_b, row_a)
-    first, last = (
+    return [
         jnp.concatenate([above[:, j:j + 1], end, below[:, j:j + 1]], axis=0)
         for j, end in zip((0, COLS - 1), ends)
-    )
-    return pair_sends(first, last, "xline")
+    ]
 
 
 def per_device(amplitude, inline_slope, crossline_slope):
     tile = amplitude[0]
     dips = (inline_slope.reshape(1, TRACES), crossline_slope.reshape(1, TRACES))
-    vintages = lax.axis_size("vintage")
+    vintages, width = lax.axis_size("vintage"), lax.axis_size("xline")
     along, across = ((0,), (1,), (2,)), ((0, 2, 4, 6), (1, 3, 5))
     sends = pair_sends(tile[:1], tile[-1:], "inline")
     outer = jnp.where(lax.axis_index("inline") == lax.axis_size("inline") - 1, tile[:1], tile[-1:])
     rows = swap((*sends, outer), "inline", range(vintages), along)
-    sends = edge_columns((tile[:, :1], tile[:, -1:]), rows)
+    first, last = edge_columns((tile[:, :1], tile[:, -1:]), rows)
     rows = [rows[n] for n in (1, 2, 0)]
-    cols = swap(sends, "xline", [0], across)
-    semb0, attr0 = attributes(head_kernel, "head", tile, *rows, *cols[::-1], *dips)
+    both = "vintage", "xline"
+    left = lax.ppermute(last, both, [(x, width + x + 1) for x in range(width - 1)])
+    right = lax.ppermute(first, both, [(x + 1, width + x) for x in range(width - 1)])
+    cols = lax.ppermute(jnp.concatenate([left, right], axis=0), "vintage", [(1, 0)])
+    semb0, attr0 = attributes(head_kernel, "head", tile, *rows, cols, *dips)
     got = [lax.ppermute(attr0, "vintage", [(0, k)]) for k in (12, 4, 8)]
-    cols = swap(lax.optimization_barrier((*sends, attr0))[:2], "xline", range(1, vintages), across)
+    first, last = lax.optimization_barrier((first, last, attr0))[:2]
+    cols = swap(pair_sends(first, last, "xline"), "xline", range(1, vintages), across)
     joined = lax.optimization_barrier((*got, *cols))
     got, cols = joined[:3], joined[3:]
     held = jnp.where(lax.axis_index("vintage") == 0, attr0, got[0] + got[1] + got[2])

time: 39.5 us -> 38.1 us (0.965)
  the two profiles are of different devices: /device:TPU:186 before, /device:TPU:184 now
where the time goes in v9:
time: 38.1 us; the launch traced here: 37.5 us
  starting transfers between devices  22.2 us (58%)
  waiting for transfers between devices  9.19 us (24%)
  Pallas kernels  2.73 us (7%)
  local copies, waits for them, and re-layouts  1.73 us (5%)
  between operations  0.89 us (2%)
  other arithmetic  0.84 us (2%)
    ppermute x5, starting transfers between devices, swap(): lax.ppermute(sends[n], ('vintage', axis), low + [(b, a) for a, b in low])  15.5 us
    ppermute x3, waiting for transfers between devices, per_device(): lax.ppermute(held, 'vintage', [(s, to[n]) for s, to in FANOUT.items()])  7.42 us
    ppermute x3, starting transfers between devices, per_device(): lax.ppermute(held, 'vintage', [(s, to[n]) for s, to in FANOUT.items()])  2.63 us
    ppermute x3, starting transfers between devices, per_device(): got = [lax.ppermute(attr0, 'vintage', [(0, k)]) for k in (12, 4, 8)]  2.01 us
    ppermute x5, waiting for transfers between devices, swap(): lax.ppermute(sends[n], ('vintage', axis), low + [(b, a) for a, b in low])  1.76 us
    pallas_call x2, Pallas kernels, attributes(): pl.pallas_call(kernel, out_shape=(jax.ShapeDtypeStruct((ROWS, COLS, TIME_...  1.53 us
    pallas_call x1, Pallas kernels, correlate(): pl.pallas_call(correl_kernel, out_shape=jax.ShapeDtypeStruct((ROWS, COLS,...  1.2 us
    slice x1, local copies, waits for them, and re-layouts, per_device(): first, last = edge_columns((tile[:, :1], tile[:, -1:]), rows)  0.89 us
  transfers between devices with their start and end apart: 14, of which 3 were waited for; matrix products, arithmetic and copies ran while one was open for 3% of the time, Pallas kernels for 4%

profile of v9, /device:TPU:184, one launch (start us, length us, event | category | flops | bytes accessed | tf_op | source)
XLA Modules:
  0.0 37.5 jit_solution(15372731962984383874)
XLA Ops:
  0.6 0.7 %select_bitcast_fusion = (f32[1,16,256]{2,1,0:T(8,128)S(1)}, f32[1,16,256]{2,1,0:T(8,128)S(1)}, f32[1,16,256]{2,1,0:T(8,128)S(1)}) fusion(f32[1,8,16,256]{3,2,1,0:T(8,128)} %param.3, pred[]{:T(512)S(6)} %eq.13, pred[]{:T(512)S(6)} %eq.14), kind=kLoop, calls=%fused_computation.4 | loop fusion | flops 12288 | bytes 81922 | tf_op jit(solution)/shard_map/jit(_where)/select_n | solution.py:192
  1.4 0.0 copy-start
  1.4 2.0 %collective-permute-start.2 = (f32[1,16,256]{2,1,0:T(8,128)S(1)}, f32[1,16,256]{2,1,0:T(8,128)S(1)}, u32[]{:S(2)}, u32[]{:S(2)}) collective-permute-start(f32[1,16,256]{2,1,0:T(8,128)S(1)} %get-tuple-element.26), channel_id=1, source_target_pairs={{0,8},{32,40},{64,72},{96,104},{128,136},{160,168},{192,200},{224,... | collective-permute-start | bytes 49160 | tf_op jit(solution)/shard_map/ppermute | solution.py:200
  3.4 6.0 %collective-permute-start = (f32[1,16,256]{2,1,0:T(8,128)S(1)}, f32[1,16,256]{2,1,0:T(8,128)S(1)}, u32[]{:S(2)}, u32[]{:S(2)}) collective-permute-start(f32[1,16,256]{2,1,0:T(8,128)S(1)} %get-tuple-element.27), channel_id=1, source_target_pairs={{8,16},{40,48},{72,80},{104,112},{136,144},{168,176},{200,208},{23... | collective-permute-start | bytes 49160 | tf_op jit(solution)/shard_map/ppermute | solution.py:200
  9.5 0.7 %collective-permute-start.1 = (f32[1,16,256]{2,1,0:T(8,128)S(1)}, f32[1,16,256]{2,1,0:T(8,128)S(1)}, u32[]{:S(2)}, u32[]{:S(2)}) collective-permute-start(f32[1,16,256]{2,1,0:T(8,128)S(1)} %get-tuple-element.28), channel_id=1, source_target_pairs={{16,24},{48,56},{80,88},{112,120},{144,152},{176,184},{208,216},{2... | collective-permute-start | bytes 49160 | tf_op jit(solution)/shard_map/ppermute | solution.py:200
  10.1 0.9 %fusion = (f32[8,1,256]{2,1,0:T(1,128)S(1)}, f32[8,1,256]{2,1,0:T(1,128)S(1)}) fusion(f32[8,16,256]{2,1,0:T(8,128)} %bitcast.9), kind=kLoop, calls=%fused_computation.11 | loop fusion | bytes 32768 | tf_op jit(solution)/shard_map/slice | solution.py:222
  11.0 0.0 collective-permute-done.2.row_01
  11.1 0.1 collective-permute-done.row_12
  11.2 0.0 collective-permute-done.1.row_23
  11.2 0.7 %collective-permute-start.4 = (f32[10,1,256]{2,1,0:T(1,128)S(1)}, f32[10,1,256]{2,1,0:T(1,128)S(1)}, u32[]{:S(2)}, u32[]{:S(2)}) collective-permute-start(f32[10,1,256]{2,1,0:T(1,128)S(1)} %pad_maximum_fusion.2), channel_id=1, source_target_pairs={{1,32},{2,33},{3,34},{4,35},{5,36},{6,37},{7,38},{9,40},{10,41},{1... | collective-permute-start | bytes 30728 | tf_op jit(solution)/shard_map/ppermute | solution.py:226
  11.9 0.7 %collective-permute-start.3 = (f32[10,1,256]{2,1,0:T(1,128)S(1)}, f32[10,1,256]{2,1,0:T(1,128)S(1)}, u32[]{:S(2)}, u32[]{:S(2)}) collective-permute-start(f32[10,1,256]{2,1,0:T(1,128)S(1)} %pad_maximum_fusion.1), channel_id=1, source_target_pairs={{0,33},{1,34},{2,35},{3,36},{4,37},{5,38},{6,39},{8,41},{9,42},{10... | collective-permute-start | bytes 30728 | tf_op jit(solution)/shard_map/ppermute | solution.py:225
  12.6 0.0 collective-permute-done.4
  12.6 0.0 collective-permute-done.3
  12.6 0.7 %collective-permute-start.5 = (f32[20,1,256]{2,1,0:T(1,128)S(1)}, f32[20,1,256]{2,1,0:T(1,128)S(1)}, u32[]{:S(2)}, u32[]{:S(2)}) collective-permute-start(f32[20,1,256]{2,1,0:T(1,128)S(1)} %pad_maximum_fusion), channel_id=1, source_target_pairs={{32,0},{33,1},{34,2},{35,3},{36,4},{37,5},{38,6},{39,7},{40,8},{41... | collective-permute-start | bytes 61448 | tf_op jit(solution)/shard_map/ppermute | solution.py:227
  13.3 0.0 copy-start.1
  13.3 0.0 copy-start.2
  13.3 0.7 %copy-done.1 = s32[1,8,16]{2,1,0:T(8,128)S(1)} copy-done((s32[1,8,16]{2,1,0:T(8,128)S(1)}, s32[1,8,16]{2,1,0:T(8,128)}, u32[]{:S(2)}) %copy-start.1) | copy-done | bytes 536
  14.0 0.1 reshape.78.dip_il
  14.1 0.0 copy-done.2
  14.1 0.1 reshape.79.dip_xl
  14.2 0.0 collective-permute-done.5.cols
  14.2 0.0 copy-done
  14.2 0.7 %collective-permute-start.8 = (f32[256,128]{1,0:T(8,128)S(1)}, f32[256,128]{1,0:T(8,128)S(1)}, u32[]{:S(2)}, u32[]{:S(2)}) collective-permute-start(f32[256,128]{1,0:T(8,128)S(1)} %get-tuple-element.13.attr_head), channel_id=1, source_target_pairs={{0,256},{1,257},{2,258},{3,259},{4,260},{5,261},{6,262},{7,263},{8... | collective-permute-start | bytes 393224 | tf_op jit(solution)/shard_map/ppermute | solution.py:229
  14.9 0.7 %collective-permute-start.7 = (f32[256,128]{1,0:T(8,128)S(1)}, f32[256,128]{1,0:T(8,128)S(1)}, u32[]{:S(2)}, u32[]{:S(2)}) collective-permute-start(f32[256,128]{1,0:T(8,128)S(1)} %get-tuple-element.13.attr_head), channel_id=1, source_target_pairs={{0,128},{1,129},{2,130},{3,131},{4,132},{5,133},{6,134},{7,135},{8... | collective-permute-start | bytes 393224 | tf_op jit(solution)/shard_map/ppermute | solution.py:229
  15.6 0.7 %collective-permute-start.6 = (f32[256,128]{1,0:T(8,128)S(1)}, f32[256,128]{1,0:T(8,128)S(1)}, u32[]{:S(2)}, u32[]{:S(2)}) collective-permute-start(f32[256,128]{1,0:T(8,128)S(1)} %get-tuple-element.13.attr_head), channel_id=1, source_target_pairs={{0,384},{1,385},{2,386},{3,387},{4,388},{5,389},{6,390},{7,391},{8... | collective-permute-start | bytes 393224 | tf_op jit(solution)/shard_map/ppermute | solution.py:229
  16.3 0.7 %collective-permute-start.10 = (f32[10,1,256]{2,1,0:T(1,128)S(1)}, f32[10,1,256]{2,1,0:T(1,128)S(1)}, u32[]{:S(2)}, u32[]{:S(2)}) collective-permute-start(f32[10,1,256]{2,1,0:T(1,128)S(1)} %get-tuple-element.31), channel_id=1, source_target_pairs={{33,34},{35,36},{37,38},{65,66},{67,68},{69,70},{97,98},{99,100},{... | collective-permute-start | bytes 30728 | tf_op jit(solution)/shard_map/ppermute | solution.py:200
  16.9 6.1 %collective-permute-start.9 = (f32[10,1,256]{2,1,0:T(1,128)S(1)}, f32[10,1,256]{2,1,0:T(1,128)S(1)}, u32[]{:S(2)}, u32[]{:S(2)}) collective-permute-start(f32[10,1,256]{2,1,0:T(1,128)S(1)} %get-tuple-element.32), channel_id=1, source_target_pairs={{32,33},{34,35},{36,37},{38,39},{64,65},{66,67},{68,69},{70,71},{9... | collective-permute-start | bytes 30728 | tf_op jit(solution)/shard_map/ppermute | solution.py:200
  23.1 0.0 collective-permute-done.10.col_b
  23.1 1.6 %collective-permute-done.9.col_a = f32[10,1,256]{2,1,0:T(1,128)S(1)} collective-permute-done((f32[10,1,256]{2,1,0:T(1,128)S(1)}, f32[10,1,256]{2,1,0:T(1,128)S(1)}, u32[]{:S(2)}, u32[]{:S(2)}) %collective-permute-start.9) | collective-permute-done | bytes 10272 | tf_op jit(solution)/shard_map/ppermute | solution.py:200
  24.7 0.0 collective-permute-done.8
  24.7 0.0 collective-permute-done.7
  24.7 0.0 collective-permute-done.6
  24.8 0.7 %collective-permute-start.13 = (f32[256,128]{1,0:T(8,128)S(1)}, f32[256,128]{1,0:T(8,128)S(1)}, u32[]{:S(2)}, u32[]{:S(2)}) collective-permute-start(f32[256,128]{1,0:T(8,128)S(1)} %add_select_fusion.held), channel_id=1, source_target_pairs={{0,96},{128,224},{256,352},{384,480},{1,97},{129,225},{257,353},{3... | collective-permute-start | bytes 393224 | tf_op jit(solution)/shard_map/ppermute | solution.py:235
  25.4 1.3 %collective-permute-start.12 = (f32[256,128]{1,0:T(8,128)S(1)}, f32[256,128]{1,0:T(8,128)S(1)}, u32[]{:S(2)}, u32[]{:S(2)}) collective-permute-start(f32[256,128]{1,0:T(8,128)S(1)} %add_select_fusion.held), channel_id=1, source_target_pairs={{0,64},{128,192},{256,320},{384,448},{1,65},{129,193},{257,321},{3... | collective-permute-start | bytes 393224 | tf_op jit(solution)/shard_map/ppermute | solution.py:235
  26.7 0.7 %collective-permute-start.11 = (f32[256,128]{1,0:T(8,128)S(1)}, f32[256,128]{1,0:T(8,128)S(1)}, u32[]{:S(2)}, u32[]{:S(2)}) collective-permute-start(f32[256,128]{1,0:T(8,128)S(1)} %add_select_fusion.held), channel_id=1, source_target_pairs={{0,32},{128,160},{256,288},{384,416},{1,33},{129,161},{257,289},{3... | collective-permute-start | bytes 393224 | tf_op jit(solution)/shard_map/ppermute | solution.py:235
  27.4 1.5 %tail.1 = (f32[8,16,256]{2,1,0:T(8,128)}, f32[256,128]{1,0:T(8,128)S(1)}) custom-call(f32[8,16,256]{2,1,0:T(8,128)S(1)} %bitcast.11, f32[1,16,256]{2,1,0:T(8,128)S(1)} %collective-permute-done.row_12, f32[1,16,256]{2,1,0:T(8,128)S(1)} %collective-permute-done.1.row_23, f32[1,16,256]{2,1,0:T(8,128)S(1)} %collective-permute-done.2.row_01, ...), custom_call_target="tpu_custom_call" | custom-call | tf_op jit(solution)/shard_map/tail/pallas_call | solution.py:155
  28.9 0.0 collective-permute-done.13.far1
  28.9 7.4 %collective-permute-done.12.far2 = f32[256,128]{1,0:T(8,128)S(1)} collective-permute-done((f32[256,128]{1,0:T(8,128)S(1)}, f32[256,128]{1,0:T(8,128)S(1)}, u32[]{:S(2)}, u32[]{:S(2)}) %collective-permute-start.12) | collective-permute-done | bytes 131104 | tf_op jit(solution)/shard_map/ppermute | solution.py:235
  36.3 0.0 collective-permute-done.11.far3
  36.3 1.2 %correlate.1 = f32[8,16,264]{2,1,0:T(8,128)} custom-call(f32[256,128]{1,0:T(8,128)S(1)} %get-tuple-element.20.mon, f32[256,128]{1,0:T(8,128)S(1)} %add_select_fusion.held, f32[256,128]{1,0:T(8,128)S(1)} %collective-permute-done.11.far3, f32[256,128]{1,0:T(8,128)S(1)} %collective-permute-done.12.far2, f32[256,128]{1,0:T(8,128)S(1)} %collective-permute-done.13.far1), custom_call_target="tpu_custom_call" | custom-call | tf_op jit(solution)/shard_map/correlate/pallas_call | solution.py:176
  (8 shorter events, 0.1 us)
Async XLA Ops:
  1.4 12.8 %copy-start = (f32[1,8,16,256]{3,2,1,0:T(8,128)S(1)}, f32[1,8,16,256]{3,2,1,0:T(8,128)}, u32[]{:S(2)}) copy-start(f32[1,8,16,256]{3,2,1,0:T(8,128)} %param.3) | copy-start | bytes 393220
  1.4 9.7 %collective-permute-start.2 = (f32[1,16,256]{2,1,0:T(8,128)S(1)}, f32[1,16,256]{2,1,0:T(8,128)S(1)}, u32[]{:S(2)}, u32[]{:S(2)}) collective-permute-start(f32[1,16,256]{2,1,0:T(8,128)S(1)} %get-tuple-element.26), channel_id=1, source_target_pairs={{0,8},{32,40},{64,72},{96,104},{128,136},{160,168},{192,200},{224,... | collective-permute-start | bytes 49160 | tf_op jit(solution)/shard_map/ppermute | solution.py:200
  3.4 7.8 %collective-permute-start = (f32[1,16,256]{2,1,0:T(8,128)S(1)}, f32[1,16,256]{2,1,0:T(8,128)S(1)}, u32[]{:S(2)}, u32[]{:S(2)}) collective-permute-start(f32[1,16,256]{2,1,0:T(8,128)S(1)} %get-tuple-element.27), channel_id=1, source_target_pairs={{8,16},{40,48},{72,80},{104,112},{136,144},{168,176},{200,208},{23... | collective-permute-start | bytes 49160 | tf_op jit(solution)/shard_map/ppermute | solution.py:200
  9.5 1.7 %collective-permute-start.1 = (f32[1,16,256]{2,1,0:T(8,128)S(1)}, f32[1,16,256]{2,1,0:T(8,128)S(1)}, u32[]{:S(2)}, u32[]{:S(2)}) collective-permute-start(f32[1,16,256]{2,1,0:T(8,128)S(1)} %get-tuple-element.28), channel_id=1, source_target_pairs={{16,24},{48,56},{80,88},{112,120},{144,152},{176,184},{208,216},{2... | collective-permute-start | bytes 49160 | tf_op jit(solution)/shard_map/ppermute | solution.py:200
  11.2 1.4 %collective-permute-start.4 = (f32[10,1,256]{2,1,0:T(1,128)S(1)}, f32[10,1,256]{2,1,0:T(1,128)S(1)}, u32[]{:S(2)}, u32[]{:S(2)}) collective-permute-start(f32[10,1,256]{2,1,0:T(1,128)S(1)} %pad_maximum_fusion.2), channel_id=1, source_target_pairs={{1,32},{2,33},{3,34},{4,35},{5,36},{6,37},{7,38},{9,40},{10,41},{1... | collective-permute-start | bytes 30728 | tf_op jit(solution)/shard_map/ppermute | solution.py:226
  11.9 0.7 %collective-permute-start.3 = (f32[10,1,256]{2,1,0:T(1,128)S(1)}, f32[10,1,256]{2,1,0:T(1,128)S(1)}, u32[]{:S(2)}, u32[]{:S(2)}) collective-permute-start(f32[10,1,256]{2,1,0:T(1,128)S(1)} %pad_maximum_fusion.1), channel_id=1, source_target_pairs={{0,33},{1,34},{2,35},{3,36},{4,37},{5,38},{6,39},{8,41},{9,42},{10... | collective-permute-start | bytes 30728 | tf_op jit(solution)/shard_map/ppermute | solution.py:225
  12.6 1.5 %collective-permute-start.5 = (f32[20,1,256]{2,1,0:T(1,128)S(1)}, f32[20,1,256]{2,1,0:T(1,128)S(1)}, u32[]{:S(2)}, u32[]{:S(2)}) collective-permute-start(f32[20,1,256]{2,1,0:T(1,128)S(1)} %pad_maximum_fusion), channel_id=1, source_target_pairs={{32,0},{33,1},{34,2},{35,3},{36,4},{37,5},{38,6},{39,7},{40,8},{41... | collective-permute-start | bytes 61448 | tf_op jit(solution)/shard_map/ppermute | solution.py:227
  13.3 0.7 %copy-start.1 = (s32[1,8,16]{2,1,0:T(8,128)S(1)}, s32[1,8,16]{2,1,0:T(8,128)}, u32[]{:S(2)}) copy-start(s32[1,8,16]{2,1,0:T(8,128)} %param.4) | copy-start | bytes 1540
  13.3 0.8 %copy-start.2 = (s32[1,8,16]{2,1,0:T(8,128)S(1)}, s32[1,8,16]{2,1,0:T(8,128)}, u32[]{:S(2)}) copy-start(s32[1,8,16]{2,1,0:T(8,128)} %param.5) | copy-start | bytes 1540
  14.2 10.5 %collective-permute-start.8 = (f32[256,128]{1,0:T(8,128)S(1)}, f32[256,128]{1,0:T(8,128)S(1)}, u32[]{:S(2)}, u32[]{:S(2)}) collective-permute-start(f32[256,128]{1,0:T(8,128)S(1)} %get-tuple-element.13.attr_head), channel_id=1, source_target_pairs={{0,256},{1,257},{2,258},{3,259},{4,260},{5,261},{6,262},{7,263},{8... | collective-permute-start | bytes 393224 | tf_op jit(solution)/shard_map/ppermute | solution.py:229
  14.9 9.8 %collective-permute-start.7 = (f32[256,128]{1,0:T(8,128)S(1)}, f32[256,128]{1,0:T(8,128)S(1)}, u32[]{:S(2)}, u32[]{:S(2)}) collective-permute-start(f32[256,128]{1,0:T(8,128)S(1)} %get-tuple-element.13.attr_head), channel_id=1, source_target_pairs={{0,128},{1,129},{2,130},{3,131},{4,132},{5,133},{6,134},{7,135},{8... | collective-permute-start | bytes 393224 | tf_op jit(solution)/shard_map/ppermute | solution.py:229
  15.6 9.2 %collective-permute-start.6 = (f32[256,128]{1,0:T(8,128)S(1)}, f32[256,128]{1,0:T(8,128)S(1)}, u32[]{:S(2)}, u32[]{:S(2)}) collective-permute-start(f32[256,128]{1,0:T(8,128)S(1)} %get-tuple-element.13.attr_head), channel_id=1, source_target_pairs={{0,384},{1,385},{2,386},{3,387},{4,388},{5,389},{6,390},{7,391},{8... | collective-permute-start | bytes 393224 | tf_op jit(solution)/shard_map/ppermute | solution.py:229
  16.3 6.8 %collective-permute-start.10 = (f32[10,1,256]{2,1,0:T(1,128)S(1)}, f32[10,1,256]{2,1,0:T(1,128)S(1)}, u32[]{:S(2)}, u32[]{:S(2)}) collective-permute-start(f32[10,1,256]{2,1,0:T(1,128)S(1)} %get-tuple-element.31), channel_id=1, source_target_pairs={{33,34},{35,36},{37,38},{65,66},{67,68},{69,70},{97,98},{99,100},{... | collective-permute-start | bytes 30728 | tf_op jit(solution)/shard_map/ppermute | solution.py:200
  16.9 7.8 %collective-permute-start.9 = (f32[10,1,256]{2,1,0:T(1,128)S(1)}, f32[10,1,256]{2,1,0:T(1,128)S(1)}, u32[]{:S(2)}, u32[]{:S(2)}) collective-permute-start(f32[10,1,256]{2,1,0:T(1,128)S(1)} %get-tuple-element.32), channel_id=1, source_target_pairs={{32,33},{34,35},{36,37},{38,39},{64,65},{66,67},{68,69},{70,71},{9... | collective-permute-start | bytes 30728 | tf_op jit(solution)/shard_map/ppermute | solution.py:200
  24.8 4.2 %collective-permute-start.13 = (f32[256,128]{1,0:T(8,128)S(1)}, f32[256,128]{1,0:T(8,128)S(1)}, u32[]{:S(2)}, u32[]{:S(2)}) collective-permute-start(f32[256,128]{1,0:T(8,128)S(1)} %add_select_fusion.held), channel_id=1, source_target_pairs={{0,96},{128,224},{256,352},{384,480},{1,97},{129,225},{257,353},{3... | collective-permute-start | bytes 393224 | tf_op jit(solution)/shard_map/ppermute | solution.py:235
  25.4 10.9 %collective-permute-start.12 = (f32[256,128]{1,0:T(8,128)S(1)}, f32[256,128]{1,0:T(8,128)S(1)}, u32[]{:S(2)}, u32[]{:S(2)}) collective-permute-start(f32[256,128]{1,0:T(8,128)S(1)} %add_select_fusion.held), channel_id=1, source_target_pairs={{0,64},{128,192},{256,320},{384,448},{1,65},{129,193},{257,321},{3... | collective-permute-start | bytes 393224 | tf_op jit(solution)/shard_map/ppermute | solution.py:235
  26.7 9.6 %collective-permute-start.11 = (f32[256,128]{1,0:T(8,128)S(1)}, f32[256,128]{1,0:T(8,128)S(1)}, u32[]{:S(2)}, u32[]{:S(2)}) collective-permute-start(f32[256,128]{1,0:T(8,128)S(1)} %add_select_fusion.held), channel_id=1, source_target_pairs={{0,32},{128,160},{256,288},{384,416},{1,33},{129,161},{257,289},{3... | collective-permute-start | bytes 393224 | tf_op jit(solution)/shard_map/ppermute | solution.py:235

commit v10 on v9

--- a/solution.py
+++ b/solution.py
@@ -229,8 +229,8 @@
     got = [lax.ppermute(attr0, "vintage", [(0, k)]) for k in (12, 4, 8)]
     first, last = lax.optimization_barrier((first, last, attr0))[:2]
     cols = swap(pair_sends(first, last, "xline"), "xline", range(1, vintages), across)
-    joined = lax.optimization_barrier((*got, *cols))
-    got, cols = joined[:3], joined[3:]
+    *got, col_b = lax.optimization_barrier((*got, cols[1]))
+    cols = cols[0], col_b
     held = jnp.where(lax.axis_index("vintage") == 0, attr0, got[0] + got[1] + got[2])
     far = [lax.ppermute(held, "vintage", [(s, to[n]) for s, to in FANOUT.items()]) for n in (2, 1, 0)]
     semb, attr = attributes(tail_kernel, "tail", tile, *rows, *cols, *dips, semb0, attr0)

time: 38.1 us -> 42.1 us (1.10)
  the two profiles are of different devices: /device:TPU:184 before, /device:TPU:176 now
where the time goes in v10:
time: 42.1 us; the launch traced here: 41.6 us
  starting transfers between devices  20.8 us (49%)
  waiting for transfers between devices  14.6 us (35%)
  Pallas kernels  2.72 us (6%)
  local copies, waits for them, and re-layouts  1.73 us (4%)
  between operations  0.9 us (2%)
  other arithmetic  0.85 us (2%)
    ppermute x5, starting transfers between devices, swap(): lax.ppermute(sends[n], ('vintage', axis), low + [(b, a) for a, b in low])  12.3 us
    ppermute x3, waiting for transfers between devices, per_device(): got = [lax.ppermute(attr0, 'vintage', [(0, k)]) for k in (12, 4, 8)]  11.8 us
    ppermute x3, starting transfers between devices, per_device(): lax.ppermute(held, 'vintage', [(s, to[n]) for s, to in FANOUT.items()])  3.89 us
    ppermute x5, waiting for transfers between devices, swap(): lax.ppermute(sends[n], ('vintage', axis), low + [(b, a) for a, b in low])  2.81 us
    ppermute x3, starting transfers between devices, per_device(): got = [lax.ppermute(attr0, 'vintage', [(0, k)]) for k in (12, 4, 8)]  2.63 us
    pallas_call x2, Pallas kernels, attributes(): pl.pallas_call(kernel, out_shape=(jax.ShapeDtypeStruct((ROWS, COLS, TIME_...  1.51 us
    pallas_call x1, Pallas kernels, correlate(): pl.pallas_call(correl_kernel, out_shape=jax.ShapeDtypeStruct((ROWS, COLS,...  1.21 us
    slice x1, local copies, waits for them, and re-layouts, per_device(): first, last = edge_columns((tile[:, :1], tile[:, -1:]), rows)  0.89 us
  transfers between devices with their start and end apart: 14, of which 3 were waited for; matrix products, arithmetic and copies ran while one was open for 3% of the time, Pallas kernels for 4%

profile of v10, /device:TPU:176, one launch (start us, length us, event | category | flops | bytes accessed | tf_op | source)
XLA Modules:
  0.0 41.6 jit_solution(17758978192770571586)
XLA Ops:
  0.6 0.7 %select_bitcast_fusion = (f32[1,16,256]{2,1,0:T(8,128)S(1)}, f32[1,16,256]{2,1,0:T(8,128)S(1)}, f32[1,16,256]{2,1,0:T(8,128)S(1)}) fusion(f32[1,8,16,256]{3,2,1,0:T(8,128)} %param.3, pred[]{:T(512)S(6)} %eq.13, pred[]{:T(512)S(6)} %eq.14), kind=kLoop, calls=%fused_computation.4 | loop fusion | flops 12288 | bytes 81922 | tf_op jit(solution)/shard_map/jit(_where)/select_n | solution.py:192
  1.4 0.0 copy-start
  1.4 2.0 %collective-permute-start.2 = (f32[1,16,256]{2,1,0:T(8,128)S(1)}, f32[1,16,256]{2,1,0:T(8,128)S(1)}, u32[]{:S(2)}, u32[]{:S(2)}) collective-permute-start(f32[1,16,256]{2,1,0:T(8,128)S(1)} %get-tuple-element.24), channel_id=1, source_target_pairs={{0,8},{32,40},{64,72},{96,104},{128,136},{160,168},{192,200},{224,... | collective-permute-start | bytes 49160 | tf_op jit(solution)/shard_map/ppermute | solution.py:200
  3.4 6.0 %collective-permute-start = (f32[1,16,256]{2,1,0:T(8,128)S(1)}, f32[1,16,256]{2,1,0:T(8,128)S(1)}, u32[]{:S(2)}, u32[]{:S(2)}) collective-permute-start(f32[1,16,256]{2,1,0:T(8,128)S(1)} %get-tuple-element.25), channel_id=1, source_target_pairs={{8,16},{40,48},{72,80},{104,112},{136,144},{168,176},{200,208},{23... | collective-permute-start | bytes 49160 | tf_op jit(solution)/shard_map/ppermute | solution.py:200
  9.5 0.7 %collective-permute-start.1 = (f32[1,16,256]{2,1,0:T(8,128)S(1)}, f32[1,16,256]{2,1,0:T(8,128)S(1)}, u32[]{:S(2)}, u32[]{:S(2)}) collective-permute-start(f32[1,16,256]{2,1,0:T(8,128)S(1)} %get-tuple-element.26), channel_id=1, source_target_pairs={{16,24},{48,56},{80,88},{112,120},{144,152},{176,184},{208,216},{2... | collective-permute-start | bytes 49160 | tf_op jit(solution)/shard_map/ppermute | solution.py:200
  10.1 0.9 %fusion = (f32[8,1,256]{2,1,0:T(1,128)S(1)}, f32[8,1,256]{2,1,0:T(1,128)S(1)}) fusion(f32[8,16,256]{2,1,0:T(8,128)} %bitcast.9), kind=kLoop, calls=%fused_computation.11 | loop fusion | bytes 32768 | tf_op jit(solution)/shard_map/slice | solution.py:222
  11.0 0.0 collective-permute-done.2.row_01
  11.1 0.1 collective-permute-done.row_12
  11.2 0.0 collective-permute-done.1.row_23
  11.2 0.7 %collective-permute-start.4 = (f32[10,1,256]{2,1,0:T(1,128)S(1)}, f32[10,1,256]{2,1,0:T(1,128)S(1)}, u32[]{:S(2)}, u32[]{:S(2)}) collective-permute-start(f32[10,1,256]{2,1,0:T(1,128)S(1)} %pad_maximum_fusion.1), channel_id=1, source_target_pairs={{1,32},{2,33},{3,34},{4,35},{5,36},{6,37},{7,38},{9,40},{10,41},{1... | collective-permute-start | bytes 30728 | tf_op jit(solution)/shard_map/ppermute | solution.py:226
  11.9 0.7 %collective-permute-start.3 = (f32[10,1,256]{2,1,0:T(1,128)S(1)}, f32[10,1,256]{2,1,0:T(1,128)S(1)}, u32[]{:S(2)}, u32[]{:S(2)}) collective-permute-start(f32[10,1,256]{2,1,0:T(1,128)S(1)} %pad_maximum_fusion.2), channel_id=1, source_target_pairs={{0,33},{1,34},{2,35},{3,36},{4,37},{5,38},{6,39},{8,41},{9,42},{10... | collective-permute-start | bytes 30728 | tf_op jit(solution)/shard_map/ppermute | solution.py:225
  12.6 0.0 collective-permute-done.4
  12.6 0.0 collective-permute-done.3
  12.6 0.7 %collective-permute-start.5 = (f32[20,1,256]{2,1,0:T(1,128)S(1)}, f32[20,1,256]{2,1,0:T(1,128)S(1)}, u32[]{:S(2)}, u32[]{:S(2)}) collective-permute-start(f32[20,1,256]{2,1,0:T(1,128)S(1)} %pad_maximum_fusion), channel_id=1, source_target_pairs={{32,0},{33,1},{34,2},{35,3},{36,4},{37,5},{38,6},{39,7},{40,8},{41... | collective-permute-start | bytes 61448 | tf_op jit(solution)/shard_map/ppermute | solution.py:227
  13.3 0.0 copy-start.1
  13.3 0.0 copy-start.2
  13.3 0.7 %copy-done.1 = s32[1,8,16]{2,1,0:T(8,128)S(1)} copy-done((s32[1,8,16]{2,1,0:T(8,128)S(1)}, s32[1,8,16]{2,1,0:T(8,128)}, u32[]{:S(2)}) %copy-start.1) | copy-done | bytes 536
  14.0 0.1 reshape.78.dip_il
  14.1 0.0 copy-done.2
  14.1 0.1 reshape.79.dip_xl
  14.2 0.0 collective-permute-done.5.cols
  14.2 0.0 copy-done
  14.2 0.7 %collective-permute-start.9 = (f32[256,128]{1,0:T(8,128)S(1)}, f32[256,128]{1,0:T(8,128)S(1)}, u32[]{:S(2)}, u32[]{:S(2)}) collective-permute-start(f32[256,128]{1,0:T(8,128)S(1)} %get-tuple-element.12.attr_head), channel_id=1, source_target_pairs={{0,256},{1,257},{2,258},{3,259},{4,260},{5,261},{6,262},{7,263},{8... | collective-permute-start | bytes 393224 | tf_op jit(solution)/shard_map/ppermute | solution.py:229
  14.9 0.7 %collective-permute-start.8 = (f32[256,128]{1,0:T(8,128)S(1)}, f32[256,128]{1,0:T(8,128)S(1)}, u32[]{:S(2)}, u32[]{:S(2)}) collective-permute-start(f32[256,128]{1,0:T(8,128)S(1)} %get-tuple-element.12.attr_head), channel_id=1, source_target_pairs={{0,128},{1,129},{2,130},{3,131},{4,132},{5,133},{6,134},{7,135},{8... | collective-permute-start | bytes 393224 | tf_op jit(solution)/shard_map/ppermute | solution.py:229
  15.6 1.3 %collective-permute-start.7 = (f32[256,128]{1,0:T(8,128)S(1)}, f32[256,128]{1,0:T(8,128)S(1)}, u32[]{:S(2)}, u32[]{:S(2)}) collective-permute-start(f32[256,128]{1,0:T(8,128)S(1)} %get-tuple-element.12.attr_head), channel_id=1, source_target_pairs={{0,384},{1,385},{2,386},{3,387},{4,388},{5,389},{6,390},{7,391},{8... | collective-permute-start | bytes 393224 | tf_op jit(solution)/shard_map/ppermute | solution.py:229
  16.9 0.7 %collective-permute-start.10 = (f32[10,1,256]{2,1,0:T(1,128)S(1)}, f32[10,1,256]{2,1,0:T(1,128)S(1)}, u32[]{:S(2)}, u32[]{:S(2)}) collective-permute-start(f32[10,1,256]{2,1,0:T(1,128)S(1)} %get-tuple-element.29), channel_id=1, source_target_pairs={{33,34},{35,36},{37,38},{65,66},{67,68},{69,70},{97,98},{99,100},{... | collective-permute-start | bytes 30728 | tf_op jit(solution)/shard_map/ppermute | solution.py:200
  17.6 0.0 collective-permute-done.10.col_b
  17.6 0.0 collective-permute-done.9
  17.6 0.0 collective-permute-done.8
  17.6 11.7 %collective-permute-done.7 = f32[256,128]{1,0:T(8,128)S(1)} collective-permute-done((f32[256,128]{1,0:T(8,128)S(1)}, f32[256,128]{1,0:T(8,128)S(1)}, u32[]{:S(2)}, u32[]{:S(2)}) %collective-permute-start.7) | collective-permute-done | bytes 131104 | tf_op jit(solution)/shard_map/ppermute | solution.py:229
  29.4 1.3 %collective-permute-start.13 = (f32[256,128]{1,0:T(8,128)S(1)}, f32[256,128]{1,0:T(8,128)S(1)}, u32[]{:S(2)}, u32[]{:S(2)}) collective-permute-start(f32[256,128]{1,0:T(8,128)S(1)} %add_select_fusion.held), channel_id=1, source_target_pairs={{0,96},{128,224},{256,352},{384,480},{1,97},{129,225},{257,353},{3... | collective-permute-start | bytes 393224 | tf_op jit(solution)/shard_map/ppermute | solution.py:235
  30.7 1.3 %collective-permute-start.12 = (f32[256,128]{1,0:T(8,128)S(1)}, f32[256,128]{1,0:T(8,128)S(1)}, u32[]{:S(2)}, u32[]{:S(2)}) collective-permute-start(f32[256,128]{1,0:T(8,128)S(1)} %add_select_fusion.held), channel_id=1, source_target_pairs={{0,64},{128,192},{256,320},{384,448},{1,65},{129,193},{257,321},{3... | collective-permute-start | bytes 393224 | tf_op jit(solution)/shard_map/ppermute | solution.py:235
  32.0 1.3 %collective-permute-start.11 = (f32[256,128]{1,0:T(8,128)S(1)}, f32[256,128]{1,0:T(8,128)S(1)}, u32[]{:S(2)}, u32[]{:S(2)}) collective-permute-start(f32[256,128]{1,0:T(8,128)S(1)} %add_select_fusion.held), channel_id=1, source_target_pairs={{0,32},{128,160},{256,288},{384,416},{1,33},{129,161},{257,289},{3... | collective-permute-start | bytes 393224 | tf_op jit(solution)/shard_map/ppermute | solution.py:235
  33.3 2.9 %collective-permute-start.6 = (f32[10,1,256]{2,1,0:T(1,128)S(1)}, f32[10,1,256]{2,1,0:T(1,128)S(1)}, u32[]{:S(2)}, u32[]{:S(2)}) collective-permute-start(f32[10,1,256]{2,1,0:T(1,128)S(1)} %get-tuple-element.30), channel_id=1, source_target_pairs={{32,33},{34,35},{36,37},{38,39},{64,65},{66,67},{68,69},{70,71},{9... | collective-permute-start | bytes 30728 | tf_op jit(solution)/shard_map/ppermute | solution.py:200
  36.2 2.7 %collective-permute-done.6.col_a = f32[10,1,256]{2,1,0:T(1,128)S(1)} collective-permute-done((f32[10,1,256]{2,1,0:T(1,128)S(1)}, f32[10,1,256]{2,1,0:T(1,128)S(1)}, u32[]{:S(2)}, u32[]{:S(2)}) %collective-permute-start.6) | collective-permute-done | bytes 10272 | tf_op jit(solution)/shard_map/ppermute | solution.py:200
  38.9 1.5 %tail.1 = (f32[8,16,256]{2,1,0:T(8,128)}, f32[256,128]{1,0:T(8,128)S(1)}) custom-call(f32[8,16,256]{2,1,0:T(8,128)S(1)} %bitcast.11, f32[1,16,256]{2,1,0:T(8,128)S(1)} %collective-permute-done.row_12, f32[1,16,256]{2,1,0:T(8,128)S(1)} %collective-permute-done.1.row_23, f32[1,16,256]{2,1,0:T(8,128)S(1)} %collective-permute-done.2.row_01, ...), custom_call_target="tpu_custom_call" | custom-call | tf_op jit(solution)/shard_map/tail/pallas_call | solution.py:155
  40.3 0.0 collective-permute-done.13.far1
  40.4 0.0 collective-permute-done.12.far2
  40.4 0.0 collective-permute-done.11.far3
  40.4 1.2 %correlate.1 = f32[8,16,264]{2,1,0:T(8,128)} custom-call(f32[256,128]{1,0:T(8,128)S(1)} %get-tuple-element.18.mon, f32[256,128]{1,0:T(8,128)S(1)} %add_select_fusion.held, f32[256,128]{1,0:T(8,128)S(1)} %collective-permute-done.11.far3, f32[256,128]{1,0:T(8,128)S(1)} %collective-permute-done.12.far2, f32[256,128]{1,0:T(8,128)S(1)} %collective-permute-done.13.far1), custom_call_target="tpu_custom_call" | custom-call | tf_op jit(solution)/shard_map/correlate/pallas_call | solution.py:176
  (8 shorter events, 0.1 us)
Async XLA Ops:
  1.4 12.8 %copy-start = (f32[1,8,16,256]{3,2,1,0:T(8,128)S(1)}, f32[1,8,16,256]{3,2,1,0:T(8,128)}, u32[]{:S(2)}) copy-start(f32[1,8,16,256]{3,2,1,0:T(8,128)} %param.3) | copy-start | bytes 393220
  1.4 9.7 %collective-permute-start.2 = (f32[1,16,256]{2,1,0:T(8,128)S(1)}, f32[1,16,256]{2,1,0:T(8,128)S(1)}, u32[]{:S(2)}, u32[]{:S(2)}) collective-permute-start(f32[1,16,256]{2,1,0:T(8,128)S(1)} %get-tuple-element.24), channel_id=1, source_target_pairs={{0,8},{32,40},{64,72},{96,104},{128,136},{160,168},{192,200},{224,... | collective-permute-start | bytes 49160 | tf_op jit(solution)/shard_map/ppermute | solution.py:200
  3.4 7.8 %collective-permute-start = (f32[1,16,256]{2,1,0:T(8,128)S(1)}, f32[1,16,256]{2,1,0:T(8,128)S(1)}, u32[]{:S(2)}, u32[]{:S(2)}) collective-permute-start(f32[1,16,256]{2,1,0:T(8,128)S(1)} %get-tuple-element.25), channel_id=1, source_target_pairs={{8,16},{40,48},{72,80},{104,112},{136,144},{168,176},{200,208},{23... | collective-permute-start | bytes 49160 | tf_op jit(solution)/shard_map/ppermute | solution.py:200
  9.5 1.7 %collective-permute-start.1 = (f32[1,16,256]{2,1,0:T(8,128)S(1)}, f32[1,16,256]{2,1,0:T(8,128)S(1)}, u32[]{:S(2)}, u32[]{:S(2)}) collective-permute-start(f32[1,16,256]{2,1,0:T(8,128)S(1)} %get-tuple-element.26), channel_id=1, source_target_pairs={{16,24},{48,56},{80,88},{112,120},{144,152},{176,184},{208,216},{2... | collective-permute-start | bytes 49160 | tf_op jit(solution)/shard_map/ppermute | solution.py:200
  11.2 1.4 %collective-permute-start.4 = (f32[10,1,256]{2,1,0:T(1,128)S(1)}, f32[10,1,256]{2,1,0:T(1,128)S(1)}, u32[]{:S(2)}, u32[]{:S(2)}) collective-permute-start(f32[10,1,256]{2,1,0:T(1,128)S(1)} %pad_maximum_fusion.1), channel_id=1, source_target_pairs={{1,32},{2,33},{3,34},{4,35},{5,36},{6,37},{7,38},{9,40},{10,41},{1... | collective-permute-start | bytes 30728 | tf_op jit(solution)/shard_map/ppermute | solution.py:226
  11.9 0.7 %collective-permute-start.3 = (f32[10,1,256]{2,1,0:T(1,128)S(1)}, f32[10,1,256]{2,1,0:T(1,128)S(1)}, u32[]{:S(2)}, u32[]{:S(2)}) collective-permute-start(f32[10,1,256]{2,1,0:T(1,128)S(1)} %pad_maximum_fusion.2), channel_id=1, source_target_pairs={{0,33},{1,34},{2,35},{3,36},{4,37},{5,38},{6,39},{8,41},{9,42},{10... | collective-permute-start | bytes 30728 | tf_op jit(solution)/shard_map/ppermute | solution.py:225
  12.6 1.5 %collective-permute-start.5 = (f32[20,1,256]{2,1,0:T(1,128)S(1)}, f32[20,1,256]{2,1,0:T(1,128)S(1)}, u32[]{:S(2)}, u32[]{:S(2)}) collective-permute-start(f32[20,1,256]{2,1,0:T(1,128)S(1)} %pad_maximum_fusion), channel_id=1, source_target_pairs={{32,0},{33,1},{34,2},{35,3},{36,4},{37,5},{38,6},{39,7},{40,8},{41... | collective-permute-start | bytes 61448 | tf_op jit(solution)/shard_map/ppermute | solution.py:227
  13.3 0.7 %copy-start.1 = (s32[1,8,16]{2,1,0:T(8,128)S(1)}, s32[1,8,16]{2,1,0:T(8,128)}, u32[]{:S(2)}) copy-start(s32[1,8,16]{2,1,0:T(8,128)} %param.4) | copy-start | bytes 1540
  13.3 0.8 %copy-start.2 = (s32[1,8,16]{2,1,0:T(8,128)S(1)}, s32[1,8,16]{2,1,0:T(8,128)}, u32[]{:S(2)}) copy-start(s32[1,8,16]{2,1,0:T(8,128)} %param.5) | copy-start | bytes 1540
  14.2 3.4 %collective-permute-start.9 = (f32[256,128]{1,0:T(8,128)S(1)}, f32[256,128]{1,0:T(8,128)S(1)}, u32[]{:S(2)}, u32[]{:S(2)}) collective-permute-start(f32[256,128]{1,0:T(8,128)S(1)} %get-tuple-element.12.attr_head), channel_id=1, source_target_pairs={{0,256},{1,257},{2,258},{3,259},{4,260},{5,261},{6,262},{7,263},{8... | collective-permute-start | bytes 393224 | tf_op jit(solution)/shard_map/ppermute | solution.py:229
  14.9 2.7 %collective-permute-start.8 = (f32[256,128]{1,0:T(8,128)S(1)}, f32[256,128]{1,0:T(8,128)S(1)}, u32[]{:S(2)}, u32[]{:S(2)}) collective-permute-start(f32[256,128]{1,0:T(8,128)S(1)} %get-tuple-element.12.attr_head), channel_id=1, source_target_pairs={{0,128},{1,129},{2,130},{3,131},{4,132},{5,133},{6,134},{7,135},{8... | collective-permute-start | bytes 393224 | tf_op jit(solution)/shard_map/ppermute | solution.py:229
  15.6 13.8 %collective-permute-start.7 = (f32[256,128]{1,0:T(8,128)S(1)}, f32[256,128]{1,0:T(8,128)S(1)}, u32[]{:S(2)}, u32[]{:S(2)}) collective-permute-start(f32[256,128]{1,0:T(8,128)S(1)} %get-tuple-element.12.attr_head), channel_id=1, source_target_pairs={{0,384},{1,385},{2,386},{3,387},{4,388},{5,389},{6,390},{7,391},{8... | collective-permute-start | bytes 393224 | tf_op jit(solution)/shard_map/ppermute | solution.py:229
  16.9 0.7 %collective-permute-start.10 = (f32[10,1,256]{2,1,0:T(1,128)S(1)}, f32[10,1,256]{2,1,0:T(1,128)S(1)}, u32[]{:S(2)}, u32[]{:S(2)}) collective-permute-start(f32[10,1,256]{2,1,0:T(1,128)S(1)} %get-tuple-element.29), channel_id=1, source_target_pairs={{33,34},{35,36},{37,38},{65,66},{67,68},{69,70},{97,98},{99,100},{... | collective-permute-start | bytes 30728 | tf_op jit(solution)/shard_map/ppermute | solution.py:200
  29.4 11.0 %collective-permute-start.13 = (f32[256,128]{1,0:T(8,128)S(1)}, f32[256,128]{1,0:T(8,128)S(1)}, u32[]{:S(2)}, u32[]{:S(2)}) collective-permute-start(f32[256,128]{1,0:T(8,128)S(1)} %add_select_fusion.held), channel_id=1, source_target_pairs={{0,96},{128,224},{256,352},{384,480},{1,97},{129,225},{257,353},{3... | collective-permute-start | bytes 393224 | tf_op jit(solution)/shard_map/ppermute | solution.py:235
  30.7 9.7 %collective-permute-start.12 = (f32[256,128]{1,0:T(8,128)S(1)}, f32[256,128]{1,0:T(8,128)S(1)}, u32[]{:S(2)}, u32[]{:S(2)}) collective-permute-start(f32[256,128]{1,0:T(8,128)S(1)} %add_select_fusion.held), channel_id=1, source_target_pairs={{0,64},{128,192},{256,320},{384,448},{1,65},{129,193},{257,321},{3... | collective-permute-start | bytes 393224 | tf_op jit(solution)/shard_map/ppermute | solution.py:235
  32.0 8.4 %collective-permute-start.11 = (f32[256,128]{1,0:T(8,128)S(1)}, f32[256,128]{1,0:T(8,128)S(1)}, u32[]{:S(2)}, u32[]{:S(2)}) collective-permute-start(f32[256,128]{1,0:T(8,128)S(1)} %add_select_fusion.held), channel_id=1, source_target_pairs={{0,32},{128,160},{256,288},{384,416},{1,33},{129,161},{257,289},{3... | collective-permute-start | bytes 393224 | tf_op jit(solution)/shard_map/ppermute | solution.py:235
  33.3 5.6 %collective-permute-start.6 = (f32[10,1,256]{2,1,0:T(1,128)S(1)}, f32[10,1,256]{2,1,0:T(1,128)S(1)}, u32[]{:S(2)}, u32[]{:S(2)}) collective-permute-start(f32[10,1,256]{2,1,0:T(1,128)S(1)} %get-tuple-element.30), channel_id=1, source_target_pairs={{32,33},{34,35},{36,37},{38,39},{64,65},{66,67},{68,69},{70,71},{9... | collective-permute-start | bytes 30728 | tf_op jit(solution)/shard_map/ppermute | solution.py:200

commit v11 on v9

--- a/solution.py
+++ b/solution.py
@@ -226,7 +226,7 @@
     right = lax.ppermute(first, both, [(x + 1, width + x) for x in range(width - 1)])
     cols = lax.ppermute(jnp.concatenate([left, right], axis=0), "vintage", [(1, 0)])
     semb0, attr0 = attributes(head_kernel, "head", tile, *rows, cols, *dips)
-    got = [lax.ppermute(attr0, "vintage", [(0, k)]) for k in (12, 4, 8)]
+    got = [lax.ppermute(attr0, "vintage", [(0, k)]) for k in (8, 4, 12)]
     first, last = lax.optimization_barrier((first, last, attr0))[:2]
     cols = swap(pair_sends(first, last, "xline"), "xline", range(1, vintages), across)
     joined = lax.optimization_barrier((*got, *cols))

time: 38.1 us -> 38.4 us (level)
  the two profiles are of different devices: /device:TPU:184 before, /device:TPU:168 now
where the time goes in v11:
time: 38.4 us; the launch traced here: 37.9 us
  starting transfers between devices  22.2 us (58%)
  waiting for transfers between devices  9.52 us (25%)
  Pallas kernels  2.73 us (7%)
  local copies, waits for them, and re-layouts  1.73 us (5%)
  between operations  0.89 us (2%)
  other arithmetic  0.84 us (2%)
    ppermute x5, starting transfers between devices, swap(): lax.ppermute(sends[n], ('vintage', axis), low + [(b, a) for a, b in low])  15.5 us
    ppermute x3, waiting for transfers between devices, per_device(): lax.ppermute(held, 'vintage', [(s, to[n]) for s, to in FANOUT.items()])  7.74 us
    ppermute x3, starting transfers between devices, per_device(): lax.ppermute(held, 'vintage', [(s, to[n]) for s, to in FANOUT.items()])  2.63 us
    ppermute x3, starting transfers between devices, per_device(): got = [lax.ppermute(attr0, 'vintage', [(0, k)]) for k in (8, 4, 12)]  2.01 us
    ppermute x5, waiting for transfers between devices, swap(): lax.ppermute(sends[n], ('vintage', axis), low + [(b, a) for a, b in low])  1.76 us
    pallas_call x2, Pallas kernels, attributes(): pl.pallas_call(kernel, out_shape=(jax.ShapeDtypeStruct((ROWS, COLS, TIME_...  1.53 us
    pallas_call x1, Pallas kernels, correlate(): pl.pallas_call(correl_kernel, out_shape=jax.ShapeDtypeStruct((ROWS, COLS,...  1.2 us
    slice x1, local copies, waits for them, and re-layouts, per_device(): first, last = edge_columns((tile[:, :1], tile[:, -1:]), rows)  0.89 us
  transfers between devices with their start and end apart: 14, of which 3 were waited for; matrix products, arithmetic and copies ran while one was open for 3% of the time, Pallas kernels for 4%

profile of v11, /device:TPU:168, one launch (start us, length us, event | category | flops | bytes accessed | tf_op | source)
XLA Modules:
  0.0 37.9 jit_solution(11730646792989348510)
XLA Ops:
  0.6 0.7 %select_bitcast_fusion = (f32[1,16,256]{2,1,0:T(8,128)S(1)}, f32[1,16,256]{2,1,0:T(8,128)S(1)}, f32[1,16,256]{2,1,0:T(8,128)S(1)}) fusion(f32[1,8,16,256]{3,2,1,0:T(8,128)} %param.3, pred[]{:T(512)S(6)} %eq.13, pred[]{:T(512)S(6)} %eq.14), kind=kLoop, calls=%fused_computation.4 | loop fusion | flops 12288 | bytes 81922 | tf_op jit(solution)/shard_map/jit(_where)/select_n | solution.py:192
  1.4 0.0 copy-start
  1.4 2.0 %collective-permute-start.2 = (f32[1,16,256]{2,1,0:T(8,128)S(1)}, f32[1,16,256]{2,1,0:T(8,128)S(1)}, u32[]{:S(2)}, u32[]{:S(2)}) collective-permute-start(f32[1,16,256]{2,1,0:T(8,128)S(1)} %get-tuple-element.26), channel_id=1, source_target_pairs={{0,8},{32,40},{64,72},{96,104},{128,136},{160,168},{192,200},{224,... | collective-permute-start | bytes 49160 | tf_op jit(solution)/shard_map/ppermute | solution.py:200
  3.4 6.0 %collective-permute-start = (f32[1,16,256]{2,1,0:T(8,128)S(1)}, f32[1,16,256]{2,1,0:T(8,128)S(1)}, u32[]{:S(2)}, u32[]{:S(2)}) collective-permute-start(f32[1,16,256]{2,1,0:T(8,128)S(1)} %get-tuple-element.27), channel_id=1, source_target_pairs={{8,16},{40,48},{72,80},{104,112},{136,144},{168,176},{200,208},{23... | collective-permute-start | bytes 49160 | tf_op jit(solution)/shard_map/ppermute | solution.py:200
  9.5 0.7 %collective-permute-start.1 = (f32[1,16,256]{2,1,0:T(8,128)S(1)}, f32[1,16,256]{2,1,0:T(8,128)S(1)}, u32[]{:S(2)}, u32[]{:S(2)}) collective-permute-start(f32[1,16,256]{2,1,0:T(8,128)S(1)} %get-tuple-element.28), channel_id=1, source_target_pairs={{16,24},{48,56},{80,88},{112,120},{144,152},{176,184},{208,216},{2... | collective-permute-start | bytes 49160 | tf_op jit(solution)/shard_map/ppermute | solution.py:200
  10.1 0.9 %fusion = (f32[8,1,256]{2,1,0:T(1,128)S(1)}, f32[8,1,256]{2,1,0:T(1,128)S(1)}) fusion(f32[8,16,256]{2,1,0:T(8,128)} %bitcast.9), kind=kLoop, calls=%fused_computation.11 | loop fusion | bytes 32768 | tf_op jit(solution)/shard_map/slice | solution.py:222
  11.0 0.0 collective-permute-done.2.row_01
  11.1 0.1 collective-permute-done.row_12
  11.2 0.0 collective-permute-done.1.row_23
  11.2 0.7 %collective-permute-start.4 = (f32[10,1,256]{2,1,0:T(1,128)S(1)}, f32[10,1,256]{2,1,0:T(1,128)S(1)}, u32[]{:S(2)}, u32[]{:S(2)}) collective-permute-start(f32[10,1,256]{2,1,0:T(1,128)S(1)} %pad_maximum_fusion.2), channel_id=1, source_target_pairs={{1,32},{2,33},{3,34},{4,35},{5,36},{6,37},{7,38},{9,40},{10,41},{1... | collective-permute-start | bytes 30728 | tf_op jit(solution)/shard_map/ppermute | solution.py:226
  11.9 0.7 %collective-permute-start.3 = (f32[10,1,256]{2,1,0:T(1,128)S(1)}, f32[10,1,256]{2,1,0:T(1,128)S(1)}, u32[]{:S(2)}, u32[]{:S(2)}) collective-permute-start(f32[10,1,256]{2,1,0:T(1,128)S(1)} %pad_maximum_fusion.1), channel_id=1, source_target_pairs={{0,33},{1,34},{2,35},{3,36},{4,37},{5,38},{6,39},{8,41},{9,42},{10... | collective-permute-start | bytes 30728 | tf_op jit(solution)/shard_map/ppermute | solution.py:225
  12.6 0.0 collective-permute-done.4
  12.6 0.0 collective-permute-done.3
  12.6 0.7 %collective-permute-start.5 = (f32[20,1,256]{2,1,0:T(1,128)S(1)}, f32[20,1,256]{2,1,0:T(1,128)S(1)}, u32[]{:S(2)}, u32[]{:S(2)}) collective-permute-start(f32[20,1,256]{2,1,0:T(1,128)S(1)} %pad_maximum_fusion), channel_id=1, source_target_pairs={{32,0},{33,1},{34,2},{35,3},{36,4},{37,5},{38,6},{39,7},{40,8},{41... | collective-permute-start | bytes 61448 | tf_op jit(solution)/shard_map/ppermute | solution.py:227
  13.3 0.0 copy-start.1
  13.3 0.0 copy-start.2
  13.3 0.7 %copy-done.1 = s32[1,8,16]{2,1,0:T(8,128)S(1)} copy-done((s32[1,8,16]{2,1,0:T(8,128)S(1)}, s32[1,8,16]{2,1,0:T(8,128)}, u32[]{:S(2)}) %copy-start.1) | copy-done | bytes 536
  14.0 0.1 reshape.78.dip_il
  14.1 0.0 copy-done.2
  14.1 0.1 reshape.79.dip_xl
  14.2 0.0 collective-permute-done.5.cols
  14.2 0.0 copy-done
  14.2 0.7 %collective-permute-start.8 = (f32[256,128]{1,0:T(8,128)S(1)}, f32[256,128]{1,0:T(8,128)S(1)}, u32[]{:S(2)}, u32[]{:S(2)}) collective-permute-start(f32[256,128]{1,0:T(8,128)S(1)} %get-tuple-element.13.attr_head), channel_id=1, source_target_pairs={{0,384},{1,385},{2,386},{3,387},{4,388},{5,389},{6,390},{7,391},{8... | collective-permute-start | bytes 393224 | tf_op jit(solution)/shard_map/ppermute | solution.py:229
  14.9 0.7 %collective-permute-start.7 = (f32[256,128]{1,0:T(8,128)S(1)}, f32[256,128]{1,0:T(8,128)S(1)}, u32[]{:S(2)}, u32[]{:S(2)}) collective-permute-start(f32[256,128]{1,0:T(8,128)S(1)} %get-tuple-element.13.attr_head), channel_id=1, source_target_pairs={{0,128},{1,129},{2,130},{3,131},{4,132},{5,133},{6,134},{7,135},{8... | collective-permute-start | bytes 393224 | tf_op jit(solution)/shard_map/ppermute | solution.py:229
  15.6 0.7 %collective-permute-start.6 = (f32[256,128]{1,0:T(8,128)S(1)}, f32[256,128]{1,0:T(8,128)S(1)}, u32[]{:S(2)}, u32[]{:S(2)}) collective-permute-start(f32[256,128]{1,0:T(8,128)S(1)} %get-tuple-element.13.attr_head), channel_id=1, source_target_pairs={{0,256},{1,257},{2,258},{3,259},{4,260},{5,261},{6,262},{7,263},{8... | collective-permute-start | bytes 393224 | tf_op jit(solution)/shard_map/ppermute | solution.py:229
  16.3 0.7 %collective-permute-start.10 = (f32[10,1,256]{2,1,0:T(1,128)S(1)}, f32[10,1,256]{2,1,0:T(1,128)S(1)}, u32[]{:S(2)}, u32[]{:S(2)}) collective-permute-start(f32[10,1,256]{2,1,0:T(1,128)S(1)} %get-tuple-element.31), channel_id=1, source_target_pairs={{33,34},{35,36},{37,38},{65,66},{67,68},{69,70},{97,98},{99,100},{... | collective-permute-start | bytes 30728 | tf_op jit(solution)/shard_map/ppermute | solution.py:200
  16.9 6.1 %collective-permute-start.9 = (f32[10,1,256]{2,1,0:T(1,128)S(1)}, f32[10,1,256]{2,1,0:T(1,128)S(1)}, u32[]{:S(2)}, u32[]{:S(2)}) collective-permute-start(f32[10,1,256]{2,1,0:T(1,128)S(1)} %get-tuple-element.32), channel_id=1, source_target_pairs={{32,33},{34,35},{36,37},{38,39},{64,65},{66,67},{68,69},{70,71},{9... | collective-permute-start | bytes 30728 | tf_op jit(solution)/shard_map/ppermute | solution.py:200
  23.1 0.0 collective-permute-done.10.col_b
  23.1 1.6 %collective-permute-done.9.col_a = f32[10,1,256]{2,1,0:T(1,128)S(1)} collective-permute-done((f32[10,1,256]{2,1,0:T(1,128)S(1)}, f32[10,1,256]{2,1,0:T(1,128)S(1)}, u32[]{:S(2)}, u32[]{:S(2)}) %collective-permute-start.9) | collective-permute-done | bytes 10272 | tf_op jit(solution)/shard_map/ppermute | solution.py:200
  24.7 0.0 collective-permute-done.8
  24.7 0.0 collective-permute-done.7
  24.7 0.0 collective-permute-done.6
  24.8 0.7 %collective-permute-start.13 = (f32[256,128]{1,0:T(8,128)S(1)}, f32[256,128]{1,0:T(8,128)S(1)}, u32[]{:S(2)}, u32[]{:S(2)}) collective-permute-start(f32[256,128]{1,0:T(8,128)S(1)} %add_select_fusion.held), channel_id=1, source_target_pairs={{0,96},{128,224},{256,352},{384,480},{1,97},{129,225},{257,353},{3... | collective-permute-start | bytes 393224 | tf_op jit(solution)/shard_map/ppermute | solution.py:235
  25.4 1.3 %collective-permute-start.12 = (f32[256,128]{1,0:T(8,128)S(1)}, f32[256,128]{1,0:T(8,128)S(1)}, u32[]{:S(2)}, u32[]{:S(2)}) collective-permute-start(f32[256,128]{1,0:T(8,128)S(1)} %add_select_fusion.held), channel_id=1, source_target_pairs={{0,64},{128,192},{256,320},{384,448},{1,65},{129,193},{257,321},{3... | collective-permute-start | bytes 393224 | tf_op jit(solution)/shard_map/ppermute | solution.py:235
  26.7 0.7 %collective-permute-start.11 = (f32[256,128]{1,0:T(8,128)S(1)}, f32[256,128]{1,0:T(8,128)S(1)}, u32[]{:S(2)}, u32[]{:S(2)}) collective-permute-start(f32[256,128]{1,0:T(8,128)S(1)} %add_select_fusion.held), channel_id=1, source_target_pairs={{0,32},{128,160},{256,288},{384,416},{1,33},{129,161},{257,289},{3... | collective-permute-start | bytes 393224 | tf_op jit(solution)/shard_map/ppermute | solution.py:235
  27.4 1.5 %tail.1 = (f32[8,16,256]{2,1,0:T(8,128)}, f32[256,128]{1,0:T(8,128)S(1)}) custom-call(f32[8,16,256]{2,1,0:T(8,128)S(1)} %bitcast.11, f32[1,16,256]{2,1,0:T(8,128)S(1)} %collective-permute-done.row_12, f32[1,16,256]{2,1,0:T(8,128)S(1)} %collective-permute-done.1.row_23, f32[1,16,256]{2,1,0:T(8,128)S(1)} %collective-permute-done.2.row_01, ...), custom_call_target="tpu_custom_call" | custom-call | tf_op jit(solution)/shard_map/tail/pallas_call | solution.py:155
  28.9 0.0 collective-permute-done.13.far1
  28.9 7.7 %collective-permute-done.12.far2 = f32[256,128]{1,0:T(8,128)S(1)} collective-permute-done((f32[256,128]{1,0:T(8,128)S(1)}, f32[256,128]{1,0:T(8,128)S(1)}, u32[]{:S(2)}, u32[]{:S(2)}) %collective-permute-start.12) | collective-permute-done | bytes 131104 | tf_op jit(solution)/shard_map/ppermute | solution.py:235
  36.7 0.0 collective-permute-done.11.far3
  36.7 1.2 %correlate.1 = f32[8,16,264]{2,1,0:T(8,128)} custom-call(f32[256,128]{1,0:T(8,128)S(1)} %get-tuple-element.20.mon, f32[256,128]{1,0:T(8,128)S(1)} %add_select_fusion.held, f32[256,128]{1,0:T(8,128)S(1)} %collective-permute-done.11.far3, f32[256,128]{1,0:T(8,128)S(1)} %collective-permute-done.12.far2, f32[256,128]{1,0:T(8,128)S(1)} %collective-permute-done.13.far1), custom_call_target="tpu_custom_call" | custom-call | tf_op jit(solution)/shard_map/correlate/pallas_call | solution.py:176
  (8 shorter events, 0.1 us)
Async XLA Ops:
  1.4 12.8 %copy-start = (f32[1,8,16,256]{3,2,1,0:T(8,128)S(1)}, f32[1,8,16,256]{3,2,1,0:T(8,128)}, u32[]{:S(2)}) copy-start(f32[1,8,16,256]{3,2,1,0:T(8,128)} %param.3) | copy-start | bytes 393220
  1.4 9.7 %collective-permute-start.2 = (f32[1,16,256]{2,1,0:T(8,128)S(1)}, f32[1,16,256]{2,1,0:T(8,128)S(1)}, u32[]{:S(2)}, u32[]{:S(2)}) collective-permute-start(f32[1,16,256]{2,1,0:T(8,128)S(1)} %get-tuple-element.26), channel_id=1, source_target_pairs={{0,8},{32,40},{64,72},{96,104},{128,136},{160,168},{192,200},{224,... | collective-permute-start | bytes 49160 | tf_op jit(solution)/shard_map/ppermute | solution.py:200
  3.4 7.8 %collective-permute-start = (f32[1,16,256]{2,1,0:T(8,128)S(1)}, f32[1,16,256]{2,1,0:T(8,128)S(1)}, u32[]{:S(2)}, u32[]{:S(2)}) collective-permute-start(f32[1,16,256]{2,1,0:T(8,128)S(1)} %get-tuple-element.27), channel_id=1, source_target_pairs={{8,16},{40,48},{72,80},{104,112},{136,144},{168,176},{200,208},{23... | collective-permute-start | bytes 49160 | tf_op jit(solution)/shard_map/ppermute | solution.py:200
  9.5 1.7 %collective-permute-start.1 = (f32[1,16,256]{2,1,0:T(8,128)S(1)}, f32[1,16,256]{2,1,0:T(8,128)S(1)}, u32[]{:S(2)}, u32[]{:S(2)}) collective-permute-start(f32[1,16,256]{2,1,0:T(8,128)S(1)} %get-tuple-element.28), channel_id=1, source_target_pairs={{16,24},{48,56},{80,88},{112,120},{144,152},{176,184},{208,216},{2... | collective-permute-start | bytes 49160 | tf_op jit(solution)/shard_map/ppermute | solution.py:200
  11.2 1.4 %collective-permute-start.4 = (f32[10,1,256]{2,1,0:T(1,128)S(1)}, f32[10,1,256]{2,1,0:T(1,128)S(1)}, u32[]{:S(2)}, u32[]{:S(2)}) collective-permute-start(f32[10,1,256]{2,1,0:T(1,128)S(1)} %pad_maximum_fusion.2), channel_id=1, source_target_pairs={{1,32},{2,33},{3,34},{4,35},{5,36},{6,37},{7,38},{9,40},{10,41},{1... | collective-permute-start | bytes 30728 | tf_op jit(solution)/shard_map/ppermute | solution.py:226
  11.9 0.7 %collective-permute-start.3 = (f32[10,1,256]{2,1,0:T(1,128)S(1)}, f32[10,1,256]{2,1,0:T(1,128)S(1)}, u32[]{:S(2)}, u32[]{:S(2)}) collective-permute-start(f32[10,1,256]{2,1,0:T(1,128)S(1)} %pad_maximum_fusion.1), channel_id=1, source_target_pairs={{0,33},{1,34},{2,35},{3,36},{4,37},{5,38},{6,39},{8,41},{9,42},{10... | collective-permute-start | bytes 30728 | tf_op jit(solution)/shard_map/ppermute | solution.py:225
  12.6 1.5 %collective-permute-start.5 = (f32[20,1,256]{2,1,0:T(1,128)S(1)}, f32[20,1,256]{2,1,0:T(1,128)S(1)}, u32[]{:S(2)}, u32[]{:S(2)}) collective-permute-start(f32[20,1,256]{2,1,0:T(1,128)S(1)} %pad_maximum_fusion), channel_id=1, source_target_pairs={{32,0},{33,1},{34,2},{35,3},{36,4},{37,5},{38,6},{39,7},{40,8},{41... | collective-permute-start | bytes 61448 | tf_op jit(solution)/shard_map/ppermute | solution.py:227
  13.3 0.7 %copy-start.1 = (s32[1,8,16]{2,1,0:T(8,128)S(1)}, s32[1,8,16]{2,1,0:T(8,128)}, u32[]{:S(2)}) copy-start(s32[1,8,16]{2,1,0:T(8,128)} %param.4) | copy-start | bytes 1540
  13.3 0.8 %copy-start.2 = (s32[1,8,16]{2,1,0:T(8,128)S(1)}, s32[1,8,16]{2,1,0:T(8,128)}, u32[]{:S(2)}) copy-start(s32[1,8,16]{2,1,0:T(8,128)} %param.5) | copy-start | bytes 1540
  14.2 10.5 %collective-permute-start.8 = (f32[256,128]{1,0:T(8,128)S(1)}, f32[256,128]{1,0:T(8,128)S(1)}, u32[]{:S(2)}, u32[]{:S(2)}) collective-permute-start(f32[256,128]{1,0:T(8,128)S(1)} %get-tuple-element.13.attr_head), channel_id=1, source_target_pairs={{0,384},{1,385},{2,386},{3,387},{4,388},{5,389},{6,390},{7,391},{8... | collective-permute-start | bytes 393224 | tf_op jit(solution)/shard_map/ppermute | solution.py:229
  14.9 9.8 %collective-permute-start.7 = (f32[256,128]{1,0:T(8,128)S(1)}, f32[256,128]{1,0:T(8,128)S(1)}, u32[]{:S(2)}, u32[]{:S(2)}) collective-permute-start(f32[256,128]{1,0:T(8,128)S(1)} %get-tuple-element.13.attr_head), channel_id=1, source_target_pairs={{0,128},{1,129},{2,130},{3,131},{4,132},{5,133},{6,134},{7,135},{8... | collective-permute-start | bytes 393224 | tf_op jit(solution)/shard_map/ppermute | solution.py:229
  15.6 9.2 %collective-permute-start.6 = (f32[256,128]{1,0:T(8,128)S(1)}, f32[256,128]{1,0:T(8,128)S(1)}, u32[]{:S(2)}, u32[]{:S(2)}) collective-permute-start(f32[256,128]{1,0:T(8,128)S(1)} %get-tuple-element.13.attr_head), channel_id=1, source_target_pairs={{0,256},{1,257},{2,258},{3,259},{4,260},{5,261},{6,262},{7,263},{8... | collective-permute-start | bytes 393224 | tf_op jit(solution)/shard_map/ppermute | solution.py:229
  16.3 6.8 %collective-permute-start.10 = (f32[10,1,256]{2,1,0:T(1,128)S(1)}, f32[10,1,256]{2,1,0:T(1,128)S(1)}, u32[]{:S(2)}, u32[]{:S(2)}) collective-permute-start(f32[10,1,256]{2,1,0:T(1,128)S(1)} %get-tuple-element.31), channel_id=1, source_target_pairs={{33,34},{35,36},{37,38},{65,66},{67,68},{69,70},{97,98},{99,100},{... | collective-permute-start | bytes 30728 | tf_op jit(solution)/shard_map/ppermute | solution.py:200
  16.9 7.8 %collective-permute-start.9 = (f32[10,1,256]{2,1,0:T(1,128)S(1)}, f32[10,1,256]{2,1,0:T(1,128)S(1)}, u32[]{:S(2)}, u32[]{:S(2)}) collective-permute-start(f32[10,1,256]{2,1,0:T(1,128)S(1)} %get-tuple-element.32), channel_id=1, source_target_pairs={{32,33},{34,35},{36,37},{38,39},{64,65},{66,67},{68,69},{70,71},{9... | collective-permute-start | bytes 30728 | tf_op jit(solution)/shard_map/ppermute | solution.py:200
  24.8 4.2 %collective-permute-start.13 = (f32[256,128]{1,0:T(8,128)S(1)}, f32[256,128]{1,0:T(8,128)S(1)}, u32[]{:S(2)}, u32[]{:S(2)}) collective-permute-start(f32[256,128]{1,0:T(8,128)S(1)} %add_select_fusion.held), channel_id=1, source_target_pairs={{0,96},{128,224},{256,352},{384,480},{1,97},{129,225},{257,353},{3... | collective-permute-start | bytes 393224 | tf_op jit(solution)/shard_map/ppermute | solution.py:235
  25.4 11.2 %collective-permute-start.12 = (f32[256,128]{1,0:T(8,128)S(1)}, f32[256,128]{1,0:T(8,128)S(1)}, u32[]{:S(2)}, u32[]{:S(2)}) collective-permute-start(f32[256,128]{1,0:T(8,128)S(1)} %add_select_fusion.held), channel_id=1, source_target_pairs={{0,64},{128,192},{256,320},{384,448},{1,65},{129,193},{257,321},{3... | collective-permute-start | bytes 393224 | tf_op jit(solution)/shard_map/ppermute | solution.py:235
  26.7 9.9 %collective-permute-start.11 = (f32[256,128]{1,0:T(8,128)S(1)}, f32[256,128]{1,0:T(8,128)S(1)}, u32[]{:S(2)}, u32[]{:S(2)}) collective-permute-start(f32[256,128]{1,0:T(8,128)S(1)} %add_select_fusion.held), channel_id=1, source_target_pairs={{0,32},{128,160},{256,288},{384,416},{1,33},{129,161},{257,289},{3... | collective-permute-start | bytes 393224 | tf_op jit(solution)/shard_map/ppermute | solution.py:235

commit v12 on v11

--- a/solution.py
+++ b/solution.py
@@ -226,7 +226,7 @@
     right = lax.ppermute(first, both, [(x + 1, width + x) for x in range(width - 1)])
     cols = lax.ppermute(jnp.concatenate([left, right], axis=0), "vintage", [(1, 0)])
     semb0, attr0 = attributes(head_kernel, "head", tile, *rows, cols, *dips)
-    got = [lax.ppermute(attr0, "vintage", [(0, k)]) for k in (8, 4, 12)]
+    got = [lax.ppermute(attr0, "vintage", [(0, k)]) for k in (4, 12, 8)]
     first, last = lax.optimization_barrier((first, last, attr0))[:2]
     cols = swap(pair_sends(first, last, "xline"), "xline", range(1, vintages), across)
     joined = lax.optimization_barrier((*got, *cols))

time: 38.4 us -> 37.6 us (0.979)
  the two profiles are of different devices: /device:TPU:168 before, /device:TPU:152 now
where the time goes in v12:
time: 37.6 us; the launch traced here: 37.1 us
  starting transfers between devices  22.2 us (59%)
  waiting for transfers between devices  8.75 us (23%)
  Pallas kernels  2.73 us (7%)
  local copies, waits for them, and re-layouts  1.73 us (5%)
  between operations  0.89 us (2%)
  other arithmetic  0.84 us (2%)
    ppermute x5, starting transfers between devices, swap(): lax.ppermute(sends[n], ('vintage', axis), low + [(b, a) for a, b in low])  15.5 us
    ppermute x3, waiting for transfers between devices, per_device(): lax.ppermute(held, 'vintage', [(s, to[n]) for s, to in FANOUT.items()])  6.97 us
    ppermute x3, starting transfers between devices, per_device(): lax.ppermute(held, 'vintage', [(s, to[n]) for s, to in FANOUT.items()])  2.63 us
    ppermute x3, starting transfers between devices, per_device(): got = [lax.ppermute(attr0, 'vintage', [(0, k)]) for k in (4, 12, 8)]  2.01 us
    ppermute x5, waiting for transfers between devices, swap(): lax.ppermute(sends[n], ('vintage', axis), low + [(b, a) for a, b in low])  1.76 us
    pallas_call x2, Pallas kernels, attributes(): pl.pallas_call(kernel, out_shape=(jax.ShapeDtypeStruct((ROWS, COLS, TIME_...  1.53 us
    pallas_call x1, Pallas kernels, correlate(): pl.pallas_call(correl_kernel, out_shape=jax.ShapeDtypeStruct((ROWS, COLS,...  1.2 us
    slice x1, local copies, waits for them, and re-layouts, per_device(): first, last = edge_columns((tile[:, :1], tile[:, -1:]), rows)  0.89 us
  transfers between devices with their start and end apart: 14, of which 3 were waited for; matrix products, arithmetic and copies ran while one was open for 3% of the time, Pallas kernels for 4%

profile of v12, /device:TPU:152, one launch (start us, length us, event | category | flops | bytes accessed | tf_op | source)
XLA Modules:
  0.0 37.1 jit_solution(764469164076288219)
XLA Ops:
  0.6 0.7 %select_bitcast_fusion = (f32[1,16,256]{2,1,0:T(8,128)S(1)}, f32[1,16,256]{2,1,0:T(8,128)S(1)}, f32[1,16,256]{2,1,0:T(8,128)S(1)}) fusion(f32[1,8,16,256]{3,2,1,0:T(8,128)} %param.3, pred[]{:T(512)S(6)} %eq.13, pred[]{:T(512)S(6)} %eq.14), kind=kLoop, calls=%fused_computation.4 | loop fusion | flops 12288 | bytes 81922 | tf_op jit(solution)/shard_map/jit(_where)/select_n | solution.py:192
  1.4 0.0 copy-start
  1.4 2.0 %collective-permute-start.2 = (f32[1,16,256]{2,1,0:T(8,128)S(1)}, f32[1,16,256]{2,1,0:T(8,128)S(1)}, u32[]{:S(2)}, u32[]{:S(2)}) collective-permute-start(f32[1,16,256]{2,1,0:T(8,128)S(1)} %get-tuple-element.26), channel_id=1, source_target_pairs={{0,8},{32,40},{64,72},{96,104},{128,136},{160,168},{192,200},{224,... | collective-permute-start | bytes 49160 | tf_op jit(solution)/shard_map/ppermute | solution.py:200
  3.4 6.0 %collective-permute-start = (f32[1,16,256]{2,1,0:T(8,128)S(1)}, f32[1,16,256]{2,1,0:T(8,128)S(1)}, u32[]{:S(2)}, u32[]{:S(2)}) collective-permute-start(f32[1,16,256]{2,1,0:T(8,128)S(1)} %get-tuple-element.27), channel_id=1, source_target_pairs={{8,16},{40,48},{72,80},{104,112},{136,144},{168,176},{200,208},{23... | collective-permute-start | bytes 49160 | tf_op jit(solution)/shard_map/ppermute | solution.py:200
  9.5 0.7 %collective-permute-start.1 = (f32[1,16,256]{2,1,0:T(8,128)S(1)}, f32[1,16,256]{2,1,0:T(8,128)S(1)}, u32[]{:S(2)}, u32[]{:S(2)}) collective-permute-start(f32[1,16,256]{2,1,0:T(8,128)S(1)} %get-tuple-element.28), channel_id=1, source_target_pairs={{16,24},{48,56},{80,88},{112,120},{144,152},{176,184},{208,216},{2... | collective-permute-start | bytes 49160 | tf_op jit(solution)/shard_map/ppermute | solution.py:200
  10.1 0.9 %fusion = (f32[8,1,256]{2,1,0:T(1,128)S(1)}, f32[8,1,256]{2,1,0:T(1,128)S(1)}) fusion(f32[8,16,256]{2,1,0:T(8,128)} %bitcast.9), kind=kLoop, calls=%fused_computation.11 | loop fusion | bytes 32768 | tf_op jit(solution)/shard_map/slice | solution.py:222
  11.0 0.0 collective-permute-done.2.row_01
  11.1 0.1 collective-permute-done.row_12
  11.2 0.0 collective-permute-done.1.row_23
  11.2 0.7 %collective-permute-start.4 = (f32[10,1,256]{2,1,0:T(1,128)S(1)}, f32[10,1,256]{2,1,0:T(1,128)S(1)}, u32[]{:S(2)}, u32[]{:S(2)}) collective-permute-start(f32[10,1,256]{2,1,0:T(1,128)S(1)} %pad_maximum_fusion.2), channel_id=1, source_target_pairs={{1,32},{2,33},{3,34},{4,35},{5,36},{6,37},{7,38},{9,40},{10,41},{1... | collective-permute-start | bytes 30728 | tf_op jit(solution)/shard_map/ppermute | solution.py:226
  11.9 0.7 %collective-permute-start.3 = (f32[10,1,256]{2,1,0:T(1,128)S(1)}, f32[10,1,256]{2,1,0:T(1,128)S(1)}, u32[]{:S(2)}, u32[]{:S(2)}) collective-permute-start(f32[10,1,256]{2,1,0:T(1,128)S(1)} %pad_maximum_fusion.1), channel_id=1, source_target_pairs={{0,33},{1,34},{2,35},{3,36},{4,37},{5,38},{6,39},{8,41},{9,42},{10... | collective-permute-start | bytes 30728 | tf_op jit(solution)/shard_map/ppermute | solution.py:225
  12.6 0.0 collective-permute-done.4
  12.6 0.0 collective-permute-done.3
  12.6 0.7 %collective-permute-start.5 = (f32[20,1,256]{2,1,0:T(1,128)S(1)}, f32[20,1,256]{2,1,0:T(1,128)S(1)}, u32[]{:S(2)}, u32[]{:S(2)}) collective-permute-start(f32[20,1,256]{2,1,0:T(1,128)S(1)} %pad_maximum_fusion), channel_id=1, source_target_pairs={{32,0},{33,1},{34,2},{35,3},{36,4},{37,5},{38,6},{39,7},{40,8},{41... | collective-permute-start | bytes 61448 | tf_op jit(solution)/shard_map/ppermute | solution.py:227
  13.3 0.0 copy-start.1
  13.3 0.0 copy-start.2
  13.3 0.7 %copy-done.1 = s32[1,8,16]{2,1,0:T(8,128)S(1)} copy-done((s32[1,8,16]{2,1,0:T(8,128)S(1)}, s32[1,8,16]{2,1,0:T(8,128)}, u32[]{:S(2)}) %copy-start.1) | copy-done | bytes 536
  14.0 0.1 reshape.78.dip_il
  14.1 0.0 copy-done.2
  14.1 0.1 reshape.79.dip_xl
  14.2 0.0 collective-permute-done.5.cols
  14.2 0.0 copy-done
  14.2 0.7 %collective-permute-start.8 = (f32[256,128]{1,0:T(8,128)S(1)}, f32[256,128]{1,0:T(8,128)S(1)}, u32[]{:S(2)}, u32[]{:S(2)}) collective-permute-start(f32[256,128]{1,0:T(8,128)S(1)} %get-tuple-element.13.attr_head), channel_id=1, source_target_pairs={{0,256},{1,257},{2,258},{3,259},{4,260},{5,261},{6,262},{7,263},{8... | collective-permute-start | bytes 393224 | tf_op jit(solution)/shard_map/ppermute | solution.py:229
  14.9 0.7 %collective-permute-start.7 = (f32[256,128]{1,0:T(8,128)S(1)}, f32[256,128]{1,0:T(8,128)S(1)}, u32[]{:S(2)}, u32[]{:S(2)}) collective-permute-start(f32[256,128]{1,0:T(8,128)S(1)} %get-tuple-element.13.attr_head), channel_id=1, source_target_pairs={{0,384},{1,385},{2,386},{3,387},{4,388},{5,389},{6,390},{7,391},{8... | collective-permute-start | bytes 393224 | tf_op jit(solution)/shard_map/ppermute | solution.py:229
  15.6 0.7 %collective-permute-start.6 = (f32[256,128]{1,0:T(8,128)S(1)}, f32[256,128]{1,0:T(8,128)S(1)}, u32[]{:S(2)}, u32[]{:S(2)}) collective-permute-start(f32[256,128]{1,0:T(8,128)S(1)} %get-tuple-element.13.attr_head), channel_id=1, source_target_pairs={{0,128},{1,129},{2,130},{3,131},{4,132},{5,133},{6,134},{7,135},{8... | collective-permute-start | bytes 393224 | tf_op jit(solution)/shard_map/ppermute | solution.py:229
  16.3 0.7 %collective-permute-start.10 = (f32[10,1,256]{2,1,0:T(1,128)S(1)}, f32[10,1,256]{2,1,0:T(1,128)S(1)}, u32[]{:S(2)}, u32[]{:S(2)}) collective-permute-start(f32[10,1,256]{2,1,0:T(1,128)S(1)} %get-tuple-element.31), channel_id=1, source_target_pairs={{33,34},{35,36},{37,38},{65,66},{67,68},{69,70},{97,98},{99,100},{... | collective-permute-start | bytes 30728 | tf_op jit(solution)/shard_map/ppermute | solution.py:200
  16.9 6.1 %collective-permute-start.9 = (f32[10,1,256]{2,1,0:T(1,128)S(1)}, f32[10,1,256]{2,1,0:T(1,128)S(1)}, u32[]{:S(2)}, u32[]{:S(2)}) collective-permute-start(f32[10,1,256]{2,1,0:T(1,128)S(1)} %get-tuple-element.32), channel_id=1, source_target_pairs={{32,33},{34,35},{36,37},{38,39},{64,65},{66,67},{68,69},{70,71},{9... | collective-permute-start | bytes 30728 | tf_op jit(solution)/shard_map/ppermute | solution.py:200
  23.1 0.0 collective-permute-done.10.col_b
  23.1 1.6 %collective-permute-done.9.col_a = f32[10,1,256]{2,1,0:T(1,128)S(1)} collective-permute-done((f32[10,1,256]{2,1,0:T(1,128)S(1)}, f32[10,1,256]{2,1,0:T(1,128)S(1)}, u32[]{:S(2)}, u32[]{:S(2)}) %collective-permute-start.9) | collective-permute-done | bytes 10272 | tf_op jit(solution)/shard_map/ppermute | solution.py:200
  24.7 0.0 collective-permute-done.8
  24.7 0.0 collective-permute-done.7
  24.7 0.0 collective-permute-done.6
  24.8 0.7 %collective-permute-start.13 = (f32[256,128]{1,0:T(8,128)S(1)}, f32[256,128]{1,0:T(8,128)S(1)}, u32[]{:S(2)}, u32[]{:S(2)}) collective-permute-start(f32[256,128]{1,0:T(8,128)S(1)} %add_select_fusion.held), channel_id=1, source_target_pairs={{0,96},{128,224},{256,352},{384,480},{1,97},{129,225},{257,353},{3... | collective-permute-start | bytes 393224 | tf_op jit(solution)/shard_map/ppermute | solution.py:235
  25.4 1.3 %collective-permute-start.12 = (f32[256,128]{1,0:T(8,128)S(1)}, f32[256,128]{1,0:T(8,128)S(1)}, u32[]{:S(2)}, u32[]{:S(2)}) collective-permute-start(f32[256,128]{1,0:T(8,128)S(1)} %add_select_fusion.held), channel_id=1, source_target_pairs={{0,64},{128,192},{256,320},{384,448},{1,65},{129,193},{257,321},{3... | collective-permute-start | bytes 393224 | tf_op jit(solution)/shard_map/ppermute | solution.py:235
  26.7 0.7 %collective-permute-start.11 = (f32[256,128]{1,0:T(8,128)S(1)}, f32[256,128]{1,0:T(8,128)S(1)}, u32[]{:S(2)}, u32[]{:S(2)}) collective-permute-start(f32[256,128]{1,0:T(8,128)S(1)} %add_select_fusion.held), channel_id=1, source_target_pairs={{0,32},{128,160},{256,288},{384,416},{1,33},{129,161},{257,289},{3... | collective-permute-start | bytes 393224 | tf_op jit(solution)/shard_map/ppermute | solution.py:235
  27.4 1.5 %tail.1 = (f32[8,16,256]{2,1,0:T(8,128)}, f32[256,128]{1,0:T(8,128)S(1)}) custom-call(f32[8,16,256]{2,1,0:T(8,128)S(1)} %bitcast.11, f32[1,16,256]{2,1,0:T(8,128)S(1)} %collective-permute-done.row_12, f32[1,16,256]{2,1,0:T(8,128)S(1)} %collective-permute-done.1.row_23, f32[1,16,256]{2,1,0:T(8,128)S(1)} %collective-permute-done.2.row_01, ...), custom_call_target="tpu_custom_call" | custom-call | tf_op jit(solution)/shard_map/tail/pallas_call | solution.py:155
  28.9 0.0 collective-permute-done.13.far1
  28.9 7.0 %collective-permute-done.12.far2 = f32[256,128]{1,0:T(8,128)S(1)} collective-permute-done((f32[256,128]{1,0:T(8,128)S(1)}, f32[256,128]{1,0:T(8,128)S(1)}, u32[]{:S(2)}, u32[]{:S(2)}) %collective-permute-start.12) | collective-permute-done | bytes 131104 | tf_op jit(solution)/shard_map/ppermute | solution.py:235
  35.9 0.0 collective-permute-done.11.far3
  35.9 1.2 %correlate.1 = f32[8,16,264]{2,1,0:T(8,128)} custom-call(f32[256,128]{1,0:T(8,128)S(1)} %get-tuple-element.20.mon, f32[256,128]{1,0:T(8,128)S(1)} %add_select_fusion.held, f32[256,128]{1,0:T(8,128)S(1)} %collective-permute-done.11.far3, f32[256,128]{1,0:T(8,128)S(1)} %collective-permute-done.12.far2, f32[256,128]{1,0:T(8,128)S(1)} %collective-permute-done.13.far1), custom_call_target="tpu_custom_call" | custom-call | tf_op jit(solution)/shard_map/correlate/pallas_call | solution.py:176
  (8 shorter events, 0.1 us)
Async XLA Ops:
  1.4 12.8 %copy-start = (f32[1,8,16,256]{3,2,1,0:T(8,128)S(1)}, f32[1,8,16,256]{3,2,1,0:T(8,128)}, u32[]{:S(2)}) copy-start(f32[1,8,16,256]{3,2,1,0:T(8,128)} %param.3) | copy-start | bytes 393220
  1.4 9.7 %collective-permute-start.2 = (f32[1,16,256]{2,1,0:T(8,128)S(1)}, f32[1,16,256]{2,1,0:T(8,128)S(1)}, u32[]{:S(2)}, u32[]{:S(2)}) collective-permute-start(f32[1,16,256]{2,1,0:T(8,128)S(1)} %get-tuple-element.26), channel_id=1, source_target_pairs={{0,8},{32,40},{64,72},{96,104},{128,136},{160,168},{192,200},{224,... | collective-permute-start | bytes 49160 | tf_op jit(solution)/shard_map/ppermute | solution.py:200
  3.4 7.8 %collective-permute-start = (f32[1,16,256]{2,1,0:T(8,128)S(1)}, f32[1,16,256]{2,1,0:T(8,128)S(1)}, u32[]{:S(2)}, u32[]{:S(2)}) collective-permute-start(f32[1,16,256]{2,1,0:T(8,128)S(1)} %get-tuple-element.27), channel_id=1, source_target_pairs={{8,16},{40,48},{72,80},{104,112},{136,144},{168,176},{200,208},{23... | collective-permute-start | bytes 49160 | tf_op jit(solution)/shard_map/ppermute | solution.py:200
  9.5 1.7 %collective-permute-start.1 = (f32[1,16,256]{2,1,0:T(8,128)S(1)}, f32[1,16,256]{2,1,0:T(8,128)S(1)}, u32[]{:S(2)}, u32[]{:S(2)}) collective-permute-start(f32[1,16,256]{2,1,0:T(8,128)S(1)} %get-tuple-element.28), channel_id=1, source_target_pairs={{16,24},{48,56},{80,88},{112,120},{144,152},{176,184},{208,216},{2... | collective-permute-start | bytes 49160 | tf_op jit(solution)/shard_map/ppermute | solution.py:200
  11.2 1.4 %collective-permute-start.4 = (f32[10,1,256]{2,1,0:T(1,128)S(1)}, f32[10,1,256]{2,1,0:T(1,128)S(1)}, u32[]{:S(2)}, u32[]{:S(2)}) collective-permute-start(f32[10,1,256]{2,1,0:T(1,128)S(1)} %pad_maximum_fusion.2), channel_id=1, source_target_pairs={{1,32},{2,33},{3,34},{4,35},{5,36},{6,37},{7,38},{9,40},{10,41},{1... | collective-permute-start | bytes 30728 | tf_op jit(solution)/shard_map/ppermute | solution.py:226
  11.9 0.7 %collective-permute-start.3 = (f32[10,1,256]{2,1,0:T(1,128)S(1)}, f32[10,1,256]{2,1,0:T(1,128)S(1)}, u32[]{:S(2)}, u32[]{:S(2)}) collective-permute-start(f32[10,1,256]{2,1,0:T(1,128)S(1)} %pad_maximum_fusion.1), channel_id=1, source_target_pairs={{0,33},{1,34},{2,35},{3,36},{4,37},{5,38},{6,39},{8,41},{9,42},{10... | collective-permute-start | bytes 30728 | tf_op jit(solution)/shard_map/ppermute | solution.py:225
  12.6 1.5 %collective-permute-start.5 = (f32[20,1,256]{2,1,0:T(1,128)S(1)}, f32[20,1,256]{2,1,0:T(1,128)S(1)}, u32[]{:S(2)}, u32[]{:S(2)}) collective-permute-start(f32[20,1,256]{2,1,0:T(1,128)S(1)} %pad_maximum_fusion), channel_id=1, source_target_pairs={{32,0},{33,1},{34,2},{35,3},{36,4},{37,5},{38,6},{39,7},{40,8},{41... | collective-permute-start | bytes 61448 | tf_op jit(solution)/shard_map/ppermute | solution.py:227
  13.3 0.7 %copy-start.1 = (s32[1,8,16]{2,1,0:T(8,128)S(1)}, s32[1,8,16]{2,1,0:T(8,128)}, u32[]{:S(2)}) copy-start(s32[1,8,16]{2,1,0:T(8,128)} %param.4) | copy-start | bytes 1540
  13.3 0.8 %copy-start.2 = (s32[1,8,16]{2,1,0:T(8,128)S(1)}, s32[1,8,16]{2,1,0:T(8,128)}, u32[]{:S(2)}) copy-start(s32[1,8,16]{2,1,0:T(8,128)} %param.5) | copy-start | bytes 1540
  14.2 10.5 %collective-permute-start.8 = (f32[256,128]{1,0:T(8,128)S(1)}, f32[256,128]{1,0:T(8,128)S(1)}, u32[]{:S(2)}, u32[]{:S(2)}) collective-permute-start(f32[256,128]{1,0:T(8,128)S(1)} %get-tuple-element.13.attr_head), channel_id=1, source_target_pairs={{0,256},{1,257},{2,258},{3,259},{4,260},{5,261},{6,262},{7,263},{8... | collective-permute-start | bytes 393224 | tf_op jit(solution)/shard_map/ppermute | solution.py:229
  14.9 9.8 %collective-permute-start.7 = (f32[256,128]{1,0:T(8,128)S(1)}, f32[256,128]{1,0:T(8,128)S(1)}, u32[]{:S(2)}, u32[]{:S(2)}) collective-permute-start(f32[256,128]{1,0:T(8,128)S(1)} %get-tuple-element.13.attr_head), channel_id=1, source_target_pairs={{0,384},{1,385},{2,386},{3,387},{4,388},{5,389},{6,390},{7,391},{8... | collective-permute-start | bytes 393224 | tf_op jit(solution)/shard_map/ppermute | solution.py:229
  15.6 9.2 %collective-permute-start.6 = (f32[256,128]{1,0:T(8,128)S(1)}, f32[256,128]{1,0:T(8,128)S(1)}, u32[]{:S(2)}, u32[]{:S(2)}) collective-permute-start(f32[256,128]{1,0:T(8,128)S(1)} %get-tuple-element.13.attr_head), channel_id=1, source_target_pairs={{0,128},{1,129},{2,130},{3,131},{4,132},{5,133},{6,134},{7,135},{8... | collective-permute-start | bytes 393224 | tf_op jit(solution)/shard_map/ppermute | solution.py:229
  16.3 6.8 %collective-permute-start.10 = (f32[10,1,256]{2,1,0:T(1,128)S(1)}, f32[10,1,256]{2,1,0:T(1,128)S(1)}, u32[]{:S(2)}, u32[]{:S(2)}) collective-permute-start(f32[10,1,256]{2,1,0:T(1,128)S(1)} %get-tuple-element.31), channel_id=1, source_target_pairs={{33,34},{35,36},{37,38},{65,66},{67,68},{69,70},{97,98},{99,100},{... | collective-permute-start | bytes 30728 | tf_op jit(solution)/shard_map/ppermute | solution.py:200
  16.9 7.8 %collective-permute-start.9 = (f32[10,1,256]{2,1,0:T(1,128)S(1)}, f32[10,1,256]{2,1,0:T(1,128)S(1)}, u32[]{:S(2)}, u32[]{:S(2)}) collective-permute-start(f32[10,1,256]{2,1,0:T(1,128)S(1)} %get-tuple-element.32), channel_id=1, source_target_pairs={{32,33},{34,35},{36,37},{38,39},{64,65},{66,67},{68,69},{70,71},{9... | collective-permute-start | bytes 30728 | tf_op jit(solution)/shard_map/ppermute | solution.py:200
  24.8 4.2 %collective-permute-start.13 = (f32[256,128]{1,0:T(8,128)S(1)}, f32[256,128]{1,0:T(8,128)S(1)}, u32[]{:S(2)}, u32[]{:S(2)}) collective-permute-start(f32[256,128]{1,0:T(8,128)S(1)} %add_select_fusion.held), channel_id=1, source_target_pairs={{0,96},{128,224},{256,352},{384,480},{1,97},{129,225},{257,353},{3... | collective-permute-start | bytes 393224 | tf_op jit(solution)/shard_map/ppermute | solution.py:235
  25.4 10.5 %collective-permute-start.12 = (f32[256,128]{1,0:T(8,128)S(1)}, f32[256,128]{1,0:T(8,128)S(1)}, u32[]{:S(2)}, u32[]{:S(2)}) collective-permute-start(f32[256,128]{1,0:T(8,128)S(1)} %add_select_fusion.held), channel_id=1, source_target_pairs={{0,64},{128,192},{256,320},{384,448},{1,65},{129,193},{257,321},{3... | collective-permute-start | bytes 393224 | tf_op jit(solution)/shard_map/ppermute | solution.py:235
  26.7 9.2 %collective-permute-start.11 = (f32[256,128]{1,0:T(8,128)S(1)}, f32[256,128]{1,0:T(8,128)S(1)}, u32[]{:S(2)}, u32[]{:S(2)}) collective-permute-start(f32[256,128]{1,0:T(8,128)S(1)} %add_select_fusion.held), channel_id=1, source_target_pairs={{0,32},{128,160},{256,288},{384,416},{1,33},{129,161},{257,289},{3... | collective-permute-start | bytes 393224 | tf_op jit(solution)/shard_map/ppermute | solution.py:235

commit v13 on v12

--- a/solution.py
+++ b/solution.py
@@ -229,8 +229,8 @@
     got = [lax.ppermute(attr0, "vintage", [(0, k)]) for k in (4, 12, 8)]
     first, last = lax.optimization_barrier((first, last, attr0))[:2]
     cols = swap(pair_sends(first, last, "xline"), "xline", range(1, vintages), across)
-    joined = lax.optimization_barrier((*got, *cols))
-    got, cols = joined[:3], joined[3:]
+    joined = lax.optimization_barrier((*cols[::-1], *got))
+    got, cols = joined[2:], joined[1::-1]
     held = jnp.where(lax.axis_index("vintage") == 0, attr0, got[0] + got[1] + got[2])
     far = [lax.ppermute(held, "vintage", [(s, to[n]) for s, to in FANOUT.items()]) for n in (2, 1, 0)]
     semb, attr = attributes(tail_kernel, "tail", tile, *rows, *cols, *dips, semb0, attr0)

time: 37.6 us -> 37.9 us (level)
  the two profiles are of different devices: /device:TPU:152 before, /device:TPU:321 now
where the time goes in v13:
time: 37.9 us; the launch traced here: 37.4 us
  starting transfers between devices  18.6 us (49%)
  waiting for transfers between devices  12.7 us (34%)
  Pallas kernels  2.73 us (7%)
  local copies, waits for them, and re-layouts  1.73 us (5%)
  between operations  0.86 us (2%)
  other arithmetic  0.84 us (2%)
    ppermute x5, starting transfers between devices, swap(): lax.ppermute(sends[n], ('vintage', axis), low + [(b, a) for a, b in low])  10 us
    ppermute x5, waiting for transfers between devices, swap(): lax.ppermute(sends[n], ('vintage', axis), low + [(b, a) for a, b in low])  6.43 us
    ppermute x1, waiting for transfers between devices, per_device(): lax.ppermute(first, both, [(x + 1, width + x) for x in range(width - 1)])  2.94 us
    ppermute x1, waiting for transfers between devices, per_device(): lax.ppermute(last, both, [(x, width + x + 1) for x in range(width - 1)])  2.86 us
    ppermute x3, starting transfers between devices, per_device(): lax.ppermute(held, 'vintage', [(s, to[n]) for s, to in FANOUT.items()])  2.63 us
    ppermute x3, starting transfers between devices, per_device(): got = [lax.ppermute(attr0, 'vintage', [(0, k)]) for k in (4, 12, 8)]  2.01 us
    pallas_call x2, Pallas kernels, attributes(): pl.pallas_call(kernel, out_shape=(jax.ShapeDtypeStruct((ROWS, COLS, TIME_...  1.53 us
    ppermute x1, starting transfers between devices, per_device(): lax.ppermute(first, both, [(x + 1, width + x) for x in range(width - 1)])  1.29 us
  transfers between devices with their start and end apart: 14, of which 6 were waited for; matrix products, arithmetic and copies ran while one was open for 3% of the time, Pallas kernels for 4%

profile of v13, /device:TPU:321, one launch (start us, length us, event | category | flops | bytes accessed | tf_op | source)
XLA Modules:
  0.0 37.4 jit_solution(5871825773329623537)
XLA Ops:
  0.6 0.7 %select_bitcast_fusion = (f32[1,16,256]{2,1,0:T(8,128)S(1)}, f32[1,16,256]{2,1,0:T(8,128)S(1)}, f32[1,16,256]{2,1,0:T(8,128)S(1)}) fusion(f32[1,8,16,256]{3,2,1,0:T(8,128)} %param.3, pred[]{:T(512)S(6)} %eq.13, pred[]{:T(512)S(6)} %eq.14), kind=kLoop, calls=%fused_computation.4 | loop fusion | flops 12288 | bytes 81922 | tf_op jit(solution)/shard_map/jit(_where)/select_n | solution.py:192
  1.4 0.0 copy-start
  1.4 0.8 %collective-permute-start.2 = (f32[1,16,256]{2,1,0:T(8,128)S(1)}, f32[1,16,256]{2,1,0:T(8,128)S(1)}, u32[]{:S(2)}, u32[]{:S(2)}) collective-permute-start(f32[1,16,256]{2,1,0:T(8,128)S(1)} %get-tuple-element.26), channel_id=1, source_target_pairs={{0,8},{32,40},{64,72},{96,104},{128,136},{160,168},{192,200},{224,... | collective-permute-start | bytes 49160 | tf_op jit(solution)/shard_map/ppermute | solution.py:200
  2.2 2.5 %collective-permute-start = (f32[1,16,256]{2,1,0:T(8,128)S(1)}, f32[1,16,256]{2,1,0:T(8,128)S(1)}, u32[]{:S(2)}, u32[]{:S(2)}) collective-permute-start(f32[1,16,256]{2,1,0:T(8,128)S(1)} %get-tuple-element.27), channel_id=1, source_target_pairs={{8,16},{40,48},{72,80},{104,112},{136,144},{168,176},{200,208},{23... | collective-permute-start | bytes 49160 | tf_op jit(solution)/shard_map/ppermute | solution.py:200
  4.7 2.1 %collective-permute-start.1 = (f32[1,16,256]{2,1,0:T(8,128)S(1)}, f32[1,16,256]{2,1,0:T(8,128)S(1)}, u32[]{:S(2)}, u32[]{:S(2)}) collective-permute-start(f32[1,16,256]{2,1,0:T(8,128)S(1)} %get-tuple-element.28), channel_id=1, source_target_pairs={{16,24},{48,56},{80,88},{112,120},{144,152},{176,184},{208,216},{2... | collective-permute-start | bytes 49160 | tf_op jit(solution)/shard_map/ppermute | solution.py:200
  6.9 0.9 %fusion = (f32[8,1,256]{2,1,0:T(1,128)S(1)}, f32[8,1,256]{2,1,0:T(1,128)S(1)}) fusion(f32[8,16,256]{2,1,0:T(8,128)} %bitcast.9), kind=kLoop, calls=%fused_computation.11 | loop fusion | bytes 32768 | tf_op jit(solution)/shard_map/slice | solution.py:222
  7.8 0.0 collective-permute-done.2.row_01
  7.8 1.2 %collective-permute-done.row_12 = f32[1,16,256]{2,1,0:T(8,128)S(1)} collective-permute-done((f32[1,16,256]{2,1,0:T(8,128)S(1)}, f32[1,16,256]{2,1,0:T(8,128)S(1)}, u32[]{:S(2)}, u32[]{:S(2)}) %collective-permute-start) | collective-permute-done | bytes 16416 | tf_op jit(solution)/shard_map/ppermute | solution.py:200
  8.9 1.4 %collective-permute-done.1.row_23 = f32[1,16,256]{2,1,0:T(8,128)S(1)} collective-permute-done((f32[1,16,256]{2,1,0:T(8,128)S(1)}, f32[1,16,256]{2,1,0:T(8,128)S(1)}, u32[]{:S(2)}, u32[]{:S(2)}) %collective-permute-start.1) | collective-permute-done | bytes 16416 | tf_op jit(solution)/shard_map/ppermute | solution.py:200
  10.4 1.3 %collective-permute-start.4 = (f32[10,1,256]{2,1,0:T(1,128)S(1)}, f32[10,1,256]{2,1,0:T(1,128)S(1)}, u32[]{:S(2)}, u32[]{:S(2)}) collective-permute-start(f32[10,1,256]{2,1,0:T(1,128)S(1)} %pad_maximum_fusion.1), channel_id=1, source_target_pairs={{1,32},{2,33},{3,34},{4,35},{5,36},{6,37},{7,38},{9,40},{10,41},{1... | collective-permute-start | bytes 30728 | tf_op jit(solution)/shard_map/ppermute | solution.py:226
  11.7 1.3 %collective-permute-start.3 = (f32[10,1,256]{2,1,0:T(1,128)S(1)}, f32[10,1,256]{2,1,0:T(1,128)S(1)}, u32[]{:S(2)}, u32[]{:S(2)}) collective-permute-start(f32[10,1,256]{2,1,0:T(1,128)S(1)} %pad_maximum_fusion.2), channel_id=1, source_target_pairs={{0,33},{1,34},{2,35},{3,36},{4,37},{5,38},{6,39},{8,41},{9,42},{10... | collective-permute-start | bytes 30728 | tf_op jit(solution)/shard_map/ppermute | solution.py:225
  13.0 2.9 %collective-permute-done.4 = f32[10,1,256]{2,1,0:T(1,128)S(1)} collective-permute-done((f32[10,1,256]{2,1,0:T(1,128)S(1)}, f32[10,1,256]{2,1,0:T(1,128)S(1)}, u32[]{:S(2)}, u32[]{:S(2)}) %collective-permute-start.4) | collective-permute-done | bytes 10272 | tf_op jit(solution)/shard_map/ppermute | solution.py:226
  16.0 2.9 %collective-permute-done.3 = f32[10,1,256]{2,1,0:T(1,128)S(1)} collective-permute-done((f32[10,1,256]{2,1,0:T(1,128)S(1)}, f32[10,1,256]{2,1,0:T(1,128)S(1)}, u32[]{:S(2)}, u32[]{:S(2)}) %collective-permute-start.3) | collective-permute-done | bytes 10272 | tf_op jit(solution)/shard_map/ppermute | solution.py:225
  18.8 1.3 %collective-permute-start.5 = (f32[20,1,256]{2,1,0:T(1,128)S(1)}, f32[20,1,256]{2,1,0:T(1,128)S(1)}, u32[]{:S(2)}, u32[]{:S(2)}) collective-permute-start(f32[20,1,256]{2,1,0:T(1,128)S(1)} %pad_maximum_fusion), channel_id=1, source_target_pairs={{32,0},{33,1},{34,2},{35,3},{36,4},{37,5},{38,6},{39,7},{40,8},{41... | collective-permute-start | bytes 61448 | tf_op jit(solution)/shard_map/ppermute | solution.py:227
  20.1 0.0 copy-start.1
  20.2 0.0 copy-start.2
  20.2 0.7 %copy-done.1 = s32[1,8,16]{2,1,0:T(8,128)S(1)} copy-done((s32[1,8,16]{2,1,0:T(8,128)S(1)}, s32[1,8,16]{2,1,0:T(8,128)}, u32[]{:S(2)}) %copy-start.1) | copy-done | bytes 536
  20.8 0.1 reshape.78.dip_il
  20.9 0.0 copy-done.2
  20.9 0.1 reshape.79.dip_xl
  21.0 0.0 collective-permute-done.5.cols
  21.0 0.0 copy-done
  21.0 0.7 %collective-permute-start.10 = (f32[256,128]{1,0:T(8,128)S(1)}, f32[256,128]{1,0:T(8,128)S(1)}, u32[]{:S(2)}, u32[]{:S(2)}) collective-permute-start(f32[256,128]{1,0:T(8,128)S(1)} %get-tuple-element.13.attr_head), channel_id=1, source_target_pairs={{0,256},{1,257},{2,258},{3,259},{4,260},{5,261},{6,262},{7,263},{8... | collective-permute-start | bytes 393224 | tf_op jit(solution)/shard_map/ppermute | solution.py:229
  21.7 0.7 %collective-permute-start.9 = (f32[256,128]{1,0:T(8,128)S(1)}, f32[256,128]{1,0:T(8,128)S(1)}, u32[]{:S(2)}, u32[]{:S(2)}) collective-permute-start(f32[256,128]{1,0:T(8,128)S(1)} %get-tuple-element.13.attr_head), channel_id=1, source_target_pairs={{0,384},{1,385},{2,386},{3,387},{4,388},{5,389},{6,390},{7,391},{8... | collective-permute-start | bytes 393224 | tf_op jit(solution)/shard_map/ppermute | solution.py:229
  22.4 0.7 %collective-permute-start.8 = (f32[256,128]{1,0:T(8,128)S(1)}, f32[256,128]{1,0:T(8,128)S(1)}, u32[]{:S(2)}, u32[]{:S(2)}) collective-permute-start(f32[256,128]{1,0:T(8,128)S(1)} %get-tuple-element.13.attr_head), channel_id=1, source_target_pairs={{0,128},{1,129},{2,130},{3,131},{4,132},{5,133},{6,134},{7,135},{8... | collective-permute-start | bytes 393224 | tf_op jit(solution)/shard_map/ppermute | solution.py:229
  23.1 1.9 %collective-permute-start.7 = (f32[10,1,256]{2,1,0:T(1,128)S(1)}, f32[10,1,256]{2,1,0:T(1,128)S(1)}, u32[]{:S(2)}, u32[]{:S(2)}) collective-permute-start(f32[10,1,256]{2,1,0:T(1,128)S(1)} %get-tuple-element.31), channel_id=1, source_target_pairs={{32,33},{34,35},{36,37},{38,39},{64,65},{66,67},{68,69},{70,71},{9... | collective-permute-start | bytes 30728 | tf_op jit(solution)/shard_map/ppermute | solution.py:200
  25.0 2.7 %collective-permute-start.6 = (f32[10,1,256]{2,1,0:T(1,128)S(1)}, f32[10,1,256]{2,1,0:T(1,128)S(1)}, u32[]{:S(2)}, u32[]{:S(2)}) collective-permute-start(f32[10,1,256]{2,1,0:T(1,128)S(1)} %get-tuple-element.32), channel_id=1, source_target_pairs={{33,34},{35,36},{37,38},{65,66},{67,68},{69,70},{97,98},{99,100},{... | collective-permute-start | bytes 30728 | tf_op jit(solution)/shard_map/ppermute | solution.py:200
  27.7 0.0 collective-permute-done.7.col_a
  27.7 3.8 %collective-permute-done.6.col_b = f32[10,1,256]{2,1,0:T(1,128)S(1)} collective-permute-done((f32[10,1,256]{2,1,0:T(1,128)S(1)}, f32[10,1,256]{2,1,0:T(1,128)S(1)}, u32[]{:S(2)}, u32[]{:S(2)}) %collective-permute-start.6) | collective-permute-done | bytes 10272 | tf_op jit(solution)/shard_map/ppermute | solution.py:200
  31.5 0.0 collective-permute-done.10
  31.6 0.0 collective-permute-done.9
  31.6 0.0 collective-permute-done.8
  31.6 0.7 %collective-permute-start.13 = (f32[256,128]{1,0:T(8,128)S(1)}, f32[256,128]{1,0:T(8,128)S(1)}, u32[]{:S(2)}, u32[]{:S(2)}) collective-permute-start(f32[256,128]{1,0:T(8,128)S(1)} %add_select_fusion.held), channel_id=1, source_target_pairs={{0,96},{128,224},{256,352},{384,480},{1,97},{129,225},{257,353},{3... | collective-permute-start | bytes 393224 | tf_op jit(solution)/shard_map/ppermute | solution.py:235
  32.3 0.7 %collective-permute-start.12 = (f32[256,128]{1,0:T(8,128)S(1)}, f32[256,128]{1,0:T(8,128)S(1)}, u32[]{:S(2)}, u32[]{:S(2)}) collective-permute-start(f32[256,128]{1,0:T(8,128)S(1)} %add_select_fusion.held), channel_id=1, source_target_pairs={{0,64},{128,192},{256,320},{384,448},{1,65},{129,193},{257,321},{3... | collective-permute-start | bytes 393224 | tf_op jit(solution)/shard_map/ppermute | solution.py:235
  33.0 1.3 %collective-permute-start.11 = (f32[256,128]{1,0:T(8,128)S(1)}, f32[256,128]{1,0:T(8,128)S(1)}, u32[]{:S(2)}, u32[]{:S(2)}) collective-permute-start(f32[256,128]{1,0:T(8,128)S(1)} %add_select_fusion.held), channel_id=1, source_target_pairs={{0,32},{128,160},{256,288},{384,416},{1,33},{129,161},{257,289},{3... | collective-permute-start | bytes 393224 | tf_op jit(solution)/shard_map/ppermute | solution.py:235
  34.2 1.5 %tail.1 = (f32[8,16,256]{2,1,0:T(8,128)}, f32[256,128]{1,0:T(8,128)S(1)}) custom-call(f32[8,16,256]{2,1,0:T(8,128)S(1)} %bitcast.11, f32[1,16,256]{2,1,0:T(8,128)S(1)} %collective-permute-done.row_12, f32[1,16,256]{2,1,0:T(8,128)S(1)} %collective-permute-done.1.row_23, f32[1,16,256]{2,1,0:T(8,128)S(1)} %collective-permute-done.2.row_01, ...), custom_call_target="tpu_custom_call" | custom-call | tf_op jit(solution)/shard_map/tail/pallas_call | solution.py:155
  35.8 0.0 collective-permute-done.13.far1
  35.8 0.0 collective-permute-done.12.far2
  35.8 0.4 %collective-permute-done.11.far3 = f32[256,128]{1,0:T(8,128)S(1)} collective-permute-done((f32[256,128]{1,0:T(8,128)S(1)}, f32[256,128]{1,0:T(8,128)S(1)}, u32[]{:S(2)}, u32[]{:S(2)}) %collective-permute-start.11) | collective-permute-done | bytes 131104 | tf_op jit(solution)/shard_map/ppermute | solution.py:235
  36.2 1.2 %correlate.1 = f32[8,16,264]{2,1,0:T(8,128)} custom-call(f32[256,128]{1,0:T(8,128)S(1)} %get-tuple-element.20.mon, f32[256,128]{1,0:T(8,128)S(1)} %add_select_fusion.held, f32[256,128]{1,0:T(8,128)S(1)} %collective-permute-done.11.far3, f32[256,128]{1,0:T(8,128)S(1)} %collective-permute-done.12.far2, f32[256,128]{1,0:T(8,128)S(1)} %collective-permute-done.13.far1), custom_call_target="tpu_custom_call" | custom-call | tf_op jit(solution)/shard_map/correlate/pallas_call | solution.py:176
  (8 shorter events, 0.1 us)
Async XLA Ops:
  1.4 19.6 %copy-start = (f32[1,8,16,256]{3,2,1,0:T(8,128)S(1)}, f32[1,8,16,256]{3,2,1,0:T(8,128)}, u32[]{:S(2)}) copy-start(f32[1,8,16,256]{3,2,1,0:T(8,128)} %param.3) | copy-start | bytes 393220
  1.4 6.4 %collective-permute-start.2 = (f32[1,16,256]{2,1,0:T(8,128)S(1)}, f32[1,16,256]{2,1,0:T(8,128)S(1)}, u32[]{:S(2)}, u32[]{:S(2)}) collective-permute-start(f32[1,16,256]{2,1,0:T(8,128)S(1)} %get-tuple-element.26), channel_id=1, source_target_pairs={{0,8},{32,40},{64,72},{96,104},{128,136},{160,168},{192,200},{224,... | collective-permute-start | bytes 49160 | tf_op jit(solution)/shard_map/ppermute | solution.py:200
  2.2 6.8 %collective-permute-start = (f32[1,16,256]{2,1,0:T(8,128)S(1)}, f32[1,16,256]{2,1,0:T(8,128)S(1)}, u32[]{:S(2)}, u32[]{:S(2)}) collective-permute-start(f32[1,16,256]{2,1,0:T(8,128)S(1)} %get-tuple-element.27), channel_id=1, source_target_pairs={{8,16},{40,48},{72,80},{104,112},{136,144},{168,176},{200,208},{23... | collective-permute-start | bytes 49160 | tf_op jit(solution)/shard_map/ppermute | solution.py:200
  4.7 5.7 %collective-permute-start.1 = (f32[1,16,256]{2,1,0:T(8,128)S(1)}, f32[1,16,256]{2,1,0:T(8,128)S(1)}, u32[]{:S(2)}, u32[]{:S(2)}) collective-permute-start(f32[1,16,256]{2,1,0:T(8,128)S(1)} %get-tuple-element.28), channel_id=1, source_target_pairs={{16,24},{48,56},{80,88},{112,120},{144,152},{176,184},{208,216},{2... | collective-permute-start | bytes 49160 | tf_op jit(solution)/shard_map/ppermute | solution.py:200
  10.4 5.6 %collective-permute-start.4 = (f32[10,1,256]{2,1,0:T(1,128)S(1)}, f32[10,1,256]{2,1,0:T(1,128)S(1)}, u32[]{:S(2)}, u32[]{:S(2)}) collective-permute-start(f32[10,1,256]{2,1,0:T(1,128)S(1)} %pad_maximum_fusion.1), channel_id=1, source_target_pairs={{1,32},{2,33},{3,34},{4,35},{5,36},{6,37},{7,38},{9,40},{10,41},{1... | collective-permute-start | bytes 30728 | tf_op jit(solution)/shard_map/ppermute | solution.py:226
  11.7 7.1 %collective-permute-start.3 = (f32[10,1,256]{2,1,0:T(1,128)S(1)}, f32[10,1,256]{2,1,0:T(1,128)S(1)}, u32[]{:S(2)}, u32[]{:S(2)}) collective-permute-start(f32[10,1,256]{2,1,0:T(1,128)S(1)} %pad_maximum_fusion.2), channel_id=1, source_target_pairs={{0,33},{1,34},{2,35},{3,36},{4,37},{5,38},{6,39},{8,41},{9,42},{10... | collective-permute-start | bytes 30728 | tf_op jit(solution)/shard_map/ppermute | solution.py:225
  18.8 2.2 %collective-permute-start.5 = (f32[20,1,256]{2,1,0:T(1,128)S(1)}, f32[20,1,256]{2,1,0:T(1,128)S(1)}, u32[]{:S(2)}, u32[]{:S(2)}) collective-permute-start(f32[20,1,256]{2,1,0:T(1,128)S(1)} %pad_maximum_fusion), channel_id=1, source_target_pairs={{32,0},{33,1},{34,2},{35,3},{36,4},{37,5},{38,6},{39,7},{40,8},{41... | collective-permute-start | bytes 61448 | tf_op jit(solution)/shard_map/ppermute | solution.py:227
  20.1 0.7 %copy-start.1 = (s32[1,8,16]{2,1,0:T(8,128)S(1)}, s32[1,8,16]{2,1,0:T(8,128)}, u32[]{:S(2)}) copy-start(s32[1,8,16]{2,1,0:T(8,128)} %param.4) | copy-start | bytes 1540
  20.2 0.8 %copy-start.2 = (s32[1,8,16]{2,1,0:T(8,128)S(1)}, s32[1,8,16]{2,1,0:T(8,128)}, u32[]{:S(2)}) copy-start(s32[1,8,16]{2,1,0:T(8,128)} %param.5) | copy-start | bytes 1540
  21.0 10.5 %collective-permute-start.10 = (f32[256,128]{1,0:T(8,128)S(1)}, f32[256,128]{1,0:T(8,128)S(1)}, u32[]{:S(2)}, u32[]{:S(2)}) collective-permute-start(f32[256,128]{1,0:T(8,128)S(1)} %get-tuple-element.13.attr_head), channel_id=1, source_target_pairs={{0,256},{1,257},{2,258},{3,259},{4,260},{5,261},{6,262},{7,263},{8... | collective-permute-start | bytes 393224 | tf_op jit(solution)/shard_map/ppermute | solution.py:229
  21.7 9.8 %collective-permute-start.9 = (f32[256,128]{1,0:T(8,128)S(1)}, f32[256,128]{1,0:T(8,128)S(1)}, u32[]{:S(2)}, u32[]{:S(2)}) collective-permute-start(f32[256,128]{1,0:T(8,128)S(1)} %get-tuple-element.13.attr_head), channel_id=1, source_target_pairs={{0,384},{1,385},{2,386},{3,387},{4,388},{5,389},{6,390},{7,391},{8... | collective-permute-start | bytes 393224 | tf_op jit(solution)/shard_map/ppermute | solution.py:229
  22.4 9.2 %collective-permute-start.8 = (f32[256,128]{1,0:T(8,128)S(1)}, f32[256,128]{1,0:T(8,128)S(1)}, u32[]{:S(2)}, u32[]{:S(2)}) collective-permute-start(f32[256,128]{1,0:T(8,128)S(1)} %get-tuple-element.13.attr_head), channel_id=1, source_target_pairs={{0,128},{1,129},{2,130},{3,131},{4,132},{5,133},{6,134},{7,135},{8... | collective-permute-start | bytes 393224 | tf_op jit(solution)/shard_map/ppermute | solution.py:229
  23.1 4.6 %collective-permute-start.7 = (f32[10,1,256]{2,1,0:T(1,128)S(1)}, f32[10,1,256]{2,1,0:T(1,128)S(1)}, u32[]{:S(2)}, u32[]{:S(2)}) collective-permute-start(f32[10,1,256]{2,1,0:T(1,128)S(1)} %get-tuple-element.31), channel_id=1, source_target_pairs={{32,33},{34,35},{36,37},{38,39},{64,65},{66,67},{68,69},{70,71},{9... | collective-permute-start | bytes 30728 | tf_op jit(solution)/shard_map/ppermute | solution.py:200
  25.0 6.5 %collective-permute-start.6 = (f32[10,1,256]{2,1,0:T(1,128)S(1)}, f32[10,1,256]{2,1,0:T(1,128)S(1)}, u32[]{:S(2)}, u32[]{:S(2)}) collective-permute-start(f32[10,1,256]{2,1,0:T(1,128)S(1)} %get-tuple-element.32), channel_id=1, source_target_pairs={{33,34},{35,36},{37,38},{65,66},{67,68},{69,70},{97,98},{99,100},{... | collective-permute-start | bytes 30728 | tf_op jit(solution)/shard_map/ppermute | solution.py:200
  31.6 4.2 %collective-permute-start.13 = (f32[256,128]{1,0:T(8,128)S(1)}, f32[256,128]{1,0:T(8,128)S(1)}, u32[]{:S(2)}, u32[]{:S(2)}) collective-permute-start(f32[256,128]{1,0:T(8,128)S(1)} %add_select_fusion.held), channel_id=1, source_target_pairs={{0,96},{128,224},{256,352},{384,480},{1,97},{129,225},{257,353},{3... | collective-permute-start | bytes 393224 | tf_op jit(solution)/shard_map/ppermute | solution.py:235
  32.3 3.5 %collective-permute-start.12 = (f32[256,128]{1,0:T(8,128)S(1)}, f32[256,128]{1,0:T(8,128)S(1)}, u32[]{:S(2)}, u32[]{:S(2)}) collective-permute-start(f32[256,128]{1,0:T(8,128)S(1)} %add_select_fusion.held), channel_id=1, source_target_pairs={{0,64},{128,192},{256,320},{384,448},{1,65},{129,193},{257,321},{3... | collective-permute-start | bytes 393224 | tf_op jit(solution)/shard_map/ppermute | solution.py:235
  33.0 3.2 %collective-permute-start.11 = (f32[256,128]{1,0:T(8,128)S(1)}, f32[256,128]{1,0:T(8,128)S(1)}, u32[]{:S(2)}, u32[]{:S(2)}) collective-permute-start(f32[256,128]{1,0:T(8,128)S(1)} %add_select_fusion.held), channel_id=1, source_target_pairs={{0,32},{128,160},{256,288},{384,416},{1,33},{129,161},{257,289},{3... | collective-permute-start | bytes 393224 | tf_op jit(solution)/shard_map/ppermute | solution.py:235

commit v14 on v12

--- a/solution.py
+++ b/solution.py
@@ -1,3 +1,5 @@
+import functools
+
 import jax
 import jax.numpy as jnp
 from jax import lax
@@ -132,18 +134,20 @@
     factor = NWIN / jnp.sqrt(mon_energy * base_energy + EPS)
     sub = lax.broadcasted_iota(jnp.int32, (8, TRACES), 0)
     width = TIME_SAMPLES // NWIN
-    for lag in range(LAGS):
-        level = []
+    for first in range(8):
+        lags = range(first, LAGS, 8)
+        sums = [[] for _ in lags]
         for w in range(NWIN):
-            acc = None
-            for r in range(w * width, (w + 1) * width, 8):
-                term = mon[pl.ds(r, 8), :] * base[pl.ds(r + lag, 8), :]
-                acc = term if acc is None else acc + term
-            level.append(acc)
-        level = [pair_sum(level[w], level[w + 4], 4, sub < 4) for w in range(4)]
-        level = [pair_sum(level[w], level[w + 2], 2, (sub & 2) == 0) for w in range(2)]
-        row = pair_sum(level[0], level[1], 1, (sub & 1) == 0)
-        result[pl.ds(lag * 8, 8), :] = row * factor
+            row = w * width
+            m = [mon[pl.ds(row + 8 * k, 8), :] for k in range(width // 8)]
+            b = [base[pl.ds(row + first + 8 * k, 8), :] for k in range(width // 8 + len(lags) - 1)]
+            for n, level in enumerate(sums):
+                level.append(functools.reduce(jnp.add, [x * y for x, y in zip(m, b[n:])]))
+        for lag, level in zip(lags, sums):
+            level = [pair_sum(level[w], level[w + 4], 4, sub < 4) for w in range(4)]
+            level = [pair_sum(level[w], level[w + 2], 2, (sub & 2) == 0) for w in range(2)]
+            row = pair_sum(level[0], level[1], 1, (sub & 1) == 0)
+            result[pl.ds(lag * 8, 8), :] = row * factor
     out[...] = result[...].T.reshape(ROWS, COLS, LAGS * NWIN)
 
 

time: 37.6 us -> 37.6 us (level)
  no operation moved by 1% of the time
where the time goes in v14:
time: 37.6 us; the launch traced here: 37.1 us
  starting transfers between devices  22.2 us (59%)
  waiting for transfers between devices  8.75 us (23%)
  Pallas kernels  2.73 us (7%)
  local copies, waits for them, and re-layouts  1.73 us (5%)
  between operations  0.89 us (2%)
  other arithmetic  0.84 us (2%)
    ppermute x5, starting transfers between devices, swap(): lax.ppermute(sends[n], ('vintage', axis), low + [(b, a) for a, b in low])  15.5 us
    ppermute x3, waiting for transfers between devices, per_device(): lax.ppermute(held, 'vintage', [(s, to[n]) for s, to in FANOUT.items()])  6.97 us
    ppermute x3, starting transfers between devices, per_device(): lax.ppermute(held, 'vintage', [(s, to[n]) for s, to in FANOUT.items()])  2.63 us
    ppermute x3, starting transfers between devices, per_device(): got = [lax.ppermute(attr0, 'vintage', [(0, k)]) for k in (4, 12, 8)]  2.01 us
    ppermute x5, waiting for transfers between devices, swap(): lax.ppermute(sends[n], ('vintage', axis), low + [(b, a) for a, b in low])  1.76 us
    pallas_call x2, Pallas kernels, attributes(): pl.pallas_call(kernel, out_shape=(jax.ShapeDtypeStruct((ROWS, COLS, TIME_...  1.53 us
    pallas_call x1, Pallas kernels, correlate(): pl.pallas_call(correl_kernel, out_shape=jax.ShapeDtypeStruct((ROWS, COLS,...  1.2 us
    slice x1, local copies, waits for them, and re-layouts, per_device(): first, last = edge_columns((tile[:, :1], tile[:, -1:]), rows)  0.89 us
  transfers between devices with their start and end apart: 14, of which 3 were waited for; matrix products, arithmetic and copies ran while one was open for 3% of the time, Pallas kernels for 4%

profile of v14, /device:TPU:152, one launch (start us, length us, event | category | flops | bytes accessed | tf_op | source)
XLA Modules:
  0.0 37.1 jit_solution(4172784827509453089)
XLA Ops:
  0.6 0.7 %select_bitcast_fusion = (f32[1,16,256]{2,1,0:T(8,128)S(1)}, f32[1,16,256]{2,1,0:T(8,128)S(1)}, f32[1,16,256]{2,1,0:T(8,128)S(1)}) fusion(f32[1,8,16,256]{3,2,1,0:T(8,128)} %param.3, pred[]{:T(512)S(6)} %eq.13, pred[]{:T(512)S(6)} %eq.14), kind=kLoop, calls=%fused_computation.4 | loop fusion | flops 12288 | bytes 81922 | tf_op jit(solution)/shard_map/jit(_where)/select_n | solution.py:196
  1.4 0.0 copy-start
  1.4 2.0 %collective-permute-start.2 = (f32[1,16,256]{2,1,0:T(8,128)S(1)}, f32[1,16,256]{2,1,0:T(8,128)S(1)}, u32[]{:S(2)}, u32[]{:S(2)}) collective-permute-start(f32[1,16,256]{2,1,0:T(8,128)S(1)} %get-tuple-element.26), channel_id=1, source_target_pairs={{0,8},{32,40},{64,72},{96,104},{128,136},{160,168},{192,200},{224,... | collective-permute-start | bytes 49160 | tf_op jit(solution)/shard_map/ppermute | solution.py:204
  3.4 6.0 %collective-permute-start = (f32[1,16,256]{2,1,0:T(8,128)S(1)}, f32[1,16,256]{2,1,0:T(8,128)S(1)}, u32[]{:S(2)}, u32[]{:S(2)}) collective-permute-start(f32[1,16,256]{2,1,0:T(8,128)S(1)} %get-tuple-element.27), channel_id=1, source_target_pairs={{8,16},{40,48},{72,80},{104,112},{136,144},{168,176},{200,208},{23... | collective-permute-start | bytes 49160 | tf_op jit(solution)/shard_map/ppermute | solution.py:204
  9.5 0.7 %collective-permute-start.1 = (f32[1,16,256]{2,1,0:T(8,128)S(1)}, f32[1,16,256]{2,1,0:T(8,128)S(1)}, u32[]{:S(2)}, u32[]{:S(2)}) collective-permute-start(f32[1,16,256]{2,1,0:T(8,128)S(1)} %get-tuple-element.28), channel_id=1, source_target_pairs={{16,24},{48,56},{80,88},{112,120},{144,152},{176,184},{208,216},{2... | collective-permute-start | bytes 49160 | tf_op jit(solution)/shard_map/ppermute | solution.py:204
  10.1 0.9 %fusion = (f32[8,1,256]{2,1,0:T(1,128)S(1)}, f32[8,1,256]{2,1,0:T(1,128)S(1)}) fusion(f32[8,16,256]{2,1,0:T(8,128)} %bitcast.9), kind=kLoop, calls=%fused_computation.11 | loop fusion | bytes 32768 | tf_op jit(solution)/shard_map/slice | solution.py:226
  11.0 0.0 collective-permute-done.2.row_01
  11.1 0.1 collective-permute-done.row_12
  11.2 0.0 collective-permute-done.1.row_23
  11.2 0.7 %collective-permute-start.4 = (f32[10,1,256]{2,1,0:T(1,128)S(1)}, f32[10,1,256]{2,1,0:T(1,128)S(1)}, u32[]{:S(2)}, u32[]{:S(2)}) collective-permute-start(f32[10,1,256]{2,1,0:T(1,128)S(1)} %pad_maximum_fusion.2), channel_id=1, source_target_pairs={{1,32},{2,33},{3,34},{4,35},{5,36},{6,37},{7,38},{9,40},{10,41},{1... | collective-permute-start | bytes 30728 | tf_op jit(solution)/shard_map/ppermute | solution.py:230
  11.9 0.7 %collective-permute-start.3 = (f32[10,1,256]{2,1,0:T(1,128)S(1)}, f32[10,1,256]{2,1,0:T(1,128)S(1)}, u32[]{:S(2)}, u32[]{:S(2)}) collective-permute-start(f32[10,1,256]{2,1,0:T(1,128)S(1)} %pad_maximum_fusion.1), channel_id=1, source_target_pairs={{0,33},{1,34},{2,35},{3,36},{4,37},{5,38},{6,39},{8,41},{9,42},{10... | collective-permute-start | bytes 30728 | tf_op jit(solution)/shard_map/ppermute | solution.py:229
  12.6 0.0 collective-permute-done.4
  12.6 0.0 collective-permute-done.3
  12.6 0.7 %collective-permute-start.5 = (f32[20,1,256]{2,1,0:T(1,128)S(1)}, f32[20,1,256]{2,1,0:T(1,128)S(1)}, u32[]{:S(2)}, u32[]{:S(2)}) collective-permute-start(f32[20,1,256]{2,1,0:T(1,128)S(1)} %pad_maximum_fusion), channel_id=1, source_target_pairs={{32,0},{33,1},{34,2},{35,3},{36,4},{37,5},{38,6},{39,7},{40,8},{41... | collective-permute-start | bytes 61448 | tf_op jit(solution)/shard_map/ppermute | solution.py:231
  13.3 0.0 copy-start.1
  13.3 0.0 copy-start.2
  13.3 0.7 %copy-done.1 = s32[1,8,16]{2,1,0:T(8,128)S(1)} copy-done((s32[1,8,16]{2,1,0:T(8,128)S(1)}, s32[1,8,16]{2,1,0:T(8,128)}, u32[]{:S(2)}) %copy-start.1) | copy-done | bytes 536
  14.0 0.1 reshape.78.dip_il
  14.1 0.0 copy-done.2
  14.1 0.1 reshape.79.dip_xl
  14.2 0.0 collective-permute-done.5.cols
  14.2 0.0 copy-done
  14.2 0.7 %collective-permute-start.8 = (f32[256,128]{1,0:T(8,128)S(1)}, f32[256,128]{1,0:T(8,128)S(1)}, u32[]{:S(2)}, u32[]{:S(2)}) collective-permute-start(f32[256,128]{1,0:T(8,128)S(1)} %get-tuple-element.13.attr_head), channel_id=1, source_target_pairs={{0,256},{1,257},{2,258},{3,259},{4,260},{5,261},{6,262},{7,263},{8... | collective-permute-start | bytes 393224 | tf_op jit(solution)/shard_map/ppermute | solution.py:233
  14.9 0.7 %collective-permute-start.7 = (f32[256,128]{1,0:T(8,128)S(1)}, f32[256,128]{1,0:T(8,128)S(1)}, u32[]{:S(2)}, u32[]{:S(2)}) collective-permute-start(f32[256,128]{1,0:T(8,128)S(1)} %get-tuple-element.13.attr_head), channel_id=1, source_target_pairs={{0,384},{1,385},{2,386},{3,387},{4,388},{5,389},{6,390},{7,391},{8... | collective-permute-start | bytes 393224 | tf_op jit(solution)/shard_map/ppermute | solution.py:233
  15.6 0.7 %collective-permute-start.6 = (f32[256,128]{1,0:T(8,128)S(1)}, f32[256,128]{1,0:T(8,128)S(1)}, u32[]{:S(2)}, u32[]{:S(2)}) collective-permute-start(f32[256,128]{1,0:T(8,128)S(1)} %get-tuple-element.13.attr_head), channel_id=1, source_target_pairs={{0,128},{1,129},{2,130},{3,131},{4,132},{5,133},{6,134},{7,135},{8... | collective-permute-start | bytes 393224 | tf_op jit(solution)/shard_map/ppermute | solution.py:233
  16.3 0.7 %collective-permute-start.10 = (f32[10,1,256]{2,1,0:T(1,128)S(1)}, f32[10,1,256]{2,1,0:T(1,128)S(1)}, u32[]{:S(2)}, u32[]{:S(2)}) collective-permute-start(f32[10,1,256]{2,1,0:T(1,128)S(1)} %get-tuple-element.31), channel_id=1, source_target_pairs={{33,34},{35,36},{37,38},{65,66},{67,68},{69,70},{97,98},{99,100},{... | collective-permute-start | bytes 30728 | tf_op jit(solution)/shard_map/ppermute | solution.py:204
  16.9 6.1 %collective-permute-start.9 = (f32[10,1,256]{2,1,0:T(1,128)S(1)}, f32[10,1,256]{2,1,0:T(1,128)S(1)}, u32[]{:S(2)}, u32[]{:S(2)}) collective-permute-start(f32[10,1,256]{2,1,0:T(1,128)S(1)} %get-tuple-element.32), channel_id=1, source_target_pairs={{32,33},{34,35},{36,37},{38,39},{64,65},{66,67},{68,69},{70,71},{9... | collective-permute-start | bytes 30728 | tf_op jit(solution)/shard_map/ppermute | solution.py:204
  23.1 0.0 collective-permute-done.10.col_b
  23.1 1.6 %collective-permute-done.9.col_a = f32[10,1,256]{2,1,0:T(1,128)S(1)} collective-permute-done((f32[10,1,256]{2,1,0:T(1,128)S(1)}, f32[10,1,256]{2,1,0:T(1,128)S(1)}, u32[]{:S(2)}, u32[]{:S(2)}) %collective-permute-start.9) | collective-permute-done | bytes 10272 | tf_op jit(solution)/shard_map/ppermute | solution.py:204
  24.7 0.0 collective-permute-done.8
  24.7 0.0 collective-permute-done.7
  24.7 0.0 collective-permute-done.6
  24.8 0.7 %collective-permute-start.13 = (f32[256,128]{1,0:T(8,128)S(1)}, f32[256,128]{1,0:T(8,128)S(1)}, u32[]{:S(2)}, u32[]{:S(2)}) collective-permute-start(f32[256,128]{1,0:T(8,128)S(1)} %add_select_fusion.held), channel_id=1, source_target_pairs={{0,96},{128,224},{256,352},{384,480},{1,97},{129,225},{257,353},{3... | collective-permute-start | bytes 393224 | tf_op jit(solution)/shard_map/ppermute | solution.py:239
  25.4 1.3 %collective-permute-start.12 = (f32[256,128]{1,0:T(8,128)S(1)}, f32[256,128]{1,0:T(8,128)S(1)}, u32[]{:S(2)}, u32[]{:S(2)}) collective-permute-start(f32[256,128]{1,0:T(8,128)S(1)} %add_select_fusion.held), channel_id=1, source_target_pairs={{0,64},{128,192},{256,320},{384,448},{1,65},{129,193},{257,321},{3... | collective-permute-start | bytes 393224 | tf_op jit(solution)/shard_map/ppermute | solution.py:239
  26.7 0.7 %collective-permute-start.11 = (f32[256,128]{1,0:T(8,128)S(1)}, f32[256,128]{1,0:T(8,128)S(1)}, u32[]{:S(2)}, u32[]{:S(2)}) collective-permute-start(f32[256,128]{1,0:T(8,128)S(1)} %add_select_fusion.held), channel_id=1, source_target_pairs={{0,32},{128,160},{256,288},{384,416},{1,33},{129,161},{257,289},{3... | collective-permute-start | bytes 393224 | tf_op jit(solution)/shard_map/ppermute | solution.py:239
  27.4 1.5 %tail.1 = (f32[8,16,256]{2,1,0:T(8,128)}, f32[256,128]{1,0:T(8,128)S(1)}) custom-call(f32[8,16,256]{2,1,0:T(8,128)S(1)} %bitcast.11, f32[1,16,256]{2,1,0:T(8,128)S(1)} %collective-permute-done.row_12, f32[1,16,256]{2,1,0:T(8,128)S(1)} %collective-permute-done.1.row_23, f32[1,16,256]{2,1,0:T(8,128)S(1)} %collective-permute-done.2.row_01, ...), custom_call_target="tpu_custom_call" | custom-call | tf_op jit(solution)/shard_map/tail/pallas_call | solution.py:159
  28.9 0.0 collective-permute-done.13.far1
  28.9 7.0 %collective-permute-done.12.far2 = f32[256,128]{1,0:T(8,128)S(1)} collective-permute-done((f32[256,128]{1,0:T(8,128)S(1)}, f32[256,128]{1,0:T(8,128)S(1)}, u32[]{:S(2)}, u32[]{:S(2)}) %collective-permute-start.12) | collective-permute-done | bytes 131104 | tf_op jit(solution)/shard_map/ppermute | solution.py:239
  35.9 0.0 collective-permute-done.11.far3
  35.9 1.2 %correlate.1 = f32[8,16,264]{2,1,0:T(8,128)} custom-call(f32[256,128]{1,0:T(8,128)S(1)} %get-tuple-element.20.mon, f32[256,128]{1,0:T(8,128)S(1)} %add_select_fusion.held, f32[256,128]{1,0:T(8,128)S(1)} %collective-permute-done.11.far3, f32[256,128]{1,0:T(8,128)S(1)} %collective-permute-done.12.far2, f32[256,128]{1,0:T(8,128)S(1)} %collective-permute-done.13.far1), custom_call_target="tpu_custom_call" | custom-call | tf_op jit(solution)/shard_map/correlate/pallas_call | solution.py:180
  (8 shorter events, 0.1 us)
Async XLA Ops:
  1.4 12.8 %copy-start = (f32[1,8,16,256]{3,2,1,0:T(8,128)S(1)}, f32[1,8,16,256]{3,2,1,0:T(8,128)}, u32[]{:S(2)}) copy-start(f32[1,8,16,256]{3,2,1,0:T(8,128)} %param.3) | copy-start | bytes 393220
  1.4 9.7 %collective-permute-start.2 = (f32[1,16,256]{2,1,0:T(8,128)S(1)}, f32[1,16,256]{2,1,0:T(8,128)S(1)}, u32[]{:S(2)}, u32[]{:S(2)}) collective-permute-start(f32[1,16,256]{2,1,0:T(8,128)S(1)} %get-tuple-element.26), channel_id=1, source_target_pairs={{0,8},{32,40},{64,72},{96,104},{128,136},{160,168},{192,200},{224,... | collective-permute-start | bytes 49160 | tf_op jit(solution)/shard_map/ppermute | solution.py:204
  3.4 7.8 %collective-permute-start = (f32[1,16,256]{2,1,0:T(8,128)S(1)}, f32[1,16,256]{2,1,0:T(8,128)S(1)}, u32[]{:S(2)}, u32[]{:S(2)}) collective-permute-start(f32[1,16,256]{2,1,0:T(8,128)S(1)} %get-tuple-element.27), channel_id=1, source_target_pairs={{8,16},{40,48},{72,80},{104,112},{136,144},{168,176},{200,208},{23... | collective-permute-start | bytes 49160 | tf_op jit(solution)/shard_map/ppermute | solution.py:204
  9.5 1.7 %collective-permute-start.1 = (f32[1,16,256]{2,1,0:T(8,128)S(1)}, f32[1,16,256]{2,1,0:T(8,128)S(1)}, u32[]{:S(2)}, u32[]{:S(2)}) collective-permute-start(f32[1,16,256]{2,1,0:T(8,128)S(1)} %get-tuple-element.28), channel_id=1, source_target_pairs={{16,24},{48,56},{80,88},{112,120},{144,152},{176,184},{208,216},{2... | collective-permute-start | bytes 49160 | tf_op jit(solution)/shard_map/ppermute | solution.py:204
  11.2 1.4 %collective-permute-start.4 = (f32[10,1,256]{2,1,0:T(1,128)S(1)}, f32[10,1,256]{2,1,0:T(1,128)S(1)}, u32[]{:S(2)}, u32[]{:S(2)}) collective-permute-start(f32[10,1,256]{2,1,0:T(1,128)S(1)} %pad_maximum_fusion.2), channel_id=1, source_target_pairs={{1,32},{2,33},{3,34},{4,35},{5,36},{6,37},{7,38},{9,40},{10,41},{1... | collective-permute-start | bytes 30728 | tf_op jit(solution)/shard_map/ppermute | solution.py:230
  11.9 0.7 %collective-permute-start.3 = (f32[10,1,256]{2,1,0:T(1,128)S(1)}, f32[10,1,256]{2,1,0:T(1,128)S(1)}, u32[]{:S(2)}, u32[]{:S(2)}) collective-permute-start(f32[10,1,256]{2,1,0:T(1,128)S(1)} %pad_maximum_fusion.1), channel_id=1, source_target_pairs={{0,33},{1,34},{2,35},{3,36},{4,37},{5,38},{6,39},{8,41},{9,42},{10... | collective-permute-start | bytes 30728 | tf_op jit(solution)/shard_map/ppermute | solution.py:229
  12.6 1.5 %collective-permute-start.5 = (f32[20,1,256]{2,1,0:T(1,128)S(1)}, f32[20,1,256]{2,1,0:T(1,128)S(1)}, u32[]{:S(2)}, u32[]{:S(2)}) collective-permute-start(f32[20,1,256]{2,1,0:T(1,128)S(1)} %pad_maximum_fusion), channel_id=1, source_target_pairs={{32,0},{33,1},{34,2},{35,3},{36,4},{37,5},{38,6},{39,7},{40,8},{41... | collective-permute-start | bytes 61448 | tf_op jit(solution)/shard_map/ppermute | solution.py:231
  13.3 0.7 %copy-start.1 = (s32[1,8,16]{2,1,0:T(8,128)S(1)}, s32[1,8,16]{2,1,0:T(8,128)}, u32[]{:S(2)}) copy-start(s32[1,8,16]{2,1,0:T(8,128)} %param.4) | copy-start | bytes 1540
  13.3 0.8 %copy-start.2 = (s32[1,8,16]{2,1,0:T(8,128)S(1)}, s32[1,8,16]{2,1,0:T(8,128)}, u32[]{:S(2)}) copy-start(s32[1,8,16]{2,1,0:T(8,128)} %param.5) | copy-start | bytes 1540
  14.2 10.5 %collective-permute-start.8 = (f32[256,128]{1,0:T(8,128)S(1)}, f32[256,128]{1,0:T(8,128)S(1)}, u32[]{:S(2)}, u32[]{:S(2)}) collective-permute-start(f32[256,128]{1,0:T(8,128)S(1)} %get-tuple-element.13.attr_head), channel_id=1, source_target_pairs={{0,256},{1,257},{2,258},{3,259},{4,260},{5,261},{6,262},{7,263},{8... | collective-permute-start | bytes 393224 | tf_op jit(solution)/shard_map/ppermute | solution.py:233
  14.9 9.8 %collective-permute-start.7 = (f32[256,128]{1,0:T(8,128)S(1)}, f32[256,128]{1,0:T(8,128)S(1)}, u32[]{:S(2)}, u32[]{:S(2)}) collective-permute-start(f32[256,128]{1,0:T(8,128)S(1)} %get-tuple-element.13.attr_head), channel_id=1, source_target_pairs={{0,384},{1,385},{2,386},{3,387},{4,388},{5,389},{6,390},{7,391},{8... | collective-permute-start | bytes 393224 | tf_op jit(solution)/shard_map/ppermute | solution.py:233
  15.6 9.2 %collective-permute-start.6 = (f32[256,128]{1,0:T(8,128)S(1)}, f32[256,128]{1,0:T(8,128)S(1)}, u32[]{:S(2)}, u32[]{:S(2)}) collective-permute-start(f32[256,128]{1,0:T(8,128)S(1)} %get-tuple-element.13.attr_head), channel_id=1, source_target_pairs={{0,128},{1,129},{2,130},{3,131},{4,132},{5,133},{6,134},{7,135},{8... | collective-permute-start | bytes 393224 | tf_op jit(solution)/shard_map/ppermute | solution.py:233
  16.3 6.8 %collective-permute-start.10 = (f32[10,1,256]{2,1,0:T(1,128)S(1)}, f32[10,1,256]{2,1,0:T(1,128)S(1)}, u32[]{:S(2)}, u32[]{:S(2)}) collective-permute-start(f32[10,1,256]{2,1,0:T(1,128)S(1)} %get-tuple-element.31), channel_id=1, source_target_pairs={{33,34},{35,36},{37,38},{65,66},{67,68},{69,70},{97,98},{99,100},{... | collective-permute-start | bytes 30728 | tf_op jit(solution)/shard_map/ppermute | solution.py:204
  16.9 7.8 %collective-permute-start.9 = (f32[10,1,256]{2,1,0:T(1,128)S(1)}, f32[10,1,256]{2,1,0:T(1,128)S(1)}, u32[]{:S(2)}, u32[]{:S(2)}) collective-permute-start(f32[10,1,256]{2,1,0:T(1,128)S(1)} %get-tuple-element.32), channel_id=1, source_target_pairs={{32,33},{34,35},{36,37},{38,39},{64,65},{66,67},{68,69},{70,71},{9... | collective-permute-start | bytes 30728 | tf_op jit(solution)/shard_map/ppermute | solution.py:204
  24.8 4.2 %collective-permute-start.13 = (f32[256,128]{1,0:T(8,128)S(1)}, f32[256,128]{1,0:T(8,128)S(1)}, u32[]{:S(2)}, u32[]{:S(2)}) collective-permute-start(f32[256,128]{1,0:T(8,128)S(1)} %add_select_fusion.held), channel_id=1, source_target_pairs={{0,96},{128,224},{256,352},{384,480},{1,97},{129,225},{257,353},{3... | collective-permute-start | bytes 393224 | tf_op jit(solution)/shard_map/ppermute | solution.py:239
  25.4 10.5 %collective-permute-start.12 = (f32[256,128]{1,0:T(8,128)S(1)}, f32[256,128]{1,0:T(8,128)S(1)}, u32[]{:S(2)}, u32[]{:S(2)}) collective-permute-start(f32[256,128]{1,0:T(8,128)S(1)} %add_select_fusion.held), channel_id=1, source_target_pairs={{0,64},{128,192},{256,320},{384,448},{1,65},{129,193},{257,321},{3... | collective-permute-start | bytes 393224 | tf_op jit(solution)/shard_map/ppermute | solution.py:239
  26.7 9.2 %collective-permute-start.11 = (f32[256,128]{1,0:T(8,128)S(1)}, f32[256,128]{1,0:T(8,128)S(1)}, u32[]{:S(2)}, u32[]{:S(2)}) collective-permute-start(f32[256,128]{1,0:T(8,128)S(1)} %add_select_fusion.held), channel_id=1, source_target_pairs={{0,32},{128,160},{256,288},{384,416},{1,33},{129,161},{257,289},{3... | collective-permute-start | bytes 393224 | tf_op jit(solution)/shard_map/ppermute | solution.py:239

commit v15 on v12

--- a/solution.py
+++ b/solution.py
@@ -32,7 +32,7 @@
     @pl.when(lax.axis_index("vintage") == 0)
     def _():
         edges = cols[0:ROWS + 2], cols[ROWS + 2:]
-        attr_body(tile, row_12, row_23, row_01, edges, dip_il, dip_xl, *rest)
+        attr_body(tile, row_12, row_23, row_01, edges, dip_il, dip_xl, *rest[:-1])
 
 
 def tail_kernel(tile, row_12, row_23, row_01, col_a, col_b, dip_il, dip_xl, semb_head, attr_head,
@@ -41,18 +41,19 @@
 
     @pl.when(head)
     def _():
-        semb_out[...] = semb_head[...]
+        semb_out[...] = semb_head[...].T.reshape(ROWS, COLS, TIME_SAMPLES)
         attr_out[...] = attr_head[...]
 
     @pl.when(jnp.logical_not(head))
     def _():
         odd = lax.rem(lax.axis_index("xline"), 2) == 1
         edges = jnp.where(odd, col_a[...], col_b[...]), jnp.where(odd, col_b[...], col_a[...])
-        attr_body(tile, row_12, row_23, row_01, edges, dip_il, dip_xl, semb_out, attr_out, *scratch)
-
-
-def attr_body(tile, row_12, row_23, row_01, edges, dip_il, dip_xl, semb_out, attr_out,
-              rim, moved, inner, sums, three):
+        attr_body(tile, row_12, row_23, row_01, edges, dip_il, dip_xl, scratch[-1], attr_out, *scratch[:-1])
+        semb_out[...] = scratch[-1][...].T.reshape(ROWS, COLS, TIME_SAMPLES)
+
+
+def attr_body(tile, row_12, row_23, row_01, edges, dip_il, dip_xl, three, attr_out,
+              rim, moved, inner, sums):
     odd_row = lax.rem(lax.axis_index("inline"), 2) == 1
     rim[1:ROWS + 1, 1:COLS + 1, :] = tile[...]
     row_a, row_b = row_01[0] + row_23[0], row_12[0]
@@ -98,7 +99,6 @@
         semb = numer / (9.0 * denom + EPS)
         three[pl.ds(r, 8), :] = semb
         attr_out[pl.ds(r, 8), :] = semb * sums[0, pl.ds(r + RT, 8), :] * (1.0 / 9.0)
-    semb_out[...] = three[...].T.reshape(ROWS, COLS, TIME_SAMPLES)
 
 
 def pair_sum(x, y, half, low):
@@ -151,11 +151,11 @@
     return [pl.BlockSpec(memory_space=pltpu.VMEM)] * n
 
 
-def attributes(kernel, name, *args):
+def attributes(kernel, name, semb_shape, *args):
     return pl.pallas_call(
         kernel,
         out_shape=(
-            jax.ShapeDtypeStruct((ROWS, COLS, TIME_SAMPLES), jnp.float32),
+            jax.ShapeDtypeStruct(semb_shape, jnp.float32),
             jax.ShapeDtypeStruct((TIME_SAMPLES, TRACES), jnp.float32),
         ),
         in_specs=vmem(len(args)),
@@ -225,7 +225,7 @@
     left = lax.ppermute(last, both, [(x, width + x + 1) for x in range(width - 1)])
     right = lax.ppermute(first, both, [(x + 1, width + x) for x in range(width - 1)])
     cols = lax.ppermute(jnp.concatenate([left, right], axis=0), "vintage", [(1, 0)])
-    semb0, attr0 = attributes(head_kernel, "head", tile, *rows, cols, *dips)
+    semb0, attr0 = attributes(head_kernel, "head", (TIME_SAMPLES, TRACES), tile, *rows, cols, *dips)
     got = [lax.ppermute(attr0, "vintage", [(0, k)]) for k in (4, 12, 8)]
     first, last = lax.optimization_barrier((first, last, attr0))[:2]
     cols = swap(pair_sends(first, last, "xline"), "xline", range(1, vintages), across)
@@ -233,7 +233,7 @@
     got, cols = joined[:3], joined[3:]
     held = jnp.where(lax.axis_index("vintage") == 0, attr0, got[0] + got[1] + got[2])
     far = [lax.ppermute(held, "vintage", [(s, to[n]) for s, to in FANOUT.items()]) for n in (2, 1, 0)]
-    semb, attr = attributes(tail_kernel, "tail", tile, *rows, *cols, *dips, semb0, attr0)
+    semb, attr = attributes(tail_kernel, "tail", (ROWS, COLS, TIME_SAMPLES), tile, *rows, *cols, *dips, semb0, attr0)
     correl = correlate(attr, held, far)
     return (semb[None], correl[None])
 

time: 37.6 us -> 37.6 us (level)
  no operation moved by 1% of the time
where the time goes in v15:
time: 37.6 us; the launch traced here: 37.1 us
  starting transfers between devices  22.2 us (59%)
  waiting for transfers between devices  8.7 us (23%)
  Pallas kernels  2.73 us (7%)
  local copies, waits for them, and re-layouts  1.73 us (5%)
  between operations  0.89 us (2%)
  other arithmetic  0.84 us (2%)
    ppermute x5, starting transfers between devices, swap(): lax.ppermute(sends[n], ('vintage', axis), low + [(b, a) for a, b in low])  15.5 us
    ppermute x3, waiting for transfers between devices, per_device(): lax.ppermute(held, 'vintage', [(s, to[n]) for s, to in FANOUT.items()])  6.92 us
    ppermute x3, starting transfers between devices, per_device(): lax.ppermute(held, 'vintage', [(s, to[n]) for s, to in FANOUT.items()])  2.63 us
    ppermute x3, starting transfers between devices, per_device(): got = [lax.ppermute(attr0, 'vintage', [(0, k)]) for k in (4, 12, 8)]  2.01 us
    ppermute x5, waiting for transfers between devices, swap(): lax.ppermute(sends[n], ('vintage', axis), low + [(b, a) for a, b in low])  1.76 us
    pallas_call x2, Pallas kernels, attributes(): pl.pallas_call(kernel, out_shape=(jax.ShapeDtypeStruct(semb_shape, jnp.fl...  1.53 us
    pallas_call x1, Pallas kernels, correlate(): pl.pallas_call(correl_kernel, out_shape=jax.ShapeDtypeStruct((ROWS, COLS,...  1.2 us
    slice x1, local copies, waits for them, and re-layouts, per_device(): first, last = edge_columns((tile[:, :1], tile[:, -1:]), rows)  0.89 us
  transfers between devices with their start and end apart: 14, of which 3 were waited for; matrix products, arithmetic and copies ran while one was open for 3% of the time, Pallas kernels for 4%

profile of v15, /device:TPU:152, one launch (start us, length us, event | category | flops | bytes accessed | tf_op | source)
XLA Modules:
  0.0 37.1 jit_solution(109306841692481039)
XLA Ops:
  0.6 0.7 %select_bitcast_fusion = (f32[1,16,256]{2,1,0:T(8,128)S(1)}, f32[1,16,256]{2,1,0:T(8,128)S(1)}, f32[1,16,256]{2,1,0:T(8,128)S(1)}) fusion(f32[1,8,16,256]{3,2,1,0:T(8,128)} %param.3, pred[]{:T(512)S(6)} %eq.13, pred[]{:T(512)S(6)} %eq.14), kind=kLoop, calls=%fused_computation.4 | loop fusion | flops 12288 | bytes 81922 | tf_op jit(solution)/shard_map/jit(_where)/select_n | solution.py:192
  1.4 0.0 copy-start
  1.4 2.0 %collective-permute-start.2 = (f32[1,16,256]{2,1,0:T(8,128)S(1)}, f32[1,16,256]{2,1,0:T(8,128)S(1)}, u32[]{:S(2)}, u32[]{:S(2)}) collective-permute-start(f32[1,16,256]{2,1,0:T(8,128)S(1)} %get-tuple-element.26), channel_id=1, source_target_pairs={{0,8},{32,40},{64,72},{96,104},{128,136},{160,168},{192,200},{224,... | collective-permute-start | bytes 49160 | tf_op jit(solution)/shard_map/ppermute | solution.py:200
  3.4 6.0 %collective-permute-start = (f32[1,16,256]{2,1,0:T(8,128)S(1)}, f32[1,16,256]{2,1,0:T(8,128)S(1)}, u32[]{:S(2)}, u32[]{:S(2)}) collective-permute-start(f32[1,16,256]{2,1,0:T(8,128)S(1)} %get-tuple-element.27), channel_id=1, source_target_pairs={{8,16},{40,48},{72,80},{104,112},{136,144},{168,176},{200,208},{23... | collective-permute-start | bytes 49160 | tf_op jit(solution)/shard_map/ppermute | solution.py:200
  9.5 0.7 %collective-permute-start.1 = (f32[1,16,256]{2,1,0:T(8,128)S(1)}, f32[1,16,256]{2,1,0:T(8,128)S(1)}, u32[]{:S(2)}, u32[]{:S(2)}) collective-permute-start(f32[1,16,256]{2,1,0:T(8,128)S(1)} %get-tuple-element.28), channel_id=1, source_target_pairs={{16,24},{48,56},{80,88},{112,120},{144,152},{176,184},{208,216},{2... | collective-permute-start | bytes 49160 | tf_op jit(solution)/shard_map/ppermute | solution.py:200
  10.1 0.9 %fusion = (f32[8,1,256]{2,1,0:T(1,128)S(1)}, f32[8,1,256]{2,1,0:T(1,128)S(1)}) fusion(f32[8,16,256]{2,1,0:T(8,128)} %bitcast.9), kind=kLoop, calls=%fused_computation.11 | loop fusion | bytes 32768 | tf_op jit(solution)/shard_map/slice | solution.py:222
  11.0 0.0 collective-permute-done.2.row_01
  11.1 0.1 collective-permute-done.row_12
  11.2 0.0 collective-permute-done.1.row_23
  11.2 0.7 %collective-permute-start.4 = (f32[10,1,256]{2,1,0:T(1,128)S(1)}, f32[10,1,256]{2,1,0:T(1,128)S(1)}, u32[]{:S(2)}, u32[]{:S(2)}) collective-permute-start(f32[10,1,256]{2,1,0:T(1,128)S(1)} %pad_maximum_fusion.2), channel_id=1, source_target_pairs={{1,32},{2,33},{3,34},{4,35},{5,36},{6,37},{7,38},{9,40},{10,41},{1... | collective-permute-start | bytes 30728 | tf_op jit(solution)/shard_map/ppermute | solution.py:226
  11.9 0.7 %collective-permute-start.3 = (f32[10,1,256]{2,1,0:T(1,128)S(1)}, f32[10,1,256]{2,1,0:T(1,128)S(1)}, u32[]{:S(2)}, u32[]{:S(2)}) collective-permute-start(f32[10,1,256]{2,1,0:T(1,128)S(1)} %pad_maximum_fusion.1), channel_id=1, source_target_pairs={{0,33},{1,34},{2,35},{3,36},{4,37},{5,38},{6,39},{8,41},{9,42},{10... | collective-permute-start | bytes 30728 | tf_op jit(solution)/shard_map/ppermute | solution.py:225
  12.6 0.0 collective-permute-done.4
  12.6 0.0 collective-permute-done.3
  12.6 0.7 %collective-permute-start.5 = (f32[20,1,256]{2,1,0:T(1,128)S(1)}, f32[20,1,256]{2,1,0:T(1,128)S(1)}, u32[]{:S(2)}, u32[]{:S(2)}) collective-permute-start(f32[20,1,256]{2,1,0:T(1,128)S(1)} %pad_maximum_fusion), channel_id=1, source_target_pairs={{32,0},{33,1},{34,2},{35,3},{36,4},{37,5},{38,6},{39,7},{40,8},{41... | collective-permute-start | bytes 61448 | tf_op jit(solution)/shard_map/ppermute | solution.py:227
  13.3 0.0 copy-start.1
  13.3 0.0 copy-start.2
  13.3 0.7 %copy-done.1 = s32[1,8,16]{2,1,0:T(8,128)S(1)} copy-done((s32[1,8,16]{2,1,0:T(8,128)S(1)}, s32[1,8,16]{2,1,0:T(8,128)}, u32[]{:S(2)}) %copy-start.1) | copy-done | bytes 536
  14.0 0.1 reshape.78.dip_il
  14.1 0.0 copy-done.2
  14.1 0.1 reshape.79.dip_xl
  14.2 0.0 collective-permute-done.5.cols
  14.2 0.0 copy-done
  14.2 0.7 %collective-permute-start.8 = (f32[256,128]{1,0:T(8,128)S(1)}, f32[256,128]{1,0:T(8,128)S(1)}, u32[]{:S(2)}, u32[]{:S(2)}) collective-permute-start(f32[256,128]{1,0:T(8,128)S(1)} %get-tuple-element.13.attr_head), channel_id=1, source_target_pairs={{0,256},{1,257},{2,258},{3,259},{4,260},{5,261},{6,262},{7,263},{8... | collective-permute-start | bytes 393224 | tf_op jit(solution)/shard_map/ppermute | solution.py:229
  14.9 0.7 %collective-permute-start.7 = (f32[256,128]{1,0:T(8,128)S(1)}, f32[256,128]{1,0:T(8,128)S(1)}, u32[]{:S(2)}, u32[]{:S(2)}) collective-permute-start(f32[256,128]{1,0:T(8,128)S(1)} %get-tuple-element.13.attr_head), channel_id=1, source_target_pairs={{0,384},{1,385},{2,386},{3,387},{4,388},{5,389},{6,390},{7,391},{8... | collective-permute-start | bytes 393224 | tf_op jit(solution)/shard_map/ppermute | solution.py:229
  15.6 0.7 %collective-permute-start.6 = (f32[256,128]{1,0:T(8,128)S(1)}, f32[256,128]{1,0:T(8,128)S(1)}, u32[]{:S(2)}, u32[]{:S(2)}) collective-permute-start(f32[256,128]{1,0:T(8,128)S(1)} %get-tuple-element.13.attr_head), channel_id=1, source_target_pairs={{0,128},{1,129},{2,130},{3,131},{4,132},{5,133},{6,134},{7,135},{8... | collective-permute-start | bytes 393224 | tf_op jit(solution)/shard_map/ppermute | solution.py:229
  16.3 0.7 %collective-permute-start.10 = (f32[10,1,256]{2,1,0:T(1,128)S(1)}, f32[10,1,256]{2,1,0:T(1,128)S(1)}, u32[]{:S(2)}, u32[]{:S(2)}) collective-permute-start(f32[10,1,256]{2,1,0:T(1,128)S(1)} %get-tuple-element.31), channel_id=1, source_target_pairs={{33,34},{35,36},{37,38},{65,66},{67,68},{69,70},{97,98},{99,100},{... | collective-permute-start | bytes 30728 | tf_op jit(solution)/shard_map/ppermute | solution.py:200
  16.9 6.1 %collective-permute-start.9 = (f32[10,1,256]{2,1,0:T(1,128)S(1)}, f32[10,1,256]{2,1,0:T(1,128)S(1)}, u32[]{:S(2)}, u32[]{:S(2)}) collective-permute-start(f32[10,1,256]{2,1,0:T(1,128)S(1)} %get-tuple-element.32), channel_id=1, source_target_pairs={{32,33},{34,35},{36,37},{38,39},{64,65},{66,67},{68,69},{70,71},{9... | collective-permute-start | bytes 30728 | tf_op jit(solution)/shard_map/ppermute | solution.py:200
  23.1 0.0 collective-permute-done.10.col_b
  23.1 1.6 %collective-permute-done.9.col_a = f32[10,1,256]{2,1,0:T(1,128)S(1)} collective-permute-done((f32[10,1,256]{2,1,0:T(1,128)S(1)}, f32[10,1,256]{2,1,0:T(1,128)S(1)}, u32[]{:S(2)}, u32[]{:S(2)}) %collective-permute-start.9) | collective-permute-done | bytes 10272 | tf_op jit(solution)/shard_map/ppermute | solution.py:200
  24.7 0.0 collective-permute-done.8
  24.7 0.0 collective-permute-done.7
  24.7 0.0 collective-permute-done.6
  24.8 0.7 %collective-permute-start.13 = (f32[256,128]{1,0:T(8,128)S(1)}, f32[256,128]{1,0:T(8,128)S(1)}, u32[]{:S(2)}, u32[]{:S(2)}) collective-permute-start(f32[256,128]{1,0:T(8,128)S(1)} %add_select_fusion.held), channel_id=1, source_target_pairs={{0,96},{128,224},{256,352},{384,480},{1,97},{129,225},{257,353},{3... | collective-permute-start | bytes 393224 | tf_op jit(solution)/shard_map/ppermute | solution.py:235
  25.4 1.3 %collective-permute-start.12 = (f32[256,128]{1,0:T(8,128)S(1)}, f32[256,128]{1,0:T(8,128)S(1)}, u32[]{:S(2)}, u32[]{:S(2)}) collective-permute-start(f32[256,128]{1,0:T(8,128)S(1)} %add_select_fusion.held), channel_id=1, source_target_pairs={{0,64},{128,192},{256,320},{384,448},{1,65},{129,193},{257,321},{3... | collective-permute-start | bytes 393224 | tf_op jit(solution)/shard_map/ppermute | solution.py:235
  26.7 0.7 %collective-permute-start.11 = (f32[256,128]{1,0:T(8,128)S(1)}, f32[256,128]{1,0:T(8,128)S(1)}, u32[]{:S(2)}, u32[]{:S(2)}) collective-permute-start(f32[256,128]{1,0:T(8,128)S(1)} %add_select_fusion.held), channel_id=1, source_target_pairs={{0,32},{128,160},{256,288},{384,416},{1,33},{129,161},{257,289},{3... | collective-permute-start | bytes 393224 | tf_op jit(solution)/shard_map/ppermute | solution.py:235
  27.4 1.5 %tail.1 = (f32[8,16,256]{2,1,0:T(8,128)}, f32[256,128]{1,0:T(8,128)S(1)}) custom-call(f32[8,16,256]{2,1,0:T(8,128)S(1)} %bitcast.11, f32[1,16,256]{2,1,0:T(8,128)S(1)} %collective-permute-done.row_12, f32[1,16,256]{2,1,0:T(8,128)S(1)} %collective-permute-done.1.row_23, f32[1,16,256]{2,1,0:T(8,128)S(1)} %collective-permute-done.2.row_01, ...), custom_call_target="tpu_custom_call" | custom-call | tf_op jit(solution)/shard_map/tail/pallas_call | solution.py:155
  28.9 0.0 collective-permute-done.13.far1
  28.9 6.9 %collective-permute-done.12.far2 = f32[256,128]{1,0:T(8,128)S(1)} collective-permute-done((f32[256,128]{1,0:T(8,128)S(1)}, f32[256,128]{1,0:T(8,128)S(1)}, u32[]{:S(2)}, u32[]{:S(2)}) %collective-permute-start.12) | collective-permute-done | bytes 131104 | tf_op jit(solution)/shard_map/ppermute | solution.py:235
  35.8 0.0 collective-permute-done.11.far3
  35.9 1.2 %correlate.1 = f32[8,16,264]{2,1,0:T(8,128)} custom-call(f32[256,128]{1,0:T(8,128)S(1)} %get-tuple-element.20.mon, f32[256,128]{1,0:T(8,128)S(1)} %add_select_fusion.held, f32[256,128]{1,0:T(8,128)S(1)} %collective-permute-done.11.far3, f32[256,128]{1,0:T(8,128)S(1)} %collective-permute-done.12.far2, f32[256,128]{1,0:T(8,128)S(1)} %collective-permute-done.13.far1), custom_call_target="tpu_custom_call" | custom-call | tf_op jit(solution)/shard_map/correlate/pallas_call | solution.py:176
  (8 shorter events, 0.1 us)
Async XLA Ops:
  1.4 12.8 %copy-start = (f32[1,8,16,256]{3,2,1,0:T(8,128)S(1)}, f32[1,8,16,256]{3,2,1,0:T(8,128)}, u32[]{:S(2)}) copy-start(f32[1,8,16,256]{3,2,1,0:T(8,128)} %param.3) | copy-start | bytes 393220
  1.4 9.7 %collective-permute-start.2 = (f32[1,16,256]{2,1,0:T(8,128)S(1)}, f32[1,16,256]{2,1,0:T(8,128)S(1)}, u32[]{:S(2)}, u32[]{:S(2)}) collective-permute-start(f32[1,16,256]{2,1,0:T(8,128)S(1)} %get-tuple-element.26), channel_id=1, source_target_pairs={{0,8},{32,40},{64,72},{96,104},{128,136},{160,168},{192,200},{224,... | collective-permute-start | bytes 49160 | tf_op jit(solution)/shard_map/ppermute | solution.py:200
  3.4 7.8 %collective-permute-start = (f32[1,16,256]{2,1,0:T(8,128)S(1)}, f32[1,16,256]{2,1,0:T(8,128)S(1)}, u32[]{:S(2)}, u32[]{:S(2)}) collective-permute-start(f32[1,16,256]{2,1,0:T(8,128)S(1)} %get-tuple-element.27), channel_id=1, source_target_pairs={{8,16},{40,48},{72,80},{104,112},{136,144},{168,176},{200,208},{23... | collective-permute-start | bytes 49160 | tf_op jit(solution)/shard_map/ppermute | solution.py:200
  9.5 1.7 %collective-permute-start.1 = (f32[1,16,256]{2,1,0:T(8,128)S(1)}, f32[1,16,256]{2,1,0:T(8,128)S(1)}, u32[]{:S(2)}, u32[]{:S(2)}) collective-permute-start(f32[1,16,256]{2,1,0:T(8,128)S(1)} %get-tuple-element.28), channel_id=1, source_target_pairs={{16,24},{48,56},{80,88},{112,120},{144,152},{176,184},{208,216},{2... | collective-permute-start | bytes 49160 | tf_op jit(solution)/shard_map/ppermute | solution.py:200
  11.2 1.4 %collective-permute-start.4 = (f32[10,1,256]{2,1,0:T(1,128)S(1)}, f32[10,1,256]{2,1,0:T(1,128)S(1)}, u32[]{:S(2)}, u32[]{:S(2)}) collective-permute-start(f32[10,1,256]{2,1,0:T(1,128)S(1)} %pad_maximum_fusion.2), channel_id=1, source_target_pairs={{1,32},{2,33},{3,34},{4,35},{5,36},{6,37},{7,38},{9,40},{10,41},{1... | collective-permute-start | bytes 30728 | tf_op jit(solution)/shard_map/ppermute | solution.py:226
  11.9 0.7 %collective-permute-start.3 = (f32[10,1,256]{2,1,0:T(1,128)S(1)}, f32[10,1,256]{2,1,0:T(1,128)S(1)}, u32[]{:S(2)}, u32[]{:S(2)}) collective-permute-start(f32[10,1,256]{2,1,0:T(1,128)S(1)} %pad_maximum_fusion.1), channel_id=1, source_target_pairs={{0,33},{1,34},{2,35},{3,36},{4,37},{5,38},{6,39},{8,41},{9,42},{10... | collective-permute-start | bytes 30728 | tf_op jit(solution)/shard_map/ppermute | solution.py:225
  12.6 1.5 %collective-permute-start.5 = (f32[20,1,256]{2,1,0:T(1,128)S(1)}, f32[20,1,256]{2,1,0:T(1,128)S(1)}, u32[]{:S(2)}, u32[]{:S(2)}) collective-permute-start(f32[20,1,256]{2,1,0:T(1,128)S(1)} %pad_maximum_fusion), channel_id=1, source_target_pairs={{32,0},{33,1},{34,2},{35,3},{36,4},{37,5},{38,6},{39,7},{40,8},{41... | collective-permute-start | bytes 61448 | tf_op jit(solution)/shard_map/ppermute | solution.py:227
  13.3 0.7 %copy-start.1 = (s32[1,8,16]{2,1,0:T(8,128)S(1)}, s32[1,8,16]{2,1,0:T(8,128)}, u32[]{:S(2)}) copy-start(s32[1,8,16]{2,1,0:T(8,128)} %param.4) | copy-start | bytes 1540
  13.3 0.8 %copy-start.2 = (s32[1,8,16]{2,1,0:T(8,128)S(1)}, s32[1,8,16]{2,1,0:T(8,128)}, u32[]{:S(2)}) copy-start(s32[1,8,16]{2,1,0:T(8,128)} %param.5) | copy-start | bytes 1540
  14.2 10.5 %collective-permute-start.8 = (f32[256,128]{1,0:T(8,128)S(1)}, f32[256,128]{1,0:T(8,128)S(1)}, u32[]{:S(2)}, u32[]{:S(2)}) collective-permute-start(f32[256,128]{1,0:T(8,128)S(1)} %get-tuple-element.13.attr_head), channel_id=1, source_target_pairs={{0,256},{1,257},{2,258},{3,259},{4,260},{5,261},{6,262},{7,263},{8... | collective-permute-start | bytes 393224 | tf_op jit(solution)/shard_map/ppermute | solution.py:229
  14.9 9.8 %collective-permute-start.7 = (f32[256,128]{1,0:T(8,128)S(1)}, f32[256,128]{1,0:T(8,128)S(1)}, u32[]{:S(2)}, u32[]{:S(2)}) collective-permute-start(f32[256,128]{1,0:T(8,128)S(1)} %get-tuple-element.13.attr_head), channel_id=1, source_target_pairs={{0,384},{1,385},{2,386},{3,387},{4,388},{5,389},{6,390},{7,391},{8... | collective-permute-start | bytes 393224 | tf_op jit(solution)/shard_map/ppermute | solution.py:229
  15.6 9.2 %collective-permute-start.6 = (f32[256,128]{1,0:T(8,128)S(1)}, f32[256,128]{1,0:T(8,128)S(1)}, u32[]{:S(2)}, u32[]{:S(2)}) collective-permute-start(f32[256,128]{1,0:T(8,128)S(1)} %get-tuple-element.13.attr_head), channel_id=1, source_target_pairs={{0,128},{1,129},{2,130},{3,131},{4,132},{5,133},{6,134},{7,135},{8... | collective-permute-start | bytes 393224 | tf_op jit(solution)/shard_map/ppermute | solution.py:229
  16.3 6.8 %collective-permute-start.10 = (f32[10,1,256]{2,1,0:T(1,128)S(1)}, f32[10,1,256]{2,1,0:T(1,128)S(1)}, u32[]{:S(2)}, u32[]{:S(2)}) collective-permute-start(f32[10,1,256]{2,1,0:T(1,128)S(1)} %get-tuple-element.31), channel_id=1, source_target_pairs={{33,34},{35,36},{37,38},{65,66},{67,68},{69,70},{97,98},{99,100},{... | collective-permute-start | bytes 30728 | tf_op jit(solution)/shard_map/ppermute | solution.py:200
  16.9 7.8 %collective-permute-start.9 = (f32[10,1,256]{2,1,0:T(1,128)S(1)}, f32[10,1,256]{2,1,0:T(1,128)S(1)}, u32[]{:S(2)}, u32[]{:S(2)}) collective-permute-start(f32[10,1,256]{2,1,0:T(1,128)S(1)} %get-tuple-element.32), channel_id=1, source_target_pairs={{32,33},{34,35},{36,37},{38,39},{64,65},{66,67},{68,69},{70,71},{9... | collective-permute-start | bytes 30728 | tf_op jit(solution)/shard_map/ppermute | solution.py:200
  24.8 4.2 %collective-permute-start.13 = (f32[256,128]{1,0:T(8,128)S(1)}, f32[256,128]{1,0:T(8,128)S(1)}, u32[]{:S(2)}, u32[]{:S(2)}) collective-permute-start(f32[256,128]{1,0:T(8,128)S(1)} %add_select_fusion.held), channel_id=1, source_target_pairs={{0,96},{128,224},{256,352},{384,480},{1,97},{129,225},{257,353},{3... | collective-permute-start | bytes 393224 | tf_op jit(solution)/shard_map/ppermute | solution.py:235
  25.4 10.4 %collective-permute-start.12 = (f32[256,128]{1,0:T(8,128)S(1)}, f32[256,128]{1,0:T(8,128)S(1)}, u32[]{:S(2)}, u32[]{:S(2)}) collective-permute-start(f32[256,128]{1,0:T(8,128)S(1)} %add_select_fusion.held), channel_id=1, source_target_pairs={{0,64},{128,192},{256,320},{384,448},{1,65},{129,193},{257,321},{3... | collective-permute-start | bytes 393224 | tf_op jit(solution)/shard_map/ppermute | solution.py:235
  26.7 9.1 %collective-permute-start.11 = (f32[256,128]{1,0:T(8,128)S(1)}, f32[256,128]{1,0:T(8,128)S(1)}, u32[]{:S(2)}, u32[]{:S(2)}) collective-permute-start(f32[256,128]{1,0:T(8,128)S(1)} %add_select_fusion.held), channel_id=1, source_target_pairs={{0,32},{128,160},{256,288},{384,416},{1,33},{129,161},{257,289},{3... | collective-permute-start | bytes 393224 | tf_op jit(solution)/shard_map/ppermute | solution.py:235

commit v16 on v12

--- a/solution.py
+++ b/solution.py
@@ -12,7 +12,7 @@
 NWIN = 8
 EPS = 1e-06
 
-FANOUT = {0: (3, 2, 1), 4: (7, 6, 5), 8: (11, 10, 9), 12: (15, 14, 13)}
+FANOUT = {0: (2, 3, 1), 4: (6, 7, 5), 8: (10, 11, 9), 12: (14, 15, 13)}
 ROWS = 8
 COLS = 16
 TRACES = ROWS * COLS

time: 37.6 us -> 37.6 us (level)
  the two profiles are of different devices: /device:TPU:152 before, /device:TPU:153 now
where the time goes in v16:
time: 37.6 us; the launch traced here: 37.1 us
  starting transfers between devices  21.3 us (57%)
  waiting for transfers between devices  9.55 us (25%)
  Pallas kernels  2.73 us (7%)
  local copies, waits for them, and re-layouts  1.73 us (5%)
  between operations  0.91 us (2%)
  other arithmetic  0.85 us (2%)
    ppermute x5, starting transfers between devices, swap(): lax.ppermute(sends[n], ('vintage', axis), low + [(b, a) for a, b in low])  14.7 us
    ppermute x3, waiting for transfers between devices, per_device(): lax.ppermute(held, 'vintage', [(s, to[n]) for s, to in FANOUT.items()])  8.49 us
    ppermute x3, starting transfers between devices, per_device(): lax.ppermute(held, 'vintage', [(s, to[n]) for s, to in FANOUT.items()])  2.63 us
    ppermute x3, starting transfers between devices, per_device(): got = [lax.ppermute(attr0, 'vintage', [(0, k)]) for k in (4, 12, 8)]  2.01 us
    pallas_call x2, Pallas kernels, attributes(): pl.pallas_call(kernel, out_shape=(jax.ShapeDtypeStruct((ROWS, COLS, TIME_...  1.53 us
    pallas_call x1, Pallas kernels, correlate(): pl.pallas_call(correl_kernel, out_shape=jax.ShapeDtypeStruct((ROWS, COLS,...  1.2 us
    ppermute x5, waiting for transfers between devices, swap(): lax.ppermute(sends[n], ('vintage', axis), low + [(b, a) for a, b in low])  1.04 us
    slice x1, local copies, waits for them, and re-layouts, per_device(): first, last = edge_columns((tile[:, :1], tile[:, -1:]), rows)  0.89 us
  transfers between devices with their start and end apart: 14, of which 2 were waited for; matrix products, arithmetic and copies ran while one was open for 3% of the time, Pallas kernels for 4%

profile of v16, /device:TPU:153, one launch (start us, length us, event | category | flops | bytes accessed | tf_op | source)
XLA Modules:
  0.0 37.1 jit_solution(9388866127821382352)
XLA Ops:
  0.6 0.7 %select_bitcast_fusion = (f32[1,16,256]{2,1,0:T(8,128)S(1)}, f32[1,16,256]{2,1,0:T(8,128)S(1)}, f32[1,16,256]{2,1,0:T(8,128)S(1)}) fusion(f32[1,8,16,256]{3,2,1,0:T(8,128)} %param.3, pred[]{:T(512)S(6)} %eq.13, pred[]{:T(512)S(6)} %eq.14), kind=kLoop, calls=%fused_computation.4 | loop fusion | flops 12288 | bytes 81922 | tf_op jit(solution)/shard_map/jit(_where)/select_n | solution.py:192
  1.4 0.0 copy-start
  1.4 2.0 %collective-permute-start.2 = (f32[1,16,256]{2,1,0:T(8,128)S(1)}, f32[1,16,256]{2,1,0:T(8,128)S(1)}, u32[]{:S(2)}, u32[]{:S(2)}) collective-permute-start(f32[1,16,256]{2,1,0:T(8,128)S(1)} %get-tuple-element.26), channel_id=1, source_target_pairs={{0,8},{32,40},{64,72},{96,104},{128,136},{160,168},{192,200},{224,... | collective-permute-start | bytes 49160 | tf_op jit(solution)/shard_map/ppermute | solution.py:200
  3.4 5.8 %collective-permute-start = (f32[1,16,256]{2,1,0:T(8,128)S(1)}, f32[1,16,256]{2,1,0:T(8,128)S(1)}, u32[]{:S(2)}, u32[]{:S(2)}) collective-permute-start(f32[1,16,256]{2,1,0:T(8,128)S(1)} %get-tuple-element.27), channel_id=1, source_target_pairs={{8,16},{40,48},{72,80},{104,112},{136,144},{168,176},{200,208},{23... | collective-permute-start | bytes 49160 | tf_op jit(solution)/shard_map/ppermute | solution.py:200
  9.2 0.7 %collective-permute-start.1 = (f32[1,16,256]{2,1,0:T(8,128)S(1)}, f32[1,16,256]{2,1,0:T(8,128)S(1)}, u32[]{:S(2)}, u32[]{:S(2)}) collective-permute-start(f32[1,16,256]{2,1,0:T(8,128)S(1)} %get-tuple-element.28), channel_id=1, source_target_pairs={{16,24},{48,56},{80,88},{112,120},{144,152},{176,184},{208,216},{2... | collective-permute-start | bytes 49160 | tf_op jit(solution)/shard_map/ppermute | solution.py:200
  9.9 0.9 %fusion = (f32[8,1,256]{2,1,0:T(1,128)S(1)}, f32[8,1,256]{2,1,0:T(1,128)S(1)}) fusion(f32[8,16,256]{2,1,0:T(8,128)} %bitcast.9), kind=kLoop, calls=%fused_computation.11 | loop fusion | bytes 32768 | tf_op jit(solution)/shard_map/slice | solution.py:222
  10.8 0.0 collective-permute-done.2.row_01
  10.8 0.0 collective-permute-done.row_12
  10.8 0.0 collective-permute-done.1.row_23
  10.8 0.7 %collective-permute-start.4 = (f32[10,1,256]{2,1,0:T(1,128)S(1)}, f32[10,1,256]{2,1,0:T(1,128)S(1)}, u32[]{:S(2)}, u32[]{:S(2)}) collective-permute-start(f32[10,1,256]{2,1,0:T(1,128)S(1)} %pad_maximum_fusion.2), channel_id=1, source_target_pairs={{1,32},{2,33},{3,34},{4,35},{5,36},{6,37},{7,38},{9,40},{10,41},{1... | collective-permute-start | bytes 30728 | tf_op jit(solution)/shard_map/ppermute | solution.py:226
  11.5 0.7 %collective-permute-start.3 = (f32[10,1,256]{2,1,0:T(1,128)S(1)}, f32[10,1,256]{2,1,0:T(1,128)S(1)}, u32[]{:S(2)}, u32[]{:S(2)}) collective-permute-start(f32[10,1,256]{2,1,0:T(1,128)S(1)} %pad_maximum_fusion.1), channel_id=1, source_target_pairs={{0,33},{1,34},{2,35},{3,36},{4,37},{5,38},{6,39},{8,41},{9,42},{10... | collective-permute-start | bytes 30728 | tf_op jit(solution)/shard_map/ppermute | solution.py:225
  12.2 0.0 collective-permute-done.4
  12.2 0.0 collective-permute-done.3
  12.3 0.7 %collective-permute-start.5 = (f32[20,1,256]{2,1,0:T(1,128)S(1)}, f32[20,1,256]{2,1,0:T(1,128)S(1)}, u32[]{:S(2)}, u32[]{:S(2)}) collective-permute-start(f32[20,1,256]{2,1,0:T(1,128)S(1)} %pad_maximum_fusion), channel_id=1, source_target_pairs={{32,0},{33,1},{34,2},{35,3},{36,4},{37,5},{38,6},{39,7},{40,8},{41... | collective-permute-start | bytes 61448 | tf_op jit(solution)/shard_map/ppermute | solution.py:227
  12.9 0.0 copy-start.1
  12.9 0.0 copy-start.2
  13.0 0.7 %copy-done.1 = s32[1,8,16]{2,1,0:T(8,128)S(1)} copy-done((s32[1,8,16]{2,1,0:T(8,128)S(1)}, s32[1,8,16]{2,1,0:T(8,128)}, u32[]{:S(2)}) %copy-start.1) | copy-done | bytes 536
  13.6 0.1 reshape.78.dip_il
  13.7 0.0 copy-done.2
  13.7 0.1 reshape.79.dip_xl
  13.8 0.0 collective-permute-done.5.cols
  13.8 0.0 copy-done
  13.8 0.7 %collective-permute-start.8 = (f32[256,128]{1,0:T(8,128)S(1)}, f32[256,128]{1,0:T(8,128)S(1)}, u32[]{:S(2)}, u32[]{:S(2)}) collective-permute-start(f32[256,128]{1,0:T(8,128)S(1)} %get-tuple-element.13.attr_head), channel_id=1, source_target_pairs={{0,256},{1,257},{2,258},{3,259},{4,260},{5,261},{6,262},{7,263},{8... | collective-permute-start | bytes 393224 | tf_op jit(solution)/shard_map/ppermute | solution.py:229
  14.5 0.7 %collective-permute-start.7 = (f32[256,128]{1,0:T(8,128)S(1)}, f32[256,128]{1,0:T(8,128)S(1)}, u32[]{:S(2)}, u32[]{:S(2)}) collective-permute-start(f32[256,128]{1,0:T(8,128)S(1)} %get-tuple-element.13.attr_head), channel_id=1, source_target_pairs={{0,384},{1,385},{2,386},{3,387},{4,388},{5,389},{6,390},{7,391},{8... | collective-permute-start | bytes 393224 | tf_op jit(solution)/shard_map/ppermute | solution.py:229
  15.2 0.7 %collective-permute-start.6 = (f32[256,128]{1,0:T(8,128)S(1)}, f32[256,128]{1,0:T(8,128)S(1)}, u32[]{:S(2)}, u32[]{:S(2)}) collective-permute-start(f32[256,128]{1,0:T(8,128)S(1)} %get-tuple-element.13.attr_head), channel_id=1, source_target_pairs={{0,128},{1,129},{2,130},{3,131},{4,132},{5,133},{6,134},{7,135},{8... | collective-permute-start | bytes 393224 | tf_op jit(solution)/shard_map/ppermute | solution.py:229
  15.9 0.7 %collective-permute-start.10 = (f32[10,1,256]{2,1,0:T(1,128)S(1)}, f32[10,1,256]{2,1,0:T(1,128)S(1)}, u32[]{:S(2)}, u32[]{:S(2)}) collective-permute-start(f32[10,1,256]{2,1,0:T(1,128)S(1)} %get-tuple-element.31), channel_id=1, source_target_pairs={{33,34},{35,36},{37,38},{65,66},{67,68},{69,70},{97,98},{99,100},{... | collective-permute-start | bytes 30728 | tf_op jit(solution)/shard_map/ppermute | solution.py:200
  16.5 5.6 %collective-permute-start.9 = (f32[10,1,256]{2,1,0:T(1,128)S(1)}, f32[10,1,256]{2,1,0:T(1,128)S(1)}, u32[]{:S(2)}, u32[]{:S(2)}) collective-permute-start(f32[10,1,256]{2,1,0:T(1,128)S(1)} %get-tuple-element.32), channel_id=1, source_target_pairs={{32,33},{34,35},{36,37},{38,39},{64,65},{66,67},{68,69},{70,71},{9... | collective-permute-start | bytes 30728 | tf_op jit(solution)/shard_map/ppermute | solution.py:200
  22.1 0.0 collective-permute-done.10.col_b
  22.1 1.0 %collective-permute-done.9.col_a = f32[10,1,256]{2,1,0:T(1,128)S(1)} collective-permute-done((f32[10,1,256]{2,1,0:T(1,128)S(1)}, f32[10,1,256]{2,1,0:T(1,128)S(1)}, u32[]{:S(2)}, u32[]{:S(2)}) %collective-permute-start.9) | collective-permute-done | bytes 10272 | tf_op jit(solution)/shard_map/ppermute | solution.py:200
  23.2 0.0 collective-permute-done.8
  23.2 0.0 collective-permute-done.7
  23.2 0.0 collective-permute-done.6
  23.2 0.7 %collective-permute-start.13 = (f32[256,128]{1,0:T(8,128)S(1)}, f32[256,128]{1,0:T(8,128)S(1)}, u32[]{:S(2)}, u32[]{:S(2)}) collective-permute-start(f32[256,128]{1,0:T(8,128)S(1)} %add_select_fusion.held), channel_id=1, source_target_pairs={{0,64},{128,192},{256,320},{384,448},{1,65},{129,193},{257,321},{3... | collective-permute-start | bytes 393224 | tf_op jit(solution)/shard_map/ppermute | solution.py:235
  23.9 1.3 %collective-permute-start.12 = (f32[256,128]{1,0:T(8,128)S(1)}, f32[256,128]{1,0:T(8,128)S(1)}, u32[]{:S(2)}, u32[]{:S(2)}) collective-permute-start(f32[256,128]{1,0:T(8,128)S(1)} %add_select_fusion.held), channel_id=1, source_target_pairs={{0,96},{128,224},{256,352},{384,480},{1,97},{129,225},{257,353},{3... | collective-permute-start | bytes 393224 | tf_op jit(solution)/shard_map/ppermute | solution.py:235
  25.2 0.7 %collective-permute-start.11 = (f32[256,128]{1,0:T(8,128)S(1)}, f32[256,128]{1,0:T(8,128)S(1)}, u32[]{:S(2)}, u32[]{:S(2)}) collective-permute-start(f32[256,128]{1,0:T(8,128)S(1)} %add_select_fusion.held), channel_id=1, source_target_pairs={{0,32},{128,160},{256,288},{384,416},{1,33},{129,161},{257,289},{3... | collective-permute-start | bytes 393224 | tf_op jit(solution)/shard_map/ppermute | solution.py:235
  25.9 1.5 %tail.1 = (f32[8,16,256]{2,1,0:T(8,128)}, f32[256,128]{1,0:T(8,128)S(1)}) custom-call(f32[8,16,256]{2,1,0:T(8,128)S(1)} %bitcast.11, f32[1,16,256]{2,1,0:T(8,128)S(1)} %collective-permute-done.row_12, f32[1,16,256]{2,1,0:T(8,128)S(1)} %collective-permute-done.1.row_23, f32[1,16,256]{2,1,0:T(8,128)S(1)} %collective-permute-done.2.row_01, ...), custom_call_target="tpu_custom_call" | custom-call | tf_op jit(solution)/shard_map/tail/pallas_call | solution.py:155
  27.4 0.0 collective-permute-done.13.far1
  27.4 8.5 %collective-permute-done.12.far2 = f32[256,128]{1,0:T(8,128)S(1)} collective-permute-done((f32[256,128]{1,0:T(8,128)S(1)}, f32[256,128]{1,0:T(8,128)S(1)}, u32[]{:S(2)}, u32[]{:S(2)}) %collective-permute-start.12) | collective-permute-done | bytes 131104 | tf_op jit(solution)/shard_map/ppermute | solution.py:235
  35.9 0.0 collective-permute-done.11.far3
  35.9 1.2 %correlate.1 = f32[8,16,264]{2,1,0:T(8,128)} custom-call(f32[256,128]{1,0:T(8,128)S(1)} %get-tuple-element.20.mon, f32[256,128]{1,0:T(8,128)S(1)} %add_select_fusion.held, f32[256,128]{1,0:T(8,128)S(1)} %collective-permute-done.11.far3, f32[256,128]{1,0:T(8,128)S(1)} %collective-permute-done.12.far2, f32[256,128]{1,0:T(8,128)S(1)} %collective-permute-done.13.far1), custom_call_target="tpu_custom_call" | custom-call | tf_op jit(solution)/shard_map/correlate/pallas_call | solution.py:176
  (8 shorter events, 0.1 us)
Async XLA Ops:
  1.4 12.4 %copy-start = (f32[1,8,16,256]{3,2,1,0:T(8,128)S(1)}, f32[1,8,16,256]{3,2,1,0:T(8,128)}, u32[]{:S(2)}) copy-start(f32[1,8,16,256]{3,2,1,0:T(8,128)} %param.3) | copy-start | bytes 393220
  1.4 9.4 %collective-permute-start.2 = (f32[1,16,256]{2,1,0:T(8,128)S(1)}, f32[1,16,256]{2,1,0:T(8,128)S(1)}, u32[]{:S(2)}, u32[]{:S(2)}) collective-permute-start(f32[1,16,256]{2,1,0:T(8,128)S(1)} %get-tuple-element.26), channel_id=1, source_target_pairs={{0,8},{32,40},{64,72},{96,104},{128,136},{160,168},{192,200},{224,... | collective-permute-start | bytes 49160 | tf_op jit(solution)/shard_map/ppermute | solution.py:200
  3.4 7.3 %collective-permute-start = (f32[1,16,256]{2,1,0:T(8,128)S(1)}, f32[1,16,256]{2,1,0:T(8,128)S(1)}, u32[]{:S(2)}, u32[]{:S(2)}) collective-permute-start(f32[1,16,256]{2,1,0:T(8,128)S(1)} %get-tuple-element.27), channel_id=1, source_target_pairs={{8,16},{40,48},{72,80},{104,112},{136,144},{168,176},{200,208},{23... | collective-permute-start | bytes 49160 | tf_op jit(solution)/shard_map/ppermute | solution.py:200
  9.2 1.6 %collective-permute-start.1 = (f32[1,16,256]{2,1,0:T(8,128)S(1)}, f32[1,16,256]{2,1,0:T(8,128)S(1)}, u32[]{:S(2)}, u32[]{:S(2)}) collective-permute-start(f32[1,16,256]{2,1,0:T(8,128)S(1)} %get-tuple-element.28), channel_id=1, source_target_pairs={{16,24},{48,56},{80,88},{112,120},{144,152},{176,184},{208,216},{2... | collective-permute-start | bytes 49160 | tf_op jit(solution)/shard_map/ppermute | solution.py:200
  10.8 1.4 %collective-permute-start.4 = (f32[10,1,256]{2,1,0:T(1,128)S(1)}, f32[10,1,256]{2,1,0:T(1,128)S(1)}, u32[]{:S(2)}, u32[]{:S(2)}) collective-permute-start(f32[10,1,256]{2,1,0:T(1,128)S(1)} %pad_maximum_fusion.2), channel_id=1, source_target_pairs={{1,32},{2,33},{3,34},{4,35},{5,36},{6,37},{7,38},{9,40},{10,41},{1... | collective-permute-start | bytes 30728 | tf_op jit(solution)/shard_map/ppermute | solution.py:226
  11.5 0.7 %collective-permute-start.3 = (f32[10,1,256]{2,1,0:T(1,128)S(1)}, f32[10,1,256]{2,1,0:T(1,128)S(1)}, u32[]{:S(2)}, u32[]{:S(2)}) collective-permute-start(f32[10,1,256]{2,1,0:T(1,128)S(1)} %pad_maximum_fusion.1), channel_id=1, source_target_pairs={{0,33},{1,34},{2,35},{3,36},{4,37},{5,38},{6,39},{8,41},{9,42},{10... | collective-permute-start | bytes 30728 | tf_op jit(solution)/shard_map/ppermute | solution.py:225
  12.3 1.5 %collective-permute-start.5 = (f32[20,1,256]{2,1,0:T(1,128)S(1)}, f32[20,1,256]{2,1,0:T(1,128)S(1)}, u32[]{:S(2)}, u32[]{:S(2)}) collective-permute-start(f32[20,1,256]{2,1,0:T(1,128)S(1)} %pad_maximum_fusion), channel_id=1, source_target_pairs={{32,0},{33,1},{34,2},{35,3},{36,4},{37,5},{38,6},{39,7},{40,8},{41... | collective-permute-start | bytes 61448 | tf_op jit(solution)/shard_map/ppermute | solution.py:227
  12.9 0.7 %copy-start.1 = (s32[1,8,16]{2,1,0:T(8,128)S(1)}, s32[1,8,16]{2,1,0:T(8,128)}, u32[]{:S(2)}) copy-start(s32[1,8,16]{2,1,0:T(8,128)} %param.4) | copy-start | bytes 1540
  12.9 0.8 %copy-start.2 = (s32[1,8,16]{2,1,0:T(8,128)S(1)}, s32[1,8,16]{2,1,0:T(8,128)}, u32[]{:S(2)}) copy-start(s32[1,8,16]{2,1,0:T(8,128)} %param.5) | copy-start | bytes 1540
  13.8 9.4 %collective-permute-start.8 = (f32[256,128]{1,0:T(8,128)S(1)}, f32[256,128]{1,0:T(8,128)S(1)}, u32[]{:S(2)}, u32[]{:S(2)}) collective-permute-start(f32[256,128]{1,0:T(8,128)S(1)} %get-tuple-element.13.attr_head), channel_id=1, source_target_pairs={{0,256},{1,257},{2,258},{3,259},{4,260},{5,261},{6,262},{7,263},{8... | collective-permute-start | bytes 393224 | tf_op jit(solution)/shard_map/ppermute | solution.py:229
  14.5 8.7 %collective-permute-start.7 = (f32[256,128]{1,0:T(8,128)S(1)}, f32[256,128]{1,0:T(8,128)S(1)}, u32[]{:S(2)}, u32[]{:S(2)}) collective-permute-start(f32[256,128]{1,0:T(8,128)S(1)} %get-tuple-element.13.attr_head), channel_id=1, source_target_pairs={{0,384},{1,385},{2,386},{3,387},{4,388},{5,389},{6,390},{7,391},{8... | collective-permute-start | bytes 393224 | tf_op jit(solution)/shard_map/ppermute | solution.py:229
  15.2 8.0 %collective-permute-start.6 = (f32[256,128]{1,0:T(8,128)S(1)}, f32[256,128]{1,0:T(8,128)S(1)}, u32[]{:S(2)}, u32[]{:S(2)}) collective-permute-start(f32[256,128]{1,0:T(8,128)S(1)} %get-tuple-element.13.attr_head), channel_id=1, source_target_pairs={{0,128},{1,129},{2,130},{3,131},{4,132},{5,133},{6,134},{7,135},{8... | collective-permute-start | bytes 393224 | tf_op jit(solution)/shard_map/ppermute | solution.py:229
  15.9 6.3 %collective-permute-start.10 = (f32[10,1,256]{2,1,0:T(1,128)S(1)}, f32[10,1,256]{2,1,0:T(1,128)S(1)}, u32[]{:S(2)}, u32[]{:S(2)}) collective-permute-start(f32[10,1,256]{2,1,0:T(1,128)S(1)} %get-tuple-element.31), channel_id=1, source_target_pairs={{33,34},{35,36},{37,38},{65,66},{67,68},{69,70},{97,98},{99,100},{... | collective-permute-start | bytes 30728 | tf_op jit(solution)/shard_map/ppermute | solution.py:200
  16.5 6.6 %collective-permute-start.9 = (f32[10,1,256]{2,1,0:T(1,128)S(1)}, f32[10,1,256]{2,1,0:T(1,128)S(1)}, u32[]{:S(2)}, u32[]{:S(2)}) collective-permute-start(f32[10,1,256]{2,1,0:T(1,128)S(1)} %get-tuple-element.32), channel_id=1, source_target_pairs={{32,33},{34,35},{36,37},{38,39},{64,65},{66,67},{68,69},{70,71},{9... | collective-permute-start | bytes 30728 | tf_op jit(solution)/shard_map/ppermute | solution.py:200
  23.2 4.2 %collective-permute-start.13 = (f32[256,128]{1,0:T(8,128)S(1)}, f32[256,128]{1,0:T(8,128)S(1)}, u32[]{:S(2)}, u32[]{:S(2)}) collective-permute-start(f32[256,128]{1,0:T(8,128)S(1)} %add_select_fusion.held), channel_id=1, source_target_pairs={{0,64},{128,192},{256,320},{384,448},{1,65},{129,193},{257,321},{3... | collective-permute-start | bytes 393224 | tf_op jit(solution)/shard_map/ppermute | solution.py:235
  23.9 12.0 %collective-permute-start.12 = (f32[256,128]{1,0:T(8,128)S(1)}, f32[256,128]{1,0:T(8,128)S(1)}, u32[]{:S(2)}, u32[]{:S(2)}) collective-permute-start(f32[256,128]{1,0:T(8,128)S(1)} %add_select_fusion.held), channel_id=1, source_target_pairs={{0,96},{128,224},{256,352},{384,480},{1,97},{129,225},{257,353},{3... | collective-permute-start | bytes 393224 | tf_op jit(solution)/shard_map/ppermute | solution.py:235
  25.2 10.7 %collective-permute-start.11 = (f32[256,128]{1,0:T(8,128)S(1)}, f32[256,128]{1,0:T(8,128)S(1)}, u32[]{:S(2)}, u32[]{:S(2)}) collective-permute-start(f32[256,128]{1,0:T(8,128)S(1)} %add_select_fusion.held), channel_id=1, source_target_pairs={{0,32},{128,160},{256,288},{384,416},{1,33},{129,161},{257,289},{3... | collective-permute-start | bytes 393224 | tf_op jit(solution)/shard_map/ppermute | solution.py:235
